TPU v7x, 32 devices: a whole 2x2x4 slice. The times are simulated.
32 devices in a mesh: expert: 4 (over x, core), node: 8 (over z, y).
Axes of the slice: x: 2, y: 2, z: 4, core: 2. Of those that a mesh axis runs over, the one named last changes fastest.
Arguments:
- tokens: bfloat16 [2, 8192, 1024], P(None, ('expert', 'node')), may hold values from -6 to 6
- routing: int32 [2, 8192], P(None, ('expert', 'node')), may hold values from 0 to 3, as said below
- out_grad: bfloat16 [2, 8192, 512], P(None, ('expert', 'node')), may hold values from -6 to 6
- weights: float32 [8, 4, 1024, 512], P('node', 'expert'), may hold values from -5 to 5
- momentum: float32 [8, 4, 1024, 512], P('node', 'expert'), may hold values from -8 to 8
Outputs:
- new_weights: float32 [8, 4, 1024, 512], P('node', 'expert')
- new_momentum: float32 [8, 4, 1024, 512], P('node', 'expert')
- in_grad: bfloat16 [2, 8192, 1024], P(None, ('expert', 'node'))
Inputs may be any that keep to these rules, and one draw needn't show every extreme that they name: `routing`: within each block of 256 rows of one round (the rows of one device), no expert is named more than 128 times; in every round each node has one expert that is named exactly 128 times in each of that node's blocks.
All inputs are finite; a program needn't handle non-finite values.
Results may differ from a plain program's by a relative error of at most 0.0065.
Values may be sent and summed in bfloat16 or wider, within the bound.
No kernel may reach another device: no remote copies, remote signals or barrier semaphores. Data moves between devices by JAX's collectives and lax.ppermute only.
A program may use at most 64 MiB of HBM per device.

v0:
```python
import math

import jax
import jax.numpy as jnp
from jax import lax
from jax.sharding import PartitionSpec as P

ROUNDS = 2
NS_STEPS = 3


def shifted(block, axis, distance):
    devices = range(lax.axis_size(axis))
    route = [((i - distance) % len(devices), i) for i in devices]
    return lax.ppermute(block, axis, route)


def dispatch_table(route, experts_all, capacity):
    labels = jnp.arange(experts_all, dtype=jnp.int32)
    onehot = (route[:, None] == labels[None, :]).astype(jnp.int32)
    slot_rank = jnp.sum(onehot * (jnp.cumsum(onehot, axis=0) - 1), axis=1)
    target = route * capacity + slot_rank
    slot_ids = jnp.arange(experts_all * capacity, dtype=jnp.int32)
    return (slot_ids[:, None] == target[None, :]).astype(jnp.bfloat16)


def orthogonalize(moment):
    frob_norm = jnp.sqrt(jnp.sum(moment * moment))
    orthog = (moment / (frob_norm + 1e-07)).astype(jnp.bfloat16)
    for sweep in range(NS_STEPS):
        gram_matrix = lax.dot_general(
            orthog, orthog, (((0,), (0,)), ((), ())), preferred_element_type=jnp.float32
        ).astype(jnp.bfloat16)
        square = jnp.dot(gram_matrix, gram_matrix, preferred_element_type=jnp.float32)
        polynom = (-4.775 * gram_matrix.astype(jnp.float32) + 2.0315 * square).astype(jnp.bfloat16)
        orthog = (
            3.4445 * orthog.astype(jnp.float32)
            + jnp.dot(orthog, polynom, preferred_element_type=jnp.float32)
        ).astype(jnp.bfloat16)
    return orthog


def on_device(tokens, routing, out_grad, weights, momentum):
    row_count = tokens.shape[1]
    model_width = tokens.shape[2]
    hidden_width = out_grad.shape[2]
    capacity = row_count // 2
    experts_all = weights.shape[1] * lax.axis_size("expert")
    factor = 1.0 / math.sqrt(model_width)
    step_size = 0.1 * math.sqrt(model_width)
    weight = weights[0, 0]
    moment = momentum[0, 0]
    tables = []
    sent_rows = []
    sent_grads = []
    for round_index in range(ROUNDS):
        dispatch = dispatch_table(routing[round_index], experts_all, capacity)
        tables.append(dispatch)
        sent_rows.append(
            jnp.dot(dispatch, tokens[round_index], preferred_element_type=jnp.float32)
            .astype(jnp.bfloat16)
            .reshape(experts_all, capacity, model_width)
        )
        sent_grads.append(
            jnp.dot(dispatch, out_grad[round_index], preferred_element_type=jnp.float32)
            .astype(jnp.bfloat16)
            .reshape(experts_all, capacity, hidden_width)
        )
    in_grads = []
    for round_index in range(ROUNDS):
        got_rows, got_grads = (
            lax.all_to_all(
                sent_rows[round_index], "expert", split_axis=0, concat_axis=0, tiled=True
            ),
            lax.all_to_all(
                sent_grads[round_index], "expert", split_axis=0, concat_axis=0, tiled=True
            ),
        )
        got_rows = got_rows.reshape(-1, model_width)
        got_grads = got_grads.reshape(-1, hidden_width)
        shaped = weight.astype(jnp.bfloat16)
        preact = jnp.dot(got_rows, shaped, preferred_element_type=jnp.float32) * factor
        slopes = (got_grads.astype(jnp.float32) * 2.0 * jnp.maximum(preact, 0.0)).astype(
            jnp.bfloat16
        )
        backward = (
            lax.dot_general(
                slopes, shaped, (((1,), (1,)), ((), ())), preferred_element_type=jnp.float32
            )
            * factor
        )
        backward = backward.astype(jnp.bfloat16).reshape(-1, capacity, model_width)
        grad_w = (
            lax.dot_general(
                got_rows, slopes, (((0,), (0,)), ((), ())), preferred_element_type=jnp.float32
            )
            * factor
        )
        returned = lax.all_to_all(
            backward, "expert", split_axis=0, concat_axis=0, tiled=True
        ).reshape(-1, model_width)
        in_grads.append(
            lax.dot_general(
                tables[round_index],
                returned,
                (((0,), (0,)), ((), ())),
                preferred_element_type=jnp.float32,
            ).astype(jnp.bfloat16)
        )
        moment = 0.9 * moment + grad_w
        orthog = orthogonalize(moment)
        stepped = weight - step_size * orthog.astype(jnp.float32)
        shared = stepped.astype(jnp.bfloat16)
        near_left = shifted(shared, "node", 1)
        near_right = shifted(shared, "node", -1)
        far_left = shifted(shared, "node", 2)
        far_right = shifted(shared, "node", -2)
        neighbours = near_left.astype(jnp.float32) + near_right.astype(jnp.float32)
        neighbours = neighbours + far_left.astype(jnp.float32) + far_right.astype(jnp.float32)
        weight = 0.4 * stepped + 0.15 * neighbours
    return (weight[None, None], moment[None, None], jnp.stack(in_grads))


def solution(mesh):
    return jax.shard_map(
        on_device,
        mesh=mesh,
        in_specs=(
            P(None, ("expert", "node"), None),
            P(None, ("expert", "node")),
            P(None, ("expert", "node"), None),
            P("node", "expert", None, None),
            P("node", "expert", None, None),
        ),
        out_specs=(
            P("node", "expert", None, None),
            P("node", "expert", None, None),
            P(None, ("expert", "node"), None),
        ),
        check_vma=False,
    )
```

profile of v0, /device:TPU:0, one launch (start us, length us, event | category | flops | bytes accessed | tf_op | source)
XLA Modules:
  0.0 252.5 jit_solution(7411990706743633536)
XLA Ops:
  7.5 4.2 %all-to-all-start.1 = ((bf16[4,128,512]{2,1,0:T(8,128)(2,1)}), bf16[4,128,512]{2,1,0:T(8,128)(2,1)S(1)}, u32[]{:S(2)}, u32[]{:S(2)}) async-start(bf16[4,128,512]{2,1,0:T(8,128)(2,1)} %bitcast.12), calls=%async_computation.1 | async-start | bytes 1048576 | tf_op jit(solution)/shard_map/all_to_all | solution.py:75
  13.2 7.4 %all-to-all-done.1 = bf16[4,128,512]{2,1,0:T(8,128)(2,1)S(1)} async-done(((bf16[4,128,512]{2,1,0:T(8,128)(2,1)}), bf16[4,128,512]{2,1,0:T(8,128)(2,1)S(1)}, u32[]{:S(2)}, u32[]{:S(2)}) %all-to-all-start.1) | async-done | bytes 524320 | tf_op jit(solution)/shard_map/all_to_all | solution.py:75
  21.4 3.5 %all-to-all-start = ((bf16[4,128,1024]{2,1,0:T(8,128)(2,1)}), bf16[4,128,1024]{2,1,0:T(8,128)(2,1)S(1)}, u32[]{:S(2)}, u32[]{:S(2)}) async-start(bf16[4,128,1024]{2,1,0:T(8,128)(2,1)} %bitcast.128), calls=%async_computation | async-start | bytes 2097152 | tf_op jit(solution)/shard_map/all_to_all | solution.py:72
  27.1 12.2 %all-to-all-done = bf16[4,128,1024]{2,1,0:T(8,128)(2,1)S(1)} async-done(((bf16[4,128,1024]{2,1,0:T(8,128)(2,1)}), bf16[4,128,1024]{2,1,0:T(8,128)(2,1)S(1)}, u32[]{:S(2)}, u32[]{:S(2)}) %all-to-all-start) | async-done | bytes 1048608 | tf_op jit(solution)/shard_map/all_to_all | solution.py:72
  41.4 2.7 %multiply_reduce_fusion.1 = (f32[]{:T(128)}, f32[1024,512]{1,0:T(8,128)}) fusion(bf16[512,1024]{1,0:T(8,128)(2,1)S(1)} %bitcast.124, bf16[512,512]{1,0:T(8,128)(2,1)S(1)} %fusion.17, f32[1,1,1024,512]{3,2,1,0:T(8,128)S(1)} %copy-done.7), kind=kOutput, calls=%fused_computation.18 | convolution fusion | flops 539492352 | bytes 5767172 | tf_op jit(solution)/shard_map/dot_general | solution.py:94
  44.8 3.8 %convolution_convert_fusion.11 = bf16[512,512]{1,0:T(8,128)(2,1)} fusion(f32[1024,512]{1,0:T(8,128)} %get-tuple-element.8, f32[]{:T(128)S(6)} %add.88), kind=kOutput, calls=%fused_computation.56 | convolution fusion | flops 538181632 | bytes 2621444 | tf_op jit(solution)/shard_map/dot_general | solution.py:31
  48.6 4.1 %add_convert_fusion.5 = bf16[1024,512]{1,0:T(8,128)(2,1)S(1)} fusion(bf16[512,512]{1,0:T(8,128)(2,1)} %convolution_convert_fusion.11, f32[1024,512]{1,0:T(8,128)} %get-tuple-element.8, f32[]{:T(128)S(6)} %add.88), kind=kOutput, calls=%fused_computation.16 | convolution fusion | flops 810811392 | bytes 3670020 | tf_op jit(solution)/shard_map/dot_general | solution.py:38
  54.2 3.5 %add_convert_fusion.4 = bf16[1024,512]{1,0:T(8,128)(2,1)} fusion(bf16[1024,512]{1,0:T(8,128)(2,1)S(1)} %add_convert_fusion.5, bf16[512,512]{1,0:T(8,128)(2,1)} %convolution_convert_fusion.10), kind=kOutput, calls=%fused_computation.15 | convolution fusion | flops 808714240 | bytes 2621440 | tf_op jit(solution)/shard_map/dot_general | solution.py:38
  60.0 4.4 %fusion.80 = (bf16[1024,512]{1,0:T(8,128)(2,1)}, f32[1024,512]{1,0:T(8,128)}) fusion(bf16[1024,512]{1,0:T(8,128)(2,1)} %add_convert_fusion.4, bf16[512,512]{1,0:T(8,128)(2,1)S(1)} %convolution_convert_fusion.9, f32[1,1,1024,512]{3,2,1,0:T(8,128)S(1)} %copy-done), kind=kOutput, calls=%fused_computation.133 | convolution fusion | flops 810811392 | bytes 6815744 | tf_op jit(solution)/shard_map/dot_general | solution.py:38
  66.6 3.0 %collective-permute-start.1 = (bf16[1024,512]{1,0:T(8,128)(2,1)}, bf16[1024,512]{1,0:T(8,128)(2,1)}, u32[]{:S(2)}, u32[]{:S(2)}) collective-permute-start(bf16[1024,512]{1,0:T(8,128)(2,1)} %get-tuple-element.9), channel_id=1, source_target_pairs={{1,0},{2,1},{3,2},{4,3},{5,4},{6,5},{7,6},{0,7},{9,8},{10,9},{11,1... | collective-permute-start | bytes 3145736 | tf_op jit(solution)/shard_map/ppermute | solution.py:15
  69.7 3.8 %collective-permute-start.3 = (bf16[1024,512]{1,0:T(8,128)(2,1)}, bf16[1024,512]{1,0:T(8,128)(2,1)}, u32[]{:S(2)}, u32[]{:S(2)}) collective-permute-start(bf16[1024,512]{1,0:T(8,128)(2,1)} %get-tuple-element.9), channel_id=1, source_target_pairs={{2,0},{3,1},{4,2},{5,3},{6,4},{7,5},{0,6},{1,7},{10,8},{11,9},{12,... | collective-permute-start | bytes 3145736 | tf_op jit(solution)/shard_map/ppermute | solution.py:15
  74.6 3.5 %all-to-all-start.3 = ((bf16[4,128,512]{2,1,0:T(8,128)(2,1)}), bf16[4,128,512]{2,1,0:T(8,128)(2,1)S(1)}, u32[]{:S(2)}, u32[]{:S(2)}) async-start(bf16[4,128,512]{2,1,0:T(8,128)(2,1)} %bitcast.25), calls=%async_computation.3 | async-start | bytes 1048576 | tf_op jit(solution)/shard_map/all_to_all | solution.py:75
  80.6 6.3 %all-to-all-done.3 = bf16[4,128,512]{2,1,0:T(8,128)(2,1)S(1)} async-done(((bf16[4,128,512]{2,1,0:T(8,128)(2,1)}), bf16[4,128,512]{2,1,0:T(8,128)(2,1)S(1)}, u32[]{:S(2)}, u32[]{:S(2)}) %all-to-all-start.3) | async-done | bytes 524320 | tf_op jit(solution)/shard_map/all_to_all | solution.py:75
  87.7 3.5 %all-to-all-start.2 = ((bf16[4,128,1024]{2,1,0:T(8,128)(2,1)}), bf16[4,128,1024]{2,1,0:T(8,128)(2,1)S(1)}, u32[]{:S(2)}, u32[]{:S(2)}) async-start(bf16[4,128,1024]{2,1,0:T(8,128)(2,1)} %bitcast.127), calls=%async_computation.2 | async-start | bytes 2097152 | tf_op jit(solution)/shard_map/all_to_all | solution.py:72
  93.4 2.9 %multiply_convert_fusion.1 = bf16[512,1024]{1,0:T(8,128)(2,1)} fusion(bf16[512,512]{1,0:T(8,128)(2,1)} %copy-done.4, f32[1,1,1024,512]{3,2,1,0:T(8,128)S(1)} %copy-done), kind=kOutput, calls=%fused_computation.4 | convolution fusion | flops 537919488 | bytes 3670016 | tf_op jit(solution)/shard_map/dot_general | solution.py:87
  96.4 15.2 %collective-permute-done = bf16[1024,512]{1,0:T(8,128)(2,1)} collective-permute-done((bf16[1024,512]{1,0:T(8,128)(2,1)}, bf16[1024,512]{1,0:T(8,128)(2,1)}, u32[]{:S(2)}, u32[]{:S(2)}) %collective-permute-start) | collective-permute-done | bytes 1048608 | tf_op jit(solution)/shard_map/ppermute | solution.py:15
  113.7 4.7 %collective-permute-done.2 = bf16[1024,512]{1,0:T(8,128)(2,1)} collective-permute-done((bf16[1024,512]{1,0:T(8,128)(2,1)}, bf16[1024,512]{1,0:T(8,128)(2,1)}, u32[]{:S(2)}, u32[]{:S(2)}) %collective-permute-start.2) | collective-permute-done | bytes 1048608 | tf_op jit(solution)/shard_map/ppermute | solution.py:15
  118.5 18.7 %collective-permute-done.3 = bf16[1024,512]{1,0:T(8,128)(2,1)} collective-permute-done((bf16[1024,512]{1,0:T(8,128)(2,1)}, bf16[1024,512]{1,0:T(8,128)(2,1)}, u32[]{:S(2)}, u32[]{:S(2)}) %collective-permute-start.3) | collective-permute-done | bytes 1048608 | tf_op jit(solution)/shard_map/ppermute | solution.py:15
  137.2 2.9 %multiply_add_fusion.1 = f32[1024,512]{1,0:T(8,128)S(1)} fusion(bf16[1024,512]{1,0:T(8,128)(2,1)} %collective-permute-done.3, bf16[1024,512]{1,0:T(8,128)(2,1)} %collective-permute-done.2, bf16[1024,512]{1,0:T(8,128)(2,1)} %collective-permute-done.1, bf16[1024,512]{1,0:T(8,128)(2,1)} %collective-permute-done, f32[1024,512]{1,0:T(8,128)S(1)} %copy-done.2), kind=kLoop, calls=%fused_computation.13 | loop fusion | flops 5242880 | bytes 8388608 | tf_op jit(solution)/shard_map/add | solution.py:120
  140.1 4.4 %all-to-all-start.4 = ((bf16[4,128,1024]{2,1,0:T(8,128)(2,1)}), bf16[4,128,1024]{2,1,0:T(8,128)(2,1)}, u32[]{:S(2)}, u32[]{:S(2)}) async-start(bf16[4,128,1024]{2,1,0:T(8,128)(2,1)} %bitcast.125), calls=%async_computation.4 | async-start | bytes 2097152 | tf_op jit(solution)/shard_map/all_to_all | solution.py:99
  146.7 2.7 %multiply_reduce_fusion = (f32[]{:T(128)}, f32[1024,512]{1,0:T(8,128)}) fusion(bf16[512,1024]{1,0:T(8,128)(2,1)S(1)} %bitcast.122, bf16[512,512]{1,0:T(8,128)(2,1)S(1)} %fusion.16, f32[1024,512]{1,0:T(8,128)S(1)} %copy-done.1), kind=kOutput, calls=%fused_computation.11 | convolution fusion | flops 539492352 | bytes 5767172 | tf_op jit(solution)/shard_map/dot_general | solution.py:94
  150.1 3.8 %convolution_convert_fusion.8 = bf16[512,512]{1,0:T(8,128)(2,1)} fusion(f32[1024,512]{1,0:T(8,128)} %get-tuple-element.12, f32[]{:T(128)S(6)} %add.101), kind=kOutput, calls=%fused_computation.53 | convolution fusion | flops 538181632 | bytes 2621444 | tf_op jit(solution)/shard_map/dot_general | solution.py:31
  153.9 3.8 %add_convert_fusion.2 = bf16[1024,512]{1,0:T(8,128)(2,1)S(1)} fusion(bf16[512,512]{1,0:T(8,128)(2,1)} %convolution_convert_fusion.8, f32[1024,512]{1,0:T(8,128)} %get-tuple-element.12, f32[]{:T(128)S(6)} %add.101), kind=kOutput, calls=%fused_computation.9 | convolution fusion | flops 810811392 | bytes 3670020 | tf_op jit(solution)/shard_map/dot_general | solution.py:38
  160.2 3.3 %add_convert_fusion.1 = bf16[1024,512]{1,0:T(8,128)(2,1)S(1)} fusion(bf16[1024,512]{1,0:T(8,128)(2,1)} %copy-done.13, bf16[512,512]{1,0:T(8,128)(2,1)} %convolution_convert_fusion.7), kind=kOutput, calls=%fused_computation.8 | convolution fusion | flops 808714240 | bytes 2621440 | tf_op jit(solution)/shard_map/dot_general | solution.py:38
  166.8 3.5 %all-to-all-start.5 = ((bf16[4,128,1024]{2,1,0:T(8,128)(2,1)}), bf16[4,128,1024]{2,1,0:T(8,128)(2,1)S(1)}, u32[]{:S(2)}, u32[]{:S(2)}) async-start(bf16[4,128,1024]{2,1,0:T(8,128)(2,1)} %bitcast.32), calls=%async_computation.5 | async-start | bytes 2097152 | tf_op jit(solution)/shard_map/all_to_all | solution.py:99
  170.3 4.9 %fusion.81 = (bf16[1024,512]{1,0:T(8,128)(2,1)}, f32[1024,512]{1,0:T(8,128)}) fusion(f32[1024,512]{1,0:T(8,128)S(1)} %multiply_add_fusion.1, bf16[1024,512]{1,0:T(8,128)(2,1)} %copy-done.10, bf16[512,512]{1,0:T(8,128)(2,1)} %convolution_convert_fusion.6), kind=kOutput, calls=%fused_computation.134 | convolution fusion | flops 810811392 | bytes 6815744 | tf_op jit(solution)/shard_map/dot_general | solution.py:38
  176.4 3.6 %collective-permute-start.5 = (bf16[1024,512]{1,0:T(8,128)(2,1)}, bf16[1024,512]{1,0:T(8,128)(2,1)}, u32[]{:S(2)}, u32[]{:S(2)}) collective-permute-start(bf16[1024,512]{1,0:T(8,128)(2,1)} %get-tuple-element.13), channel_id=1, source_target_pairs={{1,0},{2,1},{3,2},{4,3},{5,4},{6,5},{7,6},{0,7},{9,8},{10,9},{11,1... | collective-permute-start | bytes 3145736 | tf_op jit(solution)/shard_map/ppermute | solution.py:15
  180.0 3.8 %collective-permute-start.7 = (bf16[1024,512]{1,0:T(8,128)(2,1)}, bf16[1024,512]{1,0:T(8,128)(2,1)}, u32[]{:S(2)}, u32[]{:S(2)}) collective-permute-start(bf16[1024,512]{1,0:T(8,128)(2,1)} %get-tuple-element.13), channel_id=1, source_target_pairs={{2,0},{3,1},{4,2},{5,3},{6,4},{7,5},{0,6},{1,7},{10,8},{11,9},{12,... | collective-permute-start | bytes 3145736 | tf_op jit(solution)/shard_map/ppermute | solution.py:15
  189.0 33.2 %collective-permute-done.4 = bf16[1024,512]{1,0:T(8,128)(2,1)} collective-permute-done((bf16[1024,512]{1,0:T(8,128)(2,1)}, bf16[1024,512]{1,0:T(8,128)(2,1)}, u32[]{:S(2)}, u32[]{:S(2)}) %collective-permute-start.4) | collective-permute-done | bytes 1048608 | tf_op jit(solution)/shard_map/ppermute | solution.py:15
  224.6 4.6 %collective-permute-done.6 = bf16[1024,512]{1,0:T(8,128)(2,1)} collective-permute-done((bf16[1024,512]{1,0:T(8,128)(2,1)}, bf16[1024,512]{1,0:T(8,128)(2,1)}, u32[]{:S(2)}, u32[]{:S(2)}) %collective-permute-start.6) | collective-permute-done | bytes 1048608 | tf_op jit(solution)/shard_map/ppermute | solution.py:15
  229.2 19.1 %collective-permute-done.7 = bf16[1024,512]{1,0:T(8,128)(2,1)} collective-permute-done((bf16[1024,512]{1,0:T(8,128)(2,1)}, bf16[1024,512]{1,0:T(8,128)(2,1)}, u32[]{:S(2)}, u32[]{:S(2)}) %collective-permute-start.7) | collective-permute-done | bytes 1048608 | tf_op jit(solution)/shard_map/ppermute | solution.py:15
  248.3 4.2 %add_bitcast_fusion = f32[1,1,1024,512]{3,2,1,0:T(8,128)} fusion(bf16[1024,512]{1,0:T(8,128)(2,1)} %collective-permute-done.7, bf16[1024,512]{1,0:T(8,128)(2,1)} %collective-permute-done.6, bf16[1024,512]{1,0:T(8,128)(2,1)} %collective-permute-done.5, bf16[1024,512]{1,0:T(8,128)(2,1)} %collective-permute-done.4, f32[1024,512]{1,0:T(8,128)S(1)} %copy-done.3), kind=kLoop, calls=%fused_computation.5 | loop fusion | flops 5242880 | bytes 8388608 | tf_op jit(solution)/shard_map/broadcast_in_dim | solution.py:121
  (73 shorter events, 44.9 us)
Async XLA Ops:
  0.6 11.1 %copy-start.11 = (bf16[2,256,1024]{2,1,0:T(8,128)(2,1)S(1)}, bf16[2,256,1024]{2,1,0:T(8,128)(2,1)}, u32[]{:S(2)}) copy-start(bf16[2,256,1024]{2,1,0:T(8,128)(2,1)} %param.5) | copy-start | bytes 3145732
  7.5 13.1 %all-to-all-start.1 = ((bf16[4,128,512]{2,1,0:T(8,128)(2,1)}), bf16[4,128,512]{2,1,0:T(8,128)(2,1)S(1)}, u32[]{:S(2)}, u32[]{:S(2)}) async-start(bf16[4,128,512]{2,1,0:T(8,128)(2,1)} %bitcast.12), calls=%async_computation.1 | async-start | bytes 1048576 | tf_op jit(solution)/shard_map/all_to_all | solution.py:75
  13.2 26.1 %copy-start = (f32[1,1,1024,512]{3,2,1,0:T(8,128)S(1)}, f32[1,1,1024,512]{3,2,1,0:T(8,128)}, u32[]{:S(2)}) copy-start(f32[1,1,1024,512]{3,2,1,0:T(8,128)} %param.8) | copy-start | bytes 6291460
  20.6 0.8 copy-start.8
  21.4 17.9 %all-to-all-start = ((bf16[4,128,1024]{2,1,0:T(8,128)(2,1)}), bf16[4,128,1024]{2,1,0:T(8,128)(2,1)S(1)}, u32[]{:S(2)}, u32[]{:S(2)}) async-start(bf16[4,128,1024]{2,1,0:T(8,128)(2,1)} %bitcast.128), calls=%async_computation | async-start | bytes 2097152 | tf_op jit(solution)/shard_map/all_to_all | solution.py:72
  39.3 2.1 copy-start.7
  41.4 2.7 %copy-start.4 = (bf16[512,512]{1,0:T(8,128)(2,1)}, bf16[512,512]{1,0:T(8,128)(2,1)S(1)}, u32[]{:S(2)}) copy-start(bf16[512,512]{1,0:T(8,128)(2,1)S(1)} %fusion.17) | copy-start | bytes 1572868
  60.0 13.5 %copy-start.12 = (bf16[2,256,512]{2,1,0:T(8,128)(2,1)S(1)}, bf16[2,256,512]{2,1,0:T(8,128)(2,1)}, u32[]{:S(2)}) copy-start(bf16[2,256,512]{2,1,0:T(8,128)(2,1)} %param.7) | copy-start | bytes 1572868
  64.4 47.1 %collective-permute-start = (bf16[1024,512]{1,0:T(8,128)(2,1)}, bf16[1024,512]{1,0:T(8,128)(2,1)}, u32[]{:S(2)}, u32[]{:S(2)}) collective-permute-start(bf16[1024,512]{1,0:T(8,128)(2,1)} %get-tuple-element.9), channel_id=1, source_target_pairs={{7,0},{0,1},{1,2},{2,3},{3,4},{4,5},{5,6},{6,7},{15,8},{8,9},{9,10... | collective-permute-start | bytes 3145736 | tf_op jit(solution)/shard_map/ppermute | solution.py:15
  66.6 47.1 %collective-permute-start.1 = (bf16[1024,512]{1,0:T(8,128)(2,1)}, bf16[1024,512]{1,0:T(8,128)(2,1)}, u32[]{:S(2)}, u32[]{:S(2)}) collective-permute-start(bf16[1024,512]{1,0:T(8,128)(2,1)} %get-tuple-element.9), channel_id=1, source_target_pairs={{1,0},{2,1},{3,2},{4,3},{5,4},{6,5},{7,6},{0,7},{9,8},{10,9},{11,1... | collective-permute-start | bytes 3145736 | tf_op jit(solution)/shard_map/ppermute | solution.py:15
  69.7 48.8 %collective-permute-start.2 = (bf16[1024,512]{1,0:T(8,128)(2,1)}, bf16[1024,512]{1,0:T(8,128)(2,1)}, u32[]{:S(2)}, u32[]{:S(2)}) collective-permute-start(bf16[1024,512]{1,0:T(8,128)(2,1)} %get-tuple-element.9), channel_id=1, source_target_pairs={{6,0},{7,1},{0,2},{1,3},{2,4},{3,5},{4,6},{5,7},{14,8},{15,9},{8,1... | collective-permute-start | bytes 3145736 | tf_op jit(solution)/shard_map/ppermute | solution.py:15
  69.7 67.5 %collective-permute-start.3 = (bf16[1024,512]{1,0:T(8,128)(2,1)}, bf16[1024,512]{1,0:T(8,128)(2,1)}, u32[]{:S(2)}, u32[]{:S(2)}) collective-permute-start(bf16[1024,512]{1,0:T(8,128)(2,1)} %get-tuple-element.9), channel_id=1, source_target_pairs={{2,0},{3,1},{4,2},{5,3},{6,4},{7,5},{0,6},{1,7},{10,8},{11,9},{12,... | collective-permute-start | bytes 3145736 | tf_op jit(solution)/shard_map/ppermute | solution.py:15
  74.6 12.3 %all-to-all-start.3 = ((bf16[4,128,512]{2,1,0:T(8,128)(2,1)}), bf16[4,128,512]{2,1,0:T(8,128)(2,1)S(1)}, u32[]{:S(2)}, u32[]{:S(2)}) async-start(bf16[4,128,512]{2,1,0:T(8,128)(2,1)} %bitcast.25), calls=%async_computation.3 | async-start | bytes 1048576 | tf_op jit(solution)/shard_map/all_to_all | solution.py:75
  86.9 0.8 copy-start.9
  87.7 52.4 %all-to-all-start.2 = ((bf16[4,128,1024]{2,1,0:T(8,128)(2,1)}), bf16[4,128,1024]{2,1,0:T(8,128)(2,1)S(1)}, u32[]{:S(2)}, u32[]{:S(2)}) async-start(bf16[4,128,1024]{2,1,0:T(8,128)(2,1)} %bitcast.127), calls=%async_computation.2 | async-start | bytes 2097152 | tf_op jit(solution)/shard_map/all_to_all | solution.py:72
  93.4 43.8 %copy-start.2 = (f32[1024,512]{1,0:T(8,128)S(1)}, f32[1024,512]{1,0:T(8,128)}, u32[]{:S(2)}) copy-start(f32[1024,512]{1,0:T(8,128)} %get-tuple-element.10) | copy-start | bytes 6291460
  140.1 26.6 %all-to-all-start.4 = ((bf16[4,128,1024]{2,1,0:T(8,128)(2,1)}), bf16[4,128,1024]{2,1,0:T(8,128)(2,1)}, u32[]{:S(2)}, u32[]{:S(2)}) async-start(bf16[4,128,1024]{2,1,0:T(8,128)(2,1)} %bitcast.125), calls=%async_computation.4 | async-start | bytes 2097152 | tf_op jit(solution)/shard_map/all_to_all | solution.py:99
  144.6 2.1 copy-start.1
  146.7 2.7 %copy-start.5 = (bf16[512,512]{1,0:T(8,128)(2,1)}, bf16[512,512]{1,0:T(8,128)(2,1)S(1)}, u32[]{:S(2)}) copy-start(bf16[512,512]{1,0:T(8,128)(2,1)S(1)} %fusion.16) | copy-start | bytes 1572868
  157.7 1.0 copy-start.13
  163.5 1.6 copy-start.10
  163.5 1.5 copy-start.6
  166.8 19.5 %all-to-all-start.5 = ((bf16[4,128,1024]{2,1,0:T(8,128)(2,1)}), bf16[4,128,1024]{2,1,0:T(8,128)(2,1)S(1)}, u32[]{:S(2)}, u32[]{:S(2)}) async-start(bf16[4,128,1024]{2,1,0:T(8,128)(2,1)} %bitcast.32), calls=%async_computation.5 | async-start | bytes 2097152 | tf_op jit(solution)/shard_map/all_to_all | solution.py:99
  175.2 47.0 %collective-permute-start.4 = (bf16[1024,512]{1,0:T(8,128)(2,1)}, bf16[1024,512]{1,0:T(8,128)(2,1)}, u32[]{:S(2)}, u32[]{:S(2)}) collective-permute-start(bf16[1024,512]{1,0:T(8,128)(2,1)} %get-tuple-element.13), channel_id=1, source_target_pairs={{7,0},{0,1},{1,2},{2,3},{3,4},{4,5},{5,6},{6,7},{15,8},{8,9},{9,10... | collective-permute-start | bytes 3145736 | tf_op jit(solution)/shard_map/ppermute | solution.py:15
  176.4 48.2 %collective-permute-start.5 = (bf16[1024,512]{1,0:T(8,128)(2,1)}, bf16[1024,512]{1,0:T(8,128)(2,1)}, u32[]{:S(2)}, u32[]{:S(2)}) collective-permute-start(bf16[1024,512]{1,0:T(8,128)(2,1)} %get-tuple-element.13), channel_id=1, source_target_pairs={{1,0},{2,1},{3,2},{4,3},{5,4},{6,5},{7,6},{0,7},{9,8},{10,9},{11,1... | collective-permute-start | bytes 3145736 | tf_op jit(solution)/shard_map/ppermute | solution.py:15
  180.0 49.3 %collective-permute-start.6 = (bf16[1024,512]{1,0:T(8,128)(2,1)}, bf16[1024,512]{1,0:T(8,128)(2,1)}, u32[]{:S(2)}, u32[]{:S(2)}) collective-permute-start(bf16[1024,512]{1,0:T(8,128)(2,1)} %get-tuple-element.13), channel_id=1, source_target_pairs={{6,0},{7,1},{0,2},{1,3},{2,4},{3,5},{4,6},{5,7},{14,8},{15,9},{8,1... | collective-permute-start | bytes 3145736 | tf_op jit(solution)/shard_map/ppermute | solution.py:15
  180.0 68.3 %collective-permute-start.7 = (bf16[1024,512]{1,0:T(8,128)(2,1)}, bf16[1024,512]{1,0:T(8,128)(2,1)}, u32[]{:S(2)}, u32[]{:S(2)}) collective-permute-start(bf16[1024,512]{1,0:T(8,128)(2,1)} %get-tuple-element.13), channel_id=1, source_target_pairs={{2,0},{3,1},{4,2},{5,3},{6,4},{7,5},{0,6},{1,7},{10,8},{11,9},{12,... | collective-permute-start | bytes 3145736 | tf_op jit(solution)/shard_map/ppermute | solution.py:15
  186.3 62.0 %copy-start.3 = (f32[1024,512]{1,0:T(8,128)S(1)}, f32[1024,512]{1,0:T(8,128)}, u32[]{:S(2)}) copy-start(f32[1024,512]{1,0:T(8,128)} %get-tuple-element.14) | copy-start | bytes 6291460
where the time goes:
time: 253 us
  waiting for transfers between devices  126 us (50%)
  matrix products  62.8 us (25%)
  starting transfers between devices  40.3 us (16%)
  other arithmetic  17.2 us (7%)
  local copies, waits for them, and re-layouts  3.98 us (2%)
    ppermute x8, waiting for transfers between devices, shifted(): return lax.ppermute(block, axis, route)  100 us
    dot_general x6, matrix products, orthogonalize(): jnp.dot(orthog, polynom, preferred_element_type=jnp.float32)  24 us
    ppermute x8, starting transfers between devices, shifted(): return lax.ppermute(block, axis, route)  17.6 us
    dot_general x6, matrix products, orthogonalize(): lax.dot_general(orthog, orthog, (((0,), (0,)), ((), ())), preferred_eleme...  14.4 us
    all_to_all x2, waiting for transfers between devices, on_device(): lax.all_to_all(sent_grads[round_index], 'expert', split_axis=0, concat_ax...  13.7 us
    all_to_all x2, waiting for transfers between devices, on_device(): lax.all_to_all(sent_rows[round_index], 'expert', split_axis=0, concat_axi...  12.2 us
    all_to_all x2, starting transfers between devices, on_device(): lax.all_to_all(backward, 'expert', split_axis=0, concat_axis=0, tiled=True)  7.95 us
    all_to_all x2, starting transfers between devices, on_device(): lax.all_to_all(sent_grads[round_index], 'expert', split_axis=0, concat_ax...  7.71 us
  transfers between devices with their start and end apart: 14, of which 11 were waited for; matrix products, arithmetic and copies ran while one was open for 18% of the time, Pallas kernels for 0%

commit v1 on v0

v1 whole, which is shorter than its diff:
```python
import math

import jax
import jax.numpy as jnp
from jax import lax
from jax.experimental import pallas as pl
from jax.experimental.pallas import tpu as pltpu
from jax.sharding import PartitionSpec as P

ROUNDS = 2
NS_STEPS = 3
CHUNKS = 4
LEAD, LINEAR, QUADRATIC = 3.4445, -4.775, 2.0315
F32 = jnp.float32
BF16 = jnp.bfloat16
VMEM = pl.BlockSpec(memory_space=pltpu.VMEM)
SMEM = pl.BlockSpec(memory_space=pltpu.SMEM)
LIMIT = pltpu.CompilerParams(vmem_limit_bytes=56 << 20)


def shifted(block, axis, distance):
    count = lax.axis_size(axis)
    return lax.ppermute(block, axis, [((i - distance) % count, i) for i in range(count)])


def swapped(block, axis, bit):
    return lax.ppermute(block, axis, [(i, i ^ bit) for i in range(lax.axis_size(axis))])


def dot(a, b):
    return jnp.dot(a, b, preferred_element_type=F32)


def dot_first(a, b):
    return lax.dot_general(a, b, (((0,), (0,)), ((), ())), preferred_element_type=F32)


def dot_last(a, b):
    return lax.dot_general(a, b, (((1,), (1,)), ((), ())), preferred_element_type=F32)


def factors(gram):
    rest, lead = None, 1.0
    for sweep in range(NS_STEPS):
        wide = gram.astype(F32)
        polynom_wide = LINEAR * wide + QUADRATIC * dot(gram, gram)
        polynom = polynom_wide.astype(BF16)
        if sweep == 0:
            rest = polynom_wide
        else:
            rest = lead * polynom_wide + LEAD * rest + dot(rest.astype(BF16), polynom)
        lead = lead * LEAD
        if sweep < NS_STEPS - 1:
            half = (LEAD * wide + dot(gram, polynom)).astype(BF16)
            gram = (LEAD * half.astype(F32) + dot(half, polynom)).astype(BF16)
    return rest, lead


def round_kernel(blocks, place, refs):
    names = iter(refs)
    rows_refs = [next(names) for _ in range(blocks)]
    grad_refs = [next(names) for _ in range(blocks)]
    route, mine, weight, moment = (next(names) for _ in range(4))
    new_moment, slopes, stepped = (next(names) for _ in range(3))
    shares = [next(names) for _ in range(CHUNKS)]
    rows, shaped, moment_low = (next(names) for _ in range(3))
    depth, width = weight.shape
    count = rows_refs[0].shape[0]
    factor = 1.0 / math.sqrt(depth)
    step_size = 0.1 * math.sqrt(depth)
    shaped[...] = weight[...].astype(BF16)
    columns = route[...].T
    lanes = route.shape[1]
    for block in range(blocks):
        part = rows_refs[block][:, :depth]
        rows[pl.ds(block * count, count), :] = part
        pre = dot(part, shaped[...]) * factor
        for piece in range(count // lanes):
            index = block * (count // lanes) + piece
            keep = columns[:, index : index + 1] == mine[0]
            span = slice(piece * lanes, (piece + 1) * lanes)
            grads = grad_refs[block][span, place : place + width].astype(F32)
            slope = grads * 2.0 * jnp.maximum(pre[span, :], 0.0)
            slopes[pl.ds(index * lanes, lanes), :] = jnp.where(keep, slope, 0.0).astype(BF16)

    tile = min(256, depth)

    def accumulate(i, total):
        span = pl.ds(pl.multiple_of(i * tile, tile), tile)
        value = 0.9 * moment[span, :] + dot_first(rows[:, span], slopes[...]) * factor
        new_moment[span, :] = value
        moment_low[span, :] = value.astype(BF16)
        return total + jnp.sum(value * value, axis=0, keepdims=True)

    total = lax.fori_loop(0, depth // tile, accumulate, jnp.zeros((1, width), F32))
    scale = 1.0 / (jnp.sqrt(jnp.sum(total)) + 1e-07)
    gram = (dot_first(moment_low[...], moment_low[...]) * (scale * scale)).astype(BF16)
    rest, lead = factors(gram)
    rest = rest.astype(BF16)
    chunk = depth // CHUNKS
    for index in range(CHUNKS):
        span = pl.ds(index * chunk, chunk)
        low = moment_low[span, :]
        orthog = scale * (lead * low.astype(F32) + dot(low, rest))
        value = weight[span, :] - step_size * orthog
        stepped[span, :] = value
        shares[index][...] = value.astype(BF16)


def round_call(rows, grads, place, route, mine, weight, moment):
    depth, width = weight.shape
    blocks = len(rows)
    total = blocks * rows[0].shape[0]
    whole = jax.ShapeDtypeStruct((depth, width), F32)
    share = jax.ShapeDtypeStruct((depth // CHUNKS, width), BF16)
    result = pl.pallas_call(
        lambda *refs: round_kernel(blocks, place, refs),
        out_shape=[whole, jax.ShapeDtypeStruct((total, width), BF16), whole] + [share] * CHUNKS,
        in_specs=[VMEM] * (2 * blocks + 1) + [SMEM, VMEM, VMEM],
        out_specs=[VMEM] * (3 + CHUNKS),
        scratch_shapes=[
            pltpu.VMEM((total, depth), BF16),
            pltpu.VMEM((depth, width), BF16),
            pltpu.VMEM((depth, width), BF16),
        ],
        compiler_params=LIMIT,
        name="muon_round",
    )(*rows, *grads, route, mine, weight, moment)
    return result[0], result[1], result[2], result[3:]


def backward_kernel(slopes, weight, out):
    depth = weight.shape[0]
    factor = 1.0 / math.sqrt(depth)
    shaped = weight[...].astype(BF16)
    count = out.shape[1]
    for block in range(out.shape[0]):
        part = slopes[pl.ds(block * count, count), :]
        out[block] = (dot_last(part, shaped) * factor).astype(BF16)


def backward_call(slopes, weight, blocks):
    depth = weight.shape[0]
    return pl.pallas_call(
        backward_kernel,
        out_shape=jax.ShapeDtypeStruct((blocks, slopes.shape[0] // blocks, depth), BF16),
        in_specs=[VMEM, VMEM],
        out_specs=VMEM,
        compiler_params=LIMIT,
        name="row_gradients",
    )(slopes, weight)


def combine_kernel(stepped, left, right, near, *rest):
    out = rest[-1]
    total = left[...].astype(F32) + right[...].astype(F32) + near[...].astype(F32)
    out[...] = 0.4 * stepped[...] + 0.15 * total


def combine_call(index, stepped, left, right, near, buffer):
    chunk, width = left.shape
    place = pl.BlockSpec((chunk, width), lambda i: (index, 0))
    whole = pl.BlockSpec((chunk, width), lambda i: (0, 0))
    extra = [] if buffer is None else [buffer]
    return pl.pallas_call(
        combine_kernel,
        grid=(1,),
        out_shape=jax.ShapeDtypeStruct(stepped.shape, F32),
        in_specs=[place, whole, whole, whole] + [pl.BlockSpec(memory_space=pl.ANY)] * len(extra),
        out_specs=place,
        input_output_aliases={4: 0} if extra else {},
        compiler_params=pltpu.CompilerParams(vmem_limit_bytes=16 << 20),
        name="average",
    )(stepped, left, right, near, *extra)


def on_device(tokens, routing, out_grad, weights, momentum):
    experts = lax.axis_size("expert")
    bits = []
    bit = experts // 2
    while bit:
        bits.append(bit)
        bit //= 2
    weight = weights[0, 0]
    moment = momentum[0, 0]
    width = weight.shape[1]
    mine = lax.axis_index("expert").astype(jnp.int32).reshape(1)
    even = lax.axis_index("node") % 2 == 0

    def gathered(own):
        held = [own]
        for bit in bits:
            held = held + [swapped(item, "expert", bit) for item in held]
        return held

    def returned(parts):
        for bit in reversed(bits):
            half = parts.shape[0] // 2
            parts = parts[:half] + swapped(parts[half:], "expert", bit)
        return parts[0]

    routes = gathered(routing)
    rows = [gathered(tokens[0])]
    grads = [gathered(out_grad[0])]
    places = [0]
    packed = jnp.concatenate([tokens[1], out_grad[1]], axis=1)
    packed, _ = lax.optimization_barrier((packed, rows[0][1]))
    later = gathered(packed)
    rows.append(later)
    grads.append(later)
    places.append(tokens.shape[2])
    in_grads = []
    for index in range(ROUNDS):
        route = jnp.concatenate([item[index] for item in routes]).reshape(-1, 128)
        moment, slopes, stepped, shares = round_call(
            rows[index], grads[index], places[index], route, mine, weight, moment
        )
        partial_rows = backward_call(slopes, weight, experts)
        in_grads.append(returned(partial_rows))
        weight = None
        for chunk, share in enumerate(shares):
            left = shifted(share, "node", 2)
            right = shifted(share, "node", -2)
            other = jnp.where(even, right, left)
            near = swapped((share.astype(F32) + other.astype(F32)).astype(BF16), "node", 1)
            weight = combine_call(chunk, stepped, left, right, near, weight)
    return (weight[None, None], moment[None, None], jnp.stack(in_grads))


def solution(mesh):
    return jax.shard_map(
        on_device,
        mesh=mesh,
        in_specs=(
            P(None, ("expert", "node"), None),
            P(None, ("expert", "node")),
            P(None, ("expert", "node"), None),
            P("node", "expert", None, None),
            P("node", "expert", None, None),
        ),
        out_specs=(
            P("node", "expert", None, None),
            P("node", "expert", None, None),
            P(None, ("expert", "node"), None),
        ),
        check_vma=False,
    )
```

time: 253 us -> 191 us (0.75)
  matrix products: 62.8 us -> 0 us
  Pallas kernels: 0 us -> 40.2 us
  waiting for transfers between devices: 126 us -> 89.5 us
  other arithmetic: 17.2 us -> 3.5 us
  starting transfers between devices: 40.3 us -> 48.2 us
  local copies, waits for them, and re-layouts: 3.98 us -> 8.36 us
    dot_general x24 -> x0, matrix products: 62.8 us -> none  [the longest x6 24 us: orthogonalize(): jnp.dot(orthog, polynom, preferred_element_type=jnp.float32)]
    pallas_call x0 -> x12, Pallas kernels: none -> 40.2 us  [the longest x2 26.8 us: round_call(): pl.pallas_call(lambda *refs: round_kernel(blocks, place, refs), out_shape...]
    ppermute x8 -> x40, starting transfers between devices: 17.6 us -> 48.2 us  [the longest x16 27.9 us: shifted(): lax.ppermute(block, axis, [((i - distance) % count, i) for i in range(cou...]
    all_to_all x6 -> x0, waiting for transfers between devices: 26 us -> none  [the longest x2 13.7 us: on_device(): lax.all_to_all(sent_grads[round_index], 'expert', split_axis=0, concat_ax...]
    all_to_all x6 -> x0, starting transfers between devices: 22.7 us -> none  [the longest x2 7.95 us: on_device(): lax.all_to_all(backward, 'expert', split_axis=0, concat_axis=0, tiled=True)]
    ppermute x8 -> x40, waiting for transfers between devices: 100 us -> 89.5 us  [the longest x16 49.5 us: shifted(): lax.ppermute(block, axis, [((i - distance) % count, i) for i in range(cou...]
    mul x2 -> x0, other arithmetic: 4.34 us -> none  [on_device(): got_grads.astype(jnp.float32) * 2.0 * jnp.maximum(preact, 0.0)]
    broadcast_in_dim x1 -> x0, other arithmetic: 4.23 us -> none  [on_device(): return (weight[None, None], moment[None, None], jnp.stack(in_grads))]
  transfers between devices with their start and end apart: 14 -> 40, of which waited for: 11 -> 24; matrix products, arithmetic and copies ran while one was open for 18% -> 3% of each run, Pallas kernels for 0% -> 21%
where the time goes in v1:
time: 191 us
  waiting for transfers between devices  89.5 us (47%)
  starting transfers between devices  48.2 us (25%)
  Pallas kernels  40.2 us (21%)
  local copies, waits for them, and re-layouts  8.36 us (4%)
  other arithmetic  3.5 us (2%)
    ppermute x16, waiting for transfers between devices, shifted(): lax.ppermute(block, axis, [((i - distance) % count, i) for i in range(cou...  49.5 us
    ppermute x24, waiting for transfers between devices, swapped(): lax.ppermute(block, axis, [(i, i ^ bit) for i in range(lax.axis_size(axis...  40 us
    ppermute x16, starting transfers between devices, shifted(): lax.ppermute(block, axis, [((i - distance) % count, i) for i in range(cou...  27.9 us
    pallas_call x2, Pallas kernels, round_call(): pl.pallas_call(lambda *refs: round_kernel(blocks, place, refs), out_shape...  26.8 us
    ppermute x24, starting transfers between devices, swapped(): lax.ppermute(block, axis, [(i, i ^ bit) for i in range(lax.axis_size(axis...  20.3 us
    pallas_call x2, Pallas kernels, backward_call(): pl.pallas_call(backward_kernel, out_shape=jax.ShapeDtypeStruct((blocks, s...  9.07 us
    pallas_call x8, Pallas kernels, combine_call(): pl.pallas_call(combine_kernel, grid=(1,), out_shape=jax.ShapeDtypeStruct(...  4.3 us
    unnamed x50, local copies, waits for them, and re-layouts  4.15 us
  transfers between devices with their start and end apart: 40, of which 24 were waited for; matrix products, arithmetic and copies ran while one was open for 3% of the time, Pallas kernels for 21%

profile of v1, /device:TPU:0, one launch (start us, length us, event | category | flops | bytes accessed | tf_op | source)
XLA Modules:
  0.0 190.8 jit_solution(12019505988850091791)
XLA Ops:
  0.7 3.0 %collective-permute-start.4 = (s32[2,256]{1,0:T(2,128)}, s32[2,256]{1,0:T(2,128)S(1)}, u32[]{:S(2)}, u32[]{:S(2)}) collective-permute-start(s32[2,256]{1,0:T(2,128)} %param.6), channel_id=1, source_target_pairs={{0,16},{8,24},{16,0},{24,8},{1,17},{9,25},{17,1},{25,9},{2,18},{10... | collective-permute-start | bytes 6152 | tf_op jit(solution)/shard_map/ppermute | solution.py:27
  5.7 1.7 collective-permute-start.9
  8.1 11.8 %collective-permute-done.refs_1_ = bf16[256,1024]{1,0:T(8,128)(2,1)} collective-permute-done((bf16[256,1024]{1,0:T(8,128)(2,1)S(1)}, bf16[256,1024]{1,0:T(8,128)(2,1)}, u32[]{:S(2)}, u32[]{:S(2)}) %collective-permute-start) | collective-permute-done | bytes 524320 | tf_op jit(solution)/shard_map/ppermute | solution.py:27
  19.9 5.0 %collective-permute-done.9.refs_5_ = bf16[256,512]{1,0:T(8,128)(2,1)S(1)} collective-permute-done((bf16[256,512]{1,0:T(8,128)(2,1)S(1)}, bf16[256,512]{1,0:T(8,128)(2,1)S(1)}, u32[]{:S(2)}, u32[]{:S(2)}) %collective-permute-start.9) | collective-permute-done | bytes 262176 | tf_op jit(solution)/shard_map/ppermute | solution.py:27
  27.4 12.6 %muon_round.2 = (f32[1024,512]{1,0:T(8,128)}, bf16[1024,512]{1,0:T(8,128)(2,1)}, f32[1024,512]{1,0:T(8,128)}, bf16[256,512]{1,0:T(8,128)(2,1)}, bf16[256,512]{1,...) custom-call(bf16[256,1024]{1,0:T(8,128)(2,1)} %copy-done.9, ...), custom_call_target="tpu_custom_call" | custom-call | tf_op jit(solution)/shard_map/muon_round/pallas_call | solution.py:116
  41.6 2.3 %collective-permute-start.22 = (bf16[256,512]{1,0:T(8,128)(2,1)}, bf16[256,512]{1,0:T(8,128)(2,1)S(1)}, u32[]{:S(2)}, u32[]{:S(2)}) collective-permute-start(bf16[256,512]{1,0:T(8,128)(2,1)} %get-tuple-element.23), channel_id=1, source_target_pairs={{2,0},{3,1},{4,2},{5,3},{6,4},{7,5},{0,6},{1,7},{10,8},{11,9},{12,... | collective-permute-start | bytes 786440 | tf_op jit(solution)/shard_map/ppermute | solution.py:23
  43.8 3.8 %collective-permute-start.19 = (bf16[256,512]{1,0:T(8,128)(2,1)}, bf16[256,512]{1,0:T(8,128)(2,1)S(1)}, u32[]{:S(2)}, u32[]{:S(2)}) collective-permute-start(bf16[256,512]{1,0:T(8,128)(2,1)} %get-tuple-element.22), channel_id=1, source_target_pairs={{2,0},{3,1},{4,2},{5,3},{6,4},{7,5},{0,6},{1,7},{10,8},{11,9},{12,... | collective-permute-start | bytes 786440 | tf_op jit(solution)/shard_map/ppermute | solution.py:23
  47.7 3.6 %collective-permute-done.21.left = bf16[256,512]{1,0:T(8,128)(2,1)S(1)} collective-permute-done((bf16[256,512]{1,0:T(8,128)(2,1)}, bf16[256,512]{1,0:T(8,128)(2,1)S(1)}, u32[]{:S(2)}, u32[]{:S(2)}) %collective-permute-start.21) | collective-permute-done | bytes 262176 | tf_op jit(solution)/shard_map/ppermute | solution.py:23
  51.2 4.1 %collective-permute-start.15 = (bf16[256,512]{1,0:T(8,128)(2,1)}, bf16[256,512]{1,0:T(8,128)(2,1)S(1)}, u32[]{:S(2)}, u32[]{:S(2)}) collective-permute-start(bf16[256,512]{1,0:T(8,128)(2,1)} %get-tuple-element.21), channel_id=1, source_target_pairs={{6,0},{7,1},{0,2},{1,3},{2,4},{3,5},{4,6},{5,7},{14,8},{15,9},{8,1... | collective-permute-start | bytes 786440 | tf_op jit(solution)/shard_map/ppermute | solution.py:23
  58.6 4.5 %row_gradients.2 = bf16[4,256,1024]{2,1,0:T(8,128)(2,1)} custom-call(bf16[1024,512]{1,0:T(8,128)(2,1)} %get-tuple-element.31.slopes, f32[1024,512]{1,0:T(8,128)} %bitcast.23), custom_call_target="tpu_custom_call" | custom-call | tf_op jit(solution)/shard_map/row_gradients/pallas_call | solution.py:144
  64.6 2.0 %collective-permute-start.12 = (bf16[256,512]{1,0:T(8,128)(2,1)S(1)}, bf16[256,512]{1,0:T(8,128)(2,1)S(1)}, u32[]{:S(2)}, u32[]{:S(2)}) collective-permute-start(bf16[256,512]{1,0:T(8,128)(2,1)S(1)} %copy-done.16), channel_id=1, source_target_pairs={{6,0},{7,1},{0,2},{1,3},{2,4},{3,5},{4,6},{5,7},{14,8},{15,9},{8,1... | collective-permute-start | bytes 786440 | tf_op jit(solution)/shard_map/ppermute | solution.py:23
  68.2 1.9 %collective-permute-start.13 = (bf16[256,512]{1,0:T(8,128)(2,1)S(1)}, bf16[256,512]{1,0:T(8,128)(2,1)S(1)}, u32[]{:S(2)}, u32[]{:S(2)}) collective-permute-start(bf16[256,512]{1,0:T(8,128)(2,1)S(1)} %copy-done.16), channel_id=1, source_target_pairs={{2,0},{3,1},{4,2},{5,3},{6,4},{7,5},{0,6},{1,7},{10,8},{11,9},{12,... | collective-permute-start | bytes 786440 | tf_op jit(solution)/shard_map/ppermute | solution.py:23
  70.1 3.7 %collective-permute-done.15.left = bf16[256,512]{1,0:T(8,128)(2,1)S(1)} collective-permute-done((bf16[256,512]{1,0:T(8,128)(2,1)}, bf16[256,512]{1,0:T(8,128)(2,1)S(1)}, u32[]{:S(2)}, u32[]{:S(2)}) %collective-permute-start.15) | collective-permute-done | bytes 262176 | tf_op jit(solution)/shard_map/ppermute | solution.py:23
  73.9 5.4 %collective-permute-done.16.right = bf16[256,512]{1,0:T(8,128)(2,1)S(1)} collective-permute-done((bf16[256,512]{1,0:T(8,128)(2,1)}, bf16[256,512]{1,0:T(8,128)(2,1)S(1)}, u32[]{:S(2)}, u32[]{:S(2)}) %collective-permute-start.16) | collective-permute-done | bytes 262176 | tf_op jit(solution)/shard_map/ppermute | solution.py:23
  80.0 5.1 %collective-permute-done.12.left = bf16[256,512]{1,0:T(8,128)(2,1)S(1)} collective-permute-done((bf16[256,512]{1,0:T(8,128)(2,1)S(1)}, bf16[256,512]{1,0:T(8,128)(2,1)S(1)}, u32[]{:S(2)}, u32[]{:S(2)}) %collective-permute-start.12) | collective-permute-done | bytes 262176 | tf_op jit(solution)/shard_map/ppermute | solution.py:23
  86.6 2.6 %collective-permute-done.13.right = bf16[256,512]{1,0:T(8,128)(2,1)S(1)} collective-permute-done((bf16[256,512]{1,0:T(8,128)(2,1)S(1)}, bf16[256,512]{1,0:T(8,128)(2,1)S(1)}, u32[]{:S(2)}, u32[]{:S(2)}) %collective-permute-start.13) | collective-permute-done | bytes 262176 | tf_op jit(solution)/shard_map/ppermute | solution.py:23
  94.0 4.4 %collective-permute-done.20.near = bf16[256,512]{1,0:T(8,128)(2,1)S(1)} collective-permute-done((bf16[256,512]{1,0:T(8,128)(2,1)S(1)}, bf16[256,512]{1,0:T(8,128)(2,1)S(1)}, u32[]{:S(2)}, u32[]{:S(2)}) %collective-permute-start.20) | collective-permute-done | bytes 262176 | tf_op jit(solution)/shard_map/ppermute | solution.py:27
  100.8 3.2 %collective-permute-done.17.near = bf16[256,512]{1,0:T(8,128)(2,1)S(1)} collective-permute-done((bf16[256,512]{1,0:T(8,128)(2,1)S(1)}, bf16[256,512]{1,0:T(8,128)(2,1)S(1)}, u32[]{:S(2)}, u32[]{:S(2)}) %collective-permute-start.17) | collective-permute-done | bytes 262176 | tf_op jit(solution)/shard_map/ppermute | solution.py:27
  104.1 4.6 %collective-permute-done.14.near = bf16[256,512]{1,0:T(8,128)(2,1)S(1)} collective-permute-done((bf16[256,512]{1,0:T(8,128)(2,1)S(1)}, bf16[256,512]{1,0:T(8,128)(2,1)S(1)}, u32[]{:S(2)}, u32[]{:S(2)}) %collective-permute-start.14) | collective-permute-done | bytes 262176 | tf_op jit(solution)/shard_map/ppermute | solution.py:27
  111.4 14.2 %muon_round.3 = (f32[1024,512]{1,0:T(8,128)}, bf16[1024,512]{1,0:T(8,128)(2,1)}, f32[1024,512]{1,0:T(8,128)}, bf16[256,512]{1,0:T(8,128)(2,1)}, bf16[256,512]{1,...) custom-call(bf16[256,1536]{1,0:T(8,128)(2,1)} %copy-done.5, bf16[256,1536]{1,0:T(8,128)(2,1)} %copy-done.6, ...), custom_call_target="tpu_custom_call" | custom-call | tf_op jit(solution)/shard_map/muon_round/pallas_call | solution.py:116
  126.7 3.2 %collective-permute-start.34 = (bf16[256,512]{1,0:T(8,128)(2,1)}, bf16[256,512]{1,0:T(8,128)(2,1)S(1)}, u32[]{:S(2)}, u32[]{:S(2)}) collective-permute-start(bf16[256,512]{1,0:T(8,128)(2,1)} %get-tuple-element.29), channel_id=1, source_target_pairs={{2,0},{3,1},{4,2},{5,3},{6,4},{7,5},{0,6},{1,7},{10,8},{11,9},{12,... | collective-permute-start | bytes 786440 | tf_op jit(solution)/shard_map/ppermute | solution.py:23
  129.9 3.8 %collective-permute-start.31 = (bf16[256,512]{1,0:T(8,128)(2,1)}, bf16[256,512]{1,0:T(8,128)(2,1)S(1)}, u32[]{:S(2)}, u32[]{:S(2)}) collective-permute-start(bf16[256,512]{1,0:T(8,128)(2,1)} %get-tuple-element.28), channel_id=1, source_target_pairs={{2,0},{3,1},{4,2},{5,3},{6,4},{7,5},{0,6},{1,7},{10,8},{11,9},{12,... | collective-permute-start | bytes 786440 | tf_op jit(solution)/shard_map/ppermute | solution.py:23
  133.7 4.5 %row_gradients.3 = bf16[4,256,1024]{2,1,0:T(8,128)(2,1)} custom-call(bf16[1024,512]{1,0:T(8,128)(2,1)} %get-tuple-element.32.slopes, f32[1024,512]{1,0:T(8,128)} %copy-done), custom_call_target="tpu_custom_call" | custom-call | tf_op jit(solution)/shard_map/row_gradients/pallas_call | solution.py:144
  140.8 2.1 %collective-permute-done.34.right = bf16[256,512]{1,0:T(8,128)(2,1)S(1)} collective-permute-done((bf16[256,512]{1,0:T(8,128)(2,1)}, bf16[256,512]{1,0:T(8,128)(2,1)S(1)}, u32[]{:S(2)}, u32[]{:S(2)}) %collective-permute-start.34) | collective-permute-done | bytes 262176 | tf_op jit(solution)/shard_map/ppermute | solution.py:23
  144.7 3.8 %collective-permute-done.30.left = bf16[256,512]{1,0:T(8,128)(2,1)S(1)} collective-permute-done((bf16[256,512]{1,0:T(8,128)(2,1)}, bf16[256,512]{1,0:T(8,128)(2,1)S(1)}, u32[]{:S(2)}, u32[]{:S(2)}) %collective-permute-start.30) | collective-permute-done | bytes 262176 | tf_op jit(solution)/shard_map/ppermute | solution.py:23
  148.5 5.6 %collective-permute-done.31.right = bf16[256,512]{1,0:T(8,128)(2,1)S(1)} collective-permute-done((bf16[256,512]{1,0:T(8,128)(2,1)}, bf16[256,512]{1,0:T(8,128)(2,1)S(1)}, u32[]{:S(2)}, u32[]{:S(2)}) %collective-permute-start.31) | collective-permute-done | bytes 262176 | tf_op jit(solution)/shard_map/ppermute | solution.py:23
  154.9 4.8 %collective-permute-done.27.left = bf16[256,512]{1,0:T(8,128)(2,1)S(1)} collective-permute-done((bf16[256,512]{1,0:T(8,128)(2,1)S(1)}, bf16[256,512]{1,0:T(8,128)(2,1)S(1)}, u32[]{:S(2)}, u32[]{:S(2)}) %collective-permute-start.27) | collective-permute-done | bytes 262176 | tf_op jit(solution)/shard_map/ppermute | solution.py:23
  160.7 4.6 %collective-permute-done.28.right = bf16[256,512]{1,0:T(8,128)(2,1)S(1)} collective-permute-done((bf16[256,512]{1,0:T(8,128)(2,1)S(1)}, bf16[256,512]{1,0:T(8,128)(2,1)S(1)}, u32[]{:S(2)}, u32[]{:S(2)}) %collective-permute-start.28) | collective-permute-done | bytes 262176 | tf_op jit(solution)/shard_map/ppermute | solution.py:23
  166.9 4.1 %collective-permute-done.24.left = bf16[256,512]{1,0:T(8,128)(2,1)S(1)} collective-permute-done((bf16[256,512]{1,0:T(8,128)(2,1)S(1)}, bf16[256,512]{1,0:T(8,128)(2,1)S(1)}, u32[]{:S(2)}, u32[]{:S(2)}) %collective-permute-start.24) | collective-permute-done | bytes 262176 | tf_op jit(solution)/shard_map/ppermute | solution.py:23
  178.0 2.0 %collective-permute-done.32.near = bf16[256,512]{1,0:T(8,128)(2,1)S(1)} collective-permute-done((bf16[256,512]{1,0:T(8,128)(2,1)S(1)}, bf16[256,512]{1,0:T(8,128)(2,1)S(1)}, u32[]{:S(2)}, u32[]{:S(2)}) %collective-permute-start.32) | collective-permute-done | bytes 262176 | tf_op jit(solution)/shard_map/ppermute | solution.py:27
  180.9 4.7 %collective-permute-done.29.near = bf16[256,512]{1,0:T(8,128)(2,1)S(1)} collective-permute-done((bf16[256,512]{1,0:T(8,128)(2,1)S(1)}, bf16[256,512]{1,0:T(8,128)(2,1)S(1)}, u32[]{:S(2)}, u32[]{:S(2)}) %collective-permute-start.29) | collective-permute-done | bytes 262176 | tf_op jit(solution)/shard_map/ppermute | solution.py:27
  186.5 2.1 %collective-permute-done.26.near = bf16[256,512]{1,0:T(8,128)(2,1)S(1)} collective-permute-done((bf16[256,512]{1,0:T(8,128)(2,1)S(1)}, bf16[256,512]{1,0:T(8,128)(2,1)S(1)}, u32[]{:S(2)}, u32[]{:S(2)}) %collective-permute-start.26) | collective-permute-done | bytes 262176 | tf_op jit(solution)/shard_map/ppermute | solution.py:27
  (136 shorter events, 44.6 us)
Async XLA Ops:
  5.0 15.0 %collective-permute-start = (bf16[256,1024]{1,0:T(8,128)(2,1)S(1)}, bf16[256,1024]{1,0:T(8,128)(2,1)}, u32[]{:S(2)}, u32[]{:S(2)}) collective-permute-start(bf16[256,1024]{1,0:T(8,128)(2,1)S(1)} %get-tuple-element.33.refs_0_), channel_id=1, source_target_pairs={{0,16},{8,24},{16,0},{24,8},{1,17},{9,25},{17,1},{25,9},{2,18},{10... | collective-permute-start | bytes 1572872 | tf_op jit(solution)/shard_map/ppermute | solution.py:27
  5.1 21.4 %collective-permute-start.7 = (bf16[256,1024]{1,0:T(8,128)(2,1)S(1)}, bf16[256,1024]{1,0:T(8,128)(2,1)}, u32[]{:S(2)}, u32[]{:S(2)}) collective-permute-start(bf16[256,1024]{1,0:T(8,128)(2,1)S(1)} %get-tuple-element.33.refs_0_), channel_id=1, source_target_pairs={{0,8},{8,0},{16,24},{24,16},{1,9},{9,1},{17,25},{25,17},{2,10},{10... | collective-permute-start | bytes 1572872 | tf_op jit(solution)/shard_map/ppermute | solution.py:27
  5.7 19.3 %collective-permute-start.9 = (bf16[256,512]{1,0:T(8,128)(2,1)S(1)}, bf16[256,512]{1,0:T(8,128)(2,1)S(1)}, u32[]{:S(2)}, u32[]{:S(2)}) collective-permute-start(bf16[256,512]{1,0:T(8,128)(2,1)S(1)} %get-tuple-element.35.refs_4_), channel_id=1, source_target_pairs={{0,16},{8,24},{16,0},{24,8},{1,17},{9,25},{17,1},{25,9},{2,18},{10... | collective-permute-start | bytes 786440 | tf_op jit(solution)/shard_map/ppermute | solution.py:27
  7.5 18.5 %collective-permute-start.10 = (bf16[256,512]{1,0:T(8,128)(2,1)S(1)}, bf16[256,512]{1,0:T(8,128)(2,1)S(1)}, u32[]{:S(2)}, u32[]{:S(2)}) collective-permute-start(bf16[256,512]{1,0:T(8,128)(2,1)S(1)} %get-tuple-element.35.refs_4_), channel_id=1, source_target_pairs={{0,8},{8,0},{16,24},{24,16},{1,9},{9,1},{17,25},{25,17},{2,10},{10... | collective-permute-start | bytes 786440 | tf_op jit(solution)/shard_map/ppermute | solution.py:27
  7.6 17.4 %collective-permute-start.6 = (s32[2,256]{1,0:T(2,128)S(1)}, s32[2,256]{1,0:T(2,128)S(1)}, u32[]{:S(2)}, u32[]{:S(2)}) collective-permute-start(s32[2,256]{1,0:T(2,128)S(1)} %collective-permute-done.4), channel_id=1, source_target_pairs={{0,8},{8,0},{16,24},{24,16},{1,9},{9,1},{17,25},{25,17},{2,10},{10... | collective-permute-start | bytes 6152 | tf_op jit(solution)/shard_map/ppermute | solution.py:27
  25.0 54.3 %collective-permute-start.1 = (bf16[256,1536]{1,0:T(8,128)(2,1)S(1)}, bf16[256,1536]{1,0:T(8,128)(2,1)S(1)}, u32[]{:S(2)}, u32[]{:S(2)}) collective-permute-start(bf16[256,1536]{1,0:T(8,128)(2,1)S(1)} %pad_maximum_fusion.1.refs_0_.refs_4_), channel_id=1, source_target_pairs={{0,16},{8,24},{16,0},{24,8},{1,17},{9,25},{17,1},{25,9},{2,18},{10... | collective-permute-start | bytes 2359304 | tf_op jit(solution)/shard_map/ppermute | solution.py:27
  40.0 11.2 %collective-permute-start.21 = (bf16[256,512]{1,0:T(8,128)(2,1)}, bf16[256,512]{1,0:T(8,128)(2,1)S(1)}, u32[]{:S(2)}, u32[]{:S(2)}) collective-permute-start(bf16[256,512]{1,0:T(8,128)(2,1)} %get-tuple-element.23), channel_id=1, source_target_pairs={{6,0},{7,1},{0,2},{1,3},{2,4},{3,5},{4,6},{5,7},{14,8},{15,9},{8,1... | collective-permute-start | bytes 786440 | tf_op jit(solution)/shard_map/ppermute | solution.py:23
  41.6 15.3 %collective-permute-start.22 = (bf16[256,512]{1,0:T(8,128)(2,1)}, bf16[256,512]{1,0:T(8,128)(2,1)S(1)}, u32[]{:S(2)}, u32[]{:S(2)}) collective-permute-start(bf16[256,512]{1,0:T(8,128)(2,1)} %get-tuple-element.23), channel_id=1, source_target_pairs={{2,0},{3,1},{4,2},{5,3},{6,4},{7,5},{0,6},{1,7},{10,8},{11,9},{12,... | collective-permute-start | bytes 786440 | tf_op jit(solution)/shard_map/ppermute | solution.py:23
  43.8 20.7 %collective-permute-start.18 = (bf16[256,512]{1,0:T(8,128)(2,1)}, bf16[256,512]{1,0:T(8,128)(2,1)S(1)}, u32[]{:S(2)}, u32[]{:S(2)}) collective-permute-start(bf16[256,512]{1,0:T(8,128)(2,1)} %get-tuple-element.22), channel_id=1, source_target_pairs={{6,0},{7,1},{0,2},{1,3},{2,4},{3,5},{4,6},{5,7},{14,8},{15,9},{8,1... | collective-permute-start | bytes 786440 | tf_op jit(solution)/shard_map/ppermute | solution.py:23
  43.8 24.3 %collective-permute-start.19 = (bf16[256,512]{1,0:T(8,128)(2,1)}, bf16[256,512]{1,0:T(8,128)(2,1)S(1)}, u32[]{:S(2)}, u32[]{:S(2)}) collective-permute-start(bf16[256,512]{1,0:T(8,128)(2,1)} %get-tuple-element.22), channel_id=1, source_target_pairs={{2,0},{3,1},{4,2},{5,3},{6,4},{7,5},{0,6},{1,7},{10,8},{11,9},{12,... | collective-permute-start | bytes 786440 | tf_op jit(solution)/shard_map/ppermute | solution.py:23
  51.2 22.6 %collective-permute-start.15 = (bf16[256,512]{1,0:T(8,128)(2,1)}, bf16[256,512]{1,0:T(8,128)(2,1)S(1)}, u32[]{:S(2)}, u32[]{:S(2)}) collective-permute-start(bf16[256,512]{1,0:T(8,128)(2,1)} %get-tuple-element.21), channel_id=1, source_target_pairs={{6,0},{7,1},{0,2},{1,3},{2,4},{3,5},{4,6},{5,7},{14,8},{15,9},{8,1... | collective-permute-start | bytes 786440 | tf_op jit(solution)/shard_map/ppermute | solution.py:23
  56.9 22.4 %collective-permute-start.16 = (bf16[256,512]{1,0:T(8,128)(2,1)}, bf16[256,512]{1,0:T(8,128)(2,1)S(1)}, u32[]{:S(2)}, u32[]{:S(2)}) collective-permute-start(bf16[256,512]{1,0:T(8,128)(2,1)} %get-tuple-element.21), channel_id=1, source_target_pairs={{2,0},{3,1},{4,2},{5,3},{6,4},{7,5},{0,6},{1,7},{10,8},{11,9},{12,... | collective-permute-start | bytes 786440 | tf_op jit(solution)/shard_map/ppermute | solution.py:23
  64.6 20.5 %collective-permute-start.12 = (bf16[256,512]{1,0:T(8,128)(2,1)S(1)}, bf16[256,512]{1,0:T(8,128)(2,1)S(1)}, u32[]{:S(2)}, u32[]{:S(2)}) collective-permute-start(bf16[256,512]{1,0:T(8,128)(2,1)S(1)} %copy-done.16), channel_id=1, source_target_pairs={{6,0},{7,1},{0,2},{1,3},{2,4},{3,5},{4,6},{5,7},{14,8},{15,9},{8,1... | collective-permute-start | bytes 786440 | tf_op jit(solution)/shard_map/ppermute | solution.py:23
  68.2 21.0 %collective-permute-start.13 = (bf16[256,512]{1,0:T(8,128)(2,1)S(1)}, bf16[256,512]{1,0:T(8,128)(2,1)S(1)}, u32[]{:S(2)}, u32[]{:S(2)}) collective-permute-start(bf16[256,512]{1,0:T(8,128)(2,1)S(1)} %copy-done.16), channel_id=1, source_target_pairs={{2,0},{3,1},{4,2},{5,3},{6,4},{7,5},{0,6},{1,7},{10,8},{11,9},{12,... | collective-permute-start | bytes 786440 | tf_op jit(solution)/shard_map/ppermute | solution.py:23
  73.8 65.9 %collective-permute-start.36 = (bf16[2,256,1024]{2,1,0:T(8,128)(2,1)S(1)}, bf16[2,256,1024]{2,1,0:T(8,128)(2,1)S(1)}, u32[]{:S(2)}, u32[]{:S(2)}) collective-permute-start(bf16[2,256,1024]{2,1,0:T(8,128)(2,1)S(1)} %slice.87), channel_id=1, source_target_pairs={{0,8},{8,0},{16,24},{24,16},{1,9},{9,1},{17,25},{25,17},{2,10},{10... | collective-permute-start | bytes 3145736 | tf_op jit(solution)/shard_map/ppermute | solution.py:27
  79.3 30.9 %collective-permute-start.2 = (bf16[256,1536]{1,0:T(8,128)(2,1)S(1)}, bf16[256,1536]{1,0:T(8,128)(2,1)S(1)}, u32[]{:S(2)}, u32[]{:S(2)}) collective-permute-start(bf16[256,1536]{1,0:T(8,128)(2,1)S(1)} %pad_maximum_fusion.1.refs_0_.refs_4_), channel_id=1, source_target_pairs={{0,8},{8,0},{16,24},{24,16},{1,9},{9,1},{17,25},{25,17},{2,10},{10... | collective-permute-start | bytes 2359304 | tf_op jit(solution)/shard_map/ppermute | solution.py:27
  79.4 30.8 %collective-permute-start.3 = (bf16[256,1536]{1,0:T(8,128)(2,1)S(1)}, bf16[256,1536]{1,0:T(8,128)(2,1)S(1)}, u32[]{:S(2)}, u32[]{:S(2)}) collective-permute-start(bf16[256,1536]{1,0:T(8,128)(2,1)S(1)} %collective-permute-done.1.refs_1_.refs_5_), channel_id=1, source_target_pairs={{0,8},{8,0},{16,24},{24,16},{1,9},{9,1},{17,25},{25,17},{2,10},{10... | collective-permute-start | bytes 2359304 | tf_op jit(solution)/shard_map/ppermute | solution.py:27
  92.5 11.5 %collective-permute-start.17 = (bf16[256,512]{1,0:T(8,128)(2,1)S(1)}, bf16[256,512]{1,0:T(8,128)(2,1)S(1)}, u32[]{:S(2)}, u32[]{:S(2)}) collective-permute-start(bf16[256,512]{1,0:T(8,128)(2,1)S(1)} %add_convert_fusion.6), channel_id=1, source_target_pairs={{0,1},{1,0},{2,3},{3,2},{4,5},{5,4},{6,7},{7,6},{8,9},{9,8},{10,11... | collective-permute-start | bytes 786440 | tf_op jit(solution)/shard_map/ppermute | solution.py:27
  125.6 14.7 %collective-permute-start.33 = (bf16[256,512]{1,0:T(8,128)(2,1)}, bf16[256,512]{1,0:T(8,128)(2,1)S(1)}, u32[]{:S(2)}, u32[]{:S(2)}) collective-permute-start(bf16[256,512]{1,0:T(8,128)(2,1)} %get-tuple-element.29), channel_id=1, source_target_pairs={{6,0},{7,1},{0,2},{1,3},{2,4},{3,5},{4,6},{5,7},{14,8},{15,9},{8,1... | collective-permute-start | bytes 786440 | tf_op jit(solution)/shard_map/ppermute | solution.py:23
  126.7 16.2 %collective-permute-start.34 = (bf16[256,512]{1,0:T(8,128)(2,1)}, bf16[256,512]{1,0:T(8,128)(2,1)S(1)}, u32[]{:S(2)}, u32[]{:S(2)}) collective-permute-start(bf16[256,512]{1,0:T(8,128)(2,1)} %get-tuple-element.29), channel_id=1, source_target_pairs={{2,0},{3,1},{4,2},{5,3},{6,4},{7,5},{0,6},{1,7},{10,8},{11,9},{12,... | collective-permute-start | bytes 786440 | tf_op jit(solution)/shard_map/ppermute | solution.py:23
  129.9 18.6 %collective-permute-start.30 = (bf16[256,512]{1,0:T(8,128)(2,1)}, bf16[256,512]{1,0:T(8,128)(2,1)S(1)}, u32[]{:S(2)}, u32[]{:S(2)}) collective-permute-start(bf16[256,512]{1,0:T(8,128)(2,1)} %get-tuple-element.28), channel_id=1, source_target_pairs={{6,0},{7,1},{0,2},{1,3},{2,4},{3,5},{4,6},{5,7},{14,8},{15,9},{8,1... | collective-permute-start | bytes 786440 | tf_op jit(solution)/shard_map/ppermute | solution.py:23
  129.9 24.2 %collective-permute-start.31 = (bf16[256,512]{1,0:T(8,128)(2,1)}, bf16[256,512]{1,0:T(8,128)(2,1)S(1)}, u32[]{:S(2)}, u32[]{:S(2)}) collective-permute-start(bf16[256,512]{1,0:T(8,128)(2,1)} %get-tuple-element.28), channel_id=1, source_target_pairs={{2,0},{3,1},{4,2},{5,3},{6,4},{7,5},{0,6},{1,7},{10,8},{11,9},{12,... | collective-permute-start | bytes 786440 | tf_op jit(solution)/shard_map/ppermute | solution.py:23
  139.7 35.2 %collective-permute-start.38 = (bf16[2,256,1024]{2,1,0:T(8,128)(2,1)S(1)}, bf16[2,256,1024]{2,1,0:T(8,128)(2,1)S(1)}, u32[]{:S(2)}, u32[]{:S(2)}) collective-permute-start(bf16[2,256,1024]{2,1,0:T(8,128)(2,1)S(1)} %slice.91), channel_id=1, source_target_pairs={{0,8},{8,0},{16,24},{24,16},{1,9},{9,1},{17,25},{25,17},{2,10},{10... | collective-permute-start | bytes 3145736 | tf_op jit(solution)/shard_map/ppermute | solution.py:27
  140.8 19.0 %collective-permute-start.27 = (bf16[256,512]{1,0:T(8,128)(2,1)S(1)}, bf16[256,512]{1,0:T(8,128)(2,1)S(1)}, u32[]{:S(2)}, u32[]{:S(2)}) collective-permute-start(bf16[256,512]{1,0:T(8,128)(2,1)S(1)} %copy-done.21), channel_id=1, source_target_pairs={{6,0},{7,1},{0,2},{1,3},{2,4},{3,5},{4,6},{5,7},{14,8},{15,9},{8,1... | collective-permute-start | bytes 786440 | tf_op jit(solution)/shard_map/ppermute | solution.py:23
  142.9 22.4 %collective-permute-start.28 = (bf16[256,512]{1,0:T(8,128)(2,1)S(1)}, bf16[256,512]{1,0:T(8,128)(2,1)S(1)}, u32[]{:S(2)}, u32[]{:S(2)}) collective-permute-start(bf16[256,512]{1,0:T(8,128)(2,1)S(1)} %copy-done.21), channel_id=1, source_target_pairs={{2,0},{3,1},{4,2},{5,3},{6,4},{7,5},{0,6},{1,7},{10,8},{11,9},{12,... | collective-permute-start | bytes 786440 | tf_op jit(solution)/shard_map/ppermute | solution.py:23
  148.5 22.6 %collective-permute-start.24 = (bf16[256,512]{1,0:T(8,128)(2,1)S(1)}, bf16[256,512]{1,0:T(8,128)(2,1)S(1)}, u32[]{:S(2)}, u32[]{:S(2)}) collective-permute-start(bf16[256,512]{1,0:T(8,128)(2,1)S(1)} %copy-done.19), channel_id=1, source_target_pairs={{6,0},{7,1},{0,2},{1,3},{2,4},{3,5},{4,6},{5,7},{14,8},{15,9},{8,1... | collective-permute-start | bytes 786440 | tf_op jit(solution)/shard_map/ppermute | solution.py:23
  154.1 19.2 %collective-permute-start.25 = (bf16[256,512]{1,0:T(8,128)(2,1)S(1)}, bf16[256,512]{1,0:T(8,128)(2,1)S(1)}, u32[]{:S(2)}, u32[]{:S(2)}) collective-permute-start(bf16[256,512]{1,0:T(8,128)(2,1)S(1)} %copy-done.19), channel_id=1, source_target_pairs={{2,0},{3,1},{4,2},{5,3},{6,4},{7,5},{0,6},{1,7},{10,8},{11,9},{12,... | collective-permute-start | bytes 786440 | tf_op jit(solution)/shard_map/ppermute | solution.py:23
  159.8 29.8 %collective-permute-start.37 = (bf16[1,256,1024]{2,1,0:T(8,128)(2,1)S(1)}, bf16[1,256,1024]{2,1,0:T(8,128)(2,1)S(1)}, u32[]{:S(2)}, u32[]{:S(2)}) collective-permute-start(bf16[1,256,1024]{2,1,0:T(8,128)(2,1)S(1)} %slice.89), channel_id=1, source_target_pairs={{0,16},{8,24},{16,0},{24,8},{1,17},{9,25},{17,1},{25,9},{2,18},{10... | collective-permute-start | bytes 1572872 | tf_op jit(solution)/shard_map/ppermute | solution.py:27
  165.3 10.4 %collective-permute-start.35 = (bf16[256,512]{1,0:T(8,128)(2,1)S(1)}, bf16[256,512]{1,0:T(8,128)(2,1)S(1)}, u32[]{:S(2)}, u32[]{:S(2)}) collective-permute-start(bf16[256,512]{1,0:T(8,128)(2,1)S(1)} %add_convert_fusion), channel_id=1, source_target_pairs={{0,1},{1,0},{2,3},{3,2},{4,5},{5,4},{6,7},{7,6},{8,9},{9,8},{10,11... | collective-permute-start | bytes 786440 | tf_op jit(solution)/shard_map/ppermute | solution.py:27
  173.3 12.3 %collective-permute-start.29 = (bf16[256,512]{1,0:T(8,128)(2,1)S(1)}, bf16[256,512]{1,0:T(8,128)(2,1)S(1)}, u32[]{:S(2)}, u32[]{:S(2)}) collective-permute-start(bf16[256,512]{1,0:T(8,128)(2,1)S(1)} %add_convert_fusion.2), channel_id=1, source_target_pairs={{0,1},{1,0},{2,3},{3,2},{4,5},{5,4},{6,7},{7,6},{8,9},{9,8},{10,11... | collective-permute-start | bytes 786440 | tf_op jit(solution)/shard_map/ppermute | solution.py:27
  174.9 13.7 %collective-permute-start.26 = (bf16[256,512]{1,0:T(8,128)(2,1)S(1)}, bf16[256,512]{1,0:T(8,128)(2,1)S(1)}, u32[]{:S(2)}, u32[]{:S(2)}) collective-permute-start(bf16[256,512]{1,0:T(8,128)(2,1)S(1)} %add_convert_fusion.3), channel_id=1, source_target_pairs={{0,1},{1,0},{2,3},{3,2},{4,5},{5,4},{6,7},{7,6},{8,9},{9,8},{10,11... | collective-permute-start | bytes 786440 | tf_op jit(solution)/shard_map/ppermute | solution.py:27
  175.7 14.0 %collective-permute-start.39 = (bf16[1,256,1024]{2,1,0:T(8,128)(2,1)S(1)}, bf16[1,256,1024]{2,1,0:T(8,128)(2,1)S(1)}, u32[]{:S(2)}, u32[]{:S(2)}) collective-permute-start(bf16[1,256,1024]{2,1,0:T(8,128)(2,1)S(1)} %slice.93), channel_id=1, source_target_pairs={{0,16},{8,24},{16,0},{24,8},{1,17},{9,25},{17,1},{25,9},{2,18},{10... | collective-permute-start | bytes 1572872 | tf_op jit(solution)/shard_map/ppermute | solution.py:27
  (33 other events, 370.4 us)

commit v2 on v1

v2 whole, which is shorter than its diff:
```python
import math

import jax
import jax.numpy as jnp
from jax import lax
from jax.experimental import pallas as pl
from jax.experimental.pallas import tpu as pltpu
from jax.sharding import PartitionSpec as P


ROUNDS = 2
NS_STEPS = 3
LEAD, LINEAR, QUADRATIC = 3.4445, -4.775, 2.0315
F32 = jnp.float32
BF16 = jnp.bfloat16
VMEM = pl.BlockSpec(memory_space=pltpu.VMEM)
SMEM = pl.BlockSpec(memory_space=pltpu.SMEM)
ANY = pl.BlockSpec(memory_space=pl.ANY)


def limit(mebibytes):
    return pltpu.CompilerParams(vmem_limit_bytes=mebibytes << 20)


def swapped(block, axis, bit):
    return lax.ppermute(block, axis, [(i, i ^ bit) for i in range(lax.axis_size(axis))])


def crossed(block, axis, way):
    count = lax.axis_size(axis)
    return lax.ppermute(
        block, axis, [((i + (-way if i % 2 else way)) % count, i) for i in range(count)]
    )


def dot(a, b):
    return jnp.dot(a, b, preferred_element_type=F32)


def dot_first(a, b):
    return lax.dot_general(a, b, (((0,), (0,)), ((), ())), preferred_element_type=F32)


def dot_last(a, b):
    return lax.dot_general(a, b, (((1,), (1,)), ((), ())), preferred_element_type=F32)


def factors(gram):
    rest, lead = None, 1.0
    for sweep in range(NS_STEPS):
        wide = gram.astype(F32)
        polynom_wide = LINEAR * wide + QUADRATIC * dot(gram, gram)
        polynom = polynom_wide.astype(BF16)
        if sweep == 0:
            rest = polynom_wide
        else:
            rest = lead * polynom_wide + LEAD * rest + dot(rest.astype(BF16), polynom)
        lead = lead * LEAD
        if sweep < NS_STEPS - 1:
            half = (LEAD * wide + dot(gram, polynom)).astype(BF16)
            gram = (LEAD * half.astype(F32) + dot(half, polynom)).astype(BF16)
    return rest, lead


def mixed(stepped, first, second, near):
    total = first[...].astype(F32) + second[...].astype(F32) + near[...].astype(F32)
    return 0.4 * stepped[...] + 0.15 * total


def split(depth):
    half = depth // 2
    return half, (half, 3 * half // 4, half // 4)


def ahead_kernel(blocks, refs):
    names = iter(refs)
    rows = [next(names) for _ in range(blocks)]
    weight, pre = next(names), next(names)
    shaped = weight[...].astype(BF16)
    count, depth = rows[0].shape[0], weight.shape[0]
    for block in range(blocks):
        pre[pl.ds(block * count, count), :] = dot(rows[block][:, :depth], shaped)


def ahead_call(rows, weight):
    width = weight.shape[1]
    total = len(rows) * rows[0].shape[0]
    return pl.pallas_call(
        lambda *refs: ahead_kernel(len(rows), refs),
        out_shape=jax.ShapeDtypeStruct((total, width), F32),
        in_specs=[VMEM] * (len(rows) + 1),
        out_specs=VMEM,
        compiler_params=limit(16),
        name="ahead",
    )(*rows, weight)


def ahead_mixed_kernel(blocks, refs):
    names = iter(refs)
    rows = [next(names) for _ in range(blocks)]
    parts = [next(names) for _ in range(4)]
    weight, pre = next(names), next(names)
    value = mixed(*parts)
    weight[...] = value
    shaped = value.astype(BF16)
    count, depth = rows[0].shape[0], value.shape[0]
    for block in range(blocks):
        pre[pl.ds(block * count, count), :] = dot(rows[block][:, :depth], shaped)


def ahead_mixed_call(rows, parts):
    half, width = parts[0].shape
    total = len(rows) * rows[0].shape[0]
    return pl.pallas_call(
        lambda *refs: ahead_mixed_kernel(len(rows), refs),
        out_shape=[
            jax.ShapeDtypeStruct((half, width), F32),
            jax.ShapeDtypeStruct((total, width), F32),
        ],
        in_specs=[VMEM] * (len(rows) + 4),
        out_specs=[VMEM] * 2,
        compiler_params=limit(16),
        name="ahead_mixed",
    )(*rows, *parts)


def round_kernel(blocks, place, fresh, refs):
    names = iter(refs)
    rows_refs = [next(names) for _ in range(blocks)]
    grad_refs = [next(names) for _ in range(blocks)]
    route, mine, pre_ref, moment_ref = (next(names) for _ in range(4))
    weight_refs = [next(names) for _ in range(1 if fresh else 5)]
    moment_out, slopes_out, weight_out = (next(names) for _ in range(3))
    stepped_out = [next(names) for _ in range(2)]
    share_out = [next(names) for _ in range(2)]
    piece_out = [next(names) for _ in range(2)]
    rows, grads, pre, weight, moment, slopes, shares, moment_low, sems = names
    depth, width = weight.shape
    count = rows_refs[0].shape[0]
    half, pieces = split(depth)
    factor = 1.0 / math.sqrt(depth)
    step_size = 0.1 * math.sqrt(depth)
    used = iter(range(64))
    pending = []

    def copy(source, target):
        made = pltpu.make_async_copy(source, target, sems.at[next(used)])
        made.start()
        return made

    arrivals = []
    for block in range(blocks):
        span = pl.ds(block * count, count)
        arrivals.append(
            (
                copy(pre_ref.at[span, :], pre.at[span, :]),
                copy(grad_refs[block].at[:, pl.ds(place, width)], grads.at[span, :]),
                copy(rows_refs[block].at[:, pl.ds(0, depth)], rows.at[span, :]),
            )
        )
    moment_in = copy(moment_ref, moment)
    upper, lower = pl.ds(0, half), pl.ds(half, half)
    if fresh:
        weight_in = copy(weight_refs[0], weight)
    else:
        weight_in = copy(weight_refs[0], weight.at[upper, :])
        value = mixed(*weight_refs[1:])
        weight[lower, :] = value
        shaped = value.astype(BF16)
    columns = route[...].T
    lanes = route.shape[1]
    for block in range(blocks):
        for item in arrivals[block]:
            item.wait()
        span = pl.ds(block * count, count)
        value = pre[span, :]
        if not fresh:
            value = value + dot(rows[span, half:], shaped)
        value = value * factor
        for piece in range(count // lanes):
            index = block * (count // lanes) + piece
            keep = columns[:, index : index + 1] == mine[0]
            piece_span = pl.ds(index * lanes, lanes)
            slope = grads[piece_span, :].astype(F32) * 2.0
            slope = slope * jnp.maximum(value[piece * lanes : (piece + 1) * lanes, :], 0.0)
            slopes[piece_span, :] = jnp.where(keep, slope, 0.0).astype(BF16)
    pending.append(copy(slopes, slopes_out))
    moment_in.wait()
    tile = min(256, depth)

    def accumulate(i, total):
        span = pl.ds(pl.multiple_of(i * tile, tile), tile)
        value = 0.9 * moment[span, :] + dot_first(rows[:, span], slopes[...]) * factor
        moment[span, :] = value
        moment_low[span, :] = value.astype(BF16)
        return total + jnp.sum(value * value, axis=0, keepdims=True)

    total = lax.fori_loop(0, depth // tile, accumulate, jnp.zeros((1, width), F32))
    pending.append(copy(moment, moment_out))
    weight_in.wait()
    kept = copy(weight, weight_out)
    scale = 1.0 / (jnp.sqrt(jnp.sum(total)) + 1e-07)
    gram = (dot_first(moment_low[...], moment_low[...]) * (scale * scale)).astype(BF16)
    rest, lead = factors(gram)
    rest = rest.astype(BF16)
    kept.wait()
    for index, span in enumerate((upper, lower)):
        low = moment_low[span, :]
        orthog = scale * (lead * low.astype(F32) + dot(low, rest))
        value = weight[span, :] - step_size * orthog
        weight[span, :] = value
        shares[span, :] = value.astype(BF16)
        pending.append(copy(shares.at[span, :], share_out[index]))
        if index:
            first = pl.ds(half, pieces[1])
            second = pl.ds(half + pieces[1], pieces[2])
            pending.append(copy(shares.at[first, :], piece_out[0]))
            pending.append(copy(shares.at[second, :], piece_out[1]))
        pending.append(copy(weight.at[span, :], stepped_out[index]))
    for item in pending:
        item.wait()


def round_call(rows, grads, place, route, mine, pre, weight, moment):
    depth, width = moment.shape
    blocks = len(rows)
    total = blocks * rows[0].shape[0]
    half, pieces = split(depth)
    fresh = len(weight) == 1
    shape = jax.ShapeDtypeStruct
    result = pl.pallas_call(
        lambda *refs: round_kernel(blocks, place, fresh, refs),
        out_shape=[
            shape((depth, width), F32),
            shape((total, width), BF16),
            shape((depth, width), F32),
            shape((half, width), F32),
            shape((half, width), F32),
            shape((half, width), BF16),
            shape((half, width), BF16),
            shape((pieces[1], width), BF16),
            shape((pieces[2], width), BF16),
        ],
        in_specs=[ANY] * (2 * blocks) + [VMEM, SMEM, ANY, ANY, ANY] + [VMEM] * (len(weight) - 1),
        out_specs=[ANY] * 9,
        scratch_shapes=[
            pltpu.VMEM((total, depth), BF16),
            pltpu.VMEM((total, width), BF16),
            pltpu.VMEM((total, width), F32),
            pltpu.VMEM((depth, width), F32),
            pltpu.VMEM((depth, width), F32),
            pltpu.VMEM((total, width), BF16),
            pltpu.VMEM((depth, width), BF16),
            pltpu.VMEM((depth, width), BF16),
            pltpu.SemaphoreType.DMA((64,)),
        ],
        compiler_params=limit(24),
        name="muon_round",
    )(*rows, *grads, route, mine, pre, moment, *weight)
    return result[0], result[1], result[2], result[3:5], result[5:7], result[7:]


def backward_kernel(slopes, weight, keep, send):
    depth = weight.shape[0]
    factor = 1.0 / math.sqrt(depth)
    shaped = weight[...].astype(BF16)
    half, count = keep.shape[:2]
    for block in range(2 * half):
        part = slopes[pl.ds(block * count, count), :]
        out = keep if block < half else send
        out[block % half] = (dot_last(part, shaped) * factor).astype(BF16)


def backward_call(slopes, weight, blocks):
    depth = weight.shape[0]
    shape = jax.ShapeDtypeStruct((blocks // 2, slopes.shape[0] // blocks, depth), BF16)
    return pl.pallas_call(
        backward_kernel,
        out_shape=[shape, shape],
        in_specs=[VMEM, VMEM],
        out_specs=[VMEM, VMEM],
        compiler_params=limit(16),
        name="row_gradients",
    )(slopes, weight)


def place_call(function, index, count, parts, buffer):
    block = parts[0].shape
    rest = (0,) * (len(block) - 1)
    extra = [] if buffer is None else [buffer]

    def kernel(*refs):
        refs[-1][...] = function(*refs[: len(parts)])

    return pl.pallas_call(
        kernel,
        grid=(1,),
        out_shape=jax.ShapeDtypeStruct((count * block[0],) + block[1:], parts[0].dtype),
        in_specs=[pl.BlockSpec(block, lambda i: (0,) + rest)] * len(parts) + [ANY] * len(extra),
        out_specs=pl.BlockSpec(block, lambda i: (index,) + rest),
        input_output_aliases={len(parts): 0} if extra else {},
        compiler_params=limit(12),
    )(*parts, *extra)


def on_device(tokens, routing, out_grad, weights, momentum):
    experts = lax.axis_size("expert")
    bits = []
    bit = experts // 2
    while bit:
        bits.append(bit)
        bit //= 2
    weight = weights[0, 0]
    moment = momentum[0, 0]
    depth = weight.shape[0]
    half, pieces = split(depth)
    mine = lax.axis_index("expert").astype(jnp.int32).reshape(1)

    def gathered(own):
        held = [own]
        for bit in bits:
            held = held + [swapped(item, "expert", bit) for item in held]
        return held

    in_grad = None
    rows = [gathered(tokens[0])]
    grads = [gathered(out_grad[0])]
    routes = gathered(routing)
    packed = jnp.concatenate([tokens[1], out_grad[1]], axis=1)
    rows.append(gathered(packed))
    grads.append(rows[1])
    pre = ahead_call(rows[0], weight)
    weight_parts = [weight]
    for index in range(ROUNDS):
        route = jnp.concatenate([item[index] for item in routes]).reshape(-1, 128)
        moment, slopes, weight, stepped, shares, extra = round_call(
            rows[index], grads[index], depth if index else 0, route, mine, pre,
            weight_parts, moment,
        )
        firsts = []
        for share in (shares[0], *extra):
            firsts.append(crossed(share, "node", 2))
        seconds = []
        for share in shares:
            seconds.append(crossed(share, "node", -2))
        firsts = [firsts[0], jnp.concatenate(firsts[1:])]
        nears = []
        for piece, share in enumerate(shares):
            pair = (share.astype(F32) + firsts[piece].astype(F32)).astype(BF16)
            nears.append(swapped(pair, "node", 1))
        keep, send = backward_call(slopes, weight, experts)
        for bit in reversed(bits):
            back = swapped(send, "expert", bit)
            if keep.shape[0] > 1:
                keep, send = jnp.split(keep + back, 2)
        in_grad = place_call(lambda a, b: a[...] + b[...], index, ROUNDS, [keep, back], in_grad)
        halves = [
            [stepped[piece], firsts[piece], seconds[piece], nears[piece]]
            for piece in range(2)
        ]
        if index < ROUNDS - 1:
            upper, pre = ahead_mixed_call(rows[index + 1], halves[0])
            weight_parts = [upper, *halves[1]]
        else:
            weight = place_call(mixed, 0, 2, halves[0], None)
            weight = place_call(mixed, 1, 2, halves[1], weight)
    return (weight[None, None], moment[None, None], in_grad)


def solution(mesh):
    return jax.shard_map(
        on_device,
        mesh=mesh,
        in_specs=(
            P(None, ("expert", "node"), None),
            P(None, ("expert", "node")),
            P(None, ("expert", "node"), None),
            P("node", "expert", None, None),
            P("node", "expert", None, None),
        ),
        out_specs=(
            P("node", "expert", None, None),
            P("node", "expert", None, None),
            P(None, ("expert", "node"), None),
        ),
        check_vma=False,
    )
```

time: 191 us -> 177 us (0.927)
  waiting for transfers between devices: 89.5 us -> 99.2 us
  Pallas kernels: 40.2 us -> 31.4 us
  starting transfers between devices: 48.2 us -> 42 us
  local copies, waits for them, and re-layouts: 8.36 us -> 2.4 us
  other arithmetic: 3.5 us -> 1.43 us
    ppermute x16 -> x10, waiting for transfers between devices: 49.5 us -> 67.4 us  [crossed(): lax.ppermute(block, axis, [((i + (-way if i % 2 else way)) % count, i) fo...]
    pallas_call x12 -> x10, Pallas kernels: 40.2 us -> 31.4 us  [the longest x2 21 us: round_call(): pl.pallas_call(lambda *refs: round_kernel(blocks, place, fresh, refs), ou...]
    ppermute x24 -> x20, waiting for transfers between devices: 40 us -> 31.7 us  [swapped(): lax.ppermute(block, axis, [(i, i ^ bit) for i in range(lax.axis_size(axis...]
    ppermute x16 -> x10, starting transfers between devices: 27.9 us -> 21.2 us  [crossed(): lax.ppermute(block, axis, [((i + (-way if i % 2 else way)) % count, i) fo...]
    unnamed x50 -> x10, local copies, waits for them, and re-layouts: 4.15 us -> 0.07 us
    slice x4 -> x0, local copies, waits for them, and re-layouts: 2.89 us -> none  [returned(): parts = parts[:half] + swapped(parts[half:], 'expert', bit)]
    ppermute x24 -> x20, starting transfers between devices: 20.3 us -> 20.8 us  [swapped(): lax.ppermute(block, axis, [(i, i ^ bit) for i in range(lax.axis_size(axis...]
  transfers between devices with their start and end apart: 40 -> 30, of which waited for: 24 -> 11; matrix products, arithmetic and copies ran while one was open for 3% -> 1% of each run, Pallas kernels for 21% -> 17%
where the time goes in v2:
time: 177 us
  waiting for transfers between devices  99.2 us (56%)
  starting transfers between devices  42 us (24%)
  Pallas kernels  31.4 us (18%)
  local copies, waits for them, and re-layouts  2.4 us (1%)
    ppermute x10, waiting for transfers between devices, crossed(): lax.ppermute(block, axis, [((i + (-way if i % 2 else way)) % count, i) fo...  67.4 us
    ppermute x20, waiting for transfers between devices, swapped(): lax.ppermute(block, axis, [(i, i ^ bit) for i in range(lax.axis_size(axis...  31.7 us
    ppermute x10, starting transfers between devices, crossed(): lax.ppermute(block, axis, [((i + (-way if i % 2 else way)) % count, i) fo...  21.2 us
    pallas_call x2, Pallas kernels, round_call(): pl.pallas_call(lambda *refs: round_kernel(blocks, place, fresh, refs), ou...  21 us
    ppermute x20, starting transfers between devices, swapped(): lax.ppermute(block, axis, [(i, i ^ bit) for i in range(lax.axis_size(axis...  20.8 us
    pallas_call x4, Pallas kernels, place_call(): pl.pallas_call(kernel, grid=(1,), out_shape=jax.ShapeDtypeStruct((count *...  4.22 us
  transfers between devices with their start and end apart: 30, of which 11 were waited for; matrix products, arithmetic and copies ran while one was open for 1% of the time, Pallas kernels for 17%

profile of v2, /device:TPU:0, one launch (start us, length us, event | category | flops | bytes accessed | tf_op | source)
XLA Modules:
  0.0 177.3 jit_solution(18156632722631481384)
XLA Ops:
  0.7 1.4 slice_bitcast_fusion
  2.1 3.0 %collective-permute-start.6 = (bf16[256,1024]{1,0:T(8,128)(2,1)S(1)}, bf16[256,1024]{1,0:T(8,128)(2,1)}, u32[]{:S(2)}, u32[]{:S(2)}) collective-permute-start(bf16[256,1024]{1,0:T(8,128)(2,1)S(1)} %get-tuple-element.55.refs_0_), channel_id=1, source_target_pairs={{0,16},{8,24},{16,0},{24,8},{1,17},{9,25},{17,1},{25,9},{2,18},{10... | collective-permute-start | bytes 1572872 | tf_op jit(solution)/shard_map/ppermute | solution.py:26
  6.4 1.7 collective-permute-start.9
  8.2 9.8 %collective-permute-done.3 = s32[2,256]{1,0:T(2,128)S(1)} collective-permute-done((s32[2,256]{1,0:T(2,128)S(1)}, s32[2,256]{1,0:T(2,128)S(1)}, u32[]{:S(2)}, u32[]{:S(2)}) %collective-permute-start.3) | collective-permute-done | bytes 2080 | tf_op jit(solution)/shard_map/ppermute | solution.py:26
  18.0 2.0 %collective-permute-start = (bf16[256,1536]{1,0:T(8,128)(2,1)S(1)}, bf16[256,1536]{1,0:T(8,128)(2,1)S(1)}, u32[]{:S(2)}, u32[]{:S(2)}) collective-permute-start(bf16[256,1536]{1,0:T(8,128)(2,1)S(1)} %pad_maximum_fusion.refs_0_.refs_4_), channel_id=1, source_target_pairs={{0,16},{8,24},{16,0},{24,8},{1,17},{9,25},{17,1},{25,9},{2,18},{10... | collective-permute-start | bytes 2359304 | tf_op jit(solution)/shard_map/ppermute | solution.py:26
  21.4 2.3 %collective-permute-done.9.refs_5_ = bf16[256,512]{1,0:T(8,128)(2,1)} collective-permute-done((bf16[256,512]{1,0:T(8,128)(2,1)}, bf16[256,512]{1,0:T(8,128)(2,1)}, u32[]{:S(2)}, u32[]{:S(2)}) %collective-permute-start.9) | collective-permute-done | bytes 262176 | tf_op jit(solution)/shard_map/ppermute | solution.py:26
  23.7 2.6 %ahead.1.refs_10_ = f32[1024,512]{1,0:T(8,128)S(1)} custom-call(bf16[256,1024]{1,0:T(8,128)(2,1)S(1)} %get-tuple-element.55.refs_0_, bf16[256,1024]{1,0:T(8,128)(2,1)} %collective-permute-done.6.refs_1_, bf16[256,1024]{1,0:T(8,128)(2,1)} %collective-permute-done.7.refs_2_, bf16[256,1024]{1,0:T(8,128)(2,1)S(1)} %collective-permute-done.8.refs_3_, ...), custom_call_target="tpu_custom_call" | custom-call | tf_op jit(solution)/shard_map/ahead/pallas_call | solution.py:88
  26.4 10.1 %muon_round.2 = (f32[1024,512]{1,0:T(8,128)S(1)}, bf16[1024,512]{1,0:T(8,128)(2,1)S(1)}, f32[1024,512]{1,0:T(8,128)S(1)}, f32[512,512]{1,0:T(8,128)S(1)}, f32[51...) custom-call(bf16[256,1024]{1,0:T(8,128)(2,1)S(1)} %get-tuple-element, ...), custom_call_target="tpu_custom_call" | custom-call | tf_op jit(solution)/shard_map/muon_round/pallas_call | solution.py:231
  36.4 4.2 %collective-permute-start.15 = (bf16[384,512]{1,0:T(8,128)(2,1)S(1)}, bf16[384,512]{1,0:T(8,128)(2,1)S(1)}, u32[]{:S(2)}, u32[]{:S(2)}) collective-permute-start(bf16[384,512]{1,0:T(8,128)(2,1)S(1)} %get-tuple-element.33), channel_id=1, source_target_pairs={{2,0},{7,1},{4,2},{1,3},{6,4},{3,5},{0,6},{5,7},{10,8},{15,9},{12,... | collective-permute-start | bytes 1179656 | tf_op jit(solution)/shard_map/ppermute | solution.py:31
  41.7 1.3 row_gradients.3
  43.0 7.1 %collective-permute-done.15 = bf16[384,512]{1,0:T(8,128)(2,1)S(1)} collective-permute-done((bf16[384,512]{1,0:T(8,128)(2,1)S(1)}, bf16[384,512]{1,0:T(8,128)(2,1)S(1)}, u32[]{:S(2)}, u32[]{:S(2)}) %collective-permute-start.15) | collective-permute-done | bytes 393248 | tf_op jit(solution)/shard_map/ppermute | solution.py:31
  50.6 13.6 %collective-permute-done.16 = bf16[128,512]{1,0:T(8,128)(2,1)S(1)} collective-permute-done((bf16[128,512]{1,0:T(8,128)(2,1)S(1)}, bf16[128,512]{1,0:T(8,128)(2,1)S(1)}, u32[]{:S(2)}, u32[]{:S(2)}) %collective-permute-start.16) | collective-permute-done | bytes 131104 | tf_op jit(solution)/shard_map/ppermute | solution.py:31
  64.6 2.2 %collective-permute-start.14 = (bf16[512,512]{1,0:T(8,128)(2,1)S(1)}, bf16[512,512]{1,0:T(8,128)(2,1)S(1)}, u32[]{:S(2)}, u32[]{:S(2)}) collective-permute-start(bf16[512,512]{1,0:T(8,128)(2,1)S(1)} %add_convert_fusion.3), channel_id=1, source_target_pairs={{0,1},{1,0},{2,3},{3,2},{4,5},{5,4},{6,7},{7,6},{8,9},{9,8},{10,11... | collective-permute-start | bytes 1572872 | tf_op jit(solution)/shard_map/ppermute | solution.py:26
  66.8 9.0 %collective-permute-done.13.refs_6_ = bf16[512,512]{1,0:T(8,128)(2,1)S(1)} collective-permute-done((bf16[512,512]{1,0:T(8,128)(2,1)S(1)}, bf16[512,512]{1,0:T(8,128)(2,1)S(1)}, u32[]{:S(2)}, u32[]{:S(2)}) %collective-permute-start.13) | collective-permute-done | bytes 524320 | tf_op jit(solution)/shard_map/ppermute | solution.py:31
  75.8 3.7 %collective-permute-start.18 = (bf16[512,512]{1,0:T(8,128)(2,1)S(1)}, bf16[512,512]{1,0:T(8,128)(2,1)S(1)}, u32[]{:S(2)}, u32[]{:S(2)}) collective-permute-start(bf16[512,512]{1,0:T(8,128)(2,1)S(1)} %add_convert_fusion.2), channel_id=1, source_target_pairs={{0,1},{1,0},{2,3},{3,2},{4,5},{5,4},{6,7},{7,6},{8,9},{9,8},{10,11... | collective-permute-start | bytes 1572872 | tf_op jit(solution)/shard_map/ppermute | solution.py:26
  79.6 0.9 ahead_mixed.1
  80.5 11.1 %collective-permute-done.17.refs_15_ = bf16[512,512]{1,0:T(8,128)(2,1)S(1)} collective-permute-done((bf16[512,512]{1,0:T(8,128)(2,1)S(1)}, bf16[512,512]{1,0:T(8,128)(2,1)S(1)}, u32[]{:S(2)}, u32[]{:S(2)}) %collective-permute-start.17) | collective-permute-done | bytes 524320 | tf_op jit(solution)/shard_map/ppermute | solution.py:31
  91.9 11.0 %muon_round.3 = (f32[1024,512]{1,0:T(8,128)}, bf16[1024,512]{1,0:T(8,128)(2,1)S(1)}, f32[1024,512]{1,0:T(8,128)S(1)}, f32[512,512]{1,0:T(8,128)S(1)}, f32[512,51...) custom-call(bf16[256,1536]{1,0:T(8,128)(2,1)S(1)} %pad_maximum_fusio, ...), custom_call_target="tpu_custom_call" | custom-call | tf_op jit(solution)/shard_map/muon_round/pallas_call | solution.py:231
  102.9 11.3 %collective-permute-start.19 = (bf16[384,512]{1,0:T(8,128)(2,1)S(1)}, bf16[384,512]{1,0:T(8,128)(2,1)S(1)}, u32[]{:S(2)}, u32[]{:S(2)}) collective-permute-start(bf16[384,512]{1,0:T(8,128)(2,1)S(1)} %get-tuple-element.37), channel_id=1, source_target_pairs={{2,0},{7,1},{4,2},{1,3},{6,4},{3,5},{0,6},{5,7},{10,8},{15,9},{12,... | collective-permute-start | bytes 1179656 | tf_op jit(solution)/shard_map/ppermute | solution.py:31
  114.2 1.3 row_gradients.2
  116.1 1.6 collective-permute-start.24
  117.7 2.3 %collective-permute-start.20 = (bf16[128,512]{1,0:T(8,128)(2,1)S(1)}, bf16[128,512]{1,0:T(8,128)(2,1)S(1)}, u32[]{:S(2)}, u32[]{:S(2)}) collective-permute-start(bf16[128,512]{1,0:T(8,128)(2,1)S(1)} %get-tuple-element.38), channel_id=1, source_target_pairs={{2,0},{7,1},{4,2},{1,3},{6,4},{3,5},{0,6},{5,7},{10,8},{15,9},{12,... | collective-permute-start | bytes 393224 | tf_op jit(solution)/shard_map/ppermute | solution.py:31
  120.4 3.4 %collective-permute-done.19 = bf16[384,512]{1,0:T(8,128)(2,1)S(1)} collective-permute-done((bf16[384,512]{1,0:T(8,128)(2,1)S(1)}, bf16[384,512]{1,0:T(8,128)(2,1)S(1)}, u32[]{:S(2)}, u32[]{:S(2)}) %collective-permute-start.19) | collective-permute-done | bytes 393248 | tf_op jit(solution)/shard_map/ppermute | solution.py:31
  123.8 1.5 collective-permute-start.29
  125.3 23.2 %collective-permute-done.20 = bf16[128,512]{1,0:T(8,128)(2,1)S(1)} collective-permute-done((bf16[128,512]{1,0:T(8,128)(2,1)S(1)}, bf16[128,512]{1,0:T(8,128)(2,1)S(1)}, u32[]{:S(2)}, u32[]{:S(2)}) %collective-permute-start.20) | collective-permute-done | bytes 131104 | tf_op jit(solution)/shard_map/ppermute | solution.py:31
  148.7 3.4 %collective-permute-start.22 = (bf16[512,512]{1,0:T(8,128)(2,1)S(1)}, bf16[512,512]{1,0:T(8,128)(2,1)S(1)}, u32[]{:S(2)}, u32[]{:S(2)}) collective-permute-start(bf16[512,512]{1,0:T(8,128)(2,1)S(1)} %add_convert_fusion.1), channel_id=1, source_target_pairs={{0,1},{1,0},{2,3},{3,2},{4,5},{5,4},{6,7},{7,6},{8,9},{9,8},{10,11... | collective-permute-start | bytes 1572872 | tf_op jit(solution)/shard_map/ppermute | solution.py:26
  152.8 1.6 collective-permute-start.27
  154.4 0.9 shard_map.78.refs_2_
  155.2 18.7 %collective-permute-done.25.refs_3_ = bf16[512,512]{1,0:T(8,128)(2,1)S(1)} collective-permute-done((bf16[512,512]{1,0:T(8,128)(2,1)S(1)}, bf16[512,512]{1,0:T(8,128)(2,1)S(1)}, u32[]{:S(2)}, u32[]{:S(2)}) %collective-permute-start.25) | collective-permute-done | bytes 524320 | tf_op jit(solution)/shard_map/ppermute | solution.py:26
  173.9 1.2 shard_map.76.refs_4_
  175.2 1.3 shard_map.77
  176.5 0.8 shard_map.79
  (67 shorter events, 6.8 us)
Async XLA Ops:
  0.6 5.0 %copy-start.2 = (bf16[2,256,512]{2,1,0:T(8,128)(2,1)S(1)}, bf16[2,256,512]{2,1,0:T(8,128)(2,1)}, u32[]{:S(2)}) copy-start(bf16[2,256,512]{2,1,0:T(8,128)(2,1)} %param.7) | copy-start | bytes 1572868
  0.7 23.1 %copy-start = (f32[1,1,1024,512]{3,2,1,0:T(8,128)S(1)}, f32[1,1,1024,512]{3,2,1,0:T(8,128)}, u32[]{:S(2)}) copy-start(f32[1,1,1024,512]{3,2,1,0:T(8,128)} %param.8) | copy-start | bytes 6291460
  2.1 18.0 %collective-permute-start.6 = (bf16[256,1024]{1,0:T(8,128)(2,1)S(1)}, bf16[256,1024]{1,0:T(8,128)(2,1)}, u32[]{:S(2)}, u32[]{:S(2)}) collective-permute-start(bf16[256,1024]{1,0:T(8,128)(2,1)S(1)} %get-tuple-element.55.refs_0_), channel_id=1, source_target_pairs={{0,16},{8,24},{16,0},{24,8},{1,17},{9,25},{17,1},{25,9},{2,18},{10... | collective-permute-start | bytes 1572872 | tf_op jit(solution)/shard_map/ppermute | solution.py:26
  5.1 18.6 %collective-permute-start.7 = (bf16[256,1024]{1,0:T(8,128)(2,1)S(1)}, bf16[256,1024]{1,0:T(8,128)(2,1)}, u32[]{:S(2)}, u32[]{:S(2)}) collective-permute-start(bf16[256,1024]{1,0:T(8,128)(2,1)S(1)} %get-tuple-element.55.refs_0_), channel_id=1, source_target_pairs={{0,8},{8,0},{16,24},{24,16},{1,9},{9,1},{17,25},{25,17},{2,10},{10... | collective-permute-start | bytes 1572872 | tf_op jit(solution)/shard_map/ppermute | solution.py:26
  5.1 12.9 %collective-permute-start.3 = (s32[2,256]{1,0:T(2,128)S(1)}, s32[2,256]{1,0:T(2,128)S(1)}, u32[]{:S(2)}, u32[]{:S(2)}) collective-permute-start(s32[2,256]{1,0:T(2,128)S(1)} %copy-done.3), channel_id=1, source_target_pairs={{0,16},{8,24},{16,0},{24,8},{1,17},{9,25},{17,1},{25,9},{2,18},{10... | collective-permute-start | bytes 6152 | tf_op jit(solution)/shard_map/ppermute | solution.py:26
  5.3 14.7 %collective-permute-start.4 = (s32[2,256]{1,0:T(2,128)S(1)}, s32[2,256]{1,0:T(2,128)S(1)}, u32[]{:S(2)}, u32[]{:S(2)}) collective-permute-start(s32[2,256]{1,0:T(2,128)S(1)} %copy-done.3), channel_id=1, source_target_pairs={{0,8},{8,0},{16,24},{24,16},{1,9},{9,1},{17,25},{25,17},{2,10},{10... | collective-permute-start | bytes 6152 | tf_op jit(solution)/shard_map/ppermute | solution.py:26
  6.4 17.3 %collective-permute-start.9 = (bf16[256,512]{1,0:T(8,128)(2,1)}, bf16[256,512]{1,0:T(8,128)(2,1)}, u32[]{:S(2)}, u32[]{:S(2)}) collective-permute-start(bf16[256,512]{1,0:T(8,128)(2,1)} %get-tuple-element.57.refs_4_), channel_id=1, source_target_pairs={{0,16},{8,24},{16,0},{24,8},{1,17},{9,25},{17,1},{25,9},{2,18},{10... | collective-permute-start | bytes 786440 | tf_op jit(solution)/shard_map/ppermute | solution.py:26
  18.0 23.5 %collective-permute-start = (bf16[256,1536]{1,0:T(8,128)(2,1)S(1)}, bf16[256,1536]{1,0:T(8,128)(2,1)S(1)}, u32[]{:S(2)}, u32[]{:S(2)}) collective-permute-start(bf16[256,1536]{1,0:T(8,128)(2,1)S(1)} %pad_maximum_fusion.refs_0_.refs_4_), channel_id=1, source_target_pairs={{0,16},{8,24},{16,0},{24,8},{1,17},{9,25},{17,1},{25,9},{2,18},{10... | collective-permute-start | bytes 2359304 | tf_op jit(solution)/shard_map/ppermute | solution.py:26
  20.0 1.2 collective-permute-start.5
  20.0 3.6 %collective-permute-start.8 = (bf16[256,1024]{1,0:T(8,128)(2,1)}, bf16[256,1024]{1,0:T(8,128)(2,1)S(1)}, u32[]{:S(2)}, u32[]{:S(2)}) collective-permute-start(bf16[256,1024]{1,0:T(8,128)(2,1)} %collective-permute-done.6.refs_1_), channel_id=1, source_target_pairs={{0,8},{8,0},{16,24},{24,16},{1,9},{9,1},{17,25},{25,17},{2,10},{10... | collective-permute-start | bytes 1572872 | tf_op jit(solution)/shard_map/ppermute | solution.py:26
  21.2 5.1 %collective-permute-start.10 = (bf16[256,512]{1,0:T(8,128)(2,1)}, bf16[256,512]{1,0:T(8,128)(2,1)S(1)}, u32[]{:S(2)}, u32[]{:S(2)}) collective-permute-start(bf16[256,512]{1,0:T(8,128)(2,1)} %get-tuple-element.57.refs_4_), channel_id=1, source_target_pairs={{0,8},{8,0},{16,24},{24,16},{1,9},{9,1},{17,25},{25,17},{2,10},{10... | collective-permute-start | bytes 786440 | tf_op jit(solution)/shard_map/ppermute | solution.py:26
  23.7 2.7 %collective-permute-start.11 = (bf16[256,512]{1,0:T(8,128)(2,1)}, bf16[256,512]{1,0:T(8,128)(2,1)S(1)}, u32[]{:S(2)}, u32[]{:S(2)}) collective-permute-start(bf16[256,512]{1,0:T(8,128)(2,1)} %collective-permute-done.9.refs_5_), channel_id=1, source_target_pairs={{0,8},{8,0},{16,24},{24,16},{1,9},{9,1},{17,25},{25,17},{2,10},{10... | collective-permute-start | bytes 786440 | tf_op jit(solution)/shard_map/ppermute | solution.py:26
  36.4 13.7 %collective-permute-start.15 = (bf16[384,512]{1,0:T(8,128)(2,1)S(1)}, bf16[384,512]{1,0:T(8,128)(2,1)S(1)}, u32[]{:S(2)}, u32[]{:S(2)}) collective-permute-start(bf16[384,512]{1,0:T(8,128)(2,1)S(1)} %get-tuple-element.33), channel_id=1, source_target_pairs={{2,0},{7,1},{4,2},{1,3},{6,4},{3,5},{0,6},{5,7},{10,8},{15,9},{12,... | collective-permute-start | bytes 1179656 | tf_op jit(solution)/shard_map/ppermute | solution.py:31
  40.6 23.8 %collective-permute-start.12 = (bf16[512,512]{1,0:T(8,128)(2,1)S(1)}, bf16[512,512]{1,0:T(8,128)(2,1)S(1)}, u32[]{:S(2)}, u32[]{:S(2)}) collective-permute-start(bf16[512,512]{1,0:T(8,128)(2,1)S(1)} %get-tuple-element.28), channel_id=1, source_target_pairs={{2,0},{7,1},{4,2},{1,3},{6,4},{3,5},{0,6},{5,7},{10,8},{15,9},{12,... | collective-permute-start | bytes 1572872 | tf_op jit(solution)/shard_map/ppermute | solution.py:31
  41.1 25.7 %collective-permute-start.1 = (bf16[256,1536]{1,0:T(8,128)(2,1)S(1)}, bf16[256,1536]{1,0:T(8,128)(2,1)S(1)}, u32[]{:S(2)}, u32[]{:S(2)}) collective-permute-start(bf16[256,1536]{1,0:T(8,128)(2,1)S(1)} %pad_maximum_fusion.refs_0_.refs_4_), channel_id=1, source_target_pairs={{0,8},{8,0},{16,24},{24,16},{1,9},{9,1},{17,25},{25,17},{2,10},{10... | collective-permute-start | bytes 2359304 | tf_op jit(solution)/shard_map/ppermute | solution.py:26
  41.1 23.2 %collective-permute-start.16 = (bf16[128,512]{1,0:T(8,128)(2,1)S(1)}, bf16[128,512]{1,0:T(8,128)(2,1)S(1)}, u32[]{:S(2)}, u32[]{:S(2)}) collective-permute-start(bf16[128,512]{1,0:T(8,128)(2,1)S(1)} %get-tuple-element.34), channel_id=1, source_target_pairs={{2,0},{7,1},{4,2},{1,3},{6,4},{3,5},{0,6},{5,7},{10,8},{15,9},{12,... | collective-permute-start | bytes 393224 | tf_op jit(solution)/shard_map/ppermute | solution.py:31
  41.5 38.1 %collective-permute-start.2 = (bf16[256,1536]{1,0:T(8,128)(2,1)S(1)}, bf16[256,1536]{1,0:T(8,128)(2,1)S(1)}, u32[]{:S(2)}, u32[]{:S(2)}) collective-permute-start(bf16[256,1536]{1,0:T(8,128)(2,1)S(1)} %collective-permute-done.refs_1_.refs_5_), channel_id=1, source_target_pairs={{0,8},{8,0},{16,24},{24,16},{1,9},{9,1},{17,25},{25,17},{2,10},{10... | collective-permute-start | bytes 2359304 | tf_op jit(solution)/shard_map/ppermute | solution.py:26
  50.1 25.7 %collective-permute-start.13 = (bf16[512,512]{1,0:T(8,128)(2,1)S(1)}, bf16[512,512]{1,0:T(8,128)(2,1)S(1)}, u32[]{:S(2)}, u32[]{:S(2)}) collective-permute-start(bf16[512,512]{1,0:T(8,128)(2,1)S(1)} %get-tuple-element.28), channel_id=1, source_target_pairs={{6,0},{3,1},{0,2},{5,3},{2,4},{7,5},{4,6},{1,7},{14,8},{11,9},{8,1... | collective-permute-start | bytes 1572872 | tf_op jit(solution)/shard_map/ppermute | solution.py:31
  64.2 53.4 %collective-permute-start.28 = (bf16[2,256,1024]{2,1,0:T(8,128)(2,1)S(1)}, bf16[2,256,1024]{2,1,0:T(8,128)(2,1)S(1)}, u32[]{:S(2)}, u32[]{:S(2)}) collective-permute-start(bf16[2,256,1024]{2,1,0:T(8,128)(2,1)S(1)} %get-tuple-element.50), channel_id=1, source_target_pairs={{0,8},{8,0},{16,24},{24,16},{1,9},{9,1},{17,25},{25,17},{2,10},{10... | collective-permute-start | bytes 3145736 | tf_op jit(solution)/shard_map/ppermute | solution.py:26
  64.6 15.0 %collective-permute-start.14 = (bf16[512,512]{1,0:T(8,128)(2,1)S(1)}, bf16[512,512]{1,0:T(8,128)(2,1)S(1)}, u32[]{:S(2)}, u32[]{:S(2)}) collective-permute-start(bf16[512,512]{1,0:T(8,128)(2,1)S(1)} %add_convert_fusion.3), channel_id=1, source_target_pairs={{0,1},{1,0},{2,3},{3,2},{4,5},{5,4},{6,7},{7,6},{8,9},{9,8},{10,11... | collective-permute-start | bytes 1572872 | tf_op jit(solution)/shard_map/ppermute | solution.py:26
  66.8 24.8 %collective-permute-start.17 = (bf16[512,512]{1,0:T(8,128)(2,1)S(1)}, bf16[512,512]{1,0:T(8,128)(2,1)S(1)}, u32[]{:S(2)}, u32[]{:S(2)}) collective-permute-start(bf16[512,512]{1,0:T(8,128)(2,1)S(1)} %get-tuple-element.35), channel_id=1, source_target_pairs={{6,0},{3,1},{0,2},{5,3},{2,4},{7,5},{4,6},{1,7},{14,8},{11,9},{8,1... | collective-permute-start | bytes 1572872 | tf_op jit(solution)/shard_map/ppermute | solution.py:31
  75.8 16.0 %collective-permute-start.18 = (bf16[512,512]{1,0:T(8,128)(2,1)S(1)}, bf16[512,512]{1,0:T(8,128)(2,1)S(1)}, u32[]{:S(2)}, u32[]{:S(2)}) collective-permute-start(bf16[512,512]{1,0:T(8,128)(2,1)S(1)} %add_convert_fusion.2), channel_id=1, source_target_pairs={{0,1},{1,0},{2,3},{3,2},{4,5},{5,4},{6,7},{7,6},{8,9},{9,8},{10,11... | collective-permute-start | bytes 1572872 | tf_op jit(solution)/shard_map/ppermute | solution.py:26
  102.9 20.9 %collective-permute-start.19 = (bf16[384,512]{1,0:T(8,128)(2,1)S(1)}, bf16[384,512]{1,0:T(8,128)(2,1)S(1)}, u32[]{:S(2)}, u32[]{:S(2)}) collective-permute-start(bf16[384,512]{1,0:T(8,128)(2,1)S(1)} %get-tuple-element.37), channel_id=1, source_target_pairs={{2,0},{7,1},{4,2},{1,3},{6,4},{3,5},{0,6},{5,7},{10,8},{15,9},{12,... | collective-permute-start | bytes 1179656 | tf_op jit(solution)/shard_map/ppermute | solution.py:31
  115.5 36.7 %collective-permute-start.26 = (bf16[2,256,1024]{2,1,0:T(8,128)(2,1)S(1)}, bf16[2,256,1024]{2,1,0:T(8,128)(2,1)S(1)}, u32[]{:S(2)}, u32[]{:S(2)}) collective-permute-start(bf16[2,256,1024]{2,1,0:T(8,128)(2,1)S(1)} %get-tuple-element.46), channel_id=1, source_target_pairs={{0,8},{8,0},{16,24},{24,16},{1,9},{9,1},{17,25},{25,17},{2,10},{10... | collective-permute-start | bytes 3145736 | tf_op jit(solution)/shard_map/ppermute | solution.py:26
  115.6 33.1 %collective-permute-start.23 = (bf16[512,512]{1,0:T(8,128)(2,1)S(1)}, bf16[512,512]{1,0:T(8,128)(2,1)S(1)}, u32[]{:S(2)}, u32[]{:S(2)}) collective-permute-start(bf16[512,512]{1,0:T(8,128)(2,1)S(1)} %get-tuple-element.41), channel_id=1, source_target_pairs={{2,0},{7,1},{4,2},{1,3},{6,4},{3,5},{0,6},{5,7},{10,8},{15,9},{12,... | collective-permute-start | bytes 1572872 | tf_op jit(solution)/shard_map/ppermute | solution.py:31
  116.1 39.2 %collective-permute-start.24 = (bf16[512,512]{1,0:T(8,128)(2,1)S(1)}, bf16[512,512]{1,0:T(8,128)(2,1)S(1)}, u32[]{:S(2)}, u32[]{:S(2)}) collective-permute-start(bf16[512,512]{1,0:T(8,128)(2,1)S(1)} %get-tuple-element.41), channel_id=1, source_target_pairs={{6,0},{3,1},{0,2},{5,3},{2,4},{7,5},{4,6},{1,7},{14,8},{11,9},{8,1... | collective-permute-start | bytes 1572872 | tf_op jit(solution)/shard_map/ppermute | solution.py:31
  117.7 30.9 %collective-permute-start.20 = (bf16[128,512]{1,0:T(8,128)(2,1)S(1)}, bf16[128,512]{1,0:T(8,128)(2,1)S(1)}, u32[]{:S(2)}, u32[]{:S(2)}) collective-permute-start(bf16[128,512]{1,0:T(8,128)(2,1)S(1)} %get-tuple-element.38), channel_id=1, source_target_pairs={{2,0},{7,1},{4,2},{1,3},{6,4},{3,5},{0,6},{5,7},{10,8},{15,9},{12,... | collective-permute-start | bytes 393224 | tf_op jit(solution)/shard_map/ppermute | solution.py:31
  123.8 29.1 %collective-permute-start.29 = (bf16[1,256,1024]{2,1,0:T(8,128)(2,1)S(1)}, bf16[1,256,1024]{2,1,0:T(8,128)(2,1)S(1)}, u32[]{:S(2)}, u32[]{:S(2)}) collective-permute-start(bf16[1,256,1024]{2,1,0:T(8,128)(2,1)S(1)} %get-tuple-element.51), channel_id=1, source_target_pairs={{0,16},{8,24},{16,0},{24,8},{1,17},{9,25},{17,1},{25,9},{2,18},{10... | collective-permute-start | bytes 1572872 | tf_op jit(solution)/shard_map/ppermute | solution.py:26
  148.5 26.6 %collective-permute-start.21 = (bf16[512,512]{1,0:T(8,128)(2,1)S(1)}, bf16[512,512]{1,0:T(8,128)(2,1)S(1)}, u32[]{:S(2)}, u32[]{:S(2)}) collective-permute-start(bf16[512,512]{1,0:T(8,128)(2,1)S(1)} %get-tuple-element.39), channel_id=1, source_target_pairs={{6,0},{3,1},{0,2},{5,3},{2,4},{7,5},{4,6},{1,7},{14,8},{11,9},{8,1... | collective-permute-start | bytes 1572872 | tf_op jit(solution)/shard_map/ppermute | solution.py:31
  148.7 26.5 %collective-permute-start.22 = (bf16[512,512]{1,0:T(8,128)(2,1)S(1)}, bf16[512,512]{1,0:T(8,128)(2,1)S(1)}, u32[]{:S(2)}, u32[]{:S(2)}) collective-permute-start(bf16[512,512]{1,0:T(8,128)(2,1)S(1)} %add_convert_fusion.1), channel_id=1, source_target_pairs={{0,1},{1,0},{2,3},{3,2},{4,5},{5,4},{6,7},{7,6},{8,9},{9,8},{10,11... | collective-permute-start | bytes 1572872 | tf_op jit(solution)/shard_map/ppermute | solution.py:26
  152.2 21.7 %collective-permute-start.25 = (bf16[512,512]{1,0:T(8,128)(2,1)S(1)}, bf16[512,512]{1,0:T(8,128)(2,1)S(1)}, u32[]{:S(2)}, u32[]{:S(2)}) collective-permute-start(bf16[512,512]{1,0:T(8,128)(2,1)S(1)} %add_convert_fusion), channel_id=1, source_target_pairs={{0,1},{1,0},{2,3},{3,2},{4,5},{5,4},{6,7},{7,6},{8,9},{9,8},{10,11... | collective-permute-start | bytes 1572872 | tf_op jit(solution)/shard_map/ppermute | solution.py:26
  152.8 23.6 %collective-permute-start.27 = (bf16[1,256,1024]{2,1,0:T(8,128)(2,1)S(1)}, bf16[1,256,1024]{2,1,0:T(8,128)(2,1)S(1)}, u32[]{:S(2)}, u32[]{:S(2)}) collective-permute-start(bf16[1,256,1024]{2,1,0:T(8,128)(2,1)S(1)} %get-tuple-element.53), channel_id=1, source_target_pairs={{0,16},{8,24},{16,0},{24,8},{1,17},{9,25},{17,1},{25,9},{2,18},{10... | collective-permute-start | bytes 1572872 | tf_op jit(solution)/shard_map/ppermute | solution.py:26
  (2 other events, 7.1 us)

commit v3 on v1

v3 whole, which is shorter than its diff:
```python
import math

import jax
import jax.numpy as jnp
from jax import lax
from jax.experimental import pallas as pl
from jax.experimental.pallas import tpu as pltpu
from jax.sharding import PartitionSpec as P


ROUNDS = 2
NS_STEPS = 3
LEAD, LINEAR, QUADRATIC = 3.4445, -4.775, 2.0315
F32 = jnp.float32
BF16 = jnp.bfloat16
VMEM = pl.BlockSpec(memory_space=pltpu.VMEM)
SMEM = pl.BlockSpec(memory_space=pltpu.SMEM)
ANY = pl.BlockSpec(memory_space=pl.ANY)


def limit(mebibytes):
    return pltpu.CompilerParams(vmem_limit_bytes=mebibytes << 20)


def swapped(block, axis, bit):
    return lax.ppermute(block, axis, [(i, i ^ bit) for i in range(lax.axis_size(axis))])


def crossed(block, axis, way):
    count = lax.axis_size(axis)
    return lax.ppermute(
        block, axis, [((i + (-way if i % 2 else way)) % count, i) for i in range(count)]
    )


def dot(a, b):
    return jnp.dot(a, b, preferred_element_type=F32)


def dot_first(a, b):
    return lax.dot_general(a, b, (((0,), (0,)), ((), ())), preferred_element_type=F32)


def dot_last(a, b):
    return lax.dot_general(a, b, (((1,), (1,)), ((), ())), preferred_element_type=F32)


def factors(gram):
    rest, lead = None, 1.0
    for sweep in range(NS_STEPS):
        wide = gram.astype(F32)
        polynom_wide = LINEAR * wide + QUADRATIC * dot(gram, gram)
        polynom = polynom_wide.astype(BF16)
        if sweep == 0:
            rest = polynom_wide
        else:
            rest = lead * polynom_wide + LEAD * rest + dot(rest.astype(BF16), polynom)
        lead = lead * LEAD
        if sweep < NS_STEPS - 1:
            half = (LEAD * wide + dot(gram, polynom)).astype(BF16)
            gram = (LEAD * half.astype(F32) + dot(half, polynom)).astype(BF16)
    return rest, lead


def take(refs, start, stop):
    parts, offset = [], 0
    for ref in refs:
        low, high = max(start, offset), min(stop, offset + ref.shape[0])
        if low < high:
            parts.append(ref[low - offset : high - offset, :])
        offset += ref.shape[0]
    return parts[0] if len(parts) == 1 else jnp.concatenate(parts, axis=0)


def put(refs, start, value):
    offset, stop = 0, start + value.shape[0]
    for ref in refs:
        low, high = max(start, offset), min(stop, offset + ref.shape[0])
        if low < high:
            ref[low - offset : high - offset, :] = value[low - start : high - start, :]
        offset += ref.shape[0]


def mixed(parts, start, stop):
    stepped, first, second, near = (take(refs, start, stop) for refs in parts)
    total = first.astype(F32) + second.astype(F32) + near.astype(F32)
    return 0.4 * stepped + 0.15 * total


def split(depth):
    half, unit = depth // 2, depth // 16
    return (half, half - unit, unit), (12 * unit, 4 * unit), (half, half)


def sizes_of(arrays):
    return [len(item) for item in arrays]


def grouped(names, sizes):
    return [[next(names) for _ in range(size)] for size in sizes]


def ahead_kernel(sizes, refs):
    names = iter(refs)
    rows, parts = grouped(names, sizes[:1])[0], grouped(names, sizes[1:])
    if len(parts) == 1:
        value = parts[0][0][...]
    else:
        weight = next(names)
        value = mixed(parts, 0, weight.shape[0])
        weight[...] = value
    pre = next(names)
    shaped = value.astype(BF16)
    count, depth = rows[0].shape[0], value.shape[0]
    for block, ref in enumerate(rows):
        pre[block * count : (block + 1) * count, :] = dot(ref[:, :depth], shaped)


def ahead_call(rows, parts):
    early, width = parts[0][0].shape
    total = len(rows) * rows[0].shape[0]
    flat = [item for part in parts for item in part]
    shapes = [jax.ShapeDtypeStruct((total, width), F32)]
    if len(parts) > 1:
        shapes.insert(0, jax.ShapeDtypeStruct((early, width), F32))
    sizes = sizes_of([rows] + parts)
    return pl.pallas_call(
        lambda *refs: ahead_kernel(sizes, refs),
        out_shape=shapes,
        in_specs=[VMEM] * (len(rows) + len(flat)),
        out_specs=[VMEM] * len(shapes),
        compiler_params=limit(16),
        name="ahead",
    )(*rows, *flat)


def round_kernel(sizes, place, refs):
    names = iter(refs)
    route, mine, pre, moment = (next(names) for _ in range(4))
    rows, grads, weights, *parts = grouped(names, sizes)
    moment_out, slopes = next(names), next(names)
    depth, width = moment.shape
    _, two, _ = split(depth)
    stepped_out, share_out, one_out, two_out = grouped(names, (2, 2, 2, 2))
    late = next(names) if parts else None
    moment_low = next(names)
    count = rows[0].shape[0]
    factor = 1.0 / math.sqrt(depth)
    step_size = 0.1 * math.sqrt(depth)
    early = two[0]
    if parts:
        value = mixed(parts, early, depth)
        late[...] = value
        shaped = value.astype(BF16)
        weights = [*weights, late]
    columns = route[...].T
    lanes = route.shape[1]
    for block, ref in enumerate(rows):
        span = slice(block * count, (block + 1) * count)
        value = pre[span, :]
        if parts:
            value = value + dot(ref[:, early:depth], shaped)
        value = value * factor
        for piece in range(count // lanes):
            index = block * (count // lanes) + piece
            keep = columns[:, index : index + 1] == mine[0]
            part = slice(piece * lanes, (piece + 1) * lanes)
            slope = grads[block][part, place : place + width].astype(F32) * 2.0
            slope = slope * jnp.maximum(value[part, :], 0.0)
            slope = jnp.where(keep, slope, 0.0).astype(BF16)
            slopes[index * lanes : (index + 1) * lanes, :] = slope
    tile = min(256, depth)
    total = jnp.zeros((1, width), F32)
    for start in range(0, depth, tile):
        span = slice(start, start + tile)
        value = None
        for block, ref in enumerate(rows):
            term = dot_first(ref[:, span], slopes[block * count : (block + 1) * count, :])
            value = term if value is None else value + term
        value = 0.9 * moment[span, :] + value * factor
        moment_out[span, :] = value
        moment_low[span, :] = value.astype(BF16)
        total = total + jnp.sum(value * value, axis=0, keepdims=True)
    scale = 1.0 / (jnp.sqrt(jnp.sum(total)) + 1e-07)
    gram = (dot_first(moment_low[...], moment_low[...]) * (scale * scale)).astype(BF16)
    rest, lead = factors(gram)
    rest = rest.astype(BF16)
    for start in range(0, depth, tile):
        low = moment_low[start : start + tile, :]
        orthog = scale * (lead * low.astype(F32) + dot(low, rest))
        value = take(weights, start, start + tile) - step_size * orthog
        put(stepped_out, start, value)
        share = value.astype(BF16)
        put(share_out, start, share)
        put([share_out[0], *one_out], start, share)
        put(two_out, start, share)


def round_call(rows, grads, place, route, mine, pre, weight, moment, parts):
    depth, width = moment.shape
    total = len(rows) * rows[0].shape[0]
    one, two, near = split(depth)

    def shapes(counts, kind):
        return [jax.ShapeDtypeStruct((count, width), kind) for count in counts]

    flat = [item for part in parts for item in part]
    sizes = sizes_of([rows, grads, [weight]] + parts)
    out = shapes((depth,), F32) + shapes((total,), BF16) + shapes(two, F32)
    out = out + shapes(near + one[1:] + two, BF16) + shapes(two[1:] if parts else (), F32)
    result = pl.pallas_call(
        lambda *refs: round_kernel(sizes, place, refs),
        out_shape=out,
        in_specs=[VMEM, SMEM] + [VMEM] * (3 + 2 * len(rows) + len(flat)),
        out_specs=[VMEM] * len(out),
        scratch_shapes=[pltpu.VMEM((depth, width), BF16)],
        compiler_params=limit(24),
        name="muon_round",
    )(route, mine, pre, moment, *rows, *grads, weight, *flat)
    shares = result[4:6]
    return (
        result[0], result[1], result[2:4], shares, [shares[0], *result[6:8]], result[8:10],
        [weight, *result[10:]],
    )


def backward_kernel(refs):
    slopes, *weights, keep, send = refs
    depth = keep.shape[2]
    factor = 1.0 / math.sqrt(depth)
    shaped = take(weights, 0, depth).astype(BF16)
    half, count = keep.shape[:2]
    for block in range(2 * half):
        part = slopes[block * count : (block + 1) * count, :]
        out = keep if block < half else send
        out[block % half] = (dot_last(part, shaped) * factor).astype(BF16)


def backward_call(slopes, weights, blocks):
    depth = sum(item.shape[0] for item in weights)
    shape = jax.ShapeDtypeStruct((blocks // 2, slopes.shape[0] // blocks, depth), BF16)
    return pl.pallas_call(
        lambda *refs: backward_kernel(refs),
        out_shape=[shape, shape],
        in_specs=[VMEM] * (1 + len(weights)),
        out_specs=[VMEM, VMEM],
        compiler_params=limit(16),
        name="row_gradients",
    )(slopes, *weights)


def average_call(parts, start, stop, depth, buffer):
    flat = [item for part in parts for item in part]
    sizes = sizes_of(parts)
    extra = [] if buffer is None else [buffer]
    width = flat[0].shape[1]

    def kernel(*refs):
        names = iter(refs)
        groups = grouped(names, sizes)
        out, value, sem = list(names)[len(extra) :]
        value[...] = mixed(groups, start, stop)
        made = pltpu.make_async_copy(value, out.at[pl.ds(start, stop - start), :], sem)
        made.start()
        made.wait()

    return pl.pallas_call(
        kernel,
        out_shape=jax.ShapeDtypeStruct((depth, width), F32),
        in_specs=[VMEM] * len(flat) + [ANY] * len(extra),
        out_specs=ANY,
        scratch_shapes=[pltpu.VMEM((stop - start, width), F32), pltpu.SemaphoreType.DMA(())],
        input_output_aliases={len(flat): 0} if extra else {},
        compiler_params=limit(12),
        name="average",
    )(*flat, *extra)


def place_call(function, index, count, parts, buffer):
    block = parts[0].shape
    rest = (0,) * (len(block) - 1)
    extra = [] if buffer is None else [buffer]

    def kernel(*refs):
        refs[-1][...] = function(*refs[: len(parts)])

    return pl.pallas_call(
        kernel,
        grid=(1,),
        out_shape=jax.ShapeDtypeStruct((count * block[0],) + block[1:], parts[0].dtype),
        in_specs=[pl.BlockSpec(block, lambda i: (0,) + rest)] * len(parts) + [ANY] * len(extra),
        out_specs=pl.BlockSpec(block, lambda i: (index,) + rest),
        input_output_aliases={len(parts): 0} if extra else {},
        compiler_params=limit(12),
    )(*parts, *extra)


def on_device(tokens, routing, out_grad, weights, momentum):
    experts = lax.axis_size("expert")
    bits = []
    bit = experts // 2
    while bit:
        bits.append(bit)
        bit //= 2
    weight = weights[0, 0]
    moment = momentum[0, 0]
    depth = weight.shape[0]
    _, two, _ = split(depth)
    mine = lax.axis_index("expert").astype(jnp.int32).reshape(1)

    def gathered(own):
        held = [own]
        for bit in bits:
            held = held + [swapped(item, "expert", bit) for item in held]
        return held

    in_grad = None
    waiting = []
    first_rows = tokens[0]
    rest_tokens, rest_grad, first_rows = lax.optimization_barrier((tokens, out_grad, first_rows))
    rows = [gathered(first_rows)]
    routes = gathered(routing)
    grads = [gathered(rest_grad[0])]
    packed = jnp.concatenate([rest_tokens[1], rest_grad[1]], axis=1)
    rows.append(gathered(packed))
    grads.append(rows[1])
    (pre,) = ahead_call(rows[0], [[weight]])
    parts = []
    for index in range(ROUNDS):
        route = jnp.concatenate([item[index] for item in routes]).reshape(-1, 128)
        moment, slopes, stepped, shares, ones, twos, pieces = round_call(
            rows[index], grads[index], depth if index else 0, route, mine, pre,
            weight, moment, parts,
        )
        firsts = []
        for share in ones:
            firsts.append(crossed(share, "node", 2))
        seconds = []
        for share in twos:
            seconds.append(crossed(share, "node", -2))
        nears = []
        for piece, other in enumerate((firsts[0], jnp.concatenate(firsts[1:]))):
            pair = (shares[piece].astype(F32) + other.astype(F32)).astype(BF16)
            nears.append(swapped(pair, "node", 1))
        keep, send = backward_call(slopes, pieces, experts)
        for bit in reversed(bits):
            back = swapped(send, "expert", bit)
            if keep.shape[0] > 1:
                keep, send = jnp.split(keep + back, 2)
        waiting.append([keep, back])
        parts = [list(stepped), firsts, seconds, nears]
        if index < ROUNDS - 1:
            weight, pre = ahead_call(rows[index + 1], [stepped[:1], firsts[:2], seconds[:1], nears])
        else:
            for done, pair in enumerate(waiting):
                in_grad = place_call(lambda a, b: a[...] + b[...], done, ROUNDS, pair, in_grad)
            weight = average_call(
                [stepped[:1], firsts[:2], seconds[:1], nears], 0, two[0], depth, None
            )
            weight = average_call(parts, two[0], depth, depth, weight)
    return (weight[None, None], moment[None, None], in_grad)


def solution(mesh):
    return jax.shard_map(
        on_device,
        mesh=mesh,
        in_specs=(
            P(None, ("expert", "node"), None),
            P(None, ("expert", "node")),
            P(None, ("expert", "node"), None),
            P("node", "expert", None, None),
            P("node", "expert", None, None),
        ),
        out_specs=(
            P("node", "expert", None, None),
            P("node", "expert", None, None),
            P(None, ("expert", "node"), None),
        ),
        check_vma=False,
    )
```

time: 191 us -> 159 us (0.83)
  starting transfers between devices: 48.2 us -> 27.1 us
  Pallas kernels: 40.2 us -> 24.8 us
  waiting for transfers between devices: 89.5 us -> 101 us
  local copies, waits for them, and re-layouts: 8.36 us -> 3.2 us
  other arithmetic: 3.5 us -> 1.45 us
    ppermute x16 -> x10, waiting for transfers between devices: 49.5 us -> 69.7 us  [crossed(): lax.ppermute(block, axis, [((i + (-way if i % 2 else way)) % count, i) fo...]
    pallas_call x12 -> x10, Pallas kernels: 40.2 us -> 24.8 us  [the longest x2 14.1 us: round_call(): pl.pallas_call(lambda *refs: round_kernel(sizes, place, refs), out_shape=...]
    ppermute x16 -> x10, starting transfers between devices: 27.9 us -> 13.2 us  [crossed(): lax.ppermute(block, axis, [((i + (-way if i % 2 else way)) % count, i) fo...]
    ppermute x24 -> x20, waiting for transfers between devices: 40 us -> 31.4 us  [swapped(): lax.ppermute(block, axis, [(i, i ^ bit) for i in range(lax.axis_size(axis...]
    ppermute x24 -> x20, starting transfers between devices: 20.3 us -> 13.9 us  [swapped(): lax.ppermute(block, axis, [(i, i ^ bit) for i in range(lax.axis_size(axis...]
    unnamed x50 -> x8, local copies, waits for them, and re-layouts: 4.15 us -> 0.02 us
    slice x4 -> x0, local copies, waits for them, and re-layouts: 2.89 us -> none  [returned(): parts = parts[:half] + swapped(parts[half:], 'expert', bit)]
  transfers between devices with their start and end apart: 40 -> 30, of which waited for: 24 -> 9; matrix products, arithmetic and copies ran while one was open for 3% -> 3% of each run, Pallas kernels for 21% -> 15%
where the time goes in v3:
time: 159 us
  waiting for transfers between devices  101 us (64%)
  starting transfers between devices  27.1 us (17%)
  Pallas kernels  24.8 us (16%)
  local copies, waits for them, and re-layouts  3.2 us (2%)
    ppermute x10, waiting for transfers between devices, crossed(): lax.ppermute(block, axis, [((i + (-way if i % 2 else way)) % count, i) fo...  69.7 us
    ppermute x20, waiting for transfers between devices, swapped(): lax.ppermute(block, axis, [(i, i ^ bit) for i in range(lax.axis_size(axis...  31.4 us
    pallas_call x2, Pallas kernels, round_call(): pl.pallas_call(lambda *refs: round_kernel(sizes, place, refs), out_shape=...  14.1 us
    ppermute x20, starting transfers between devices, swapped(): lax.ppermute(block, axis, [(i, i ^ bit) for i in range(lax.axis_size(axis...  13.9 us
    ppermute x10, starting transfers between devices, crossed(): lax.ppermute(block, axis, [((i + (-way if i % 2 else way)) % count, i) fo...  13.2 us
    pallas_call x2, Pallas kernels, ahead_call(): pl.pallas_call(lambda *refs: ahead_kernel(sizes, refs), out_shape=shapes,...  3.8 us
  transfers between devices with their start and end apart: 30, of which 9 were waited for; matrix products, arithmetic and copies ran while one was open for 3% of the time, Pallas kernels for 15%

profile of v3, /device:TPU:0, one launch (start us, length us, event | category | flops | bytes accessed | tf_op | source)
XLA Modules:
  0.0 158.6 jit_solution(4572892054284674410)
XLA Ops:
  0.6 3.0 %collective-permute-start = (s32[2,256]{1,0:T(2,128)}, s32[2,256]{1,0:T(2,128)S(1)}, u32[]{:S(2)}, u32[]{:S(2)}) collective-permute-start(s32[2,256]{1,0:T(2,128)} %param.6), channel_id=1, source_target_pairs={{0,16},{8,24},{16,0},{24,8},{1,17},{9,25},{17,1},{25,9},{2,18},{10... | collective-permute-start | bytes 6152 | tf_op jit(solution)/shard_map/ppermute | solution.py:26
  3.7 1.1 slice_bitcast_fusion.1.refs_0_.refs_4_
  4.8 1.9 %slice_bitcast_fusion.2 = (bf16[256,512]{1,0:T(8,128)(2,1)}, bf16[256,512]{1,0:T(8,128)(2,1)S(1)}) fusion(bf16[2,256,512]{2,1,0:T(8,128)(2,1)} %param.7), kind=kLoop, calls=%fused_computation.7 | loop fusion | bytes 1048576 | tf_op jit(solution)/shard_map/squeeze | solution.py:323
  7.3 1.9 %collective-permute-start.6 = (bf16[256,1024]{1,0:T(8,128)(2,1)S(1)}, bf16[256,1024]{1,0:T(8,128)(2,1)}, u32[]{:S(2)}, u32[]{:S(2)}) collective-permute-start(bf16[256,1024]{1,0:T(8,128)(2,1)S(1)} %slice_bitcast_fusion.1.refs_0_.refs_4_), channel_id=1, source_target_pairs={{0,16},{8,24},{16,0},{24,8},{1,17},{9,25},{17,1},{25,9},{2,18},{10... | collective-permute-start | bytes 1572872 | tf_op jit(solution)/shard_map/ppermute | solution.py:26
  10.0 17.0 %collective-permute-done.6.refs_1_.refs_5_ = bf16[256,1024]{1,0:T(8,128)(2,1)} collective-permute-done((bf16[256,1024]{1,0:T(8,128)(2,1)S(1)}, bf16[256,1024]{1,0:T(8,128)(2,1)}, u32[]{:S(2)}, u32[]{:S(2)}) %collective-permute-start.6) | collective-permute-done | bytes 524320 | tf_op jit(solution)/shard_map/ppermute | solution.py:26
  27.6 1.5 collective-permute-done.8.refs_3_.refs_7_
  29.1 2.4 %ahead.2.refs_2_ = f32[1024,512]{1,0:T(8,128)S(1)} custom-call(bf16[256,1024]{1,0:T(8,128)(2,1)S(1)} %slice_bitcast_fusion.1.refs_0_.refs_4_, bf16[256,1024]{1,0:T(8,128)(2,1)} %collective-permute-done.6.refs_1_.refs_5_, bf16[256,1024]{1,0:T(8,128)(2,1)S(1)} %collective-permute-done.7.refs_2_.refs_6_, ...), custom_call_target="tpu_custom_call" | custom-call | tf_op jit(solution)/shard_map/ahead/pallas_call | solution.py:127
  31.6 7.5 %muon_round.2 = (f32[1024,512]{1,0:T(8,128)S(1)}, bf16[1024,512]{1,0:T(8,128)(2,1)S(1)}, f32[768,512]{1,0:T(8,128)S(1)}, f32[256,512]{1,0:T(8,128)S(1)}, bf16[51...) custom-call(s32[8,128]{1,0:T(8,128)S(1)} %pad_add_fusion.1.refs_0_, ...), custom_call_target="tpu_custom_call" | custom-call | tf_op jit(solution)/shard_map/muon_round/pallas_call | solution.py:211
  39.1 3.7 %collective-permute-start.13 = (bf16[448,512]{1,0:T(8,128)(2,1)S(1)}, bf16[448,512]{1,0:T(8,128)(2,1)S(1)}, u32[]{:S(2)}, u32[]{:S(2)}) collective-permute-start(bf16[448,512]{1,0:T(8,128)(2,1)S(1)} %get-tuple-element.38), channel_id=1, source_target_pairs={{2,0},{7,1},{4,2},{1,3},{6,4},{3,5},{0,6},{5,7},{10,8},{15,9},{12,... | collective-permute-start | bytes 1376264 | tf_op jit(solution)/shard_map/ppermute | solution.py:31
  43.7 3.3 %collective-permute-done.3.refs_1_.refs_5_.refs_9_ = bf16[256,1536]{1,0:T(8,128)(2,1)S(1)} collective-permute-done((bf16[256,1536]{1,0:T(8,128)(2,1)S(1)}, bf16[256,1536]{1,0:T(8,128)(2,1)S(1)}, u32[]{:S(2)}, u32[]{:S(2)}) %collective-permute-start.3) | collective-permute-done | bytes 786464 | tf_op jit(solution)/shard_map/ppermute | solution.py:26
  46.9 1.3 row_gradients.3
  48.2 17.4 %collective-permute-done.16.refs_17_ = bf16[64,512]{1,0:T(8,128)(2,1)S(1)} collective-permute-done((bf16[64,512]{1,0:T(8,128)(2,1)S(1)}, bf16[64,512]{1,0:T(8,128)(2,1)S(1)}, u32[]{:S(2)}, u32[]{:S(2)}) %collective-permute-start.16) | collective-permute-done | bytes 65568 | tf_op jit(solution)/shard_map/ppermute | solution.py:31
  66.1 3.6 %collective-permute-start.17 = (bf16[512,512]{1,0:T(8,128)(2,1)S(1)}, bf16[512,512]{1,0:T(8,128)(2,1)S(1)}, u32[]{:S(2)}, u32[]{:S(2)}) collective-permute-start(bf16[512,512]{1,0:T(8,128)(2,1)S(1)} %add_convert_fusion.2), channel_id=1, source_target_pairs={{0,1},{1,0},{2,3},{3,2},{4,5},{5,4},{6,7},{7,6},{8,9},{9,8},{10,11... | collective-permute-start | bytes 1572872 | tf_op jit(solution)/shard_map/ppermute | solution.py:26
  70.5 17.8 %collective-permute-done.14.refs_7_.refs_18_ = bf16[768,512]{1,0:T(8,128)(2,1)S(1)} collective-permute-done((bf16[768,512]{1,0:T(8,128)(2,1)S(1)}, bf16[768,512]{1,0:T(8,128)(2,1)S(1)}, u32[]{:S(2)}, u32[]{:S(2)}) %collective-permute-start.14) | collective-permute-done | bytes 786464 | tf_op jit(solution)/shard_map/ppermute | solution.py:31
  88.3 5.2 %collective-permute-done.15.refs_8_.refs_20_ = bf16[512,512]{1,0:T(8,128)(2,1)S(1)} collective-permute-done((bf16[512,512]{1,0:T(8,128)(2,1)S(1)}, bf16[512,512]{1,0:T(8,128)(2,1)S(1)}, u32[]{:S(2)}, u32[]{:S(2)}) %collective-permute-start.15) | collective-permute-done | bytes 524320 | tf_op jit(solution)/shard_map/ppermute | solution.py:26
  93.5 1.4 ahead.3
  94.9 6.6 %muon_round.3 = (f32[1024,512]{1,0:T(8,128)}, bf16[1024,512]{1,0:T(8,128)(2,1)S(1)}, f32[768,512]{1,0:T(8,128)S(1)}, f32[256,512]{1,0:T(8,128)S(1)}, bf16[512,51...) custom-call(s32[8,128]{1,0:T(8,128)S(1)} %pad_add_fusion.refs_0_, ...), custom_call_target="tpu_custom_call" | custom-call | tf_op jit(solution)/shard_map/muon_round/pallas_call | solution.py:211
  101.5 1.3 row_gradients.2
  102.9 2.2 %collective-permute-start.20 = (bf16[448,512]{1,0:T(8,128)(2,1)S(1)}, bf16[448,512]{1,0:T(8,128)(2,1)S(1)}, u32[]{:S(2)}, u32[]{:S(2)}) collective-permute-start(bf16[448,512]{1,0:T(8,128)(2,1)S(1)} %get-tuple-element.50), channel_id=1, source_target_pairs={{2,0},{7,1},{4,2},{1,3},{6,4},{3,5},{0,6},{5,7},{10,8},{15,9},{12,... | collective-permute-start | bytes 1376264 | tf_op jit(solution)/shard_map/ppermute | solution.py:31
  105.2 2.0 %collective-permute-start.19 = (bf16[512,512]{1,0:T(8,128)(2,1)S(1)}, bf16[512,512]{1,0:T(8,128)(2,1)S(1)}, u32[]{:S(2)}, u32[]{:S(2)}) collective-permute-start(bf16[512,512]{1,0:T(8,128)(2,1)S(1)} %get-tuple-element.49), channel_id=1, source_target_pairs={{2,0},{7,1},{4,2},{1,3},{6,4},{3,5},{0,6},{5,7},{10,8},{15,9},{12,... | collective-permute-start | bytes 1572872 | tf_op jit(solution)/shard_map/ppermute | solution.py:31
  107.8 0.6 collective-permute-start.29
  108.4 20.1 %collective-permute-done.21.refs_4_ = bf16[64,512]{1,0:T(8,128)(2,1)S(1)} collective-permute-done((bf16[64,512]{1,0:T(8,128)(2,1)S(1)}, bf16[64,512]{1,0:T(8,128)(2,1)S(1)}, u32[]{:S(2)}, u32[]{:S(2)}) %collective-permute-start.21) | collective-permute-done | bytes 65568 | tf_op jit(solution)/shard_map/ppermute | solution.py:31
  128.5 1.5 collective-permute-start.22
  130.2 2.1 %collective-permute-start.25 = (bf16[512,512]{1,0:T(8,128)(2,1)S(1)}, bf16[512,512]{1,0:T(8,128)(2,1)S(1)}, u32[]{:S(2)}, u32[]{:S(2)}) collective-permute-start(bf16[512,512]{1,0:T(8,128)(2,1)S(1)} %add_convert_fusion), channel_id=1, source_target_pairs={{0,1},{1,0},{2,3},{3,2},{4,5},{5,4},{6,7},{7,6},{8,9},{9,8},{10,11... | collective-permute-start | bytes 1572872 | tf_op jit(solution)/shard_map/ppermute | solution.py:26
  133.0 0.6 collective-permute-start.27
  133.6 2.0 %collective-permute-start.23 = (bf16[256,512]{1,0:T(8,128)(2,1)S(1)}, bf16[256,512]{1,0:T(8,128)(2,1)S(1)}, u32[]{:S(2)}, u32[]{:S(2)}) collective-permute-start(bf16[256,512]{1,0:T(8,128)(2,1)S(1)} %get-tuple-element.53), channel_id=1, source_target_pairs={{6,0},{3,1},{0,2},{5,3},{2,4},{7,5},{4,6},{1,7},{14,8},{11,9},{8,1... | collective-permute-start | bytes 786440 | tf_op jit(solution)/shard_map/ppermute | solution.py:31
  135.6 0.9 shard_map.76.refs_2_
  136.5 14.4 %collective-permute-done.22.refs_3_.refs_5_ = bf16[768,512]{1,0:T(8,128)(2,1)S(1)} collective-permute-done((bf16[768,512]{1,0:T(8,128)(2,1)S(1)}, bf16[768,512]{1,0:T(8,128)(2,1)S(1)}, u32[]{:S(2)}, u32[]{:S(2)}) %collective-permute-start.22) | collective-permute-done | bytes 786464 | tf_op jit(solution)/shard_map/ppermute | solution.py:31
  150.9 4.3 %collective-permute-done.24.refs_4_.refs_7_ = bf16[512,512]{1,0:T(8,128)(2,1)S(1)} collective-permute-done((bf16[512,512]{1,0:T(8,128)(2,1)S(1)}, bf16[512,512]{1,0:T(8,128)(2,1)S(1)}, u32[]{:S(2)}, u32[]{:S(2)}) %collective-permute-start.24) | collective-permute-done | bytes 524320 | tf_op jit(solution)/shard_map/ppermute | solution.py:26
  155.2 1.6 average.2.refs_9_
  156.8 1.0 average.3
  157.7 0.9 shard_map.77
  (64 shorter events, 5.5 us)
Async XLA Ops:
  0.6 8.6 %copy-start.2 = (bf16[2,256,1024]{2,1,0:T(8,128)(2,1)S(1)}, bf16[2,256,1024]{2,1,0:T(8,128)(2,1)}, u32[]{:S(2)}) copy-start(bf16[2,256,1024]{2,1,0:T(8,128)(2,1)} %param.5) | copy-start | bytes 3145732
  0.6 8.7 %collective-permute-start = (s32[2,256]{1,0:T(2,128)}, s32[2,256]{1,0:T(2,128)S(1)}, u32[]{:S(2)}, u32[]{:S(2)}) collective-permute-start(s32[2,256]{1,0:T(2,128)} %param.6), channel_id=1, source_target_pairs={{0,16},{8,24},{16,0},{24,8},{1,17},{9,25},{17,1},{25,9},{2,18},{10... | collective-permute-start | bytes 6152 | tf_op jit(solution)/shard_map/ppermute | solution.py:26
  3.7 5.8 %collective-permute-start.1 = (s32[2,256]{1,0:T(2,128)}, s32[2,256]{1,0:T(2,128)S(1)}, u32[]{:S(2)}, u32[]{:S(2)}) collective-permute-start(s32[2,256]{1,0:T(2,128)} %param.6), channel_id=1, source_target_pairs={{0,8},{8,0},{16,24},{24,16},{1,9},{9,1},{17,25},{25,17},{2,10},{10... | collective-permute-start | bytes 6152 | tf_op jit(solution)/shard_map/ppermute | solution.py:26
  4.8 24.3 %copy-start = (f32[1,1,1024,512]{3,2,1,0:T(8,128)S(1)}, f32[1,1,1024,512]{3,2,1,0:T(8,128)}, u32[]{:S(2)}) copy-start(f32[1,1,1024,512]{3,2,1,0:T(8,128)} %param.8) | copy-start | bytes 6291460
  6.7 24.8 %collective-permute-start.10 = (bf16[256,512]{1,0:T(8,128)(2,1)}, bf16[256,512]{1,0:T(8,128)(2,1)}, u32[]{:S(2)}, u32[]{:S(2)}) collective-permute-start(bf16[256,512]{1,0:T(8,128)(2,1)} %get-tuple-element.67.refs_8_), channel_id=1, source_target_pairs={{0,8},{8,0},{16,24},{24,16},{1,9},{9,1},{17,25},{25,17},{2,10},{10... | collective-permute-start | bytes 786440 | tf_op jit(solution)/shard_map/ppermute | solution.py:26
  7.2 20.1 %collective-permute-start.9 = (bf16[256,512]{1,0:T(8,128)(2,1)}, bf16[256,512]{1,0:T(8,128)(2,1)}, u32[]{:S(2)}, u32[]{:S(2)}) collective-permute-start(bf16[256,512]{1,0:T(8,128)(2,1)} %get-tuple-element.67.refs_8_), channel_id=1, source_target_pairs={{0,16},{8,24},{16,0},{24,8},{1,17},{9,25},{17,1},{25,9},{2,18},{10... | collective-permute-start | bytes 786440 | tf_op jit(solution)/shard_map/ppermute | solution.py:26
  7.3 19.7 %collective-permute-start.6 = (bf16[256,1024]{1,0:T(8,128)(2,1)S(1)}, bf16[256,1024]{1,0:T(8,128)(2,1)}, u32[]{:S(2)}, u32[]{:S(2)}) collective-permute-start(bf16[256,1024]{1,0:T(8,128)(2,1)S(1)} %slice_bitcast_fusion.1.refs_0_.refs_4_), channel_id=1, source_target_pairs={{0,16},{8,24},{16,0},{24,8},{1,17},{9,25},{17,1},{25,9},{2,18},{10... | collective-permute-start | bytes 1572872 | tf_op jit(solution)/shard_map/ppermute | solution.py:26
  9.4 18.2 %collective-permute-start.7 = (bf16[256,1024]{1,0:T(8,128)(2,1)S(1)}, bf16[256,1024]{1,0:T(8,128)(2,1)S(1)}, u32[]{:S(2)}, u32[]{:S(2)}) collective-permute-start(bf16[256,1024]{1,0:T(8,128)(2,1)S(1)} %slice_bitcast_fusion.1.refs_0_.refs_4_), channel_id=1, source_target_pairs={{0,8},{8,0},{16,24},{24,16},{1,9},{9,1},{17,25},{25,17},{2,10},{10... | collective-permute-start | bytes 1572872 | tf_op jit(solution)/shard_map/ppermute | solution.py:26
  9.5 17.5 %collective-permute-start.2 = (s32[2,256]{1,0:T(2,128)S(1)}, s32[2,256]{1,0:T(2,128)S(1)}, u32[]{:S(2)}, u32[]{:S(2)}) collective-permute-start(s32[2,256]{1,0:T(2,128)S(1)} %collective-permute-done), channel_id=1, source_target_pairs={{0,8},{8,0},{16,24},{24,16},{1,9},{9,1},{17,25},{25,17},{2,10},{10... | collective-permute-start | bytes 6152 | tf_op jit(solution)/shard_map/ppermute | solution.py:26
  27.0 2.1 %collective-permute-start.8 = (bf16[256,1024]{1,0:T(8,128)(2,1)}, bf16[256,1024]{1,0:T(8,128)(2,1)S(1)}, u32[]{:S(2)}, u32[]{:S(2)}) collective-permute-start(bf16[256,1024]{1,0:T(8,128)(2,1)} %collective-permute-done.6.refs_1_.refs_5_), channel_id=1, source_target_pairs={{0,8},{8,0},{16,24},{24,16},{1,9},{9,1},{17,25},{25,17},{2,10},{10... | collective-permute-start | bytes 1572872 | tf_op jit(solution)/shard_map/ppermute | solution.py:26
  27.0 20.0 %collective-permute-start.3 = (bf16[256,1536]{1,0:T(8,128)(2,1)S(1)}, bf16[256,1536]{1,0:T(8,128)(2,1)S(1)}, u32[]{:S(2)}, u32[]{:S(2)}) collective-permute-start(bf16[256,1536]{1,0:T(8,128)(2,1)S(1)} %pad_maximum_fusion.refs_0_.refs_4_.refs_8_), channel_id=1, source_target_pairs={{0,16},{8,24},{16,0},{24,8},{1,17},{9,25},{17,1},{25,9},{2,18},{10... | collective-permute-start | bytes 2359304 | tf_op jit(solution)/shard_map/ppermute | solution.py:26
  27.3 4.2 %collective-permute-start.11 = (bf16[256,512]{1,0:T(8,128)(2,1)}, bf16[256,512]{1,0:T(8,128)(2,1)S(1)}, u32[]{:S(2)}, u32[]{:S(2)}) collective-permute-start(bf16[256,512]{1,0:T(8,128)(2,1)} %collective-permute-done.9.refs_9_), channel_id=1, source_target_pairs={{0,8},{8,0},{16,24},{24,16},{1,9},{9,1},{17,25},{25,17},{2,10},{10... | collective-permute-start | bytes 786440 | tf_op jit(solution)/shard_map/ppermute | solution.py:26
  39.1 26.8 %collective-permute-start.13 = (bf16[448,512]{1,0:T(8,128)(2,1)S(1)}, bf16[448,512]{1,0:T(8,128)(2,1)S(1)}, u32[]{:S(2)}, u32[]{:S(2)}) collective-permute-start(bf16[448,512]{1,0:T(8,128)(2,1)S(1)} %get-tuple-element.38), channel_id=1, source_target_pairs={{2,0},{7,1},{4,2},{1,3},{6,4},{3,5},{0,6},{5,7},{10,8},{15,9},{12,... | collective-permute-start | bytes 1376264 | tf_op jit(solution)/shard_map/ppermute | solution.py:31
  42.8 23.3 %collective-permute-start.12 = (bf16[512,512]{1,0:T(8,128)(2,1)S(1)}, bf16[512,512]{1,0:T(8,128)(2,1)S(1)}, u32[]{:S(2)}, u32[]{:S(2)}) collective-permute-start(bf16[512,512]{1,0:T(8,128)(2,1)S(1)} %get-tuple-element.37), channel_id=1, source_target_pairs={{2,0},{7,1},{4,2},{1,3},{6,4},{3,5},{0,6},{5,7},{10,8},{15,9},{12,... | collective-permute-start | bytes 1572872 | tf_op jit(solution)/shard_map/ppermute | solution.py:31
  43.2 26.6 %collective-permute-start.4 = (bf16[256,1536]{1,0:T(8,128)(2,1)S(1)}, bf16[256,1536]{1,0:T(8,128)(2,1)S(1)}, u32[]{:S(2)}, u32[]{:S(2)}) collective-permute-start(bf16[256,1536]{1,0:T(8,128)(2,1)S(1)} %pad_maximum_fusion.refs_0_.refs_4_.refs_8_), channel_id=1, source_target_pairs={{0,8},{8,0},{16,24},{24,16},{1,9},{9,1},{17,25},{25,17},{2,10},{10... | collective-permute-start | bytes 2359304 | tf_op jit(solution)/shard_map/ppermute | solution.py:26
  43.2 22.4 %collective-permute-start.16 = (bf16[64,512]{1,0:T(8,128)(2,1)S(1)}, bf16[64,512]{1,0:T(8,128)(2,1)S(1)}, u32[]{:S(2)}, u32[]{:S(2)}) collective-permute-start(bf16[64,512]{1,0:T(8,128)(2,1)S(1)} %get-tuple-element.41), channel_id=1, source_target_pairs={{2,0},{7,1},{4,2},{1,3},{6,4},{3,5},{0,6},{5,7},{10,8},{15,9},{12,... | collective-permute-start | bytes 196616 | tf_op jit(solution)/shard_map/ppermute | solution.py:31
  46.9 23.0 %collective-permute-start.5 = (bf16[256,1536]{1,0:T(8,128)(2,1)S(1)}, bf16[256,1536]{1,0:T(8,128)(2,1)S(1)}, u32[]{:S(2)}, u32[]{:S(2)}) collective-permute-start(bf16[256,1536]{1,0:T(8,128)(2,1)S(1)} %collective-permute-done.3.refs_1_.refs_5_.refs_9_), channel_id=1, source_target_pairs={{0,8},{8,0},{16,24},{24,16},{1,9},{9,1},{17,25},{25,17},{2,10},{10... | collective-permute-start | bytes 2359304 | tf_op jit(solution)/shard_map/ppermute | solution.py:26
  65.6 22.7 %collective-permute-start.14 = (bf16[768,512]{1,0:T(8,128)(2,1)S(1)}, bf16[768,512]{1,0:T(8,128)(2,1)S(1)}, u32[]{:S(2)}, u32[]{:S(2)}) collective-permute-start(bf16[768,512]{1,0:T(8,128)(2,1)S(1)} %get-tuple-element.39), channel_id=1, source_target_pairs={{6,0},{3,1},{0,2},{5,3},{2,4},{7,5},{4,6},{1,7},{14,8},{11,9},{8,1... | collective-permute-start | bytes 2359304 | tf_op jit(solution)/shard_map/ppermute | solution.py:31
  65.9 41.3 %collective-permute-start.28 = (bf16[2,256,1024]{2,1,0:T(8,128)(2,1)S(1)}, bf16[2,256,1024]{2,1,0:T(8,128)(2,1)S(1)}, u32[]{:S(2)}, u32[]{:S(2)}) collective-permute-start(bf16[2,256,1024]{2,1,0:T(8,128)(2,1)S(1)} %get-tuple-element.62), channel_id=1, source_target_pairs={{0,8},{8,0},{16,24},{24,16},{1,9},{9,1},{17,25},{25,17},{2,10},{10... | collective-permute-start | bytes 3145736 | tf_op jit(solution)/shard_map/ppermute | solution.py:26
  66.1 22.2 %collective-permute-start.17 = (bf16[512,512]{1,0:T(8,128)(2,1)S(1)}, bf16[512,512]{1,0:T(8,128)(2,1)S(1)}, u32[]{:S(2)}, u32[]{:S(2)}) collective-permute-start(bf16[512,512]{1,0:T(8,128)(2,1)S(1)} %add_convert_fusion.2), channel_id=1, source_target_pairs={{0,1},{1,0},{2,3},{3,2},{4,5},{5,4},{6,7},{7,6},{8,9},{9,8},{10,11... | collective-permute-start | bytes 1572872 | tf_op jit(solution)/shard_map/ppermute | solution.py:26
  69.9 23.7 %collective-permute-start.15 = (bf16[512,512]{1,0:T(8,128)(2,1)S(1)}, bf16[512,512]{1,0:T(8,128)(2,1)S(1)}, u32[]{:S(2)}, u32[]{:S(2)}) collective-permute-start(bf16[512,512]{1,0:T(8,128)(2,1)S(1)} %add_convert_fusion.3), channel_id=1, source_target_pairs={{0,1},{1,0},{2,3},{3,2},{4,5},{5,4},{6,7},{7,6},{8,9},{9,8},{10,11... | collective-permute-start | bytes 1572872 | tf_op jit(solution)/shard_map/ppermute | solution.py:26
  69.9 25.0 %collective-permute-start.18 = (bf16[256,512]{1,0:T(8,128)(2,1)S(1)}, bf16[256,512]{1,0:T(8,128)(2,1)S(1)}, u32[]{:S(2)}, u32[]{:S(2)}) collective-permute-start(bf16[256,512]{1,0:T(8,128)(2,1)S(1)} %get-tuple-element.46), channel_id=1, source_target_pairs={{6,0},{3,1},{0,2},{5,3},{2,4},{7,5},{4,6},{1,7},{14,8},{11,9},{8,1... | collective-permute-start | bytes 786440 | tf_op jit(solution)/shard_map/ppermute | solution.py:31
  102.9 29.6 %collective-permute-start.26 = (bf16[2,256,1024]{2,1,0:T(8,128)(2,1)S(1)}, bf16[2,256,1024]{2,1,0:T(8,128)(2,1)S(1)}, u32[]{:S(2)}, u32[]{:S(2)}) collective-permute-start(bf16[2,256,1024]{2,1,0:T(8,128)(2,1)S(1)} %get-tuple-element.59), channel_id=1, source_target_pairs={{0,8},{8,0},{16,24},{24,16},{1,9},{9,1},{17,25},{25,17},{2,10},{10... | collective-permute-start | bytes 3145736 | tf_op jit(solution)/shard_map/ppermute | solution.py:26
  102.9 27.1 %collective-permute-start.20 = (bf16[448,512]{1,0:T(8,128)(2,1)S(1)}, bf16[448,512]{1,0:T(8,128)(2,1)S(1)}, u32[]{:S(2)}, u32[]{:S(2)}) collective-permute-start(bf16[448,512]{1,0:T(8,128)(2,1)S(1)} %get-tuple-element.50), channel_id=1, source_target_pairs={{2,0},{7,1},{4,2},{1,3},{6,4},{3,5},{0,6},{5,7},{10,8},{15,9},{12,... | collective-permute-start | bytes 1376264 | tf_op jit(solution)/shard_map/ppermute | solution.py:31
  105.2 27.1 %collective-permute-start.19 = (bf16[512,512]{1,0:T(8,128)(2,1)S(1)}, bf16[512,512]{1,0:T(8,128)(2,1)S(1)}, u32[]{:S(2)}, u32[]{:S(2)}) collective-permute-start(bf16[512,512]{1,0:T(8,128)(2,1)S(1)} %get-tuple-element.49), channel_id=1, source_target_pairs={{2,0},{7,1},{4,2},{1,3},{6,4},{3,5},{0,6},{5,7},{10,8},{15,9},{12,... | collective-permute-start | bytes 1572872 | tf_op jit(solution)/shard_map/ppermute | solution.py:31
  107.2 21.3 %collective-permute-start.21 = (bf16[64,512]{1,0:T(8,128)(2,1)S(1)}, bf16[64,512]{1,0:T(8,128)(2,1)S(1)}, u32[]{:S(2)}, u32[]{:S(2)}) collective-permute-start(bf16[64,512]{1,0:T(8,128)(2,1)S(1)} %get-tuple-element.51), channel_id=1, source_target_pairs={{2,0},{7,1},{4,2},{1,3},{6,4},{3,5},{0,6},{5,7},{10,8},{15,9},{12,... | collective-permute-start | bytes 196616 | tf_op jit(solution)/shard_map/ppermute | solution.py:31
  107.8 25.9 %collective-permute-start.29 = (bf16[1,256,1024]{2,1,0:T(8,128)(2,1)S(1)}, bf16[1,256,1024]{2,1,0:T(8,128)(2,1)S(1)}, u32[]{:S(2)}, u32[]{:S(2)}) collective-permute-start(bf16[1,256,1024]{2,1,0:T(8,128)(2,1)S(1)} %get-tuple-element.63), channel_id=1, source_target_pairs={{0,16},{8,24},{16,0},{24,8},{1,17},{9,25},{17,1},{25,9},{2,18},{10... | collective-permute-start | bytes 1572872 | tf_op jit(solution)/shard_map/ppermute | solution.py:26
  128.5 22.3 %collective-permute-start.22 = (bf16[768,512]{1,0:T(8,128)(2,1)S(1)}, bf16[768,512]{1,0:T(8,128)(2,1)S(1)}, u32[]{:S(2)}, u32[]{:S(2)}) collective-permute-start(bf16[768,512]{1,0:T(8,128)(2,1)S(1)} %get-tuple-element.52), channel_id=1, source_target_pairs={{6,0},{3,1},{0,2},{5,3},{2,4},{7,5},{4,6},{1,7},{14,8},{11,9},{8,1... | collective-permute-start | bytes 2359304 | tf_op jit(solution)/shard_map/ppermute | solution.py:31
  130.2 20.7 %collective-permute-start.25 = (bf16[512,512]{1,0:T(8,128)(2,1)S(1)}, bf16[512,512]{1,0:T(8,128)(2,1)S(1)}, u32[]{:S(2)}, u32[]{:S(2)}) collective-permute-start(bf16[512,512]{1,0:T(8,128)(2,1)S(1)} %add_convert_fusion), channel_id=1, source_target_pairs={{0,1},{1,0},{2,3},{3,2},{4,5},{5,4},{6,7},{7,6},{8,9},{9,8},{10,11... | collective-permute-start | bytes 1572872 | tf_op jit(solution)/shard_map/ppermute | solution.py:26
  132.4 22.8 %collective-permute-start.24 = (bf16[512,512]{1,0:T(8,128)(2,1)S(1)}, bf16[512,512]{1,0:T(8,128)(2,1)S(1)}, u32[]{:S(2)}, u32[]{:S(2)}) collective-permute-start(bf16[512,512]{1,0:T(8,128)(2,1)S(1)} %add_convert_fusion.1), channel_id=1, source_target_pairs={{0,1},{1,0},{2,3},{3,2},{4,5},{5,4},{6,7},{7,6},{8,9},{9,8},{10,11... | collective-permute-start | bytes 1572872 | tf_op jit(solution)/shard_map/ppermute | solution.py:26
  133.0 24.7 %collective-permute-start.27 = (bf16[1,256,1024]{2,1,0:T(8,128)(2,1)S(1)}, bf16[1,256,1024]{2,1,0:T(8,128)(2,1)S(1)}, u32[]{:S(2)}, u32[]{:S(2)}) collective-permute-start(bf16[1,256,1024]{2,1,0:T(8,128)(2,1)S(1)} %get-tuple-element.65), channel_id=1, source_target_pairs={{0,16},{8,24},{16,0},{24,8},{1,17},{9,25},{17,1},{25,9},{2,18},{10... | collective-permute-start | bytes 1572872 | tf_op jit(solution)/shard_map/ppermute | solution.py:26
  133.6 23.1 %collective-permute-start.23 = (bf16[256,512]{1,0:T(8,128)(2,1)S(1)}, bf16[256,512]{1,0:T(8,128)(2,1)S(1)}, u32[]{:S(2)}, u32[]{:S(2)}) collective-permute-start(bf16[256,512]{1,0:T(8,128)(2,1)S(1)} %get-tuple-element.53), channel_id=1, source_target_pairs={{6,0},{3,1},{0,2},{5,3},{2,4},{7,5},{4,6},{1,7},{14,8},{11,9},{8,1... | collective-permute-start | bytes 786440 | tf_op jit(solution)/shard_map/ppermute | solution.py:31
  (2 other events, 7.0 us)

commit v4 on v3

--- a/solution.py
+++ b/solution.py
@@ -116,8 +116,8 @@
         pre[block * count : (block + 1) * count, :] = dot(ref[:, :depth], shaped)
 
 
-def ahead_call(rows, parts):
-    early, width = parts[0][0].shape
+def ahead_call(rows, parts, early):
+    width = parts[0][0].shape[1]
     total = len(rows) * rows[0].shape[0]
     flat = [item for part in parts for item in part]
     shapes = [jax.ShapeDtypeStruct((total, width), F32)]
@@ -134,33 +134,13 @@
     )(*rows, *flat)
 
 
-def round_kernel(sizes, place, refs):
-    names = iter(refs)
-    route, mine, pre, moment = (next(names) for _ in range(4))
-    rows, grads, weights, *parts = grouped(names, sizes)
-    moment_out, slopes = next(names), next(names)
-    depth, width = moment.shape
-    _, two, _ = split(depth)
-    stepped_out, share_out, one_out, two_out = grouped(names, (2, 2, 2, 2))
-    late = next(names) if parts else None
-    moment_low = next(names)
-    count = rows[0].shape[0]
-    factor = 1.0 / math.sqrt(depth)
-    step_size = 0.1 * math.sqrt(depth)
-    early = two[0]
-    if parts:
-        value = mixed(parts, early, depth)
-        late[...] = value
-        shaped = value.astype(BF16)
-        weights = [*weights, late]
+def slope_rows(route, mine, rows, grads, place, pre_of, slopes):
     columns = route[...].T
     lanes = route.shape[1]
+    width = slopes.shape[1]
     for block, ref in enumerate(rows):
-        span = slice(block * count, (block + 1) * count)
-        value = pre[span, :]
-        if parts:
-            value = value + dot(ref[:, early:depth], shaped)
-        value = value * factor
+        count = ref.shape[0]
+        value = pre_of(block, ref)
         for piece in range(count // lanes):
             index = block * (count // lanes) + piece
             keep = columns[:, index : index + 1] == mine[0]
@@ -169,84 +149,212 @@
             slope = slope * jnp.maximum(value[part, :], 0.0)
             slope = jnp.where(keep, slope, 0.0).astype(BF16)
             slopes[index * lanes : (index + 1) * lanes, :] = slope
+
+
+def weight_gradient(rows, slopes, span):
+    value = None
+    for block, ref in enumerate(rows):
+        count = ref.shape[0]
+        term = dot_first(ref[:, span], slopes[block * count : (block + 1) * count, :])
+        value = term if value is None else value + term
+    return value
+
+
+def tiles(depth):
     tile = min(256, depth)
+    return [slice(start, start + tile) for start in range(0, depth, tile)]
+
+
+def local_kernel(sizes, refs):
+    names = iter(refs)
+    route, mine, weight, moment = (next(names) for _ in range(4))
+    rows, grads = grouped(names, sizes)
+    partial, slopes = names
+    depth = weight.shape[0]
+    factor = 1.0 / math.sqrt(depth)
+    shaped = weight[...].astype(BF16)
+    slope_rows(
+        route, mine, rows, grads, 0, lambda block, ref: dot(ref[...], shaped) * factor, slopes
+    )
+    for span in tiles(depth):
+        partial[span, :] = 0.9 * moment[span, :] + weight_gradient(rows, slopes, span) * factor
+
+
+def local_call(rows, grads, route, mine, weight, moment):
+    depth, width = weight.shape
+    total = len(rows) * rows[0].shape[0]
+    sizes = sizes_of([rows, grads])
+    return pl.pallas_call(
+        lambda *refs: local_kernel(sizes, refs),
+        out_shape=[
+            jax.ShapeDtypeStruct((depth, width), F32),
+            jax.ShapeDtypeStruct((total, width), BF16),
+        ],
+        in_specs=[VMEM, SMEM] + [VMEM] * (2 + 2 * len(rows)),
+        out_specs=[VMEM] * 2,
+        compiler_params=limit(16),
+        name="local_rows",
+    )(route, mine, weight, moment, *rows, *grads)
+
+
+def round_kernel(sizes, place, decay, refs):
+    names = iter(refs)
+    route, mine, pre, moment = (next(names) for _ in range(4))
+    rows, grads, weights, *parts = grouped(names, sizes)
+    moment_out, slopes, moment_low, rest_out, scale_out, stepped, share = (
+        next(names) for _ in range(7)
+    )
+    depth, width = moment.shape
+    half, early = split(depth)[2][0], split(depth)[1][0]
+    factor = 1.0 / math.sqrt(depth)
+    if parts:
+        late = next(names)
+        value = mixed(parts, early, depth)
+        late[...] = value
+        shaped = value.astype(BF16)
+
+    def pre_of(block, ref):
+        count = ref.shape[0]
+        value = pre[block * count : (block + 1) * count, :]
+        if parts:
+            value = value + dot(ref[:, early:depth], shaped)
+        return value * factor
+
+    slope_rows(route, mine, rows, grads, place, pre_of, slopes)
     total = jnp.zeros((1, width), F32)
-    for start in range(0, depth, tile):
-        span = slice(start, start + tile)
-        value = None
-        for block, ref in enumerate(rows):
-            term = dot_first(ref[:, span], slopes[block * count : (block + 1) * count, :])
-            value = term if value is None else value + term
-        value = 0.9 * moment[span, :] + value * factor
+    for span in tiles(depth):
+        value = weight_gradient(rows, slopes, span) * factor
+        value = (moment[span, :] if decay == 1.0 else decay * moment[span, :]) + value
         moment_out[span, :] = value
         moment_low[span, :] = value.astype(BF16)
         total = total + jnp.sum(value * value, axis=0, keepdims=True)
     scale = 1.0 / (jnp.sqrt(jnp.sum(total)) + 1e-07)
+    scale_out[0] = scale
     gram = (dot_first(moment_low[...], moment_low[...]) * (scale * scale)).astype(BF16)
-    rest, lead = factors(gram)
-    rest = rest.astype(BF16)
-    for start in range(0, depth, tile):
-        low = moment_low[start : start + tile, :]
-        orthog = scale * (lead * low.astype(F32) + dot(low, rest))
-        value = take(weights, start, start + tile) - step_size * orthog
-        put(stepped_out, start, value)
-        share = value.astype(BF16)
-        put(share_out, start, share)
-        put([share_out[0], *one_out], start, share)
-        put(two_out, start, share)
-
-
-def round_call(rows, grads, place, route, mine, pre, weight, moment, parts):
+    rest = factors(gram)[0].astype(BF16)
+    rest_out[...] = rest
+    step_rows(tiles(half), weights, moment_low, rest, scale, [stepped], [[share]], 0)
+
+
+def step_rows(spans, weights, moment_low, rest, scale, stepped, shares, base):
+    step_size = 0.1 * math.sqrt(moment_low.shape[0])
+    for span in spans:
+        low = moment_low[span, :]
+        orthog = scale * (LEAD**NS_STEPS * low.astype(F32) + dot(low, rest))
+        value = take(weights, span.start, span.stop) - step_size * orthog
+        put(stepped, span.start - base, value)
+        for refs in shares:
+            put(refs, span.start - base, value.astype(BF16))
+
+
+def round_call(rows, grads, place, decay, route, mine, pre, weights, moment, parts):
     depth, width = moment.shape
     total = len(rows) * rows[0].shape[0]
+    half, late = split(depth)[2][0], split(depth)[1][1]
+    shape = jax.ShapeDtypeStruct
+    flat = [item for part in parts for item in part]
+    sizes = sizes_of([rows, grads, weights] + parts)
+    out = [
+        shape((depth, width), F32),
+        shape((total, width), BF16),
+        shape((depth, width), BF16),
+        shape((width, width), BF16),
+        shape((1,), F32),
+        shape((half, width), F32),
+        shape((half, width), BF16),
+    ]
+    specs = [VMEM] * 4 + [SMEM] + [VMEM] * 2
+    if parts:
+        out.append(shape((late, width), F32))
+        specs.append(VMEM)
+    return pl.pallas_call(
+        lambda *refs: round_kernel(sizes, place, decay, refs),
+        out_shape=out,
+        in_specs=[VMEM, SMEM] + [VMEM] * (2 + 2 * len(rows) + len(weights) + len(flat)),
+        out_specs=specs,
+        compiler_params=limit(16),
+        name="muon_round",
+    )(route, mine, pre, moment, *rows, *grads, *weights, *flat)
+
+
+def second_kernel(count, refs):
+    moment_low, rest, scale, share, *names = refs
+    weights, names = names[:count], iter(names[count:])
+    stepped, share_out, *rest_out = names
+    ones, twos = rest_out[:2], rest_out[2:]
+    depth = moment_low.shape[0]
+    half = share.shape[0]
+    put(twos, 0, share[...])
+    spans = [span for span in tiles(depth) if span.start >= half]
+    step_rows(
+        spans, weights, moment_low, rest[...], scale[0], [stepped], [[share_out], ones], half
+    )
+    put(twos, half, share_out[...])
+
+
+def second_call(moment_low, rest, scale, share, weights):
+    depth, width = moment_low.shape
     one, two, near = split(depth)
-
-    def shapes(counts, kind):
-        return [jax.ShapeDtypeStruct((count, width), kind) for count in counts]
-
-    flat = [item for part in parts for item in part]
-    sizes = sizes_of([rows, grads, [weight]] + parts)
-    out = shapes((depth,), F32) + shapes((total,), BF16) + shapes(two, F32)
-    out = out + shapes(near + one[1:] + two, BF16) + shapes(two[1:] if parts else (), F32)
+    shape = jax.ShapeDtypeStruct
+    out = [shape((near[1], width), F32)]
+    out = out + [shape((size, width), BF16) for size in near[1:] + one[1:] + two]
     result = pl.pallas_call(
-        lambda *refs: round_kernel(sizes, place, refs),
+        lambda *refs: second_kernel(len(weights), refs),
         out_shape=out,
-        in_specs=[VMEM, SMEM] + [VMEM] * (3 + 2 * len(rows) + len(flat)),
+        in_specs=[VMEM] * 2 + [SMEM] + [VMEM] * (1 + len(weights)),
         out_specs=[VMEM] * len(out),
-        scratch_shapes=[pltpu.VMEM((depth, width), BF16)],
-        compiler_params=limit(24),
-        name="muon_round",
-    )(route, mine, pre, moment, *rows, *grads, weight, *flat)
-    shares = result[4:6]
-    return (
-        result[0], result[1], result[2:4], shares, [shares[0], *result[6:8]], result[8:10],
-        [weight, *result[10:]],
-    )
-
-
-def backward_kernel(refs):
-    slopes, *weights, keep, send = refs
+        compiler_params=limit(12),
+        name="second_half",
+    )(moment_low, rest, scale, share, *weights)
+    return result[0], result[1], [share, *result[2:4]], result[4:]
+
+
+def backward_kernel(sizes, refs):
+    names = iter(refs)
+    slopes, weights = grouped(names, sizes)
+    keep, send = names
     depth = keep.shape[2]
     factor = 1.0 / math.sqrt(depth)
     shaped = take(weights, 0, depth).astype(BF16)
     half, count = keep.shape[:2]
     for block in range(2 * half):
-        part = slopes[block * count : (block + 1) * count, :]
+        place = block // len(slopes) * count
+        part = slopes[block % len(slopes)][place : place + count, :]
         out = keep if block < half else send
         out[block % half] = (dot_last(part, shaped) * factor).astype(BF16)
 
 
 def backward_call(slopes, weights, blocks):
     depth = sum(item.shape[0] for item in weights)
-    shape = jax.ShapeDtypeStruct((blocks // 2, slopes.shape[0] // blocks, depth), BF16)
-    return pl.pallas_call(
-        lambda *refs: backward_kernel(refs),
+    count = sum(item.shape[0] for item in slopes) // blocks
+    shape = jax.ShapeDtypeStruct((blocks // 2, count, depth), BF16)
+    sizes = sizes_of([slopes, weights])
+    return pl.pallas_call(
+        lambda *refs: backward_kernel(sizes, refs),
         out_shape=[shape, shape],
-        in_specs=[VMEM] * (1 + len(weights)),
+        in_specs=[VMEM] * (len(slopes) + len(weights)),
         out_specs=[VMEM, VMEM],
         compiler_params=limit(16),
         name="row_gradients",
-    )(slopes, *weights)
+    )(*slopes, *weights)
+
+
+def halve_call(keep, back):
+    half = keep.shape[0] // 2
+    shape = jax.ShapeDtypeStruct((half,) + keep.shape[1:], keep.dtype)
+
+    def kernel(keep, back, first, second):
+        first[...] = keep[:half] + back[:half]
+        second[...] = keep[half:] + back[half:]
+
+    return pl.pallas_call(
+        kernel,
+        out_shape=[shape, shape],
+        in_specs=[VMEM] * 2,
+        out_specs=[VMEM] * 2,
+        compiler_params=limit(12),
+        name="halve",
+    )(keep, back)
 
 
 def average_call(parts, start, stop, depth, buffer):
@@ -311,52 +419,77 @@
     def gathered(own):
         held = [own]
         for bit in bits:
-            held = held + [swapped(item, "expert", bit) for item in held]
+            moved = []
+            for item in held:
+                moved.append(swapped(item, "expert", bit))
+            held = held + moved
         return held
 
     in_grad = None
     waiting = []
-    first_rows = tokens[0]
-    rest_tokens, rest_grad, first_rows = lax.optimization_barrier((tokens, out_grad, first_rows))
-    rows = [gathered(first_rows)]
+    own_rows, rest_tokens, rest_grad = lax.optimization_barrier(
+        (tokens[0], tokens, out_grad)
+    )
+    own_grads = rest_grad[0]
+    packed = jnp.concatenate([rest_tokens[1], rest_grad[1]], axis=1)
+    first_rows = gathered(own_rows)
     routes = gathered(routing)
-    grads = [gathered(rest_grad[0])]
-    packed = jnp.concatenate([rest_tokens[1], rest_grad[1]], axis=1)
-    rows.append(gathered(packed))
-    grads.append(rows[1])
-    (pre,) = ahead_call(rows[0], [[weight]])
+    first_grads = gathered(own_grads)
+    later = gathered(packed)
+
+    def route_of(index, items):
+        picked = [item[index] for item in items]
+        return jnp.concatenate(picked * (experts // len(picked))).reshape(-1, 128)
+
+    moment, slopes = local_call(
+        first_rows[0::2], first_grads[0::2], route_of(0, routes[0::2]), mine, weight, moment
+    )
+    all_slopes = [slopes]
+    (pre,) = ahead_call(first_rows[1::2], [[weight]], depth)
+    weights = [weight]
     parts = []
     for index in range(ROUNDS):
-        route = jnp.concatenate([item[index] for item in routes]).reshape(-1, 128)
-        moment, slopes, stepped, shares, ones, twos, pieces = round_call(
-            rows[index], grads[index], depth if index else 0, route, mine, pre,
-            weight, moment, parts,
-        )
+        if index:
+            moment, slopes, low, rest, scale, stepped, share, late = round_call(
+                later, later, depth, 0.9, route_of(index, routes), mine, pre, weights,
+                moment, parts,
+            )
+            weights = [*weights, late]
+            all_slopes = [slopes]
+        else:
+            moment, slopes, low, rest, scale, stepped, share = round_call(
+                first_rows[1::2], first_grads[1::2], 0, 1.0, route_of(0, routes[1::2]),
+                mine, pre, weights, moment, parts,
+            )
+            all_slopes.append(slopes)
+        stepped_low, share_low, ones, twos = second_call(low, rest, scale, share, weights)
         firsts = []
-        for share in ones:
-            firsts.append(crossed(share, "node", 2))
+        for item in ones:
+            firsts.append(crossed(item, "node", 2))
         seconds = []
-        for share in twos:
-            seconds.append(crossed(share, "node", -2))
+        for item in twos:
+            seconds.append(crossed(item, "node", -2))
         nears = []
-        for piece, other in enumerate((firsts[0], jnp.concatenate(firsts[1:]))):
-            pair = (shares[piece].astype(F32) + other.astype(F32)).astype(BF16)
+        others = (firsts[0], jnp.concatenate(firsts[1:]))
+        for piece, item in enumerate((share, share_low)):
+            pair = (item.astype(F32) + others[piece].astype(F32)).astype(BF16)
             nears.append(swapped(pair, "node", 1))
-        keep, send = backward_call(slopes, pieces, experts)
+        keep, send = backward_call(all_slopes, weights, experts)
         for bit in reversed(bits):
             back = swapped(send, "expert", bit)
             if keep.shape[0] > 1:
-                keep, send = jnp.split(keep + back, 2)
+                keep, send = halve_call(keep, back)
         waiting.append([keep, back])
-        parts = [list(stepped), firsts, seconds, nears]
+        halves = [stepped, stepped_low]
+        parts = [halves, firsts, seconds, nears]
+        early_parts = [halves, firsts[:2], seconds[:1], nears]
         if index < ROUNDS - 1:
-            weight, pre = ahead_call(rows[index + 1], [stepped[:1], firsts[:2], seconds[:1], nears])
+            upper, pre = ahead_call(later, early_parts, two[0])
+            weights = [upper]
         else:
             for done, pair in enumerate(waiting):
                 in_grad = place_call(lambda a, b: a[...] + b[...], done, ROUNDS, pair, in_grad)
-            weight = average_call(
-                [stepped[:1], firsts[:2], seconds[:1], nears], 0, two[0], depth, None
-            )
+            weight = average_call(early_parts, 0, two[0], depth, None)
             weight = average_call(parts, two[0], depth, depth, weight)
     return (weight[None, None], moment[None, None], in_grad)
 

time: 159 us -> 160 us (level)
  waiting for transfers between devices: 101 us -> 97.4 us
  local copies, waits for them, and re-layouts: 3.2 us -> 5.43 us
  starting transfers between devices: 27.1 us -> 29 us
  Pallas kernels: 24.8 us -> 26.6 us
    ppermute x20, waiting for transfers between devices: 31.4 us -> 27.7 us  [swapped(): lax.ppermute(block, axis, [(i, i ^ bit) for i in range(lax.axis_size(axis...]
    pallas_call x4 -> x9, Pallas kernels: 16.8 us -> 20.2 us  [the longest x2 12.3 us: round_call(): pl.pallas_call(lambda *refs: round_kernel(sizes, place, decay, refs), out...]
    ppermute x20, starting transfers between devices: 13.9 us -> 15.7 us  [swapped(): lax.ppermute(block, axis, [(i, i ^ bit) for i in range(lax.axis_size(axis...]
    pallas_call x2, Pallas kernels: 3.8 us -> 2.02 us  [ahead_call(): pl.pallas_call(lambda *refs: ahead_kernel(sizes, refs), out_shape=shapes,...]
  transfers between devices with their start and end apart: 30 -> 30, of which waited for: 9 -> 8; matrix products, arithmetic and copies ran while one was open for 3% -> 3% of each run, Pallas kernels for 15% -> 16%
where the time goes in v4:
time: 160 us
  waiting for transfers between devices  97.4 us (61%)
  starting transfers between devices  29 us (18%)
  Pallas kernels  26.6 us (17%)
  local copies, waits for them, and re-layouts  5.43 us (3%)
    ppermute x10, waiting for transfers between devices, crossed(): lax.ppermute(block, axis, [((i + (-way if i % 2 else way)) % count, i) fo...  69.7 us
    ppermute x20, waiting for transfers between devices, swapped(): lax.ppermute(block, axis, [(i, i ^ bit) for i in range(lax.axis_size(axis...  27.7 us
    ppermute x20, starting transfers between devices, swapped(): lax.ppermute(block, axis, [(i, i ^ bit) for i in range(lax.axis_size(axis...  15.7 us
    ppermute x10, starting transfers between devices, crossed(): lax.ppermute(block, axis, [((i + (-way if i % 2 else way)) % count, i) fo...  13.3 us
    pallas_call x2, Pallas kernels, round_call(): pl.pallas_call(lambda *refs: round_kernel(sizes, place, decay, refs), out...  12.3 us
  transfers between devices with their start and end apart: 30, of which 8 were waited for; matrix products, arithmetic and copies ran while one was open for 3% of the time, Pallas kernels for 16%

profile of v4, /device:TPU:0, one launch (start us, length us, event | category | flops | bytes accessed | tf_op | source)
XLA Modules:
  0.0 160.0 jit_solution(6019546221220174782)
XLA Ops:
  0.6 3.0 %collective-permute-start = (s32[2,256]{1,0:T(2,128)}, s32[2,256]{1,0:T(2,128)S(1)}, u32[]{:S(2)}, u32[]{:S(2)}) collective-permute-start(s32[2,256]{1,0:T(2,128)} %param.6), channel_id=1, source_target_pairs={{0,16},{8,24},{16,0},{24,8},{1,17},{9,25},{17,1},{25,9},{2,18},{10... | collective-permute-start | bytes 6152 | tf_op jit(solution)/shard_map/ppermute | solution.py:26
  3.7 1.9 %slice_bitcast_fusion.1.refs_4_ = bf16[256,1024]{1,0:T(8,128)(2,1)} fusion(bf16[2,256,1024]{2,1,0:T(8,128)(2,1)} %param.5), kind=kLoop, calls=%fused_computation.6 | loop fusion | bytes 1048576 | tf_op jit(solution)/shard_map/squeeze | solution.py:431
  5.5 1.9 %slice_bitcast_fusion.2 = (bf16[256,512]{1,0:T(8,128)(2,1)}, bf16[256,512]{1,0:T(8,128)(2,1)S(1)}) fusion(bf16[2,256,512]{2,1,0:T(8,128)(2,1)} %param.7), kind=kLoop, calls=%fused_computation.7 | loop fusion | bytes 1048576 | tf_op jit(solution)/shard_map/squeeze | solution.py:433
  8.0 1.7 %collective-permute-start.6 = (bf16[256,1024]{1,0:T(8,128)(2,1)}, bf16[256,1024]{1,0:T(8,128)(2,1)S(1)}, u32[]{:S(2)}, u32[]{:S(2)}) collective-permute-start(bf16[256,1024]{1,0:T(8,128)(2,1)} %slice_bitcast_fusion.1.refs_4_), channel_id=1, source_target_pairs={{0,16},{8,24},{16,0},{24,8},{1,17},{9,25},{17,1},{25,9},{2,18},{10... | collective-permute-start | bytes 1572872 | tf_op jit(solution)/shard_map/ppermute | solution.py:26
  10.4 17.2 %collective-permute-done.6.refs_0_.refs_4_ = bf16[256,1024]{1,0:T(8,128)(2,1)S(1)} collective-permute-done((bf16[256,1024]{1,0:T(8,128)(2,1)}, bf16[256,1024]{1,0:T(8,128)(2,1)S(1)}, u32[]{:S(2)}, u32[]{:S(2)}) %collective-permute-start.6) | collective-permute-done | bytes 524320 | tf_op jit(solution)/shard_map/ppermute | solution.py:26
  28.4 1.6 copy-done.1
  30.0 2.7 %local_rows.1 = (f32[1024,512]{1,0:T(8,128)S(1)}, bf16[512,512]{1,0:T(8,128)(2,1)S(1)}) custom-call(s32[8,128]{1,0:T(8,128)S(1)} %pad_add_fusion.2.refs_0_, s32[1]{0:T(128)} %bitcast.4.refs_1_, f32[1024,512]{1,0:T(8,128)S(1)} %bitcast.21, f32[1024,512]{1,0:T(8,128)S(1)} %bitcast.26, bf16[256,1024]{1,0:T(8,128)(2,1)} %slice_bitcast_fusion.1.refs_4_, ...), custom_call_target="tpu_custom_call" | custom-call | tf_op jit(solution)/shard_map/local_rows/pallas_call | solution.py:187
  33.4 6.0 %muon_round.2 = (f32[1024,512]{1,0:T(8,128)S(1)}, bf16[512,512]{1,0:T(8,128)(2,1)S(1)}, bf16[1024,512]{1,0:T(8,128)(2,1)S(1)}, bf16[512,512]{1,0:T(8,128)(2,1)S(...) custom-call(s32[8,128]{1,0:T(8,128)S(1)} %pad_add_fusion.1.refs_0_, s32[1]{0:T(128)} %bitcast.4.refs_1_, ...), custom_call_target="tpu_custom_call" | custom-call | tf_op jit(solution)/shard_map/muon_round/pallas_call | solution.py:270
  39.4 1.2 second_half.2
  40.6 3.8 %collective-permute-start.13 = (bf16[448,512]{1,0:T(8,128)(2,1)S(1)}, bf16[448,512]{1,0:T(8,128)(2,1)S(1)}, u32[]{:S(2)}, u32[]{:S(2)}) collective-permute-start(bf16[448,512]{1,0:T(8,128)(2,1)S(1)} %get-tuple-element.55), channel_id=1, source_target_pairs={{2,0},{7,1},{4,2},{1,3},{6,4},{3,5},{0,6},{5,7},{10,8},{15,9},{12,... | collective-permute-start | bytes 1376264 | tf_op jit(solution)/shard_map/ppermute | solution.py:31
  45.4 2.3 %collective-permute-done.3.refs_1_.refs_5_.refs_9_ = bf16[256,1536]{1,0:T(8,128)(2,1)S(1)} collective-permute-done((bf16[256,1536]{1,0:T(8,128)(2,1)S(1)}, bf16[256,1536]{1,0:T(8,128)(2,1)S(1)}, u32[]{:S(2)}, u32[]{:S(2)}) %collective-permute-start.3) | collective-permute-done | bytes 786464 | tf_op jit(solution)/shard_map/ppermute | solution.py:26
  47.7 19.7 %collective-permute-done.16.refs_17_ = bf16[64,512]{1,0:T(8,128)(2,1)S(1)} collective-permute-done((bf16[64,512]{1,0:T(8,128)(2,1)S(1)}, bf16[64,512]{1,0:T(8,128)(2,1)S(1)}, u32[]{:S(2)}, u32[]{:S(2)}) %collective-permute-start.16) | collective-permute-done | bytes 65568 | tf_op jit(solution)/shard_map/ppermute | solution.py:31
  67.9 3.6 %collective-permute-start.17 = (bf16[512,512]{1,0:T(8,128)(2,1)S(1)}, bf16[512,512]{1,0:T(8,128)(2,1)S(1)}, u32[]{:S(2)}, u32[]{:S(2)}) collective-permute-start(bf16[512,512]{1,0:T(8,128)(2,1)S(1)} %add_convert_fusion.2), channel_id=1, source_target_pairs={{0,1},{1,0},{2,3},{3,2},{4,5},{5,4},{6,7},{7,6},{8,9},{9,8},{10,11... | collective-permute-start | bytes 1572872 | tf_op jit(solution)/shard_map/ppermute | solution.py:26
  71.8 1.3 row_gradients.3
  73.7 16.3 %collective-permute-done.14.refs_8_.refs_18_ = bf16[768,512]{1,0:T(8,128)(2,1)S(1)} collective-permute-done((bf16[768,512]{1,0:T(8,128)(2,1)S(1)}, bf16[768,512]{1,0:T(8,128)(2,1)S(1)}, u32[]{:S(2)}, u32[]{:S(2)}) %collective-permute-start.14) | collective-permute-done | bytes 786464 | tf_op jit(solution)/shard_map/ppermute | solution.py:31
  90.0 4.0 %collective-permute-done.15.refs_9_.refs_20_ = bf16[512,512]{1,0:T(8,128)(2,1)S(1)} collective-permute-done((bf16[512,512]{1,0:T(8,128)(2,1)S(1)}, bf16[512,512]{1,0:T(8,128)(2,1)S(1)}, u32[]{:S(2)}, u32[]{:S(2)}) %collective-permute-start.15) | collective-permute-done | bytes 524320 | tf_op jit(solution)/shard_map/ppermute | solution.py:26
  94.0 1.3 ahead.3
  95.3 6.3 %muon_round.3 = (f32[1024,512]{1,0:T(8,128)}, bf16[1024,512]{1,0:T(8,128)(2,1)S(1)}, bf16[1024,512]{1,0:T(8,128)(2,1)S(1)}, bf16[512,512]{1,0:T(8,128)(2,1)S(1)}...) custom-call(s32[8,128]{1,0:T(8,128)S(1)} %pad_add_fusion.refs_0_, ...), custom_call_target="tpu_custom_call" | custom-call | tf_op jit(solution)/shard_map/muon_round/pallas_call | solution.py:270
  101.6 1.3 row_gradients.2
  103.0 1.2 second_half.3
  104.2 2.4 %collective-permute-start.20 = (bf16[448,512]{1,0:T(8,128)(2,1)S(1)}, bf16[448,512]{1,0:T(8,128)(2,1)S(1)}, u32[]{:S(2)}, u32[]{:S(2)}) collective-permute-start(bf16[448,512]{1,0:T(8,128)(2,1)S(1)} %get-tuple-element.70), channel_id=1, source_target_pairs={{2,0},{7,1},{4,2},{1,3},{6,4},{3,5},{0,6},{5,7},{10,8},{15,9},{12,... | collective-permute-start | bytes 1376264 | tf_op jit(solution)/shard_map/ppermute | solution.py:31
  106.6 1.7 %collective-permute-start.19 = (bf16[512,512]{1,0:T(8,128)(2,1)S(1)}, bf16[512,512]{1,0:T(8,128)(2,1)S(1)}, u32[]{:S(2)}, u32[]{:S(2)}) collective-permute-start(bf16[512,512]{1,0:T(8,128)(2,1)S(1)} %get-tuple-element.67.refs_3_), channel_id=1, source_target_pairs={{2,0},{7,1},{4,2},{1,3},{6,4},{3,5},{0,6},{5,7},{10,8},{15,9},{12,... | collective-permute-start | bytes 1572872 | tf_op jit(solution)/shard_map/ppermute | solution.py:31
  108.5 1.6 collective-permute-start.29
  110.1 19.8 %collective-permute-done.21.refs_4_ = bf16[64,512]{1,0:T(8,128)(2,1)S(1)} collective-permute-done((bf16[64,512]{1,0:T(8,128)(2,1)S(1)}, bf16[64,512]{1,0:T(8,128)(2,1)S(1)}, u32[]{:S(2)}, u32[]{:S(2)}) %collective-permute-start.21) | collective-permute-done | bytes 65568 | tf_op jit(solution)/shard_map/ppermute | solution.py:31
  129.8 1.4 collective-permute-start.22
  131.4 2.2 %collective-permute-start.25 = (bf16[512,512]{1,0:T(8,128)(2,1)S(1)}, bf16[512,512]{1,0:T(8,128)(2,1)S(1)}, u32[]{:S(2)}, u32[]{:S(2)}) collective-permute-start(bf16[512,512]{1,0:T(8,128)(2,1)S(1)} %add_convert_fusion), channel_id=1, source_target_pairs={{0,1},{1,0},{2,3},{3,2},{4,5},{5,4},{6,7},{7,6},{8,9},{9,8},{10,11... | collective-permute-start | bytes 1572872 | tf_op jit(solution)/shard_map/ppermute | solution.py:26
  133.9 1.5 collective-permute-start.27
  135.5 2.0 %collective-permute-start.23 = (bf16[256,512]{1,0:T(8,128)(2,1)S(1)}, bf16[256,512]{1,0:T(8,128)(2,1)S(1)}, u32[]{:S(2)}, u32[]{:S(2)}) collective-permute-start(bf16[256,512]{1,0:T(8,128)(2,1)S(1)} %get-tuple-element.73), channel_id=1, source_target_pairs={{6,0},{3,1},{0,2},{5,3},{2,4},{7,5},{4,6},{1,7},{14,8},{11,9},{8,1... | collective-permute-start | bytes 786440 | tf_op jit(solution)/shard_map/ppermute | solution.py:31
  138.3 14.0 %collective-permute-done.22.refs_4_.refs_5_ = bf16[768,512]{1,0:T(8,128)(2,1)S(1)} collective-permute-done((bf16[768,512]{1,0:T(8,128)(2,1)S(1)}, bf16[768,512]{1,0:T(8,128)(2,1)S(1)}, u32[]{:S(2)}, u32[]{:S(2)}) %collective-permute-start.22) | collective-permute-done | bytes 786464 | tf_op jit(solution)/shard_map/ppermute | solution.py:31
  152.3 4.2 %collective-permute-done.24.refs_5_.refs_7_ = bf16[512,512]{1,0:T(8,128)(2,1)S(1)} collective-permute-done((bf16[512,512]{1,0:T(8,128)(2,1)S(1)}, bf16[512,512]{1,0:T(8,128)(2,1)S(1)}, u32[]{:S(2)}, u32[]{:S(2)}) %collective-permute-start.24) | collective-permute-done | bytes 524320 | tf_op jit(solution)/shard_map/ppermute | solution.py:26
  156.5 1.6 %average.2.refs_9_ = f32[1024,512]{1,0:T(8,128)} custom-call(f32[512,512]{1,0:T(8,128)S(1)} %get-tuple-element.63.refs_0_, f32[512,512]{1,0:T(8,128)S(1)} %get-tuple-element.69.refs_1_, bf16[512,512]{1,0:T(8,128)(2,1)S(1)} %collective-permute-done.19.refs_2_, bf16[448,512]{1,0:T(8,128)(2,1)S(1)} %collective-permute-done.20.refs_3_, ...), custom_call_target="tpu_custom_call" | custom-call | tf_op jit(solution)/shard_map/average/pallas_call | solution.py:375
  158.2 1.0 average.3
  (66 shorter events, 7.4 us)
Async XLA Ops:
  0.6 9.1 %copy-start.2 = (bf16[2,256,1024]{2,1,0:T(8,128)(2,1)S(1)}, bf16[2,256,1024]{2,1,0:T(8,128)(2,1)}, u32[]{:S(2)}) copy-start(bf16[2,256,1024]{2,1,0:T(8,128)(2,1)} %param.5) | copy-start | bytes 3145732
  0.6 9.2 %collective-permute-start = (s32[2,256]{1,0:T(2,128)}, s32[2,256]{1,0:T(2,128)S(1)}, u32[]{:S(2)}, u32[]{:S(2)}) collective-permute-start(s32[2,256]{1,0:T(2,128)} %param.6), channel_id=1, source_target_pairs={{0,16},{8,24},{16,0},{24,8},{1,17},{9,25},{17,1},{25,9},{2,18},{10... | collective-permute-start | bytes 6152 | tf_op jit(solution)/shard_map/ppermute | solution.py:26
  3.7 6.3 %collective-permute-start.1 = (s32[2,256]{1,0:T(2,128)}, s32[2,256]{1,0:T(2,128)S(1)}, u32[]{:S(2)}, u32[]{:S(2)}) collective-permute-start(s32[2,256]{1,0:T(2,128)} %param.6), channel_id=1, source_target_pairs={{0,8},{8,0},{16,24},{24,16},{1,9},{9,1},{17,25},{25,17},{2,10},{10... | collective-permute-start | bytes 6152 | tf_op jit(solution)/shard_map/ppermute | solution.py:26
  5.5 22.8 %copy-start = (f32[1,1,1024,512]{3,2,1,0:T(8,128)S(1)}, f32[1,1,1024,512]{3,2,1,0:T(8,128)}, u32[]{:S(2)}) copy-start(f32[1,1,1024,512]{3,2,1,0:T(8,128)} %param.8) | copy-start | bytes 6291460
  7.5 20.5 %collective-permute-start.10 = (bf16[256,512]{1,0:T(8,128)(2,1)}, bf16[256,512]{1,0:T(8,128)(2,1)}, u32[]{:S(2)}, u32[]{:S(2)}) collective-permute-start(bf16[256,512]{1,0:T(8,128)(2,1)} %get-tuple-element.87.refs_6_), channel_id=1, source_target_pairs={{0,16},{8,24},{16,0},{24,8},{1,17},{9,25},{17,1},{25,9},{2,18},{10... | collective-permute-start | bytes 786440 | tf_op jit(solution)/shard_map/ppermute | solution.py:26
  7.6 20.7 %collective-permute-start.9 = (bf16[256,512]{1,0:T(8,128)(2,1)}, bf16[256,512]{1,0:T(8,128)(2,1)}, u32[]{:S(2)}, u32[]{:S(2)}) collective-permute-start(bf16[256,512]{1,0:T(8,128)(2,1)} %get-tuple-element.87.refs_6_), channel_id=1, source_target_pairs={{0,8},{8,0},{16,24},{24,16},{1,9},{9,1},{17,25},{25,17},{2,10},{10... | collective-permute-start | bytes 786440 | tf_op jit(solution)/shard_map/ppermute | solution.py:26
  8.0 19.7 %collective-permute-start.6 = (bf16[256,1024]{1,0:T(8,128)(2,1)}, bf16[256,1024]{1,0:T(8,128)(2,1)S(1)}, u32[]{:S(2)}, u32[]{:S(2)}) collective-permute-start(bf16[256,1024]{1,0:T(8,128)(2,1)} %slice_bitcast_fusion.1.refs_4_), channel_id=1, source_target_pairs={{0,16},{8,24},{16,0},{24,8},{1,17},{9,25},{17,1},{25,9},{2,18},{10... | collective-permute-start | bytes 1572872 | tf_op jit(solution)/shard_map/ppermute | solution.py:26
  9.9 18.5 %collective-permute-start.8 = (bf16[256,1024]{1,0:T(8,128)(2,1)}, bf16[256,1024]{1,0:T(8,128)(2,1)S(1)}, u32[]{:S(2)}, u32[]{:S(2)}) collective-permute-start(bf16[256,1024]{1,0:T(8,128)(2,1)} %slice_bitcast_fusion.1.refs_4_), channel_id=1, source_target_pairs={{0,8},{8,0},{16,24},{24,16},{1,9},{9,1},{17,25},{25,17},{2,10},{10... | collective-permute-start | bytes 1572872 | tf_op jit(solution)/shard_map/ppermute | solution.py:26
  10.0 17.7 %collective-permute-start.2 = (s32[2,256]{1,0:T(2,128)S(1)}, s32[2,256]{1,0:T(2,128)S(1)}, u32[]{:S(2)}, u32[]{:S(2)}) collective-permute-start(s32[2,256]{1,0:T(2,128)S(1)} %collective-permute-done), channel_id=1, source_target_pairs={{0,8},{8,0},{16,24},{24,16},{1,9},{9,1},{17,25},{25,17},{2,10},{10... | collective-permute-start | bytes 6152 | tf_op jit(solution)/shard_map/ppermute | solution.py:26
  27.6 5.1 %collective-permute-start.7 = (bf16[256,1024]{1,0:T(8,128)(2,1)S(1)}, bf16[256,1024]{1,0:T(8,128)(2,1)S(1)}, u32[]{:S(2)}, u32[]{:S(2)}) collective-permute-start(bf16[256,1024]{1,0:T(8,128)(2,1)S(1)} %collective-permute-done.6.refs_0_.refs_4_), channel_id=1, source_target_pairs={{0,8},{8,0},{16,24},{24,16},{1,9},{9,1},{17,25},{25,17},{2,10},{10... | collective-permute-start | bytes 1572872 | tf_op jit(solution)/shard_map/ppermute | solution.py:26
  27.7 20.0 %collective-permute-start.3 = (bf16[256,1536]{1,0:T(8,128)(2,1)S(1)}, bf16[256,1536]{1,0:T(8,128)(2,1)S(1)}, u32[]{:S(2)}, u32[]{:S(2)}) collective-permute-start(bf16[256,1536]{1,0:T(8,128)(2,1)S(1)} %pad_maximum_fusion.refs_0_.refs_4_.refs_8_), channel_id=1, source_target_pairs={{0,16},{8,24},{16,0},{24,8},{1,17},{9,25},{17,1},{25,9},{2,18},{10... | collective-permute-start | bytes 2359304 | tf_op jit(solution)/shard_map/ppermute | solution.py:26
  28.0 5.4 %collective-permute-start.11 = (bf16[256,512]{1,0:T(8,128)(2,1)}, bf16[256,512]{1,0:T(8,128)(2,1)S(1)}, u32[]{:S(2)}, u32[]{:S(2)}) collective-permute-start(bf16[256,512]{1,0:T(8,128)(2,1)} %collective-permute-done.10.refs_6_), channel_id=1, source_target_pairs={{0,8},{8,0},{16,24},{24,16},{1,9},{9,1},{17,25},{25,17},{2,10},{10... | collective-permute-start | bytes 786440 | tf_op jit(solution)/shard_map/ppermute | solution.py:26
  40.6 27.1 %collective-permute-start.13 = (bf16[448,512]{1,0:T(8,128)(2,1)S(1)}, bf16[448,512]{1,0:T(8,128)(2,1)S(1)}, u32[]{:S(2)}, u32[]{:S(2)}) collective-permute-start(bf16[448,512]{1,0:T(8,128)(2,1)S(1)} %get-tuple-element.55), channel_id=1, source_target_pairs={{2,0},{7,1},{4,2},{1,3},{6,4},{3,5},{0,6},{5,7},{10,8},{15,9},{12,... | collective-permute-start | bytes 1376264 | tf_op jit(solution)/shard_map/ppermute | solution.py:31
  44.5 27.1 %collective-permute-start.12 = (bf16[512,512]{1,0:T(8,128)(2,1)S(1)}, bf16[512,512]{1,0:T(8,128)(2,1)S(1)}, u32[]{:S(2)}, u32[]{:S(2)}) collective-permute-start(bf16[512,512]{1,0:T(8,128)(2,1)S(1)} %get-tuple-element.53.refs_3_), channel_id=1, source_target_pairs={{2,0},{7,1},{4,2},{1,3},{6,4},{3,5},{0,6},{5,7},{10,8},{15,9},{12,... | collective-permute-start | bytes 1572872 | tf_op jit(solution)/shard_map/ppermute | solution.py:31
  44.9 28.2 %collective-permute-start.4 = (bf16[256,1536]{1,0:T(8,128)(2,1)S(1)}, bf16[256,1536]{1,0:T(8,128)(2,1)S(1)}, u32[]{:S(2)}, u32[]{:S(2)}) collective-permute-start(bf16[256,1536]{1,0:T(8,128)(2,1)S(1)} %pad_maximum_fusion.refs_0_.refs_4_.refs_8_), channel_id=1, source_target_pairs={{0,8},{8,0},{16,24},{24,16},{1,9},{9,1},{17,25},{25,17},{2,10},{10... | collective-permute-start | bytes 2359304 | tf_op jit(solution)/shard_map/ppermute | solution.py:26
  44.9 22.4 %collective-permute-start.16 = (bf16[64,512]{1,0:T(8,128)(2,1)S(1)}, bf16[64,512]{1,0:T(8,128)(2,1)S(1)}, u32[]{:S(2)}, u32[]{:S(2)}) collective-permute-start(bf16[64,512]{1,0:T(8,128)(2,1)S(1)} %get-tuple-element.58), channel_id=1, source_target_pairs={{2,0},{7,1},{4,2},{1,3},{6,4},{3,5},{0,6},{5,7},{10,8},{15,9},{12,... | collective-permute-start | bytes 196616 | tf_op jit(solution)/shard_map/ppermute | solution.py:31
  47.7 25.5 %collective-permute-start.5 = (bf16[256,1536]{1,0:T(8,128)(2,1)S(1)}, bf16[256,1536]{1,0:T(8,128)(2,1)S(1)}, u32[]{:S(2)}, u32[]{:S(2)}) collective-permute-start(bf16[256,1536]{1,0:T(8,128)(2,1)S(1)} %collective-permute-done.3.refs_1_.refs_5_.refs_9_), channel_id=1, source_target_pairs={{0,8},{8,0},{16,24},{24,16},{1,9},{9,1},{17,25},{25,17},{2,10},{10... | collective-permute-start | bytes 2359304 | tf_op jit(solution)/shard_map/ppermute | solution.py:26
  67.3 22.7 %collective-permute-start.14 = (bf16[768,512]{1,0:T(8,128)(2,1)S(1)}, bf16[768,512]{1,0:T(8,128)(2,1)S(1)}, u32[]{:S(2)}, u32[]{:S(2)}) collective-permute-start(bf16[768,512]{1,0:T(8,128)(2,1)S(1)} %get-tuple-element.56), channel_id=1, source_target_pairs={{6,0},{3,1},{0,2},{5,3},{2,4},{7,5},{4,6},{1,7},{14,8},{11,9},{8,1... | collective-permute-start | bytes 2359304 | tf_op jit(solution)/shard_map/ppermute | solution.py:31
  67.9 22.1 %collective-permute-start.17 = (bf16[512,512]{1,0:T(8,128)(2,1)S(1)}, bf16[512,512]{1,0:T(8,128)(2,1)S(1)}, u32[]{:S(2)}, u32[]{:S(2)}) collective-permute-start(bf16[512,512]{1,0:T(8,128)(2,1)S(1)} %add_convert_fusion.2), channel_id=1, source_target_pairs={{0,1},{1,0},{2,3},{3,2},{4,5},{5,4},{6,7},{7,6},{8,9},{9,8},{10,11... | collective-permute-start | bytes 1572872 | tf_op jit(solution)/shard_map/ppermute | solution.py:26
  71.7 22.3 %collective-permute-start.15 = (bf16[512,512]{1,0:T(8,128)(2,1)S(1)}, bf16[512,512]{1,0:T(8,128)(2,1)S(1)}, u32[]{:S(2)}, u32[]{:S(2)}) collective-permute-start(bf16[512,512]{1,0:T(8,128)(2,1)S(1)} %add_convert_fusion.3), channel_id=1, source_target_pairs={{0,1},{1,0},{2,3},{3,2},{4,5},{5,4},{6,7},{7,6},{8,9},{9,8},{10,11... | collective-permute-start | bytes 1572872 | tf_op jit(solution)/shard_map/ppermute | solution.py:26
  73.1 35.3 %collective-permute-start.28 = (bf16[2,256,1024]{2,1,0:T(8,128)(2,1)S(1)}, bf16[2,256,1024]{2,1,0:T(8,128)(2,1)S(1)}, u32[]{:S(2)}, u32[]{:S(2)}) collective-permute-start(bf16[2,256,1024]{2,1,0:T(8,128)(2,1)S(1)} %get-tuple-element.84), channel_id=1, source_target_pairs={{0,8},{8,0},{16,24},{24,16},{1,9},{9,1},{17,25},{25,17},{2,10},{10... | collective-permute-start | bytes 3145736 | tf_op jit(solution)/shard_map/ppermute | solution.py:26
  73.2 22.1 %collective-permute-start.18 = (bf16[256,512]{1,0:T(8,128)(2,1)S(1)}, bf16[256,512]{1,0:T(8,128)(2,1)S(1)}, u32[]{:S(2)}, u32[]{:S(2)}) collective-permute-start(bf16[256,512]{1,0:T(8,128)(2,1)S(1)} %get-tuple-element.62), channel_id=1, source_target_pairs={{6,0},{3,1},{0,2},{5,3},{2,4},{7,5},{4,6},{1,7},{14,8},{11,9},{8,1... | collective-permute-start | bytes 786440 | tf_op jit(solution)/shard_map/ppermute | solution.py:31
  102.9 30.9 %collective-permute-start.26 = (bf16[2,256,1024]{2,1,0:T(8,128)(2,1)S(1)}, bf16[2,256,1024]{2,1,0:T(8,128)(2,1)S(1)}, u32[]{:S(2)}, u32[]{:S(2)}) collective-permute-start(bf16[2,256,1024]{2,1,0:T(8,128)(2,1)S(1)} %get-tuple-element.78), channel_id=1, source_target_pairs={{0,8},{8,0},{16,24},{24,16},{1,9},{9,1},{17,25},{25,17},{2,10},{10... | collective-permute-start | bytes 3145736 | tf_op jit(solution)/shard_map/ppermute | solution.py:26
  104.2 27.0 %collective-permute-start.20 = (bf16[448,512]{1,0:T(8,128)(2,1)S(1)}, bf16[448,512]{1,0:T(8,128)(2,1)S(1)}, u32[]{:S(2)}, u32[]{:S(2)}) collective-permute-start(bf16[448,512]{1,0:T(8,128)(2,1)S(1)} %get-tuple-element.70), channel_id=1, source_target_pairs={{2,0},{7,1},{4,2},{1,3},{6,4},{3,5},{0,6},{5,7},{10,8},{15,9},{12,... | collective-permute-start | bytes 1376264 | tf_op jit(solution)/shard_map/ppermute | solution.py:31
  106.6 27.0 %collective-permute-start.19 = (bf16[512,512]{1,0:T(8,128)(2,1)S(1)}, bf16[512,512]{1,0:T(8,128)(2,1)S(1)}, u32[]{:S(2)}, u32[]{:S(2)}) collective-permute-start(bf16[512,512]{1,0:T(8,128)(2,1)S(1)} %get-tuple-element.67.refs_3_), channel_id=1, source_target_pairs={{2,0},{7,1},{4,2},{1,3},{6,4},{3,5},{0,6},{5,7},{10,8},{15,9},{12,... | collective-permute-start | bytes 1572872 | tf_op jit(solution)/shard_map/ppermute | solution.py:31
  108.3 21.5 %collective-permute-start.21 = (bf16[64,512]{1,0:T(8,128)(2,1)S(1)}, bf16[64,512]{1,0:T(8,128)(2,1)S(1)}, u32[]{:S(2)}, u32[]{:S(2)}) collective-permute-start(bf16[64,512]{1,0:T(8,128)(2,1)S(1)} %get-tuple-element.71), channel_id=1, source_target_pairs={{2,0},{7,1},{4,2},{1,3},{6,4},{3,5},{0,6},{5,7},{10,8},{15,9},{12,... | collective-permute-start | bytes 196616 | tf_op jit(solution)/shard_map/ppermute | solution.py:31
  108.5 27.0 %collective-permute-start.29 = (bf16[1,256,1024]{2,1,0:T(8,128)(2,1)S(1)}, bf16[1,256,1024]{2,1,0:T(8,128)(2,1)S(1)}, u32[]{:S(2)}, u32[]{:S(2)}) collective-permute-start(bf16[1,256,1024]{2,1,0:T(8,128)(2,1)S(1)} %get-tuple-element.86), channel_id=1, source_target_pairs={{0,16},{8,24},{16,0},{24,8},{1,17},{9,25},{17,1},{25,9},{2,18},{10... | collective-permute-start | bytes 1572872 | tf_op jit(solution)/shard_map/ppermute | solution.py:26
  129.8 22.5 %collective-permute-start.22 = (bf16[768,512]{1,0:T(8,128)(2,1)S(1)}, bf16[768,512]{1,0:T(8,128)(2,1)S(1)}, u32[]{:S(2)}, u32[]{:S(2)}) collective-permute-start(bf16[768,512]{1,0:T(8,128)(2,1)S(1)} %get-tuple-element.72), channel_id=1, source_target_pairs={{6,0},{3,1},{0,2},{5,3},{2,4},{7,5},{4,6},{1,7},{14,8},{11,9},{8,1... | collective-permute-start | bytes 2359304 | tf_op jit(solution)/shard_map/ppermute | solution.py:31
  131.4 20.9 %collective-permute-start.25 = (bf16[512,512]{1,0:T(8,128)(2,1)S(1)}, bf16[512,512]{1,0:T(8,128)(2,1)S(1)}, u32[]{:S(2)}, u32[]{:S(2)}) collective-permute-start(bf16[512,512]{1,0:T(8,128)(2,1)S(1)} %add_convert_fusion), channel_id=1, source_target_pairs={{0,1},{1,0},{2,3},{3,2},{4,5},{5,4},{6,7},{7,6},{8,9},{9,8},{10,11... | collective-permute-start | bytes 1572872 | tf_op jit(solution)/shard_map/ppermute | solution.py:26
  133.7 22.8 %collective-permute-start.24 = (bf16[512,512]{1,0:T(8,128)(2,1)S(1)}, bf16[512,512]{1,0:T(8,128)(2,1)S(1)}, u32[]{:S(2)}, u32[]{:S(2)}) collective-permute-start(bf16[512,512]{1,0:T(8,128)(2,1)S(1)} %add_convert_fusion.1), channel_id=1, source_target_pairs={{0,1},{1,0},{2,3},{3,2},{4,5},{5,4},{6,7},{7,6},{8,9},{9,8},{10,11... | collective-permute-start | bytes 1572872 | tf_op jit(solution)/shard_map/ppermute | solution.py:26
  133.9 25.2 %collective-permute-start.27 = (bf16[1,256,1024]{2,1,0:T(8,128)(2,1)S(1)}, bf16[1,256,1024]{2,1,0:T(8,128)(2,1)S(1)}, u32[]{:S(2)}, u32[]{:S(2)}) collective-permute-start(bf16[1,256,1024]{2,1,0:T(8,128)(2,1)S(1)} %get-tuple-element.80), channel_id=1, source_target_pairs={{0,16},{8,24},{16,0},{24,8},{1,17},{9,25},{17,1},{25,9},{2,18},{10... | collective-permute-start | bytes 1572872 | tf_op jit(solution)/shard_map/ppermute | solution.py:26
  135.5 22.7 %collective-permute-start.23 = (bf16[256,512]{1,0:T(8,128)(2,1)S(1)}, bf16[256,512]{1,0:T(8,128)(2,1)S(1)}, u32[]{:S(2)}, u32[]{:S(2)}) collective-permute-start(bf16[256,512]{1,0:T(8,128)(2,1)S(1)} %get-tuple-element.73), channel_id=1, source_target_pairs={{6,0},{3,1},{0,2},{5,3},{2,4},{7,5},{4,6},{1,7},{14,8},{11,9},{8,1... | collective-permute-start | bytes 786440 | tf_op jit(solution)/shard_map/ppermute | solution.py:31
  (2 other events, 5.9 us)

commit v5 on v4

v5 whole, which is shorter than its diff:
```python
import math

import jax
import jax.numpy as jnp
from jax import lax
from jax.experimental import pallas as pl
from jax.experimental.pallas import tpu as pltpu
from jax.sharding import PartitionSpec as P


ROUNDS = 2
NS_STEPS = 3
LEAD, LINEAR, QUADRATIC = 3.4445, -4.775, 2.0315
F32 = jnp.float32
BF16 = jnp.bfloat16
VMEM = pl.BlockSpec(memory_space=pltpu.VMEM)
SMEM = pl.BlockSpec(memory_space=pltpu.SMEM)
ANY = pl.BlockSpec(memory_space=pl.ANY)


def limit(mebibytes):
    return pltpu.CompilerParams(vmem_limit_bytes=mebibytes << 20)


def swapped(block, axis, bit):
    return lax.ppermute(block, axis, [(i, i ^ bit) for i in range(lax.axis_size(axis))])


def crossed(block, axis, way):
    count = lax.axis_size(axis)
    return lax.ppermute(
        block, axis, [((i + (-way if i % 2 else way)) % count, i) for i in range(count)]
    )


def dot(a, b):
    return jnp.dot(a, b, preferred_element_type=F32)


def dot_first(a, b):
    return lax.dot_general(a, b, (((0,), (0,)), ((), ())), preferred_element_type=F32)


def dot_last(a, b):
    return lax.dot_general(a, b, (((1,), (1,)), ((), ())), preferred_element_type=F32)


def joined(top, corner):
    edge = top.shape[0]
    below = jnp.concatenate([top[:, edge:].T, corner], axis=1)
    return jnp.concatenate([top, below], axis=0)


def product(left, right):
    edge = left.shape[0] // 2
    return dot(left[:edge], right), dot(left[edge:], right[:, edge:])


def low(pair):
    return tuple(item.astype(BF16) for item in pair)


def mix(*terms):
    return tuple(
        sum(factor * pair[i].astype(F32) for factor, pair in terms) for i in range(2)
    )


def factors(gram):
    rest, lead = None, 1.0
    for sweep in range(NS_STEPS):
        whole = joined(*gram)
        polynom_wide = mix((LINEAR, gram), (QUADRATIC, product(whole, whole)))
        polynom = joined(*low(polynom_wide))
        if sweep == 0:
            rest = polynom_wide
        else:
            rest = mix(
                (lead, polynom_wide), (LEAD, rest), (1.0, product(joined(*low(rest)), polynom))
            )
        lead = lead * LEAD
        if sweep < NS_STEPS - 1:
            half = low(mix((LEAD, gram), (1.0, product(whole, polynom))))
            gram = low(mix((LEAD, half), (1.0, product(joined(*half), polynom))))
    return joined(*low(rest))


def take(refs, start, stop, columns=slice(None)):
    parts, offset = [], 0
    for ref in refs:
        begin, end = max(start, offset), min(stop, offset + ref.shape[0])
        if begin < end:
            parts.append(ref[begin - offset : end - offset, columns])
        offset += ref.shape[0]
    return parts[0] if len(parts) == 1 else jnp.concatenate(parts, axis=0)


def put(refs, start, value):
    offset, stop = 0, start + value.shape[0]
    for ref in refs:
        begin, end = max(start, offset), min(stop, offset + ref.shape[0])
        if begin < end:
            ref[begin - offset : end - offset, :] = value[begin - start : end - start, :]
        offset += ref.shape[0]


def mixed(parts, start, stop):
    stepped, first, second, near = (take(refs, start, stop) for refs in parts)
    total = first.astype(F32) + second.astype(F32) + near.astype(F32)
    return 0.4 * stepped + 0.15 * total


def split(depth):
    half, unit = depth // 2, depth // 16
    return (half, half - 2 * unit, 2 * unit), (12 * unit, 4 * unit)


def sizes_of(arrays):
    return [len(item) for item in arrays]


def grouped(names, sizes):
    return [[next(names) for _ in range(size)] for size in sizes]


def ahead_kernel(sizes, refs):
    names = iter(refs)
    rows, parts = grouped(names, sizes[:1])[0], grouped(names, sizes[1:])
    if len(parts) == 1:
        value = parts[0][0][...]
    else:
        weight = next(names)
        value = mixed(parts, 0, weight.shape[0])
        weight[...] = value
    pre = next(names)
    shaped = value.astype(BF16)
    place, depth = 0, value.shape[0]
    for ref in rows:
        pre[place : place + ref.shape[0], :] = dot(ref[:, :depth], shaped)
        place += ref.shape[0]


def ahead_call(rows, parts, early):
    width = parts[0][0].shape[1]
    total = sum(item.shape[0] for item in rows)
    flat = [item for part in parts for item in part]
    shapes = [jax.ShapeDtypeStruct((total, width), F32)]
    if len(parts) > 1:
        shapes.insert(0, jax.ShapeDtypeStruct((early, width), F32))
    sizes = sizes_of([rows] + parts)
    return pl.pallas_call(
        lambda *refs: ahead_kernel(sizes, refs),
        out_shape=shapes,
        in_specs=[VMEM] * (len(rows) + len(flat)),
        out_specs=[VMEM] * len(shapes),
        compiler_params=limit(16),
        name="ahead",
    )(*rows, *flat)


def slope_rows(route, mine, rows, grads, pre_of, slopes):
    columns = None if route is None else route[...].T
    place = 0
    for block, refs in enumerate(blocks_of(rows, grads)):
        count = grads[block].shape[0]
        value = pre_of(place, refs)
        lanes = count if route is None else route.shape[1]
        for start in range(0, count, lanes):
            part = slice(start, start + lanes)
            slope = grads[block][part, :].astype(F32) * 2.0 * jnp.maximum(value[part, :], 0.0)
            if route is not None:
                index = (place + start) // lanes
                slope = jnp.where(columns[:, index : index + 1] == mine[0], slope, 0.0)
            slopes[place + start : place + start + lanes, :] = slope.astype(BF16)
        place += count


def blocks_of(rows, grads):
    pieces = len(rows) // len(grads)
    return [rows[i * pieces : (i + 1) * pieces] for i in range(len(grads))]


def weight_gradient(rows, grads, slopes, span):
    value, place = None, 0
    for block, refs in enumerate(blocks_of(rows, grads)):
        count = grads[block].shape[0]
        term = dot_first(take(refs, 0, count, span), slopes[place : place + count, :])
        value = term if value is None else value + term
        place += count
    return value


def tiles(depth):
    tile = min(256, depth)
    return [slice(start, start + tile) for start in range(0, depth, tile)]


def part_kernel(sizes, decay, ready, refs):
    names = iter(refs)
    route, mine, source, moment = (next(names) for _ in range(4))
    rows, grads = grouped(names, sizes)
    partial, slopes = names
    depth = moment.shape[0]
    factor = 1.0 / math.sqrt(depth)
    shaped = None if ready else source[...].astype(BF16)

    def pre_of(place, refs):
        count = sum(ref.shape[0] for ref in refs)
        if ready:
            return source[place : place + count, :] * factor
        return dot(take(refs, 0, count), shaped) * factor

    slope_rows(route, mine, rows, grads, pre_of, slopes)
    for span in tiles(depth):
        before = moment[span, :] if decay == 1.0 else decay * moment[span, :]
        partial[span, :] = before + weight_gradient(rows, grads, slopes, span) * factor


def part_call(rows, grads, route, mine, source, moment, decay, ready):
    depth, width = moment.shape
    total = sum(item.shape[0] for item in rows)
    sizes = sizes_of([rows, grads])
    return pl.pallas_call(
        lambda *refs: part_kernel(sizes, decay, ready, refs),
        out_shape=[
            jax.ShapeDtypeStruct((depth, width), F32),
            jax.ShapeDtypeStruct((total, width), BF16),
        ],
        in_specs=[VMEM, SMEM] + [VMEM] * (2 + len(rows) + len(grads)),
        out_specs=[VMEM] * 2,
        compiler_params=limit(16),
        name="part_rows",
    )(route, mine, source, moment, *rows, *grads)


def round_kernel(sizes, decay, refs):
    names = iter(refs)
    mine, pre, moment = (next(names) for _ in range(3))
    route = None if decay < 1.0 else next(names)
    rows, grads, weights, *parts = grouped(names, sizes)
    moment_out, slopes, moment_low, rest_out, scale_out, stepped, share = (
        next(names) for _ in range(7)
    )
    depth, width = moment.shape
    half, early = split(depth)[0][0], split(depth)[1][0]
    factor = 1.0 / math.sqrt(depth)
    if parts:
        late = next(names)
        value = mixed(parts, early, depth)
        late[...] = value
        shaped = value.astype(BF16)

    def pre_of(place, refs):
        count = sum(ref.shape[0] for ref in refs)
        value = pre[place : place + count, :]
        if parts:
            value = value + dot(take(refs, 0, count, slice(early, depth)), shaped)
        return value * factor

    slope_rows(route, mine, rows, grads, pre_of, slopes)
    total = jnp.zeros((1, width), F32)
    for span in tiles(depth):
        value = weight_gradient(rows, grads, slopes, span) * factor
        value = (moment[span, :] if decay == 1.0 else decay * moment[span, :]) + value
        moment_out[span, :] = value
        moment_low[span, :] = value.astype(BF16)
        total = total + jnp.sum(value * value, axis=0, keepdims=True)
    scale = 1.0 / (jnp.sqrt(jnp.sum(total)) + 1e-07)
    scale_out[0] = scale
    edge = width // 2
    top = dot_first(moment_low[:, :edge], moment_low[...]) * (scale * scale)
    corner = dot_first(moment_low[:, edge:], moment_low[:, edge:]) * (scale * scale)
    rest = factors(low((top, corner)))
    rest_out[...] = rest
    step_rows(tiles(half), weights, moment_low, rest, scale, [stepped], [[share]], 0)


def step_rows(spans, weights, moment_low, rest, scale, stepped, shares, base):
    step_size = 0.1 * math.sqrt(moment_low.shape[0])
    for span in spans:
        low = moment_low[span, :]
        orthog = scale * (LEAD**NS_STEPS * low.astype(F32) + dot(low, rest))
        value = take(weights, span.start, span.stop) - step_size * orthog
        put(stepped, span.start - base, value)
        for refs in shares:
            put(refs, span.start - base, value.astype(BF16))


def round_call(rows, grads, decay, route, mine, pre, weights, moment, parts):
    depth, width = moment.shape
    total = sum(item.shape[0] for item in rows)
    routes = [] if decay < 1.0 else [route]
    half, late = split(depth)[0][0], split(depth)[1][1]
    shape = jax.ShapeDtypeStruct
    flat = [item for part in parts for item in part]
    sizes = sizes_of([rows, grads, weights] + parts)
    out = [
        shape((depth, width), F32),
        shape((total, width), BF16),
        shape((depth, width), BF16),
        shape((width, width), BF16),
        shape((1,), F32),
        shape((half, width), F32),
        shape((half, width), BF16),
    ]
    specs = [VMEM] * 4 + [SMEM] + [VMEM] * 2
    if parts:
        out.append(shape((late, width), F32))
        specs.append(VMEM)
    return pl.pallas_call(
        lambda *refs: round_kernel(sizes, decay, refs),
        out_shape=out,
        in_specs=[SMEM] + [VMEM] * (2 + len(routes) + sum(sizes)),
        out_specs=specs,
        compiler_params=limit(16),
        name="muon_round",
    )(mine, pre, moment, *routes, *rows, *grads, *weights, *flat)


def second_kernel(count, refs):
    moment_low, rest, scale, share, *names = refs
    weights, names = names[:count], iter(names[count:])
    stepped, *rest_out = names
    ones, twos = rest_out[:2], rest_out[2:]
    depth = moment_low.shape[0]
    half = share.shape[0]
    put(twos, 0, share[...])
    spans = [span for span in tiles(depth) if span.start >= half]
    step_rows(spans, weights, moment_low, rest[...], scale[0], [stepped], [ones], half)
    put(twos, half, take(ones, 0, depth - half))


def second_call(moment_low, rest, scale, share, weights):
    depth, width = moment_low.shape
    one, two = split(depth)
    shape = jax.ShapeDtypeStruct
    out = [shape((depth - one[0], width), F32)]
    out = out + [shape((size, width), BF16) for size in one[1:] + two]
    result = pl.pallas_call(
        lambda *refs: second_kernel(len(weights), refs),
        out_shape=out,
        in_specs=[VMEM] * 2 + [SMEM] + [VMEM] * (1 + len(weights)),
        out_specs=[VMEM] * len(out),
        compiler_params=limit(12),
        name="second_half",
    )(moment_low, rest, scale, share, *weights)
    return result[0], [share, *result[1:3]], result[3:]


def squeeze_kernel(refs):
    route, mine, *packed, rows, grads, picks = refs
    count, depth = packed[0].shape[0], rows.shape[1]
    slots = count // 2
    lanes = route.shape[1]
    kept = (route[...] == mine[0]).astype(F32)
    pieces = count // lanes
    lines = [
        jnp.concatenate([kept[i : i + 1] for i in range(b * pieces, (b + 1) * pieces)], axis=1)
        for b in range(len(packed))
    ]
    keep = jnp.concatenate(lines * (8 // len(packed)), axis=0).astype(BF16)
    before = lax.broadcasted_iota(jnp.int32, (count, count), 0)
    after = lax.broadcasted_iota(jnp.int32, (count, count), 1)
    rank = dot(keep, (before <= after).astype(BF16)) * keep.astype(F32)
    slot = (lax.broadcasted_iota(jnp.int32, (slots, count), 0) + 1).astype(F32)
    for block, ref in enumerate(packed):
        span = slice(block * slots, (block + 1) * slots)
        pick = (slot == rank[block : block + 1, :]).astype(BF16)
        picks[span, :] = pick
        rows[span, :] = dot(pick, ref[:, :depth]).astype(BF16)
        grads[span, :] = dot(pick, ref[:, depth:]).astype(BF16)


def squeeze_call(packed, route, mine, depth):
    count, total = packed[0].shape
    slots = len(packed) * (count // 2)
    shape = jax.ShapeDtypeStruct
    return pl.pallas_call(
        lambda *refs: squeeze_kernel(refs),
        out_shape=[
            shape((slots, depth), BF16),
            shape((slots, total - depth), BF16),
            shape((slots, count), BF16),
        ],
        in_specs=[VMEM, SMEM] + [VMEM] * len(packed),
        out_specs=[VMEM] * 3,
        compiler_params=limit(16),
        name="squeeze",
    )(route, mine, *packed)


def backward_kernel(sizes, where, refs):
    names = iter(refs)
    slopes, weights, picks = grouped(names, sizes)
    keep, send = names
    depth = keep.shape[2]
    factor = 1.0 / math.sqrt(depth)
    shaped = take(weights, 0, depth).astype(BF16)
    half, count = keep.shape[:2]
    step = count // 2 if picks else count
    for block in range(2 * half):
        array, place = where[block]
        part = slopes[array][place * step : (place + 1) * step, :]
        value = (dot_last(part, shaped) * factor).astype(BF16)
        if picks:
            value = dot_first(picks[0][block * step : (block + 1) * step, :], value).astype(BF16)
        out = keep if block < half else send
        out[block % half] = value


def backward_call(slopes, weights, picks, where, count):
    depth = sum(item.shape[0] for item in weights)
    shape = jax.ShapeDtypeStruct((len(where) // 2, count, depth), BF16)
    sizes = sizes_of([slopes, weights, picks])
    return pl.pallas_call(
        lambda *refs: backward_kernel(sizes, where, refs),
        out_shape=[shape, shape],
        in_specs=[VMEM] * sum(sizes),
        out_specs=[VMEM, VMEM],
        compiler_params=limit(16),
        name="backward",
    )(*slopes, *weights, *picks)


def halve_call(keep, back):
    half = keep.shape[0] // 2
    shape = jax.ShapeDtypeStruct((half,) + keep.shape[1:], keep.dtype)

    def kernel(keep, back, first, second):
        first[...] = keep[:half] + back[:half]
        second[...] = keep[half:] + back[half:]

    return pl.pallas_call(
        kernel,
        out_shape=[shape, shape],
        in_specs=[VMEM] * 2,
        out_specs=[VMEM] * 2,
        compiler_params=limit(12),
        name="halve",
    )(keep, back)


def average_call(parts, start, stop, depth, buffer):
    flat = [item for part in parts for item in part]
    sizes = sizes_of(parts)
    extra = [] if buffer is None else [buffer]
    width = flat[0].shape[1]

    def kernel(*refs):
        names = iter(refs)
        groups = grouped(names, sizes)
        out, value, sem = list(names)[len(extra) :]
        value[...] = mixed(groups, start, stop)
        made = pltpu.make_async_copy(value, out.at[pl.ds(start, stop - start), :], sem)
        made.start()
        made.wait()

    return pl.pallas_call(
        kernel,
        out_shape=jax.ShapeDtypeStruct((depth, width), F32),
        in_specs=[VMEM] * len(flat) + [ANY] * len(extra),
        out_specs=ANY,
        scratch_shapes=[pltpu.VMEM((stop - start, width), F32), pltpu.SemaphoreType.DMA(())],
        input_output_aliases={len(flat): 0} if extra else {},
        compiler_params=limit(12),
        name="average",
    )(*flat, *extra)


def place_call(function, index, count, parts, buffer):
    block = parts[0].shape
    rest = (0,) * (len(block) - 1)
    extra = [] if buffer is None else [buffer]

    def kernel(*refs):
        refs[-1][...] = function(*refs[: len(parts)])

    return pl.pallas_call(
        kernel,
        grid=(1,),
        out_shape=jax.ShapeDtypeStruct((count * block[0],) + block[1:], parts[0].dtype),
        in_specs=[pl.BlockSpec(block, lambda i: (0,) + rest)] * len(parts) + [ANY] * len(extra),
        out_specs=pl.BlockSpec(block, lambda i: (index,) + rest),
        input_output_aliases={len(parts): 0} if extra else {},
        compiler_params=limit(12),
    )(*parts, *extra)


def on_device(tokens, routing, out_grad, weights, momentum):
    experts = lax.axis_size("expert")
    bits = []
    bit = experts // 2
    while bit:
        bits.append(bit)
        bit //= 2
    weight = weights[0, 0]
    moment = momentum[0, 0]
    depth = weight.shape[0]
    _, two = split(depth)
    mine = lax.axis_index("expert").astype(jnp.int32).reshape(1)

    def gathered(own):
        held = [own]
        for bit in bits:
            moved = []
            for item in held:
                moved.append(swapped(item, "expert", bit))
            held = held + moved
        return held

    in_grad = None
    waiting = []
    count = tokens.shape[1]
    lead = count // 4
    own_rows, rest_tokens = lax.optimization_barrier((tokens[0, :lead], tokens))
    own_rest, rest_tokens, rest_grad = lax.optimization_barrier(
        (rest_tokens[0, lead:], rest_tokens, out_grad)
    )
    own_grads = rest_grad[0]
    packed = jnp.concatenate([rest_tokens[1], rest_grad[1]], axis=1)
    first_rows = list(zip(gathered(own_rows), gathered(own_rest)))

    def rows_of(blocks):
        return [piece for block in first_rows[blocks] for piece in block]

    routes = gathered(routing)
    first_grads = gathered(own_grads)
    later = gathered(packed)

    def route_of(index, items):
        picked = [item[index] for item in items]
        return jnp.concatenate(picked * (experts // len(picked))).reshape(-1, 128)

    near, direct, relayed = slice(0, None, 2), slice(1, 2), slice(3, None, 2)
    moment, slopes = part_call(
        rows_of(near), first_grads[near], route_of(0, routes[near]), mine, weight,
        moment, 0.9, False,
    )
    all_slopes = [slopes]
    (pre,) = ahead_call(rows_of(direct), [[weight]], depth)
    (relayed_pre,) = ahead_call(rows_of(relayed), [[weight]], depth)
    moment, slopes = part_call(
        rows_of(direct), first_grads[direct], route_of(0, routes[direct]), mine, pre,
        moment, 1.0, True,
    )
    all_slopes.append(slopes)
    pre = relayed_pre
    where = [[(0, block) for block in range(experts)]]
    where.insert(0, [(0, i // 2) if i % 2 == 0 else (min(i, 2), max(0, i - 3) // 2) for i in range(experts)])
    weights = [weight]
    parts, picks = [], []
    for index in range(ROUNDS):
        if index:
            moment, slopes, low, rest, scale, stepped, share, late = round_call(
                [later_rows], [later_grads], 0.9, None, mine, pre, weights, moment, parts
            )
            weights = [*weights, late]
            all_slopes = [slopes]
        else:
            moment, slopes, low, rest, scale, stepped, share = round_call(
                rows_of(relayed), first_grads[relayed], 1.0, route_of(0, routes[relayed]),
                mine, pre, weights, moment, parts,
            )
            all_slopes.append(slopes)
        stepped_low, ones, twos = second_call(low, rest, scale, share, weights)
        firsts = []
        for item in ones:
            firsts.append(crossed(item, "node", 2))
        seconds = []
        for item in twos:
            seconds.append(crossed(item, "node", -2))
        nears = []
        for piece, item in enumerate(ones):
            pair = (item.astype(F32) + firsts[piece].astype(F32)).astype(BF16)
            nears.append(swapped(pair, "node", 1))
        keep, send = backward_call(all_slopes, weights, picks, where[index], count)
        for bit in reversed(bits):
            back = swapped(send, "expert", bit)
            if keep.shape[0] > 1:
                keep, send = halve_call(keep, back)
        waiting.append([keep, back])
        halves = [stepped, stepped_low]
        parts = [halves, firsts, seconds, nears]
        early_parts = [halves, firsts[:2], seconds[:1], nears[:2]]
        if index < ROUNDS - 1:
            later_rows, later_grads, pick = squeeze_call(
                later, route_of(index + 1, routes), mine, depth
            )
            picks = [pick]
            upper, pre = ahead_call([later_rows], early_parts, two[0])
            weights = [upper]
        else:
            for done, pair in enumerate(waiting):
                in_grad = place_call(lambda a, b: a[...] + b[...], done, ROUNDS, pair, in_grad)
            weight = average_call(early_parts, 0, two[0], depth, None)
            weight = average_call(parts, two[0], depth, depth, weight)
    return (weight[None, None], moment[None, None], in_grad)


def solution(mesh):
    return jax.shard_map(
        on_device,
        mesh=mesh,
        in_specs=(
            P(None, ("expert", "node"), None),
            P(None, ("expert", "node")),
            P(None, ("expert", "node"), None),
            P("node", "expert", None, None),
            P("node", "expert", None, None),
        ),
        out_specs=(
            P("node", "expert", None, None),
            P("node", "expert", None, None),
            P(None, ("expert", "node"), None),
        ),
        check_vma=False,
    )
```

time: 160 us -> 153 us (0.956)
  waiting for transfers between devices: 97.4 us -> 84.7 us
  starting transfers between devices: 29 us -> 33 us
    ppermute x10, waiting for transfers between devices: 69.7 us -> 34.2 us  [crossed(): lax.ppermute(block, axis, [((i + (-way if i % 2 else way)) % count, i) fo...]
    ppermute x20 -> x25, waiting for transfers between devices: 27.7 us -> 50.5 us  [swapped(): lax.ppermute(block, axis, [(i, i ^ bit) for i in range(lax.axis_size(axis...]
    ppermute x20 -> x25, starting transfers between devices: 15.7 us -> 21.6 us  [swapped(): lax.ppermute(block, axis, [(i, i ^ bit) for i in range(lax.axis_size(axis...]
    ppermute x10, starting transfers between devices: 13.3 us -> 11.3 us  [crossed(): lax.ppermute(block, axis, [((i + (-way if i % 2 else way)) % count, i) fo...]
    squeeze x1, local copies, waits for them, and re-layouts: 1.91 us -> 0.04 us  [on_device(): own_grads = rest_grad[0]]
    squeeze x1 -> x2, local copies, waits for them, and re-layouts: 1.87 us -> 3.39 us  [the longest x1 1.82 us: on_device(): rest_tokens[0, lead:]]
    pallas_call x5 -> x7, Pallas kernels: 17.7 us -> 17.3 us  [the longest x2 8.89 us: round_call(): pl.pallas_call(lambda *refs: round_kernel(sizes, decay, refs), out_shape=...]
  transfers between devices with their start and end apart: 30 -> 35, of which waited for: 8 -> 11; matrix products, arithmetic and copies ran while one was open for 3% -> 4% of each run, Pallas kernels for 16% -> 17%
where the time goes in v5:
time: 153 us; the launch traced here: 152 us
  waiting for transfers between devices  84.7 us (55%)
  starting transfers between devices  33 us (22%)
  Pallas kernels  26.9 us (18%)
  local copies, waits for them, and re-layouts  5.33 us (3%)
    ppermute x25, waiting for transfers between devices, swapped(): lax.ppermute(block, axis, [(i, i ^ bit) for i in range(lax.axis_size(axis...  50.5 us
    ppermute x10, waiting for transfers between devices, crossed(): lax.ppermute(block, axis, [((i + (-way if i % 2 else way)) % count, i) fo...  34.2 us
    ppermute x25, starting transfers between devices, swapped(): lax.ppermute(block, axis, [(i, i ^ bit) for i in range(lax.axis_size(axis...  21.6 us
    ppermute x10, starting transfers between devices, crossed(): lax.ppermute(block, axis, [((i + (-way if i % 2 else way)) % count, i) fo...  11.3 us
    pallas_call x2, Pallas kernels, round_call(): pl.pallas_call(lambda *refs: round_kernel(sizes, decay, refs), out_shape=...  8.89 us
    pallas_call x2, Pallas kernels, part_call(): pl.pallas_call(lambda *refs: part_kernel(sizes, decay, ready, refs), out_...  4.13 us
    pallas_call x2, Pallas kernels, backward_call(): pl.pallas_call(lambda *refs: backward_kernel(sizes, where, refs), out_sha...  3.53 us
  transfers between devices with their start and end apart: 35, of which 11 were waited for; matrix products, arithmetic and copies ran while one was open for 4% of the time, Pallas kernels for 17%

profile of v5, /device:TPU:0, one launch (start us, length us, event | category | flops | bytes accessed | tf_op | source)
XLA Modules:
  0.0 151.5 jit_solution(13164274647166273722)
XLA Ops:
  0.6 3.0 %collective-permute-start = (s32[2,256]{1,0:T(2,128)}, s32[2,256]{1,0:T(2,128)}, u32[]{:S(2)}, u32[]{:S(2)}) collective-permute-start(s32[2,256]{1,0:T(2,128)} %param.6), channel_id=1, source_target_pairs={{0,16},{8,24},{16,0},{24,8},{1,17},{9,25},{17,1},{25,9},{2,18},{10... | collective-permute-start | bytes 6152 | tf_op jit(solution)/shard_map/ppermute | solution.py:26
  3.7 1.6 %slice_bitcast_fusion.4.refs_4_ = bf16[64,1024]{1,0:T(8,128)(2,1)} fusion(bf16[2,256,1024]{2,1,0:T(8,128)(2,1)} %param.5), kind=kLoop, calls=%fused_computation.11 | loop fusion | bytes 262144 | tf_op jit(solution)/shard_map/squeeze | solution.py:515
  5.8 1.8 %slice_bitcast_fusion.1.refs_5_ = bf16[192,1024]{1,0:T(8,128)(2,1)} fusion(bf16[2,256,1024]{2,1,0:T(8,128)(2,1)} %param.5), kind=kLoop, calls=%fused_computation.6 | loop fusion | bytes 786432 | tf_op jit(solution)/shard_map/squeeze | solution.py:517
  7.7 1.9 %collective-permute-start.8 = (bf16[192,1024]{1,0:T(8,128)(2,1)}, bf16[192,1024]{1,0:T(8,128)(2,1)S(1)}, u32[]{:S(2)}, u32[]{:S(2)}) collective-permute-start(bf16[192,1024]{1,0:T(8,128)(2,1)} %slice_bitcast_fusion.1.refs_5_), channel_id=1, source_target_pairs={{0,16},{8,24},{16,0},{24,8},{1,17},{9,25},{17,1},{25,9},{2,18},{10... | collective-permute-start | bytes 1179656 | tf_op jit(solution)/shard_map/ppermute | solution.py:26
  12.8 1.5 %collective-permute-start.3 = (bf16[256,1536]{1,0:T(8,128)(2,1)S(1)}, bf16[256,1536]{1,0:T(8,128)(2,1)S(1)}, u32[]{:S(2)}, u32[]{:S(2)}) collective-permute-start(bf16[256,1536]{1,0:T(8,128)(2,1)S(1)} %pad_maximum_fusion.refs_2_), channel_id=1, source_target_pairs={{0,16},{8,24},{16,0},{24,8},{1,17},{9,25},{17,1},{25,9},{2,18},{10... | collective-permute-start | bytes 2359304 | tf_op jit(solution)/shard_map/ppermute | solution.py:26
  14.4 6.4 %collective-permute-done.8.refs_1_.refs_5_ = bf16[192,1024]{1,0:T(8,128)(2,1)S(1)} collective-permute-done((bf16[192,1024]{1,0:T(8,128)(2,1)}, bf16[192,1024]{1,0:T(8,128)(2,1)S(1)}, u32[]{:S(2)}, u32[]{:S(2)}) %collective-permute-start.8) | collective-permute-done | bytes 393248 | tf_op jit(solution)/shard_map/ppermute | solution.py:26
  20.8 5.6 %collective-permute-done.13.refs_6_ = bf16[256,512]{1,0:T(8,128)(2,1)S(1)} collective-permute-done((bf16[256,512]{1,0:T(8,128)(2,1)S(1)}, bf16[256,512]{1,0:T(8,128)(2,1)S(1)}, u32[]{:S(2)}, u32[]{:S(2)}) %collective-permute-start.13) | collective-permute-done | bytes 262176 | tf_op jit(solution)/shard_map/ppermute | solution.py:26
  26.9 1.5 ahead.4.refs_2_
  28.4 2.6 %part_rows.2 = (f32[1024,512]{1,0:T(8,128)S(1)}, bf16[512,512]{1,0:T(8,128)(2,1)S(1)}) custom-call(s32[8,128]{1,0:T(8,128)S(1)} %pad_add_fusion.2.refs_0_, s32[1]{0:T(128)} %bitcast.refs_1_.refs_0_, f32[1024,512]{1,0:T(8,128)S(1)} %bitcast.24, f32[1024,512]{1,0:T(8,128)S(1)} %bitcast.29, bf16[64,1024]{1,0:T(8,128)(2,1)} %slice_bitcast_fusion.4.refs_4_, ...), custom_call_target="tpu_custom_call" | custom-call | tf_op jit(solution)/shard_map/part_rows/pallas_call | solution.py:223
  31.0 1.6 %part_rows.3 = (f32[1024,512]{1,0:T(8,128)S(1)}, bf16[256,512]{1,0:T(8,128)(2,1)S(1)}) custom-call(s32[8,128]{1,0:T(8,128)S(1)} %pad_add_fusion.1.refs_0_, s32[1]{0:T(128)} %bitcast.refs_1_.refs_0_, f32[256,512]{1,0:T(8,128)S(1)} %ahead.4.refs_2_, f32[1024,512]{1,0:T(8,128)S(1)} %get-tuple-element.56.refs_3_, ...), custom_call_target="tpu_custom_call" | custom-call | tf_op jit(solution)/shard_map/part_rows/pallas_call | solution.py:223
  33.1 4.2 %muon_round.2 = (f32[1024,512]{1,0:T(8,128)S(1)}, bf16[256,512]{1,0:T(8,128)(2,1)S(1)}, bf16[1024,512]{1,0:T(8,128)(2,1)S(1)}, bf16[512,512]{1,0:T(8,128)(2,1)S(...) custom-call(s32[1]{0:T(128)} %bitcast.refs_1_.refs_0_, f32[256,512]{1,0:T(8,128)S(1)} %ahead.3.refs_1_, ...), custom_call_target="tpu_custom_call" | custom-call | tf_op jit(solution)/shard_map/muon_round/pallas_call | solution.py:310
  37.4 3.4 %collective-permute-start.15 = (bf16[512,512]{1,0:T(8,128)(2,1)S(1)}, bf16[512,512]{1,0:T(8,128)(2,1)S(1)}, u32[]{:S(2)}, u32[]{:S(2)}) collective-permute-start(bf16[512,512]{1,0:T(8,128)(2,1)S(1)} %get-tuple-element.62.refs_3_), channel_id=1, source_target_pairs={{2,0},{7,1},{4,2},{1,3},{6,4},{3,5},{0,6},{5,7},{10,8},{15,9},{12,... | collective-permute-start | bytes 1572872 | tf_op jit(solution)/shard_map/ppermute | solution.py:31
  42.7 3.3 %collective-permute-start.20 = (bf16[128,512]{1,0:T(8,128)(2,1)S(1)}, bf16[128,512]{1,0:T(8,128)(2,1)S(1)}, u32[]{:S(2)}, u32[]{:S(2)}) collective-permute-start(bf16[128,512]{1,0:T(8,128)(2,1)S(1)} %get-tuple-element.70), channel_id=1, source_target_pairs={{2,0},{7,1},{4,2},{1,3},{6,4},{3,5},{0,6},{5,7},{10,8},{15,9},{12,... | collective-permute-start | bytes 393224 | tf_op jit(solution)/shard_map/ppermute | solution.py:31
  45.9 7.1 %collective-permute-done.15.refs_3_.refs_8_ = bf16[512,512]{1,0:T(8,128)(2,1)S(1)} collective-permute-done((bf16[512,512]{1,0:T(8,128)(2,1)S(1)}, bf16[512,512]{1,0:T(8,128)(2,1)S(1)}, u32[]{:S(2)}, u32[]{:S(2)}) %collective-permute-start.15) | collective-permute-done | bytes 524320 | tf_op jit(solution)/shard_map/ppermute | solution.py:31
  53.6 7.9 %collective-permute-done.16.refs_4_.refs_9_ = bf16[384,512]{1,0:T(8,128)(2,1)S(1)} collective-permute-done((bf16[384,512]{1,0:T(8,128)(2,1)S(1)}, bf16[384,512]{1,0:T(8,128)(2,1)S(1)}, u32[]{:S(2)}, u32[]{:S(2)}) %collective-permute-start.16) | collective-permute-done | bytes 393248 | tf_op jit(solution)/shard_map/ppermute | solution.py:31
  61.6 2.3 %collective-permute-start.18 = (bf16[512,512]{1,0:T(8,128)(2,1)S(1)}, bf16[512,512]{1,0:T(8,128)(2,1)S(1)}, u32[]{:S(2)}, u32[]{:S(2)}) collective-permute-start(bf16[512,512]{1,0:T(8,128)(2,1)S(1)} %add_convert_fusion.1), channel_id=1, source_target_pairs={{0,1},{1,0},{2,3},{3,2},{4,5},{5,4},{6,7},{7,6},{8,9},{9,8},{10,11... | collective-permute-start | bytes 1572872 | tf_op jit(solution)/shard_map/ppermute | solution.py:26
  64.0 1.3 backward.3
  65.8 16.8 %collective-permute-done.19.refs_7_.refs_14_ = bf16[384,512]{1,0:T(8,128)(2,1)S(1)} collective-permute-done((bf16[384,512]{1,0:T(8,128)(2,1)S(1)}, bf16[384,512]{1,0:T(8,128)(2,1)S(1)}, u32[]{:S(2)}, u32[]{:S(2)}) %collective-permute-start.19) | collective-permute-done | bytes 393248 | tf_op jit(solution)/shard_map/ppermute | solution.py:26
  82.6 1.7 %collective-permute-start.22 = (bf16[128,512]{1,0:T(8,128)(2,1)S(1)}, bf16[128,512]{1,0:T(8,128)(2,1)S(1)}, u32[]{:S(2)}, u32[]{:S(2)}) collective-permute-start(bf16[128,512]{1,0:T(8,128)(2,1)S(1)} %add_convert_fusion.5), channel_id=1, source_target_pairs={{0,1},{1,0},{2,3},{3,2},{4,5},{5,4},{6,7},{7,6},{8,9},{9,8},{10,11... | collective-permute-start | bytes 393224 | tf_op jit(solution)/shard_map/ppermute | solution.py:26
  85.8 2.4 %collective-permute-done.22.refs_15_ = bf16[128,512]{1,0:T(8,128)(2,1)S(1)} collective-permute-done((bf16[128,512]{1,0:T(8,128)(2,1)S(1)}, bf16[128,512]{1,0:T(8,128)(2,1)S(1)}, u32[]{:S(2)}, u32[]{:S(2)}) %collective-permute-start.22) | collective-permute-done | bytes 131104 | tf_op jit(solution)/shard_map/ppermute | solution.py:26
  88.2 4.7 %muon_round.3 = (f32[1024,512]{1,0:T(8,128)}, bf16[512,512]{1,0:T(8,128)(2,1)S(1)}, bf16[1024,512]{1,0:T(8,128)(2,1)S(1)}, bf16[512,512]{1,0:T(8,128)(2,1)S(1)},...) custom-call(s32[1]{0:T(128)} %bitcast.refs_1_.refs_0_, ...), custom_call_target="tpu_custom_call" | custom-call | tf_op jit(solution)/shard_map/muon_round/pallas_call | solution.py:310
  92.9 2.2 %backward.2 = (bf16[2,256,1024]{2,1,0:T(8,128)(2,1)S(1)}, bf16[2,256,1024]{2,1,0:T(8,128)(2,1)S(1)}) custom-call(bf16[512,512]{1,0:T(8,128)(2,1)S(1)} %get-tuple-element.84.refs_0_, f32[768,512]{1,0:T(8,128)S(1)} %get-tuple-element.69.refs_5_.refs_4_.refs_1_, f32[256,512]{1,0:T(8,128)S(1)} %get-tuple-element.77.refs_5_.refs_2_, ...), custom_call_target="tpu_custom_call" | custom-call | tf_op jit(solution)/shard_map/backward/pallas_call | solution.py:415
  95.2 1.2 second_half.3
  96.4 3.3 %collective-permute-start.24 = (bf16[384,512]{1,0:T(8,128)(2,1)S(1)}, bf16[384,512]{1,0:T(8,128)(2,1)S(1)}, u32[]{:S(2)}, u32[]{:S(2)}) collective-permute-start(bf16[384,512]{1,0:T(8,128)(2,1)S(1)} %get-tuple-element.79), channel_id=1, source_target_pairs={{2,0},{7,1},{4,2},{1,3},{6,4},{3,5},{0,6},{5,7},{10,8},{15,9},{12,... | collective-permute-start | bytes 1179656 | tf_op jit(solution)/shard_map/ppermute | solution.py:31
  99.9 1.4 collective-permute-start.34
  101.3 7.9 %collective-permute-done.24.refs_3_ = bf16[384,512]{1,0:T(8,128)(2,1)S(1)} collective-permute-done((bf16[384,512]{1,0:T(8,128)(2,1)S(1)}, bf16[384,512]{1,0:T(8,128)(2,1)S(1)}, u32[]{:S(2)}, u32[]{:S(2)}) %collective-permute-start.24) | collective-permute-done | bytes 393248 | tf_op jit(solution)/shard_map/ppermute | solution.py:31
  109.3 11.2 %collective-permute-done.23.refs_2_ = bf16[512,512]{1,0:T(8,128)(2,1)S(1)} collective-permute-done((bf16[512,512]{1,0:T(8,128)(2,1)S(1)}, bf16[512,512]{1,0:T(8,128)(2,1)S(1)}, u32[]{:S(2)}, u32[]{:S(2)}) %collective-permute-start.23) | collective-permute-done | bytes 524320 | tf_op jit(solution)/shard_map/ppermute | solution.py:31
  120.6 3.9 %collective-permute-start.28 = (bf16[512,512]{1,0:T(8,128)(2,1)S(1)}, bf16[512,512]{1,0:T(8,128)(2,1)S(1)}, u32[]{:S(2)}, u32[]{:S(2)}) collective-permute-start(bf16[512,512]{1,0:T(8,128)(2,1)S(1)} %add_convert_fusion), channel_id=1, source_target_pairs={{0,1},{1,0},{2,3},{3,2},{4,5},{5,4},{6,7},{7,6},{8,9},{9,8},{10,11... | collective-permute-start | bytes 1572872 | tf_op jit(solution)/shard_map/ppermute | solution.py:26
  124.8 1.4 collective-permute-start.32
  126.2 18.5 %collective-permute-done.29.refs_6_.refs_8_ = bf16[384,512]{1,0:T(8,128)(2,1)S(1)} collective-permute-done((bf16[384,512]{1,0:T(8,128)(2,1)S(1)}, bf16[384,512]{1,0:T(8,128)(2,1)S(1)}, u32[]{:S(2)}, u32[]{:S(2)}) %collective-permute-start.29) | collective-permute-done | bytes 393248 | tf_op jit(solution)/shard_map/ppermute | solution.py:26
  144.7 2.1 %collective-permute-start.30 = (bf16[128,512]{1,0:T(8,128)(2,1)S(1)}, bf16[128,512]{1,0:T(8,128)(2,1)S(1)}, u32[]{:S(2)}, u32[]{:S(2)}) collective-permute-start(bf16[128,512]{1,0:T(8,128)(2,1)S(1)} %add_convert_fusion.4), channel_id=1, source_target_pairs={{0,1},{1,0},{2,3},{3,2},{4,5},{5,4},{6,7},{7,6},{8,9},{9,8},{10,11... | collective-permute-start | bytes 393224 | tf_op jit(solution)/shard_map/ppermute | solution.py:26
  147.6 1.6 %average.2.refs_10_ = f32[1024,512]{1,0:T(8,128)} custom-call(f32[512,512]{1,0:T(8,128)S(1)} %get-tuple-element.72.refs_0_, f32[512,512]{1,0:T(8,128)S(1)} %get-tuple-element.78.refs_1_, bf16[512,512]{1,0:T(8,128)(2,1)S(1)} %collective-permute-done.23.refs_2_, bf16[384,512]{1,0:T(8,128)(2,1)S(1)} %collective-permute-done.24.refs_3_, ...), custom_call_target="tpu_custom_call" | custom-call | tf_op jit(solution)/shard_map/average/pallas_call | solution.py:458
  (83 shorter events, 13.4 us)
Async XLA Ops:
  0.6 10.1 %collective-permute-start = (s32[2,256]{1,0:T(2,128)}, s32[2,256]{1,0:T(2,128)}, u32[]{:S(2)}, u32[]{:S(2)}) collective-permute-start(s32[2,256]{1,0:T(2,128)} %param.6), channel_id=1, source_target_pairs={{0,16},{8,24},{16,0},{24,8},{1,17},{9,25},{17,1},{25,9},{2,18},{10... | collective-permute-start | bytes 6152 | tf_op jit(solution)/shard_map/ppermute | solution.py:26
  3.7 8.0 %collective-permute-start.1 = (s32[2,256]{1,0:T(2,128)}, s32[2,256]{1,0:T(2,128)S(1)}, u32[]{:S(2)}, u32[]{:S(2)}) collective-permute-start(s32[2,256]{1,0:T(2,128)} %param.6), channel_id=1, source_target_pairs={{0,8},{8,0},{16,24},{24,16},{1,9},{9,1},{17,25},{25,17},{2,10},{10... | collective-permute-start | bytes 6152 | tf_op jit(solution)/shard_map/ppermute | solution.py:26
  5.2 7.2 %collective-permute-start.10 = (bf16[64,1024]{1,0:T(8,128)(2,1)}, bf16[64,1024]{1,0:T(8,128)(2,1)}, u32[]{:S(2)}, u32[]{:S(2)}) collective-permute-start(bf16[64,1024]{1,0:T(8,128)(2,1)} %slice_bitcast_fusion.4.refs_4_), channel_id=1, source_target_pairs={{0,8},{8,0},{16,24},{24,16},{1,9},{9,1},{17,25},{25,17},{2,10},{10... | collective-permute-start | bytes 393224 | tf_op jit(solution)/shard_map/ppermute | solution.py:26
  5.8 7.1 %collective-permute-start.6 = (bf16[64,1024]{1,0:T(8,128)(2,1)}, bf16[64,1024]{1,0:T(8,128)(2,1)}, u32[]{:S(2)}, u32[]{:S(2)}) collective-permute-start(bf16[64,1024]{1,0:T(8,128)(2,1)} %slice_bitcast_fusion.4.refs_4_), channel_id=1, source_target_pairs={{0,16},{8,24},{16,0},{24,8},{1,17},{9,25},{17,1},{25,9},{2,18},{10... | collective-permute-start | bytes 393224 | tf_op jit(solution)/shard_map/ppermute | solution.py:26
  7.7 13.1 %collective-permute-start.8 = (bf16[192,1024]{1,0:T(8,128)(2,1)}, bf16[192,1024]{1,0:T(8,128)(2,1)S(1)}, u32[]{:S(2)}, u32[]{:S(2)}) collective-permute-start(bf16[192,1024]{1,0:T(8,128)(2,1)} %slice_bitcast_fusion.1.refs_5_), channel_id=1, source_target_pairs={{0,16},{8,24},{16,0},{24,8},{1,17},{9,25},{17,1},{25,9},{2,18},{10... | collective-permute-start | bytes 1179656 | tf_op jit(solution)/shard_map/ppermute | solution.py:26
  11.7 14.7 %collective-permute-start.13 = (bf16[256,512]{1,0:T(8,128)(2,1)S(1)}, bf16[256,512]{1,0:T(8,128)(2,1)S(1)}, u32[]{:S(2)}, u32[]{:S(2)}) collective-permute-start(bf16[256,512]{1,0:T(8,128)(2,1)S(1)} %get-tuple-element.97.refs_8_), channel_id=1, source_target_pairs={{0,16},{8,24},{16,0},{24,8},{1,17},{9,25},{17,1},{25,9},{2,18},{10... | collective-permute-start | bytes 786440 | tf_op jit(solution)/shard_map/ppermute | solution.py:26
  12.2 14.1 %collective-permute-start.12 = (bf16[256,512]{1,0:T(8,128)(2,1)S(1)}, bf16[256,512]{1,0:T(8,128)(2,1)S(1)}, u32[]{:S(2)}, u32[]{:S(2)}) collective-permute-start(bf16[256,512]{1,0:T(8,128)(2,1)S(1)} %get-tuple-element.97.refs_8_), channel_id=1, source_target_pairs={{0,8},{8,0},{16,24},{24,16},{1,9},{9,1},{17,25},{25,17},{2,10},{10... | collective-permute-start | bytes 786440 | tf_op jit(solution)/shard_map/ppermute | solution.py:26
  12.4 15.9 %collective-permute-start.11 = (bf16[192,1024]{1,0:T(8,128)(2,1)}, bf16[192,1024]{1,0:T(8,128)(2,1)S(1)}, u32[]{:S(2)}, u32[]{:S(2)}) collective-permute-start(bf16[192,1024]{1,0:T(8,128)(2,1)} %slice_bitcast_fusion.1.refs_5_), channel_id=1, source_target_pairs={{0,8},{8,0},{16,24},{24,16},{1,9},{9,1},{17,25},{25,17},{2,10},{10... | collective-permute-start | bytes 1179656 | tf_op jit(solution)/shard_map/ppermute | solution.py:26
  12.8 29.6 %collective-permute-start.3 = (bf16[256,1536]{1,0:T(8,128)(2,1)S(1)}, bf16[256,1536]{1,0:T(8,128)(2,1)S(1)}, u32[]{:S(2)}, u32[]{:S(2)}) collective-permute-start(bf16[256,1536]{1,0:T(8,128)(2,1)S(1)} %pad_maximum_fusion.refs_2_), channel_id=1, source_target_pairs={{0,16},{8,24},{16,0},{24,8},{1,17},{9,25},{17,1},{25,9},{2,18},{10... | collective-permute-start | bytes 2359304 | tf_op jit(solution)/shard_map/ppermute | solution.py:26
  20.7 11.8 %collective-permute-start.9 = (bf16[192,1024]{1,0:T(8,128)(2,1)S(1)}, bf16[192,1024]{1,0:T(8,128)(2,1)S(1)}, u32[]{:S(2)}, u32[]{:S(2)}) collective-permute-start(bf16[192,1024]{1,0:T(8,128)(2,1)S(1)} %collective-permute-done.8.refs_1_.refs_5_), channel_id=1, source_target_pairs={{0,8},{8,0},{16,24},{24,16},{1,9},{9,1},{17,25},{25,17},{2,10},{10... | collective-permute-start | bytes 1179656 | tf_op jit(solution)/shard_map/ppermute | solution.py:26
  26.4 6.2 %collective-permute-start.7 = (bf16[64,1024]{1,0:T(8,128)(2,1)}, bf16[64,1024]{1,0:T(8,128)(2,1)S(1)}, u32[]{:S(2)}, u32[]{:S(2)}) collective-permute-start(bf16[64,1024]{1,0:T(8,128)(2,1)} %collective-permute-done.6.refs_0_.refs_4_), channel_id=1, source_target_pairs={{0,8},{8,0},{16,24},{24,16},{1,9},{9,1},{17,25},{25,17},{2,10},{10... | collective-permute-start | bytes 393224 | tf_op jit(solution)/shard_map/ppermute | solution.py:26
  26.4 6.8 %collective-permute-start.14 = (bf16[256,512]{1,0:T(8,128)(2,1)S(1)}, bf16[256,512]{1,0:T(8,128)(2,1)S(1)}, u32[]{:S(2)}, u32[]{:S(2)}) collective-permute-start(bf16[256,512]{1,0:T(8,128)(2,1)S(1)} %collective-permute-done.13.refs_6_), channel_id=1, source_target_pairs={{0,8},{8,0},{16,24},{24,16},{1,9},{9,1},{17,25},{25,17},{2,10},{10... | collective-permute-start | bytes 786440 | tf_op jit(solution)/shard_map/ppermute | solution.py:26
  37.4 15.7 %collective-permute-start.15 = (bf16[512,512]{1,0:T(8,128)(2,1)S(1)}, bf16[512,512]{1,0:T(8,128)(2,1)S(1)}, u32[]{:S(2)}, u32[]{:S(2)}) collective-permute-start(bf16[512,512]{1,0:T(8,128)(2,1)S(1)} %get-tuple-element.62.refs_3_), channel_id=1, source_target_pairs={{2,0},{7,1},{4,2},{1,3},{6,4},{3,5},{0,6},{5,7},{10,8},{15,9},{12,... | collective-permute-start | bytes 1572872 | tf_op jit(solution)/shard_map/ppermute | solution.py:31
  40.7 23.2 %collective-permute-start.4 = (bf16[256,1536]{1,0:T(8,128)(2,1)S(1)}, bf16[256,1536]{1,0:T(8,128)(2,1)S(1)}, u32[]{:S(2)}, u32[]{:S(2)}) collective-permute-start(bf16[256,1536]{1,0:T(8,128)(2,1)S(1)} %pad_maximum_fusion.refs_2_), channel_id=1, source_target_pairs={{0,8},{8,0},{16,24},{24,16},{1,9},{9,1},{17,25},{25,17},{2,10},{10... | collective-permute-start | bytes 2359304 | tf_op jit(solution)/shard_map/ppermute | solution.py:26
  41.9 19.6 %collective-permute-start.16 = (bf16[384,512]{1,0:T(8,128)(2,1)S(1)}, bf16[384,512]{1,0:T(8,128)(2,1)S(1)}, u32[]{:S(2)}, u32[]{:S(2)}) collective-permute-start(bf16[384,512]{1,0:T(8,128)(2,1)S(1)} %get-tuple-element.64), channel_id=1, source_target_pairs={{2,0},{7,1},{4,2},{1,3},{6,4},{3,5},{0,6},{5,7},{10,8},{15,9},{12,... | collective-permute-start | bytes 1179656 | tf_op jit(solution)/shard_map/ppermute | solution.py:31
  42.4 23.0 %collective-permute-start.5 = (bf16[256,1536]{1,0:T(8,128)(2,1)S(1)}, bf16[256,1536]{1,0:T(8,128)(2,1)S(1)}, u32[]{:S(2)}, u32[]{:S(2)}) collective-permute-start(bf16[256,1536]{1,0:T(8,128)(2,1)S(1)} %collective-permute-done.3.refs_3_), channel_id=1, source_target_pairs={{0,8},{8,0},{16,24},{24,16},{1,9},{9,1},{17,25},{25,17},{2,10},{10... | collective-permute-start | bytes 2359304 | tf_op jit(solution)/shard_map/ppermute | solution.py:26
  42.7 22.7 %collective-permute-start.20 = (bf16[128,512]{1,0:T(8,128)(2,1)S(1)}, bf16[128,512]{1,0:T(8,128)(2,1)S(1)}, u32[]{:S(2)}, u32[]{:S(2)}) collective-permute-start(bf16[128,512]{1,0:T(8,128)(2,1)S(1)} %get-tuple-element.70), channel_id=1, source_target_pairs={{2,0},{7,1},{4,2},{1,3},{6,4},{3,5},{0,6},{5,7},{10,8},{15,9},{12,... | collective-permute-start | bytes 393224 | tf_op jit(solution)/shard_map/ppermute | solution.py:31
  53.0 32.0 %collective-permute-start.17 = (bf16[768,512]{1,0:T(8,128)(2,1)S(1)}, bf16[768,512]{1,0:T(8,128)(2,1)S(1)}, u32[]{:S(2)}, u32[]{:S(2)}) collective-permute-start(bf16[768,512]{1,0:T(8,128)(2,1)S(1)} %get-tuple-element.65), channel_id=1, source_target_pairs={{6,0},{3,1},{0,2},{5,3},{2,4},{7,5},{4,6},{1,7},{14,8},{11,9},{8,1... | collective-permute-start | bytes 2359304 | tf_op jit(solution)/shard_map/ppermute | solution.py:31
  61.6 23.5 %collective-permute-start.18 = (bf16[512,512]{1,0:T(8,128)(2,1)S(1)}, bf16[512,512]{1,0:T(8,128)(2,1)S(1)}, u32[]{:S(2)}, u32[]{:S(2)}) collective-permute-start(bf16[512,512]{1,0:T(8,128)(2,1)S(1)} %add_convert_fusion.1), channel_id=1, source_target_pairs={{0,1},{1,0},{2,3},{3,2},{4,5},{5,4},{6,7},{7,6},{8,9},{9,8},{10,11... | collective-permute-start | bytes 1572872 | tf_op jit(solution)/shard_map/ppermute | solution.py:26
  64.0 18.6 %collective-permute-start.19 = (bf16[384,512]{1,0:T(8,128)(2,1)S(1)}, bf16[384,512]{1,0:T(8,128)(2,1)S(1)}, u32[]{:S(2)}, u32[]{:S(2)}) collective-permute-start(bf16[384,512]{1,0:T(8,128)(2,1)S(1)} %add_convert_fusion.3), channel_id=1, source_target_pairs={{0,1},{1,0},{2,3},{3,2},{4,5},{5,4},{6,7},{7,6},{8,9},{9,8},{10,11... | collective-permute-start | bytes 1179656 | tf_op jit(solution)/shard_map/ppermute | solution.py:26
  65.4 34.4 %collective-permute-start.33 = (bf16[2,256,1024]{2,1,0:T(8,128)(2,1)S(1)}, bf16[2,256,1024]{2,1,0:T(8,128)(2,1)S(1)}, u32[]{:S(2)}, u32[]{:S(2)}) collective-permute-start(bf16[2,256,1024]{2,1,0:T(8,128)(2,1)S(1)} %get-tuple-element.94), channel_id=1, source_target_pairs={{0,8},{8,0},{16,24},{24,16},{1,9},{9,1},{17,25},{25,17},{2,10},{10... | collective-permute-start | bytes 3145736 | tf_op jit(solution)/shard_map/ppermute | solution.py:26
  65.5 22.7 %collective-permute-start.21 = (bf16[256,512]{1,0:T(8,128)(2,1)S(1)}, bf16[256,512]{1,0:T(8,128)(2,1)S(1)}, u32[]{:S(2)}, u32[]{:S(2)}) collective-permute-start(bf16[256,512]{1,0:T(8,128)(2,1)S(1)} %get-tuple-element.71), channel_id=1, source_target_pairs={{6,0},{3,1},{0,2},{5,3},{2,4},{7,5},{4,6},{1,7},{14,8},{11,9},{8,1... | collective-permute-start | bytes 786440 | tf_op jit(solution)/shard_map/ppermute | solution.py:31
  95.1 29.4 %collective-permute-start.31 = (bf16[2,256,1024]{2,1,0:T(8,128)(2,1)S(1)}, bf16[2,256,1024]{2,1,0:T(8,128)(2,1)S(1)}, u32[]{:S(2)}, u32[]{:S(2)}) collective-permute-start(bf16[2,256,1024]{2,1,0:T(8,128)(2,1)S(1)} %get-tuple-element.87), channel_id=1, source_target_pairs={{0,8},{8,0},{16,24},{24,16},{1,9},{9,1},{17,25},{25,17},{2,10},{10... | collective-permute-start | bytes 3145736 | tf_op jit(solution)/shard_map/ppermute | solution.py:26
  96.4 12.8 %collective-permute-start.24 = (bf16[384,512]{1,0:T(8,128)(2,1)S(1)}, bf16[384,512]{1,0:T(8,128)(2,1)S(1)}, u32[]{:S(2)}, u32[]{:S(2)}) collective-permute-start(bf16[384,512]{1,0:T(8,128)(2,1)S(1)} %get-tuple-element.79), channel_id=1, source_target_pairs={{2,0},{7,1},{4,2},{1,3},{6,4},{3,5},{0,6},{5,7},{10,8},{15,9},{12,... | collective-permute-start | bytes 1179656 | tf_op jit(solution)/shard_map/ppermute | solution.py:31
  99.7 20.8 %collective-permute-start.23 = (bf16[512,512]{1,0:T(8,128)(2,1)S(1)}, bf16[512,512]{1,0:T(8,128)(2,1)S(1)}, u32[]{:S(2)}, u32[]{:S(2)}) collective-permute-start(bf16[512,512]{1,0:T(8,128)(2,1)S(1)} %get-tuple-element.76.refs_3_), channel_id=1, source_target_pairs={{2,0},{7,1},{4,2},{1,3},{6,4},{3,5},{0,6},{5,7},{10,8},{15,9},{12,... | collective-permute-start | bytes 1572872 | tf_op jit(solution)/shard_map/ppermute | solution.py:31
  99.9 26.2 %collective-permute-start.34 = (bf16[1,256,1024]{2,1,0:T(8,128)(2,1)S(1)}, bf16[1,256,1024]{2,1,0:T(8,128)(2,1)S(1)}, u32[]{:S(2)}, u32[]{:S(2)}) collective-permute-start(bf16[1,256,1024]{2,1,0:T(8,128)(2,1)S(1)} %get-tuple-element.96), channel_id=1, source_target_pairs={{0,16},{8,24},{16,0},{24,8},{1,17},{9,25},{17,1},{25,9},{2,18},{10... | collective-permute-start | bytes 1572872 | tf_op jit(solution)/shard_map/ppermute | solution.py:26
  101.2 23.5 %collective-permute-start.25 = (bf16[128,512]{1,0:T(8,128)(2,1)S(1)}, bf16[128,512]{1,0:T(8,128)(2,1)S(1)}, u32[]{:S(2)}, u32[]{:S(2)}) collective-permute-start(bf16[128,512]{1,0:T(8,128)(2,1)S(1)} %get-tuple-element.80), channel_id=1, source_target_pairs={{2,0},{7,1},{4,2},{1,3},{6,4},{3,5},{0,6},{5,7},{10,8},{15,9},{12,... | collective-permute-start | bytes 393224 | tf_op jit(solution)/shard_map/ppermute | solution.py:31
  109.2 38.4 %collective-permute-start.26 = (bf16[768,512]{1,0:T(8,128)(2,1)S(1)}, bf16[768,512]{1,0:T(8,128)(2,1)S(1)}, u32[]{:S(2)}, u32[]{:S(2)}) collective-permute-start(bf16[768,512]{1,0:T(8,128)(2,1)S(1)} %get-tuple-element.81), channel_id=1, source_target_pairs={{6,0},{3,1},{0,2},{5,3},{2,4},{7,5},{4,6},{1,7},{14,8},{11,9},{8,1... | collective-permute-start | bytes 2359304 | tf_op jit(solution)/shard_map/ppermute | solution.py:31
  120.6 27.0 %collective-permute-start.28 = (bf16[512,512]{1,0:T(8,128)(2,1)S(1)}, bf16[512,512]{1,0:T(8,128)(2,1)S(1)}, u32[]{:S(2)}, u32[]{:S(2)}) collective-permute-start(bf16[512,512]{1,0:T(8,128)(2,1)S(1)} %add_convert_fusion), channel_id=1, source_target_pairs={{0,1},{1,0},{2,3},{3,2},{4,5},{5,4},{6,7},{7,6},{8,9},{9,8},{10,11... | collective-permute-start | bytes 1572872 | tf_op jit(solution)/shard_map/ppermute | solution.py:26
  124.5 20.1 %collective-permute-start.29 = (bf16[384,512]{1,0:T(8,128)(2,1)S(1)}, bf16[384,512]{1,0:T(8,128)(2,1)S(1)}, u32[]{:S(2)}, u32[]{:S(2)}) collective-permute-start(bf16[384,512]{1,0:T(8,128)(2,1)S(1)} %add_convert_fusion.2), channel_id=1, source_target_pairs={{0,1},{1,0},{2,3},{3,2},{4,5},{5,4},{6,7},{7,6},{8,9},{9,8},{10,11... | collective-permute-start | bytes 1179656 | tf_op jit(solution)/shard_map/ppermute | solution.py:26
  124.8 25.9 %collective-permute-start.32 = (bf16[1,256,1024]{2,1,0:T(8,128)(2,1)S(1)}, bf16[1,256,1024]{2,1,0:T(8,128)(2,1)S(1)}, u32[]{:S(2)}, u32[]{:S(2)}) collective-permute-start(bf16[1,256,1024]{2,1,0:T(8,128)(2,1)S(1)} %get-tuple-element.89), channel_id=1, source_target_pairs={{0,16},{8,24},{16,0},{24,8},{1,17},{9,25},{17,1},{25,9},{2,18},{10... | collective-permute-start | bytes 1572872 | tf_op jit(solution)/shard_map/ppermute | solution.py:26
  126.1 23.1 %collective-permute-start.27 = (bf16[256,512]{1,0:T(8,128)(2,1)S(1)}, bf16[256,512]{1,0:T(8,128)(2,1)S(1)}, u32[]{:S(2)}, u32[]{:S(2)}) collective-permute-start(bf16[256,512]{1,0:T(8,128)(2,1)S(1)} %get-tuple-element.82), channel_id=1, source_target_pairs={{6,0},{3,1},{0,2},{5,3},{2,4},{7,5},{4,6},{1,7},{14,8},{11,9},{8,1... | collective-permute-start | bytes 786440 | tf_op jit(solution)/shard_map/ppermute | solution.py:31
  (7 other events, 66.8 us)

commit v6 on v5

v6 whole, which is shorter than its diff:
```python
import math

import jax
import jax.numpy as jnp
from jax import lax
from jax.experimental import pallas as pl
from jax.experimental.pallas import tpu as pltpu
from jax.sharding import PartitionSpec as P


ROUNDS = 2
NS_STEPS = 3
LEAD, LINEAR, QUADRATIC = 3.4445, -4.775, 2.0315
F32 = jnp.float32
BF16 = jnp.bfloat16
VMEM = pl.BlockSpec(memory_space=pltpu.VMEM)
SMEM = pl.BlockSpec(memory_space=pltpu.SMEM)
ANY = pl.BlockSpec(memory_space=pl.ANY)


def limit(mebibytes):
    return pltpu.CompilerParams(vmem_limit_bytes=mebibytes << 20)


def swapped(block, axis, bit):
    return lax.ppermute(block, axis, [(i, i ^ bit) for i in range(lax.axis_size(axis))])


def crossed(block, axis, way):
    count = lax.axis_size(axis)
    return lax.ppermute(
        block, axis, [((i + (-way if i % 2 else way)) % count, i) for i in range(count)]
    )


def dot(a, b):
    return jnp.dot(a, b, preferred_element_type=F32)


def dot_first(a, b):
    return lax.dot_general(a, b, (((0,), (0,)), ((), ())), preferred_element_type=F32)


def dot_last(a, b):
    return lax.dot_general(a, b, (((1,), (1,)), ((), ())), preferred_element_type=F32)


def joined(top, corner):
    edge = top.shape[0]
    below = jnp.concatenate([top[:, edge:].T, corner], axis=1)
    return jnp.concatenate([top, below], axis=0)


def product(left, right):
    edge = left.shape[0] // 2
    return dot(left[:edge], right), dot(left[edge:], right[:, edge:])


def low(pair):
    return tuple(item.astype(BF16) for item in pair)


def mix(*terms):
    return tuple(
        sum(factor * pair[i].astype(F32) for factor, pair in terms) for i in range(2)
    )


def factors(gram):
    rest, lead = None, 1.0
    for sweep in range(NS_STEPS):
        whole = joined(*gram)
        polynom_wide = mix((LINEAR, gram), (QUADRATIC, product(whole, whole)))
        polynom = joined(*low(polynom_wide))
        if sweep == 0:
            rest = polynom_wide
        else:
            rest = mix(
                (lead, polynom_wide), (LEAD, rest), (1.0, product(joined(*low(rest)), polynom))
            )
        lead = lead * LEAD
        if sweep < NS_STEPS - 1:
            half = low(mix((LEAD, gram), (1.0, product(whole, polynom))))
            gram = low(mix((LEAD, half), (1.0, product(joined(*half), polynom))))
    return joined(*low(rest))


def take(refs, start, stop, columns=slice(None)):
    parts, offset = [], 0
    for ref in refs:
        begin, end = max(start, offset), min(stop, offset + ref.shape[0])
        if begin < end:
            parts.append(ref[begin - offset : end - offset, columns])
        offset += ref.shape[0]
    return parts[0] if len(parts) == 1 else jnp.concatenate(parts, axis=0)


def put(refs, start, value):
    offset, stop = 0, start + value.shape[0]
    for ref in refs:
        begin, end = max(start, offset), min(stop, offset + ref.shape[0])
        if begin < end:
            ref[begin - offset : end - offset, :] = value[begin - start : end - start, :]
        offset += ref.shape[0]


def mixed(parts, start, stop):
    stepped, first, second, near = (take(refs, start, stop) for refs in parts)
    total = first.astype(F32) + second.astype(F32) + near.astype(F32)
    return 0.4 * stepped + 0.15 * total


def split(depth):
    half, unit = depth // 2, depth // 16
    return (half, half - 2 * unit, 2 * unit), (12 * unit, 4 * unit)


def sizes_of(arrays):
    return [len(item) for item in arrays]


def grouped(names, sizes):
    return [[next(names) for _ in range(size)] for size in sizes]


def ahead_kernel(sizes, refs):
    names = iter(refs)
    rows, parts = grouped(names, sizes[:1])[0], grouped(names, sizes[1:])
    if len(parts) == 1:
        value = parts[0][0][...]
    else:
        weight = next(names)
        value = mixed(parts, 0, weight.shape[0])
        weight[...] = value
    pre = next(names)
    shaped = value.astype(BF16)
    pre[...] = dot(take(rows, 0, pre.shape[0], slice(0, value.shape[0])), shaped)


def ahead_call(rows, parts, early):
    width = parts[0][0].shape[1]
    total = sum(item.shape[0] for item in rows)
    flat = [item for part in parts for item in part]
    shapes = [jax.ShapeDtypeStruct((total, width), F32)]
    if len(parts) > 1:
        shapes.insert(0, jax.ShapeDtypeStruct((early, width), F32))
    sizes = sizes_of([rows] + parts)
    return pl.pallas_call(
        lambda *refs: ahead_kernel(sizes, refs),
        out_shape=shapes,
        in_specs=[VMEM] * (len(rows) + len(flat)),
        out_specs=[VMEM] * len(shapes),
        compiler_params=limit(16),
        name="ahead",
    )(*rows, *flat)


def slope_rows(grads, place, value, slopes):
    width = slopes.shape[1]
    columns = slice(place, place + width)
    grad = take(grads, 0, slopes.shape[0], columns).astype(F32)
    slopes[...] = (grad * 2.0 * jnp.maximum(value, 0.0)).astype(BF16)


def weight_gradient(rows, slopes, span):
    return dot_first(take(rows, 0, slopes.shape[0], span), slopes[...])


def tiles(depth):
    tile = min(256, depth)
    return [slice(start, start + tile) for start in range(0, depth, tile)]


def part_kernel(sizes, refs):
    names = iter(refs)
    weight, moment = next(names), next(names)
    rows, grads = grouped(names, sizes)
    partial, slopes = names
    depth = moment.shape[0]
    factor = 1.0 / math.sqrt(depth)
    value = dot(take(rows, 0, slopes.shape[0]), weight[...].astype(BF16)) * factor
    slope_rows(grads, 0, value, slopes)
    for span in tiles(depth):
        partial[span, :] = 0.9 * moment[span, :] + weight_gradient(rows, slopes, span) * factor


def part_call(rows, grads, weight, moment):
    depth, width = moment.shape
    total = sum(item.shape[0] for item in rows)
    sizes = sizes_of([rows, grads])
    return pl.pallas_call(
        lambda *refs: part_kernel(sizes, refs),
        out_shape=[
            jax.ShapeDtypeStruct((depth, width), F32),
            jax.ShapeDtypeStruct((total, width), BF16),
        ],
        in_specs=[VMEM] * (2 + sum(sizes)),
        out_specs=[VMEM] * 2,
        compiler_params=limit(16),
        name="part_rows",
    )(weight, moment, *rows, *grads)


def round_kernel(sizes, place, decay, refs):
    names = iter(refs)
    pre, moment = next(names), next(names)
    rows, grads, weights, *parts = grouped(names, sizes)
    moment_out, slopes, moment_low, rest_out, scale_out, stepped, share = (
        next(names) for _ in range(7)
    )
    depth, width = moment.shape
    half, early = split(depth)[0][0], split(depth)[1][0]
    factor = 1.0 / math.sqrt(depth)
    if parts:
        late = next(names)
        value = mixed(parts, early, depth)
        late[...] = value
        shaped = value.astype(BF16)

    value = pre[...]
    if parts:
        value = value + dot(take(rows, 0, pre.shape[0], slice(early, depth)), shaped)
    slope_rows(grads, place, value * factor, slopes)
    total = jnp.zeros((1, width), F32)
    for span in tiles(depth):
        value = weight_gradient(rows, slopes, span) * factor
        value = (moment[span, :] if decay == 1.0 else decay * moment[span, :]) + value
        moment_out[span, :] = value
        moment_low[span, :] = value.astype(BF16)
        total = total + jnp.sum(value * value, axis=0, keepdims=True)
    scale = 1.0 / (jnp.sqrt(jnp.sum(total)) + 1e-07)
    scale_out[0] = scale
    edge = width // 2
    top = dot_first(moment_low[:, :edge], moment_low[...]) * (scale * scale)
    corner = dot_first(moment_low[:, edge:], moment_low[:, edge:]) * (scale * scale)
    rest = factors(low((top, corner)))
    rest_out[...] = rest
    step_rows(tiles(half), weights, moment_low, rest, scale, [stepped], [[share]], 0)


def step_rows(spans, weights, moment_low, rest, scale, stepped, shares, base):
    step_size = 0.1 * math.sqrt(moment_low.shape[0])
    for span in spans:
        low = moment_low[span, :]
        orthog = scale * (LEAD**NS_STEPS * low.astype(F32) + dot(low, rest))
        value = take(weights, span.start, span.stop) - step_size * orthog
        put(stepped, span.start - base, value)
        for refs in shares:
            put(refs, span.start - base, value.astype(BF16))


def round_call(rows, grads, place, decay, pre, weights, moment, parts):
    depth, width = moment.shape
    total = sum(item.shape[0] for item in rows)
    half, late = split(depth)[0][0], split(depth)[1][1]
    shape = jax.ShapeDtypeStruct
    flat = [item for part in parts for item in part]
    sizes = sizes_of([rows, grads, weights] + parts)
    out = [
        shape((depth, width), F32),
        shape((total, width), BF16),
        shape((depth, width), BF16),
        shape((width, width), BF16),
        shape((1,), F32),
        shape((half, width), F32),
        shape((half, width), BF16),
    ]
    specs = [VMEM] * 4 + [SMEM] + [VMEM] * 2
    if parts:
        out.append(shape((late, width), F32))
        specs.append(VMEM)
    return pl.pallas_call(
        lambda *refs: round_kernel(sizes, place, decay, refs),
        out_shape=out,
        in_specs=[VMEM] * (2 + sum(sizes)),
        out_specs=specs,
        compiler_params=limit(16),
        name="muon_round",
    )(pre, moment, *rows, *grads, *weights, *flat)


def second_kernel(count, refs):
    moment_low, rest, scale, share, *names = refs
    weights, names = names[:count], iter(names[count:])
    stepped, *rest_out = names
    ones, twos = rest_out[:2], rest_out[2:]
    depth = moment_low.shape[0]
    half = share.shape[0]
    put(twos, 0, share[...])
    spans = [span for span in tiles(depth) if span.start >= half]
    step_rows(spans, weights, moment_low, rest[...], scale[0], [stepped], [ones], half)
    put(twos, half, take(ones, 0, depth - half))


def second_call(moment_low, rest, scale, share, weights):
    depth, width = moment_low.shape
    one, two = split(depth)
    shape = jax.ShapeDtypeStruct
    out = [shape((depth - one[0], width), F32)]
    out = out + [shape((size, width), BF16) for size in one[1:] + two]
    result = pl.pallas_call(
        lambda *refs: second_kernel(len(weights), refs),
        out_shape=out,
        in_specs=[VMEM] * 2 + [SMEM] + [VMEM] * (1 + len(weights)),
        out_specs=[VMEM] * len(out),
        compiler_params=limit(12),
        name="second_half",
    )(moment_low, rest, scale, share, *weights)
    return result[0], [share, *result[1:3]], result[3:]


def picked(route, experts):
    count = route.shape[1]
    slots = count // 2
    lines = -(-experts // 8) * 8
    labels = lax.broadcasted_iota(jnp.int32, (lines, count), 0)
    keep = (route == labels).astype(F32)
    before = lax.broadcasted_iota(jnp.int32, (count, count), 0)
    after = lax.broadcasted_iota(jnp.int32, (count, count), 1)
    rank = dot(keep.astype(BF16), (before <= after).astype(BF16)) * keep
    slot = (lax.broadcasted_iota(jnp.int32, (slots, count), 0) + 1).astype(F32)
    return jnp.concatenate([slot == rank[m : m + 1, :] for m in range(experts)]).astype(BF16)


def squeeze_kernel(index, experts, fresh, count, refs):
    first, *refs = refs
    sources, outs = refs[:count], refs[count:]
    if fresh:
        picks, *outs = outs
        hot = picked(first[index : index + 1, :], experts)
        picks[...] = hot
    else:
        hot = first[...]
    slots = hot.shape[0] // experts
    place = 0
    for source in sources:
        value = dot(hot, source[0]).astype(BF16)
        for m, out in enumerate(outs):
            out[:, place : place + value.shape[1]] = value[m * slots : (m + 1) * slots, :]
        place += value.shape[1]


def squeeze_call(index, first, sources, experts, fresh):
    count = sources[0].shape[1]
    slots = count // 2
    width = sum(item.shape[2] for item in sources)
    shape = jax.ShapeDtypeStruct
    outs = [shape((slots, width), BF16)] * experts
    if fresh:
        outs.insert(0, shape((experts * slots, count), BF16))

    def whole(item):
        return pl.BlockSpec(item.shape, lambda i: (0, 0))

    return pl.pallas_call(
        lambda *refs: squeeze_kernel(index, experts, fresh, len(sources), refs),
        grid=(1,),
        out_shape=outs,
        in_specs=[whole(first)]
        + [pl.BlockSpec((1,) + item.shape[1:], lambda i: (index, 0, 0)) for item in sources],
        out_specs=[whole(item) for item in outs],
        compiler_params=limit(16),
        name="squeeze",
    )(first, *sources)


def backward_kernel(sizes, where, refs):
    names = iter(refs)
    slopes, weights = grouped(names, sizes)
    outs = list(names)
    count, depth = outs[0].shape
    factor = 1.0 / math.sqrt(depth)
    shaped = take(weights, 0, depth).astype(BF16)
    for out, (array, place) in zip(outs, where):
        part = slopes[array][place * count : (place + 1) * count, :]
        out[...] = (dot_last(part, shaped) * factor).astype(BF16)


def backward_call(slopes, weights, where, count):
    depth = sum(item.shape[0] for item in weights)
    sizes = sizes_of([slopes, weights])
    return pl.pallas_call(
        lambda *refs: backward_kernel(sizes, where, refs),
        out_shape=[jax.ShapeDtypeStruct((count, depth), BF16)] * len(where),
        in_specs=[VMEM] * sum(sizes),
        out_specs=[VMEM] * len(where),
        compiler_params=limit(16),
        name="row_gradients",
    )(*slopes, *weights)


def average_call(parts, start, stop, depth, buffer):
    flat = [item for part in parts for item in part]
    sizes = sizes_of(parts)
    extra = [] if buffer is None else [buffer]
    width = flat[0].shape[1]

    def kernel(*refs):
        names = iter(refs)
        groups = grouped(names, sizes)
        out, value, sem = list(names)[len(extra) :]
        value[...] = mixed(groups, start, stop)
        made = pltpu.make_async_copy(value, out.at[pl.ds(start, stop - start), :], sem)
        made.start()
        made.wait()

    return pl.pallas_call(
        kernel,
        out_shape=jax.ShapeDtypeStruct((depth, width), F32),
        in_specs=[VMEM] * len(flat) + [ANY] * len(extra),
        out_specs=ANY,
        scratch_shapes=[pltpu.VMEM((stop - start, width), F32), pltpu.SemaphoreType.DMA(())],
        input_output_aliases={len(flat): 0} if extra else {},
        compiler_params=limit(12),
        name="average",
    )(*flat, *extra)


def finish_call(index, picks, backs, buffer):
    count, depth = picks.shape[1], backs[0].shape[1]
    extra = [] if buffer is None else [buffer]

    def kernel(*refs):
        rows = take(refs[1 : 1 + len(backs)], 0, refs[0].shape[0])
        refs[-1][0] = dot_first(refs[0][...], rows).astype(BF16)

    def whole(item):
        return pl.BlockSpec(item.shape, lambda i: (0, 0))

    return pl.pallas_call(
        kernel,
        grid=(1,),
        out_shape=jax.ShapeDtypeStruct((ROUNDS, count, depth), BF16),
        in_specs=[whole(item) for item in (picks, *backs)] + [ANY] * len(extra),
        out_specs=pl.BlockSpec((1, count, depth), lambda i: (index, 0, 0)),
        input_output_aliases={1 + len(backs): 0} if extra else {},
        compiler_params=limit(12),
        name="finish",
    )(picks, *backs, *extra)


def on_device(tokens, routing, out_grad, weights, momentum):
    experts = lax.axis_size("expert")
    weight = weights[0, 0]
    moment = momentum[0, 0]
    depth = weight.shape[0]
    _, two = split(depth)
    slots = tokens.shape[1] // 2
    route = routing ^ lax.axis_index("expert").astype(jnp.int32)

    def exchanged(items):
        got = [items[0]]
        for m in range(1, experts):
            got.append(swapped(items[m], "expert", m))
        return got

    in_grad = None
    waiting = []
    picks, *items = squeeze_call(0, route, [tokens], experts, True)
    all_picks = [picks]
    rows = exchanged(items)
    items = squeeze_call(0, picks, [out_grad], experts, False)
    grads = exchanged(items)
    picks, *items = squeeze_call(1, route, [tokens, out_grad], experts, True)
    all_picks.append(picks)
    later = exchanged(items)
    moment, slopes = part_call(rows[:2], grads[:2], weight, moment)
    all_slopes = [slopes]
    (pre,) = ahead_call(rows[2:], [[weight]], depth)
    where = [
        [(m // 2, m) if m < 2 else (1, m - 2) for m in range(experts)],
        [(0, m) for m in range(experts)],
    ]
    weights = [weight]
    parts = []
    for index in range(ROUNDS):
        if index:
            moment, slopes, low, rest, scale, stepped, share, late = round_call(
                later, later, depth, 0.9, pre, weights, moment, parts
            )
            weights = [*weights, late]
            all_slopes = [slopes]
        else:
            moment, slopes, low, rest, scale, stepped, share = round_call(
                rows[2:], grads[2:], 0, 1.0, pre, weights, moment, parts
            )
            all_slopes.append(slopes)
        stepped_low, ones, twos = second_call(low, rest, scale, share, weights)
        firsts = []
        for item in ones:
            firsts.append(crossed(item, "node", 2))
        seconds = []
        for item in twos:
            seconds.append(crossed(item, "node", -2))
        nears = []
        got = [firsts[0], jnp.concatenate(firsts[1:])]
        for piece, item in enumerate((share, jnp.concatenate(ones[1:]))):
            pair = (item.astype(F32) + got[piece].astype(F32)).astype(BF16)
            nears.append(swapped(pair, "node", 1))
        far = backward_call(all_slopes, weights, where[index][2:], slots)
        near = backward_call(all_slopes, weights, where[index][:2], slots)
        waiting.append(exchanged([*near, *far]))
        halves = [stepped, stepped_low]
        parts = [halves, firsts, seconds, nears]
        early_parts = [halves, firsts[:2], seconds[:1], nears[:2]]
        if index < ROUNDS - 1:
            upper, pre = ahead_call(later, early_parts, two[0])
            weights = [upper]
        else:
            for done, backs in enumerate(waiting):
                in_grad = finish_call(done, all_picks[done], backs, in_grad)
            weight = average_call(early_parts, 0, two[0], depth, None)
            weight = average_call(parts, two[0], depth, depth, weight)
    return (weight[None, None], moment[None, None], in_grad)


def solution(mesh):
    return jax.shard_map(
        on_device,
        mesh=mesh,
        in_specs=(
            P(None, ("expert", "node"), None),
            P(None, ("expert", "node")),
            P(None, ("expert", "node"), None),
            P("node", "expert", None, None),
            P("node", "expert", None, None),
        ),
        out_specs=(
            P("node", "expert", None, None),
            P("node", "expert", None, None),
            P(None, ("expert", "node"), None),
        ),
        check_vma=False,
    )
```

time: 153 us -> 144 us (0.941)
  starting transfers between devices: 33 us -> 28.2 us
  Pallas kernels: 26.9 us -> 23.2 us
  waiting for transfers between devices: 84.7 us -> 82.9 us
    ppermute x25 -> x19, waiting for transfers between devices: 50.5 us -> 42.1 us  [swapped(): lax.ppermute(block, axis, [(i, i ^ bit) for i in range(lax.axis_size(axis...]
    ppermute x10, waiting for transfers between devices: 34.2 us -> 40.8 us  [crossed(): lax.ppermute(block, axis, [((i + (-way if i % 2 else way)) % count, i) fo...]
    unnamed x8 -> x14, local copies, waits for them, and re-layouts: 0.02 us -> 6.58 us
    ppermute x25 -> x19, starting transfers between devices: 21.6 us -> 16.2 us  [swapped(): lax.ppermute(block, axis, [(i, i ^ bit) for i in range(lax.axis_size(axis...]
    squeeze x4 -> x0, local copies, waits for them, and re-layouts: 4.5 us -> none  [the longest x1 1.82 us: on_device(): rest_tokens[0, lead:]]
    pallas_call x9 -> x8, Pallas kernels: 15.7 us -> 13.6 us  [the longest x2 8.6 us: round_call(): pl.pallas_call(lambda *refs: round_kernel(sizes, place, decay, refs), out...]
    pallas_call x2 -> x4, Pallas kernels: 3.53 us -> 3.29 us  [backward_call(): pl.pallas_call(lambda *refs: backward_kernel(sizes, where, refs), out_sha...]
  transfers between devices with their start and end apart: 35 -> 29, of which waited for: 11 -> 11; matrix products, arithmetic and copies ran while one was open for 4% -> 0% of each run, Pallas kernels for 17% -> 9%
where the time goes in v6:
time: 144 us; the launch traced here: 143 us
  waiting for transfers between devices  82.9 us (58%)
  starting transfers between devices  28.2 us (20%)
  Pallas kernels  23.2 us (16%)
  local copies, waits for them, and re-layouts  6.58 us (5%)
    ppermute x19, waiting for transfers between devices, swapped(): lax.ppermute(block, axis, [(i, i ^ bit) for i in range(lax.axis_size(axis...  42.1 us
    ppermute x10, waiting for transfers between devices, crossed(): lax.ppermute(block, axis, [((i + (-way if i % 2 else way)) % count, i) fo...  40.8 us
    ppermute x19, starting transfers between devices, swapped(): lax.ppermute(block, axis, [(i, i ^ bit) for i in range(lax.axis_size(axis...  16.2 us
    ppermute x10, starting transfers between devices, crossed(): lax.ppermute(block, axis, [((i + (-way if i % 2 else way)) % count, i) fo...  12.1 us
    pallas_call x2, Pallas kernels, round_call(): pl.pallas_call(lambda *refs: round_kernel(sizes, place, decay, refs), out...  8.6 us
    unnamed x14, local copies, waits for them, and re-layouts  6.58 us
    pallas_call x4, Pallas kernels, backward_call(): pl.pallas_call(lambda *refs: backward_kernel(sizes, where, refs), out_sha...  3.29 us
  transfers between devices with their start and end apart: 29, of which 11 were waited for; matrix products, arithmetic and copies ran while one was open for 0% of the time, Pallas kernels for 9%

profile of v6, /device:TPU:0, one launch (start us, length us, event | category | flops | bytes accessed | tf_op | source)
XLA Modules:
  0.0 143.2 jit_solution(12347924233636992849)
XLA Ops:
  1.3 1.2 copy-done.2
  3.1 3.0 %collective-permute-start.3 = (bf16[128,1024]{1,0:T(8,128)(2,1)S(1)}, bf16[128,1024]{1,0:T(8,128)(2,1)S(1)}, u32[]{:S(2)}, u32[]{:S(2)}) collective-permute-start(bf16[128,1024]{1,0:T(8,128)(2,1)S(1)} %get-tuple-element.58), channel_id=1, source_target_pairs={{0,16},{8,24},{16,0},{24,8},{1,17},{9,25},{17,1},{25,9},{2,18},{10... | collective-permute-start | bytes 786440 | tf_op jit(solution)/shard_map/ppermute | solution.py:26
  8.1 1.7 %collective-permute-start.7 = (bf16[128,512]{1,0:T(8,128)(2,1)S(1)}, bf16[128,512]{1,0:T(8,128)(2,1)S(1)}, u32[]{:S(2)}, u32[]{:S(2)}) collective-permute-start(bf16[128,512]{1,0:T(8,128)(2,1)S(1)} %get-tuple-element.66), channel_id=1, source_target_pairs={{0,16},{8,24},{16,0},{24,8},{1,17},{9,25},{17,1},{25,9},{2,18},{10... | collective-permute-start | bytes 393224 | tf_op jit(solution)/shard_map/ppermute | solution.py:26
  9.8 3.5 %collective-permute-done.3.refs_0_.refs_2_ = bf16[128,1024]{1,0:T(8,128)(2,1)S(1)} collective-permute-done((bf16[128,1024]{1,0:T(8,128)(2,1)S(1)}, bf16[128,1024]{1,0:T(8,128)(2,1)S(1)}, u32[]{:S(2)}, u32[]{:S(2)}) %collective-permute-start.3) | collective-permute-done | bytes 262176 | tf_op jit(solution)/shard_map/ppermute | solution.py:26
  13.3 5.2 %collective-permute-done.4.refs_1_.refs_3_ = bf16[128,1024]{1,0:T(8,128)(2,1)S(1)} collective-permute-done((bf16[128,1024]{1,0:T(8,128)(2,1)S(1)}, bf16[128,1024]{1,0:T(8,128)(2,1)S(1)}, u32[]{:S(2)}, u32[]{:S(2)}) %collective-permute-start.4) | collective-permute-done | bytes 262176 | tf_op jit(solution)/shard_map/ppermute | solution.py:26
  18.5 1.6 %copy-done = f32[1,1,1024,512]{3,2,1,0:T(8,128)S(1)} copy-done((f32[1,1,1024,512]{3,2,1,0:T(8,128)S(1)}, f32[1,1,1024,512]{3,2,1,0:T(8,128)}, u32[]{:S(2)}) %copy-start) | copy-done | bytes 2097176
  20.5 1.1 copy-done.1
  21.7 1.6 %copy-done.4 = f32[1,1,1024,512]{3,2,1,0:T(8,128)S(1)} copy-done((f32[1,1,1024,512]{3,2,1,0:T(8,128)S(1)}, f32[1,1,1024,512]{3,2,1,0:T(8,128)}, u32[]{:S(2)}) %copy-start.4) | copy-done | bytes 2097176
  24.2 4.1 %muon_round.2 = (f32[1024,512]{1,0:T(8,128)S(1)}, bf16[256,512]{1,0:T(8,128)(2,1)S(1)}, bf16[1024,512]{1,0:T(8,128)(2,1)S(1)}, bf16[512,512]{1,0:T(8,128)(2,1)S(...) custom-call(f32[256,512]{1,0:T(8,128)S(1)} %ahead.2.refs_0_, ...), custom_call_target="tpu_custom_call" | custom-call | tf_op jit(solution)/shard_map/muon_round/pallas_call | solution.py:272
  28.2 3.6 %collective-permute-start.9 = (bf16[512,512]{1,0:T(8,128)(2,1)S(1)}, bf16[512,512]{1,0:T(8,128)(2,1)S(1)}, u32[]{:S(2)}, u32[]{:S(2)}) collective-permute-start(bf16[512,512]{1,0:T(8,128)(2,1)S(1)} %get-tuple-element.72.refs_3_), channel_id=1, source_target_pairs={{2,0},{7,1},{4,2},{1,3},{6,4},{3,5},{0,6},{5,7},{10,8},{15,9},{12,... | collective-permute-start | bytes 1572872 | tf_op jit(solution)/shard_map/ppermute | solution.py:31
  31.9 1.3 second_half.2
  35.0 1.5 %collective-permute-start.1 = (bf16[128,1536]{1,0:T(8,128)(2,1)S(1)}, bf16[128,1536]{1,0:T(8,128)(2,1)S(1)}, u32[]{:S(2)}, u32[]{:S(2)}) collective-permute-start(bf16[128,1536]{1,0:T(8,128)(2,1)S(1)} %get-tuple-element.56), channel_id=1, source_target_pairs={{0,16},{8,24},{16,0},{24,8},{1,17},{9,25},{17,1},{25,9},{2,18},{10... | collective-permute-start | bytes 1179656 | tf_op jit(solution)/shard_map/ppermute | solution.py:26
  36.5 18.8 %collective-permute-done.13.refs_15_ = bf16[128,512]{1,0:T(8,128)(2,1)S(1)} collective-permute-done((bf16[128,512]{1,0:T(8,128)(2,1)S(1)}, bf16[128,512]{1,0:T(8,128)(2,1)S(1)}, u32[]{:S(2)}, u32[]{:S(2)}) %collective-permute-start.13) | collective-permute-done | bytes 131104 | tf_op jit(solution)/shard_map/ppermute | solution.py:31
  55.9 3.6 %collective-permute-start.14 = (bf16[512,512]{1,0:T(8,128)(2,1)S(1)}, bf16[512,512]{1,0:T(8,128)(2,1)S(1)}, u32[]{:S(2)}, u32[]{:S(2)}) collective-permute-start(bf16[512,512]{1,0:T(8,128)(2,1)S(1)} %add_convert_fusion.2), channel_id=1, source_target_pairs={{0,1},{1,0},{2,3},{3,2},{4,5},{5,4},{6,7},{7,6},{8,9},{9,8},{10,11... | collective-permute-start | bytes 1572872 | tf_op jit(solution)/shard_map/ppermute | solution.py:26
  60.4 10.5 %collective-permute-done.2.refs_3_.refs_5_.refs_9_ = bf16[128,1536]{1,0:T(8,128)(2,1)S(1)} collective-permute-done((bf16[128,1536]{1,0:T(8,128)(2,1)S(1)}, bf16[128,1536]{1,0:T(8,128)(2,1)S(1)}, u32[]{:S(2)}, u32[]{:S(2)}) %collective-permute-start.2) | collective-permute-done | bytes 393248 | tf_op jit(solution)/shard_map/ppermute | solution.py:26
  70.8 7.2 %collective-permute-done.11.refs_8_.refs_16_ = bf16[768,512]{1,0:T(8,128)(2,1)S(1)} collective-permute-done((bf16[768,512]{1,0:T(8,128)(2,1)S(1)}, bf16[768,512]{1,0:T(8,128)(2,1)S(1)}, u32[]{:S(2)}, u32[]{:S(2)}) %collective-permute-start.11) | collective-permute-done | bytes 786464 | tf_op jit(solution)/shard_map/ppermute | solution.py:31
  78.0 4.5 %collective-permute-done.12.refs_9_.refs_18_ = bf16[512,512]{1,0:T(8,128)(2,1)S(1)} collective-permute-done((bf16[512,512]{1,0:T(8,128)(2,1)S(1)}, bf16[512,512]{1,0:T(8,128)(2,1)S(1)}, u32[]{:S(2)}, u32[]{:S(2)}) %collective-permute-start.12) | collective-permute-done | bytes 524320 | tf_op jit(solution)/shard_map/ppermute | solution.py:26
  83.3 4.5 %muon_round.3 = (f32[1024,512]{1,0:T(8,128)}, bf16[512,512]{1,0:T(8,128)(2,1)S(1)}, bf16[1024,512]{1,0:T(8,128)(2,1)S(1)}, bf16[512,512]{1,0:T(8,128)(2,1)S(1)},...) custom-call(f32[512,512]{1,0:T(8,128)S(1)} %get-tuple-element.77.refs_0_, ...), custom_call_target="tpu_custom_call" | custom-call | tf_op jit(solution)/shard_map/muon_round/pallas_call | solution.py:272
  87.9 2.4 %collective-permute-start.16 = (bf16[512,512]{1,0:T(8,128)(2,1)S(1)}, bf16[512,512]{1,0:T(8,128)(2,1)S(1)}, u32[]{:S(2)}, u32[]{:S(2)}) collective-permute-start(bf16[512,512]{1,0:T(8,128)(2,1)S(1)} %get-tuple-element.85.refs_3_), channel_id=1, source_target_pairs={{2,0},{7,1},{4,2},{1,3},{6,4},{3,5},{0,6},{5,7},{10,8},{15,9},{12,... | collective-permute-start | bytes 1572872 | tf_op jit(solution)/shard_map/ppermute | solution.py:31
  90.2 1.2 second_half.3
  91.4 1.8 %collective-permute-start.17 = (bf16[384,512]{1,0:T(8,128)(2,1)S(1)}, bf16[384,512]{1,0:T(8,128)(2,1)S(1)}, u32[]{:S(2)}, u32[]{:S(2)}) collective-permute-start(bf16[384,512]{1,0:T(8,128)(2,1)S(1)} %get-tuple-element.88), channel_id=1, source_target_pairs={{2,0},{7,1},{4,2},{1,3},{6,4},{3,5},{0,6},{5,7},{10,8},{15,9},{12,... | collective-permute-start | bytes 1179656 | tf_op jit(solution)/shard_map/ppermute | solution.py:31
  97.3 14.8 %collective-permute-done.18.refs_4_ = bf16[128,512]{1,0:T(8,128)(2,1)S(1)} collective-permute-done((bf16[128,512]{1,0:T(8,128)(2,1)S(1)}, bf16[128,512]{1,0:T(8,128)(2,1)S(1)}, u32[]{:S(2)}, u32[]{:S(2)}) %collective-permute-start.18) | collective-permute-done | bytes 131104 | tf_op jit(solution)/shard_map/ppermute | solution.py:31
  112.1 1.1 collective-permute-start.19
  113.4 1.1 collective-permute-start.23
  114.6 2.5 %collective-permute-start.22 = (bf16[512,512]{1,0:T(8,128)(2,1)S(1)}, bf16[512,512]{1,0:T(8,128)(2,1)S(1)}, u32[]{:S(2)}, u32[]{:S(2)}) collective-permute-start(bf16[512,512]{1,0:T(8,128)(2,1)S(1)} %add_convert_fusion), channel_id=1, source_target_pairs={{0,1},{1,0},{2,3},{3,2},{4,5},{5,4},{6,7},{7,6},{8,9},{9,8},{10,11... | collective-permute-start | bytes 1572872 | tf_op jit(solution)/shard_map/ppermute | solution.py:26
  117.2 3.3 %collective-permute-done.28.refs_4_ = bf16[128,1024]{1,0:T(8,128)(2,1)S(1)} collective-permute-done((bf16[128,1024]{1,0:T(8,128)(2,1)S(1)}, bf16[128,1024]{1,0:T(8,128)(2,1)S(1)}, u32[]{:S(2)}, u32[]{:S(2)}) %collective-permute-start.28) | collective-permute-done | bytes 262176 | tf_op jit(solution)/shard_map/ppermute | solution.py:26
  121.7 8.0 %collective-permute-done.24.refs_3_ = bf16[128,1024]{1,0:T(8,128)(2,1)S(1)} collective-permute-done((bf16[128,1024]{1,0:T(8,128)(2,1)S(1)}, bf16[128,1024]{1,0:T(8,128)(2,1)S(1)}, u32[]{:S(2)}, u32[]{:S(2)}) %collective-permute-start.24) | collective-permute-done | bytes 262176 | tf_op jit(solution)/shard_map/ppermute | solution.py:26
  129.6 1.1 collective-permute-start.20
  130.8 1.3 finish.2.refs_5_
  133.0 1.3 finish.3
  134.3 6.2 %collective-permute-done.21.refs_5_.refs_7_ = bf16[512,512]{1,0:T(8,128)(2,1)S(1)} collective-permute-done((bf16[512,512]{1,0:T(8,128)(2,1)S(1)}, bf16[512,512]{1,0:T(8,128)(2,1)S(1)}, u32[]{:S(2)}, u32[]{:S(2)}) %collective-permute-start.21) | collective-permute-done | bytes 524320 | tf_op jit(solution)/shard_map/ppermute | solution.py:26
  140.5 1.6 %average.2.refs_9_ = f32[1024,512]{1,0:T(8,128)} custom-call(f32[512,512]{1,0:T(8,128)S(1)} %get-tuple-element.81.refs_0_, f32[512,512]{1,0:T(8,128)S(1)} %get-tuple-element.87.refs_1_, bf16[512,512]{1,0:T(8,128)(2,1)S(1)} %collective-permute-done.16.refs_2_, bf16[384,512]{1,0:T(8,128)(2,1)S(1)} %collective-permute-done.17.refs_3_, ...), custom_call_target="tpu_custom_call" | custom-call | tf_op jit(solution)/shard_map/average/pallas_call | solution.py:407
  (63 shorter events, 16.1 us)
Async XLA Ops:
  3.1 10.2 %collective-permute-start.3 = (bf16[128,1024]{1,0:T(8,128)(2,1)S(1)}, bf16[128,1024]{1,0:T(8,128)(2,1)S(1)}, u32[]{:S(2)}, u32[]{:S(2)}) collective-permute-start(bf16[128,1024]{1,0:T(8,128)(2,1)S(1)} %get-tuple-element.58), channel_id=1, source_target_pairs={{0,16},{8,24},{16,0},{24,8},{1,17},{9,25},{17,1},{25,9},{2,18},{10... | collective-permute-start | bytes 786440 | tf_op jit(solution)/shard_map/ppermute | solution.py:26
  6.2 12.3 %collective-permute-start.4 = (bf16[128,1024]{1,0:T(8,128)(2,1)S(1)}, bf16[128,1024]{1,0:T(8,128)(2,1)S(1)}, u32[]{:S(2)}, u32[]{:S(2)}) collective-permute-start(bf16[128,1024]{1,0:T(8,128)(2,1)S(1)} %get-tuple-element.59), channel_id=1, source_target_pairs={{0,24},{8,16},{16,8},{24,0},{1,25},{9,17},{17,9},{25,1},{2,26},{10... | collective-permute-start | bytes 786440 | tf_op jit(solution)/shard_map/ppermute | solution.py:26
  6.2 14.4 %collective-permute-start.5 = (bf16[128,1024]{1,0:T(8,128)(2,1)S(1)}, bf16[128,1024]{1,0:T(8,128)(2,1)S(1)}, u32[]{:S(2)}, u32[]{:S(2)}) collective-permute-start(bf16[128,1024]{1,0:T(8,128)(2,1)S(1)} %get-tuple-element.61), channel_id=1, source_target_pairs={{0,8},{8,0},{16,24},{24,16},{1,9},{9,1},{17,25},{25,17},{2,10},{10... | collective-permute-start | bytes 786440 | tf_op jit(solution)/shard_map/ppermute | solution.py:26
  7.7 12.8 %collective-permute-start.6 = (bf16[128,512]{1,0:T(8,128)(2,1)S(1)}, bf16[128,512]{1,0:T(8,128)(2,1)S(1)}, u32[]{:S(2)}, u32[]{:S(2)}) collective-permute-start(bf16[128,512]{1,0:T(8,128)(2,1)S(1)} %get-tuple-element.64), channel_id=1, source_target_pairs={{0,8},{8,0},{16,24},{24,16},{1,9},{9,1},{17,25},{25,17},{2,10},{10... | collective-permute-start | bytes 393224 | tf_op jit(solution)/shard_map/ppermute | solution.py:26
  8.1 16.1 %collective-permute-start.7 = (bf16[128,512]{1,0:T(8,128)(2,1)S(1)}, bf16[128,512]{1,0:T(8,128)(2,1)S(1)}, u32[]{:S(2)}, u32[]{:S(2)}) collective-permute-start(bf16[128,512]{1,0:T(8,128)(2,1)S(1)} %get-tuple-element.66), channel_id=1, source_target_pairs={{0,16},{8,24},{16,0},{24,8},{1,17},{9,25},{17,1},{25,9},{2,18},{10... | collective-permute-start | bytes 393224 | tf_op jit(solution)/shard_map/ppermute | solution.py:26
  13.3 10.8 %collective-permute-start.8 = (bf16[128,512]{1,0:T(8,128)(2,1)S(1)}, bf16[128,512]{1,0:T(8,128)(2,1)S(1)}, u32[]{:S(2)}, u32[]{:S(2)}) collective-permute-start(bf16[128,512]{1,0:T(8,128)(2,1)S(1)} %get-tuple-element.67), channel_id=1, source_target_pairs={{0,24},{8,16},{16,8},{24,0},{1,25},{9,17},{17,9},{25,1},{2,26},{10... | collective-permute-start | bytes 393224 | tf_op jit(solution)/shard_map/ppermute | solution.py:26
  18.5 1.6 %copy-start = (f32[1,1,1024,512]{3,2,1,0:T(8,128)S(1)}, f32[1,1,1024,512]{3,2,1,0:T(8,128)}, u32[]{:S(2)}) copy-start(f32[1,1,1024,512]{3,2,1,0:T(8,128)} %param.8) | copy-start | bytes 6291460
  28.2 31.3 %collective-permute-start.9 = (bf16[512,512]{1,0:T(8,128)(2,1)S(1)}, bf16[512,512]{1,0:T(8,128)(2,1)S(1)}, u32[]{:S(2)}, u32[]{:S(2)}) collective-permute-start(bf16[512,512]{1,0:T(8,128)(2,1)S(1)} %get-tuple-element.72.refs_3_), channel_id=1, source_target_pairs={{2,0},{7,1},{4,2},{1,3},{6,4},{3,5},{0,6},{5,7},{10,8},{15,9},{12,... | collective-permute-start | bytes 1572872 | tf_op jit(solution)/shard_map/ppermute | solution.py:31
  31.9 2.3 %copy-start.3 = (bf16[2,256,1024]{2,1,0:T(8,128)(2,1)S(1)}, bf16[2,256,1024]{2,1,0:T(8,128)(2,1)}, u32[]{:S(2)}) copy-start(bf16[2,256,1024]{2,1,0:T(8,128)(2,1)} %refs_1_.4) | copy-start | bytes 3145732
  31.9 2.3 %copy-start.6 = (bf16[2,256,512]{2,1,0:T(8,128)(2,1)S(1)}, bf16[2,256,512]{2,1,0:T(8,128)(2,1)}, u32[]{:S(2)}) copy-start(bf16[2,256,512]{2,1,0:T(8,128)(2,1)} %refs_1_.5) | copy-start | bytes 1572868
  33.2 22.5 %collective-permute-start.10 = (bf16[384,512]{1,0:T(8,128)(2,1)S(1)}, bf16[384,512]{1,0:T(8,128)(2,1)S(1)}, u32[]{:S(2)}, u32[]{:S(2)}) collective-permute-start(bf16[384,512]{1,0:T(8,128)(2,1)S(1)} %get-tuple-element.74), channel_id=1, source_target_pairs={{2,0},{7,1},{4,2},{1,3},{6,4},{3,5},{0,6},{5,7},{10,8},{15,9},{12,... | collective-permute-start | bytes 1179656 | tf_op jit(solution)/shard_map/ppermute | solution.py:31
  33.7 21.6 %collective-permute-start.13 = (bf16[128,512]{1,0:T(8,128)(2,1)S(1)}, bf16[128,512]{1,0:T(8,128)(2,1)S(1)}, u32[]{:S(2)}, u32[]{:S(2)}) collective-permute-start(bf16[128,512]{1,0:T(8,128)(2,1)S(1)} %get-tuple-element.76), channel_id=1, source_target_pairs={{2,0},{7,1},{4,2},{1,3},{6,4},{3,5},{0,6},{5,7},{10,8},{15,9},{12,... | collective-permute-start | bytes 393224 | tf_op jit(solution)/shard_map/ppermute | solution.py:31
  34.9 24.8 %collective-permute-start = (bf16[128,1536]{1,0:T(8,128)(2,1)S(1)}, bf16[128,1536]{1,0:T(8,128)(2,1)S(1)}, u32[]{:S(2)}, u32[]{:S(2)}) collective-permute-start(bf16[128,1536]{1,0:T(8,128)(2,1)S(1)} %get-tuple-element.55), channel_id=1, source_target_pairs={{0,8},{8,0},{16,24},{24,16},{1,9},{9,1},{17,25},{25,17},{2,10},{10... | collective-permute-start | bytes 1179656 | tf_op jit(solution)/shard_map/ppermute | solution.py:26
  35.0 24.8 %collective-permute-start.1 = (bf16[128,1536]{1,0:T(8,128)(2,1)S(1)}, bf16[128,1536]{1,0:T(8,128)(2,1)S(1)}, u32[]{:S(2)}, u32[]{:S(2)}) collective-permute-start(bf16[128,1536]{1,0:T(8,128)(2,1)S(1)} %get-tuple-element.56), channel_id=1, source_target_pairs={{0,16},{8,24},{16,0},{24,8},{1,17},{9,25},{17,1},{25,9},{2,18},{10... | collective-permute-start | bytes 1179656 | tf_op jit(solution)/shard_map/ppermute | solution.py:26
  55.3 22.7 %collective-permute-start.11 = (bf16[768,512]{1,0:T(8,128)(2,1)S(1)}, bf16[768,512]{1,0:T(8,128)(2,1)S(1)}, u32[]{:S(2)}, u32[]{:S(2)}) collective-permute-start(bf16[768,512]{1,0:T(8,128)(2,1)S(1)} %get-tuple-element.75), channel_id=1, source_target_pairs={{6,0},{3,1},{0,2},{5,3},{2,4},{7,5},{4,6},{1,7},{14,8},{11,9},{8,1... | collective-permute-start | bytes 2359304 | tf_op jit(solution)/shard_map/ppermute | solution.py:31
  55.9 22.1 %collective-permute-start.14 = (bf16[512,512]{1,0:T(8,128)(2,1)S(1)}, bf16[512,512]{1,0:T(8,128)(2,1)S(1)}, u32[]{:S(2)}, u32[]{:S(2)}) collective-permute-start(bf16[512,512]{1,0:T(8,128)(2,1)S(1)} %add_convert_fusion.2), channel_id=1, source_target_pairs={{0,1},{1,0},{2,3},{3,2},{4,5},{5,4},{6,7},{7,6},{8,9},{9,8},{10,11... | collective-permute-start | bytes 1572872 | tf_op jit(solution)/shard_map/ppermute | solution.py:26
  59.7 22.9 %collective-permute-start.12 = (bf16[512,512]{1,0:T(8,128)(2,1)S(1)}, bf16[512,512]{1,0:T(8,128)(2,1)S(1)}, u32[]{:S(2)}, u32[]{:S(2)}) collective-permute-start(bf16[512,512]{1,0:T(8,128)(2,1)S(1)} %add_convert_fusion.3), channel_id=1, source_target_pairs={{0,1},{1,0},{2,3},{3,2},{4,5},{5,4},{6,7},{7,6},{8,9},{9,8},{10,11... | collective-permute-start | bytes 1572872 | tf_op jit(solution)/shard_map/ppermute | solution.py:26
  59.7 11.1 %collective-permute-start.2 = (bf16[128,1536]{1,0:T(8,128)(2,1)S(1)}, bf16[128,1536]{1,0:T(8,128)(2,1)S(1)}, u32[]{:S(2)}, u32[]{:S(2)}) collective-permute-start(bf16[128,1536]{1,0:T(8,128)(2,1)S(1)} %get-tuple-element.57), channel_id=1, source_target_pairs={{0,24},{8,16},{16,8},{24,0},{1,25},{9,17},{17,9},{25,1},{2,26},{10... | collective-permute-start | bytes 1179656 | tf_op jit(solution)/shard_map/ppermute | solution.py:26
  59.8 23.5 %collective-permute-start.15 = (bf16[256,512]{1,0:T(8,128)(2,1)S(1)}, bf16[256,512]{1,0:T(8,128)(2,1)S(1)}, u32[]{:S(2)}, u32[]{:S(2)}) collective-permute-start(bf16[256,512]{1,0:T(8,128)(2,1)S(1)} %get-tuple-element.80), channel_id=1, source_target_pairs={{6,0},{3,1},{0,2},{5,3},{2,4},{7,5},{4,6},{1,7},{14,8},{11,9},{8,1... | collective-permute-start | bytes 786440 | tf_op jit(solution)/shard_map/ppermute | solution.py:31
  87.9 25.5 %collective-permute-start.16 = (bf16[512,512]{1,0:T(8,128)(2,1)S(1)}, bf16[512,512]{1,0:T(8,128)(2,1)S(1)}, u32[]{:S(2)}, u32[]{:S(2)}) collective-permute-start(bf16[512,512]{1,0:T(8,128)(2,1)S(1)} %get-tuple-element.85.refs_3_), channel_id=1, source_target_pairs={{2,0},{7,1},{4,2},{1,3},{6,4},{3,5},{0,6},{5,7},{10,8},{15,9},{12,... | collective-permute-start | bytes 1572872 | tf_op jit(solution)/shard_map/ppermute | solution.py:31
  91.4 20.7 %collective-permute-start.17 = (bf16[384,512]{1,0:T(8,128)(2,1)S(1)}, bf16[384,512]{1,0:T(8,128)(2,1)S(1)}, u32[]{:S(2)}, u32[]{:S(2)}) collective-permute-start(bf16[384,512]{1,0:T(8,128)(2,1)S(1)} %get-tuple-element.88), channel_id=1, source_target_pairs={{2,0},{7,1},{4,2},{1,3},{6,4},{3,5},{0,6},{5,7},{10,8},{15,9},{12,... | collective-permute-start | bytes 1179656 | tf_op jit(solution)/shard_map/ppermute | solution.py:31
  93.2 18.9 %collective-permute-start.18 = (bf16[128,512]{1,0:T(8,128)(2,1)S(1)}, bf16[128,512]{1,0:T(8,128)(2,1)S(1)}, u32[]{:S(2)}, u32[]{:S(2)}) collective-permute-start(bf16[128,512]{1,0:T(8,128)(2,1)S(1)} %get-tuple-element.89), channel_id=1, source_target_pairs={{2,0},{7,1},{4,2},{1,3},{6,4},{3,5},{0,6},{5,7},{10,8},{15,9},{12,... | collective-permute-start | bytes 393224 | tf_op jit(solution)/shard_map/ppermute | solution.py:31
  95.0 19.7 %collective-permute-start.26 = (bf16[128,1024]{1,0:T(8,128)(2,1)S(1)}, bf16[128,1024]{1,0:T(8,128)(2,1)S(1)}, u32[]{:S(2)}, u32[]{:S(2)}) collective-permute-start(bf16[128,1024]{1,0:T(8,128)(2,1)S(1)} %get-tuple-element.102), channel_id=1, source_target_pairs={{0,8},{8,0},{16,24},{24,16},{1,9},{9,1},{17,25},{25,17},{2,10},{10... | collective-permute-start | bytes 786440 | tf_op jit(solution)/shard_map/ppermute | solution.py:26
  95.0 22.1 %collective-permute-start.27 = (bf16[128,1024]{1,0:T(8,128)(2,1)S(1)}, bf16[128,1024]{1,0:T(8,128)(2,1)S(1)}, u32[]{:S(2)}, u32[]{:S(2)}) collective-permute-start(bf16[128,1024]{1,0:T(8,128)(2,1)S(1)} %get-tuple-element.103), channel_id=1, source_target_pairs={{0,16},{8,24},{16,0},{24,8},{1,17},{9,25},{17,1},{25,9},{2,18},{10... | collective-permute-start | bytes 786440 | tf_op jit(solution)/shard_map/ppermute | solution.py:26
  112.1 8.4 %collective-permute-start.28 = (bf16[128,1024]{1,0:T(8,128)(2,1)S(1)}, bf16[128,1024]{1,0:T(8,128)(2,1)S(1)}, u32[]{:S(2)}, u32[]{:S(2)}) collective-permute-start(bf16[128,1024]{1,0:T(8,128)(2,1)S(1)} %get-tuple-element.104), channel_id=1, source_target_pairs={{0,24},{8,16},{16,8},{24,0},{1,25},{9,17},{17,9},{25,1},{2,26},{10... | collective-permute-start | bytes 786440 | tf_op jit(solution)/shard_map/ppermute | solution.py:26
  112.1 22.2 %collective-permute-start.19 = (bf16[768,512]{1,0:T(8,128)(2,1)S(1)}, bf16[768,512]{1,0:T(8,128)(2,1)S(1)}, u32[]{:S(2)}, u32[]{:S(2)}) collective-permute-start(bf16[768,512]{1,0:T(8,128)(2,1)S(1)} %get-tuple-element.90), channel_id=1, source_target_pairs={{6,0},{3,1},{0,2},{5,3},{2,4},{7,5},{4,6},{1,7},{14,8},{11,9},{8,1... | collective-permute-start | bytes 2359304 | tf_op jit(solution)/shard_map/ppermute | solution.py:31
  113.4 7.9 %collective-permute-start.23 = (bf16[128,1024]{1,0:T(8,128)(2,1)S(1)}, bf16[128,1024]{1,0:T(8,128)(2,1)S(1)}, u32[]{:S(2)}, u32[]{:S(2)}) collective-permute-start(bf16[128,1024]{1,0:T(8,128)(2,1)S(1)} %get-tuple-element.96), channel_id=1, source_target_pairs={{0,8},{8,0},{16,24},{24,16},{1,9},{9,1},{17,25},{25,17},{2,10},{10... | collective-permute-start | bytes 786440 | tf_op jit(solution)/shard_map/ppermute | solution.py:26
  114.6 19.7 %collective-permute-start.22 = (bf16[512,512]{1,0:T(8,128)(2,1)S(1)}, bf16[512,512]{1,0:T(8,128)(2,1)S(1)}, u32[]{:S(2)}, u32[]{:S(2)}) collective-permute-start(bf16[512,512]{1,0:T(8,128)(2,1)S(1)} %add_convert_fusion), channel_id=1, source_target_pairs={{0,1},{1,0},{2,3},{3,2},{4,5},{5,4},{6,7},{7,6},{8,9},{9,8},{10,11... | collective-permute-start | bytes 1572872 | tf_op jit(solution)/shard_map/ppermute | solution.py:26
  117.1 23.3 %collective-permute-start.21 = (bf16[512,512]{1,0:T(8,128)(2,1)S(1)}, bf16[512,512]{1,0:T(8,128)(2,1)S(1)}, u32[]{:S(2)}, u32[]{:S(2)}) collective-permute-start(bf16[512,512]{1,0:T(8,128)(2,1)S(1)} %add_convert_fusion.1), channel_id=1, source_target_pairs={{0,1},{1,0},{2,3},{3,2},{4,5},{5,4},{6,7},{7,6},{8,9},{9,8},{10,11... | collective-permute-start | bytes 1572872 | tf_op jit(solution)/shard_map/ppermute | solution.py:26
  120.5 9.2 %collective-permute-start.24 = (bf16[128,1024]{1,0:T(8,128)(2,1)S(1)}, bf16[128,1024]{1,0:T(8,128)(2,1)S(1)}, u32[]{:S(2)}, u32[]{:S(2)}) collective-permute-start(bf16[128,1024]{1,0:T(8,128)(2,1)S(1)} %get-tuple-element.97), channel_id=1, source_target_pairs={{0,16},{8,24},{16,0},{24,8},{1,17},{9,25},{17,1},{25,9},{2,18},{10... | collective-permute-start | bytes 786440 | tf_op jit(solution)/shard_map/ppermute | solution.py:26
  121.3 11.7 %collective-permute-start.25 = (bf16[128,1024]{1,0:T(8,128)(2,1)S(1)}, bf16[128,1024]{1,0:T(8,128)(2,1)S(1)}, u32[]{:S(2)}, u32[]{:S(2)}) collective-permute-start(bf16[128,1024]{1,0:T(8,128)(2,1)S(1)} %get-tuple-element.98), channel_id=1, source_target_pairs={{0,24},{8,16},{16,8},{24,0},{1,25},{9,17},{17,9},{25,1},{2,26},{10... | collective-permute-start | bytes 786440 | tf_op jit(solution)/shard_map/ppermute | solution.py:26
  129.6 12.4 %collective-permute-start.20 = (bf16[256,512]{1,0:T(8,128)(2,1)S(1)}, bf16[256,512]{1,0:T(8,128)(2,1)S(1)}, u32[]{:S(2)}, u32[]{:S(2)}) collective-permute-start(bf16[256,512]{1,0:T(8,128)(2,1)S(1)} %get-tuple-element.91), channel_id=1, source_target_pairs={{6,0},{3,1},{0,2},{5,3},{2,4},{7,5},{4,6},{1,7},{14,8},{11,9},{8,1... | collective-permute-start | bytes 786440 | tf_op jit(solution)/shard_map/ppermute | solution.py:31
  (4 other events, 5.4 us)

commit v7 on v6

--- a/solution.py
+++ b/solution.py
@@ -112,7 +112,7 @@
 
 def split(depth):
     half, unit = depth // 2, depth // 16
-    return (half, half - 2 * unit, 2 * unit), (12 * unit, 4 * unit)
+    return (half // 2, 3 * half // 2 - 2 * unit, 2 * unit), (12 * unit, 4 * unit)
 
 
 def sizes_of(arrays):
@@ -309,11 +309,11 @@
     return result[0], [share, *result[1:3]], result[3:]
 
 
-def picked(route, experts):
+def picked(route, mine, experts):
     count = route.shape[1]
     slots = count // 2
     lines = -(-experts // 8) * 8
-    labels = lax.broadcasted_iota(jnp.int32, (lines, count), 0)
+    labels = lax.broadcasted_iota(jnp.int32, (lines, count), 0) ^ mine
     keep = (route == labels).astype(F32)
     before = lax.broadcasted_iota(jnp.int32, (count, count), 0)
     after = lax.broadcasted_iota(jnp.int32, (count, count), 1)
@@ -322,46 +322,77 @@
     return jnp.concatenate([slot == rank[m : m + 1, :] for m in range(experts)]).astype(BF16)
 
 
-def squeeze_kernel(index, experts, fresh, count, refs):
-    first, *refs = refs
-    sources, outs = refs[:count], refs[count:]
-    if fresh:
-        picks, *outs = outs
-        hot = picked(first[index : index + 1, :], experts)
-        picks[...] = hot
-    else:
-        hot = first[...]
+def picks_kernel(experts, far, route_ref, mine, tokens_ref, *refs):
+    outs, (route, tokens, sems) = refs[:-3], refs[-3:]
+    made = [
+        pltpu.make_async_copy(route_ref, route, sems.at[0]),
+        pltpu.make_async_copy(tokens_ref.at[0], tokens, sems.at[1]),
+    ]
+    for item in made:
+        item.start()
+    made[0].wait()
+    picks, outs = outs[: route.shape[0]], outs[route.shape[0] :]
+    hot = None
+    for index, out in enumerate(picks):
+        value = picked(route[index : index + 1, :], mine[0], experts)
+        out[...] = value
+        hot = value if hot is None else hot
+    made[1].wait()
     slots = hot.shape[0] // experts
+    for m, out in zip(far, outs):
+        out[...] = dot(hot[m * slots : (m + 1) * slots], tokens[...]).astype(BF16)
+
+
+def picks_call(routing, mine, tokens, experts, far):
+    rounds, count, depth = tokens.shape
+    shape = jax.ShapeDtypeStruct
+    slots = count // 2
+    outs = [shape((experts * slots, count), BF16)] * rounds + [shape((slots, depth), BF16)] * len(far)
+    result = pl.pallas_call(
+        lambda *refs: picks_kernel(experts, far, *refs),
+        out_shape=outs,
+        in_specs=[ANY, SMEM, ANY],
+        out_specs=[VMEM] * len(outs),
+        scratch_shapes=[
+            pltpu.VMEM((rounds, count), jnp.int32),
+            pltpu.VMEM((count, depth), BF16),
+            pltpu.SemaphoreType.DMA((2,)),
+        ],
+        compiler_params=limit(52),
+        name="picks",
+    )(routing, mine, tokens)
+    return result[:rounds], result[rounds:]
+
+
+def squeeze_kernel(count, chosen, experts, refs):
+    picks, sources, outs = refs[0], refs[1 : 1 + count], refs[1 + count :]
+    slots = picks.shape[0] // experts
+    hot = picks[: (max(chosen) + 1) * slots, :]
     place = 0
     for source in sources:
         value = dot(hot, source[0]).astype(BF16)
-        for m, out in enumerate(outs):
+        for m, out in zip(chosen, outs):
             out[:, place : place + value.shape[1]] = value[m * slots : (m + 1) * slots, :]
         place += value.shape[1]
 
 
-def squeeze_call(index, first, sources, experts, fresh):
-    count = sources[0].shape[1]
-    slots = count // 2
+def squeeze_call(index, picks, sources, chosen, experts):
     width = sum(item.shape[2] for item in sources)
-    shape = jax.ShapeDtypeStruct
-    outs = [shape((slots, width), BF16)] * experts
-    if fresh:
-        outs.insert(0, shape((experts * slots, count), BF16))
+    outs = [jax.ShapeDtypeStruct((picks.shape[0] // experts, width), BF16)] * len(chosen)
 
     def whole(item):
         return pl.BlockSpec(item.shape, lambda i: (0, 0))
 
     return pl.pallas_call(
-        lambda *refs: squeeze_kernel(index, experts, fresh, len(sources), refs),
+        lambda *refs: squeeze_kernel(len(sources), chosen, experts, refs),
         grid=(1,),
         out_shape=outs,
-        in_specs=[whole(first)]
+        in_specs=[whole(picks)]
         + [pl.BlockSpec((1,) + item.shape[1:], lambda i: (index, 0, 0)) for item in sources],
         out_specs=[whole(item) for item in outs],
         compiler_params=limit(16),
         name="squeeze",
-    )(first, *sources)
+    )(picks, *sources)
 
 
 def backward_kernel(sizes, where, refs):
@@ -446,7 +477,7 @@
     depth = weight.shape[0]
     _, two = split(depth)
     slots = tokens.shape[1] // 2
-    route = routing ^ lax.axis_index("expert").astype(jnp.int32)
+    mine = lax.axis_index("expert").astype(jnp.int32).reshape(1)
 
     def exchanged(items):
         got = [items[0]]
@@ -456,13 +487,13 @@
 
     in_grad = None
     waiting = []
-    picks, *items = squeeze_call(0, route, [tokens], experts, True)
-    all_picks = [picks]
+    every, close = list(range(experts)), [0, 1]
+    all_picks, items = picks_call(routing, mine, tokens, experts, every[2:])
+    items = [*squeeze_call(0, all_picks[0], [tokens], close, experts), *items]
     rows = exchanged(items)
-    items = squeeze_call(0, picks, [out_grad], experts, False)
+    items = squeeze_call(0, all_picks[0], [out_grad], every, experts)
     grads = exchanged(items)
-    picks, *items = squeeze_call(1, route, [tokens, out_grad], experts, True)
-    all_picks.append(picks)
+    items = squeeze_call(1, all_picks[1], [tokens, out_grad], every, experts)
     later = exchanged(items)
     moment, slopes = part_call(rows[:2], grads[:2], weight, moment)
     all_slopes = [slopes]

time: 144 us -> 161 us (1.12)
  starting transfers between devices: 28.2 us -> 52.4 us
  local copies, waits for them, and re-layouts: 6.58 us -> 2.94 us
  waiting for transfers between devices: 82.9 us -> 80.3 us
    ppermute x10, starting transfers between devices: 12.1 us -> 29 us  [crossed(): lax.ppermute(block, axis, [((i + (-way if i % 2 else way)) % count, i) fo...]
    ppermute x19, waiting for transfers between devices: 42.1 us -> 32.8 us  [swapped(): lax.ppermute(block, axis, [(i, i ^ bit) for i in range(lax.axis_size(axis...]
    ppermute x19, starting transfers between devices: 16.2 us -> 23.4 us  [swapped(): lax.ppermute(block, axis, [(i, i ^ bit) for i in range(lax.axis_size(axis...]
    ppermute x10, waiting for transfers between devices: 40.8 us -> 47.4 us  [crossed(): lax.ppermute(block, axis, [((i + (-way if i % 2 else way)) % count, i) fo...]
    unnamed x14 -> x12, local copies, waits for them, and re-layouts: 6.58 us -> 2.94 us
  transfers between devices with their start and end apart: 29 -> 29, of which waited for: 11 -> 15; matrix products, arithmetic and copies ran while one was open for 0% -> 0% of each run, Pallas kernels for 9% -> 7%
where the time goes in v7:
time: 161 us
  waiting for transfers between devices  80.3 us (50%)
  starting transfers between devices  52.4 us (33%)
  Pallas kernels  24 us (15%)
  local copies, waits for them, and re-layouts  2.94 us (2%)
    ppermute x10, waiting for transfers between devices, crossed(): lax.ppermute(block, axis, [((i + (-way if i % 2 else way)) % count, i) fo...  47.4 us
    ppermute x19, waiting for transfers between devices, swapped(): lax.ppermute(block, axis, [(i, i ^ bit) for i in range(lax.axis_size(axis...  32.8 us
    ppermute x10, starting transfers between devices, crossed(): lax.ppermute(block, axis, [((i + (-way if i % 2 else way)) % count, i) fo...  29 us
    ppermute x19, starting transfers between devices, swapped(): lax.ppermute(block, axis, [(i, i ^ bit) for i in range(lax.axis_size(axis...  23.4 us
    pallas_call x2, Pallas kernels, round_call(): pl.pallas_call(lambda *refs: round_kernel(sizes, place, decay, refs), out...  8.2 us
    pallas_call x4, Pallas kernels, backward_call(): pl.pallas_call(lambda *refs: backward_kernel(sizes, where, refs), out_sha...  3.27 us
  transfers between devices with their start and end apart: 29, of which 15 were waited for; matrix products, arithmetic and copies ran while one was open for 0% of the time, Pallas kernels for 7%

profile of v7, /device:TPU:0, one launch (start us, length us, event | category | flops | bytes accessed | tf_op | source)
XLA Modules:
  0.0 161.2 jit_solution(6799708044204542028)
XLA Ops:
  1.4 1.5 picks.1
  2.9 3.0 %collective-permute-start.3 = (bf16[128,1024]{1,0:T(8,128)(2,1)S(1)}, bf16[128,1024]{1,0:T(8,128)(2,1)S(1)}, u32[]{:S(2)}, u32[]{:S(2)}) collective-permute-start(bf16[128,1024]{1,0:T(8,128)(2,1)S(1)} %get-tuple-element.59), channel_id=1, source_target_pairs={{0,16},{8,24},{16,0},{24,8},{1,17},{9,25},{17,1},{25,9},{2,18},{10... | collective-permute-start | bytes 786440 | tf_op jit(solution)/shard_map/ppermute | solution.py:26
  8.3 1.7 %collective-permute-start.7 = (bf16[128,512]{1,0:T(8,128)(2,1)S(1)}, bf16[128,512]{1,0:T(8,128)(2,1)S(1)}, u32[]{:S(2)}, u32[]{:S(2)}) collective-permute-start(bf16[128,512]{1,0:T(8,128)(2,1)S(1)} %get-tuple-element.67), channel_id=1, source_target_pairs={{0,16},{8,24},{16,0},{24,8},{1,17},{9,25},{17,1},{25,9},{2,18},{10... | collective-permute-start | bytes 393224 | tf_op jit(solution)/shard_map/ppermute | solution.py:26
  10.0 3.2 %collective-permute-done.3.refs_0_.refs_2_ = bf16[128,1024]{1,0:T(8,128)(2,1)S(1)} collective-permute-done((bf16[128,1024]{1,0:T(8,128)(2,1)S(1)}, bf16[128,1024]{1,0:T(8,128)(2,1)S(1)}, u32[]{:S(2)}, u32[]{:S(2)}) %collective-permute-start.3) | collective-permute-done | bytes 262176 | tf_op jit(solution)/shard_map/ppermute | solution.py:26
  13.1 5.2 %collective-permute-done.4.refs_1_.refs_3_ = bf16[128,1024]{1,0:T(8,128)(2,1)S(1)} collective-permute-done((bf16[128,1024]{1,0:T(8,128)(2,1)S(1)}, bf16[128,1024]{1,0:T(8,128)(2,1)S(1)}, u32[]{:S(2)}, u32[]{:S(2)}) %collective-permute-start.4) | collective-permute-done | bytes 262176 | tf_op jit(solution)/shard_map/ppermute | solution.py:26
  21.6 1.2 collective-permute-done.8.refs_5_
  22.8 3.9 %muon_round.2 = (f32[1024,512]{1,0:T(8,128)S(1)}, bf16[256,512]{1,0:T(8,128)(2,1)S(1)}, bf16[1024,512]{1,0:T(8,128)(2,1)S(1)}, bf16[512,512]{1,0:T(8,128)(2,1)S(...) custom-call(f32[256,512]{1,0:T(8,128)S(1)} %ahead.2.refs_0_, ...), custom_call_target="tpu_custom_call" | custom-call | tf_op jit(solution)/shard_map/muon_round/pallas_call | solution.py:272
  26.7 1.4 second_half.2
  28.1 3.7 %collective-permute-start.10 = (bf16[640,512]{1,0:T(8,128)(2,1)S(1)}, bf16[640,512]{1,0:T(8,128)(2,1)S(1)}, u32[]{:S(2)}, u32[]{:S(2)}) collective-permute-start(bf16[640,512]{1,0:T(8,128)(2,1)S(1)} %get-tuple-element.75), channel_id=1, source_target_pairs={{2,0},{7,1},{4,2},{1,3},{6,4},{3,5},{0,6},{5,7},{10,8},{15,9},{12,... | collective-permute-start | bytes 1966088 | tf_op jit(solution)/shard_map/ppermute | solution.py:31
  32.2 1.6 collective-permute-start.11
  33.8 15.9 %collective-permute-done.13.refs_15_ = bf16[128,512]{1,0:T(8,128)(2,1)S(1)} collective-permute-done((bf16[128,512]{1,0:T(8,128)(2,1)S(1)}, bf16[128,512]{1,0:T(8,128)(2,1)S(1)}, u32[]{:S(2)}, u32[]{:S(2)}) %collective-permute-start.13) | collective-permute-done | bytes 131104 | tf_op jit(solution)/shard_map/ppermute | solution.py:31
  49.9 2.3 %collective-permute-start.14 = (bf16[768,512]{1,0:T(8,128)(2,1)S(1)}, bf16[768,512]{1,0:T(8,128)(2,1)S(1)}, u32[]{:S(2)}, u32[]{:S(2)}) collective-permute-start(bf16[768,512]{1,0:T(8,128)(2,1)S(1)} %add_convert_fusion.1), channel_id=1, source_target_pairs={{0,1},{1,0},{2,3},{3,2},{4,5},{5,4},{6,7},{7,6},{8,9},{9,8},{10,11... | collective-permute-start | bytes 2359304 | tf_op jit(solution)/shard_map/ppermute | solution.py:26
  52.2 18.6 %collective-permute-start.9 = (bf16[256,512]{1,0:T(8,128)(2,1)S(1)}, bf16[256,512]{1,0:T(8,128)(2,1)S(1)}, u32[]{:S(2)}, u32[]{:S(2)}) collective-permute-start(bf16[256,512]{1,0:T(8,128)(2,1)S(1)} %get-tuple-element.73.refs_3_), channel_id=1, source_target_pairs={{2,0},{7,1},{4,2},{1,3},{6,4},{3,5},{0,6},{5,7},{10,8},{15,9},{12,... | collective-permute-start | bytes 786440 | tf_op jit(solution)/shard_map/ppermute | solution.py:31
  71.4 1.4 collective-permute-start.1
  72.9 1.8 %collective-permute-done.9.refs_6_.refs_13_ = bf16[256,512]{1,0:T(8,128)(2,1)S(1)} collective-permute-done((bf16[256,512]{1,0:T(8,128)(2,1)S(1)}, bf16[256,512]{1,0:T(8,128)(2,1)S(1)}, u32[]{:S(2)}, u32[]{:S(2)}) %collective-permute-start.9) | collective-permute-done | bytes 262176 | tf_op jit(solution)/shard_map/ppermute | solution.py:31
  74.7 1.6 collective-permute-start.2
  76.3 1.7 %collective-permute-start.12 = (bf16[256,512]{1,0:T(8,128)(2,1)S(1)}, bf16[256,512]{1,0:T(8,128)(2,1)S(1)}, u32[]{:S(2)}, u32[]{:S(2)}) collective-permute-start(bf16[256,512]{1,0:T(8,128)(2,1)S(1)} %add_convert_fusion.3), channel_id=1, source_target_pairs={{0,1},{1,0},{2,3},{3,2},{4,5},{5,4},{6,7},{7,6},{8,9},{9,8},{10,11... | collective-permute-start | bytes 786440 | tf_op jit(solution)/shard_map/ppermute | solution.py:26
  78.0 5.4 %collective-permute-done.1.refs_2_.refs_4_.refs_8_ = bf16[128,1536]{1,0:T(8,128)(2,1)S(1)} collective-permute-done((bf16[128,1536]{1,0:T(8,128)(2,1)S(1)}, bf16[128,1536]{1,0:T(8,128)(2,1)S(1)}, u32[]{:S(2)}, u32[]{:S(2)}) %collective-permute-start.1) | collective-permute-done | bytes 393248 | tf_op jit(solution)/shard_map/ppermute | solution.py:26
  83.5 7.3 %collective-permute-done.2.refs_3_.refs_5_.refs_9_ = bf16[128,1536]{1,0:T(8,128)(2,1)S(1)} collective-permute-done((bf16[128,1536]{1,0:T(8,128)(2,1)S(1)}, bf16[128,1536]{1,0:T(8,128)(2,1)S(1)}, u32[]{:S(2)}, u32[]{:S(2)}) %collective-permute-start.2) | collective-permute-done | bytes 393248 | tf_op jit(solution)/shard_map/ppermute | solution.py:26
  92.5 4.3 %muon_round.3 = (f32[1024,512]{1,0:T(8,128)}, bf16[512,512]{1,0:T(8,128)(2,1)S(1)}, bf16[1024,512]{1,0:T(8,128)(2,1)S(1)}, bf16[512,512]{1,0:T(8,128)(2,1)S(1)},...) custom-call(f32[512,512]{1,0:T(8,128)S(1)} %get-tuple-element.78.refs_0_, ...), custom_call_target="tpu_custom_call" | custom-call | tf_op jit(solution)/shard_map/muon_round/pallas_call | solution.py:272
  96.8 1.4 second_half.3
  100.1 3.8 %collective-permute-start.27 = (bf16[128,1024]{1,0:T(8,128)(2,1)S(1)}, bf16[128,1024]{1,0:T(8,128)(2,1)S(1)}, u32[]{:S(2)}, u32[]{:S(2)}) collective-permute-start(bf16[128,1024]{1,0:T(8,128)(2,1)S(1)} %get-tuple-element.103), channel_id=1, source_target_pairs={{0,16},{8,24},{16,0},{24,8},{1,17},{9,25},{17,1},{25,9},{2,18},{10... | collective-permute-start | bytes 786440 | tf_op jit(solution)/shard_map/ppermute | solution.py:26
  103.9 2.0 %collective-permute-start.19 = (bf16[768,512]{1,0:T(8,128)(2,1)S(1)}, bf16[768,512]{1,0:T(8,128)(2,1)S(1)}, u32[]{:S(2)}, u32[]{:S(2)}) collective-permute-start(bf16[768,512]{1,0:T(8,128)(2,1)S(1)} %get-tuple-element.91), channel_id=1, source_target_pairs={{6,0},{3,1},{0,2},{5,3},{2,4},{7,5},{4,6},{1,7},{14,8},{11,9},{8,1... | collective-permute-start | bytes 2359304 | tf_op jit(solution)/shard_map/ppermute | solution.py:31
  105.8 28.4 %collective-permute-done.18.refs_4_ = bf16[128,512]{1,0:T(8,128)(2,1)S(1)} collective-permute-done((bf16[128,512]{1,0:T(8,128)(2,1)S(1)}, bf16[128,512]{1,0:T(8,128)(2,1)S(1)}, u32[]{:S(2)}, u32[]{:S(2)}) %collective-permute-start.18) | collective-permute-done | bytes 131104 | tf_op jit(solution)/shard_map/ppermute | solution.py:31
  134.7 2.6 %collective-permute-start.16 = (bf16[256,512]{1,0:T(8,128)(2,1)S(1)}, bf16[256,512]{1,0:T(8,128)(2,1)S(1)}, u32[]{:S(2)}, u32[]{:S(2)}) collective-permute-start(bf16[256,512]{1,0:T(8,128)(2,1)S(1)} %get-tuple-element.86.refs_3_), channel_id=1, source_target_pairs={{2,0},{7,1},{4,2},{1,3},{6,4},{3,5},{0,6},{5,7},{10,8},{15,9},{12,... | collective-permute-start | bytes 786440 | tf_op jit(solution)/shard_map/ppermute | solution.py:31
  138.2 2.2 %collective-permute-start.23 = (bf16[128,1024]{1,0:T(8,128)(2,1)S(1)}, bf16[128,1024]{1,0:T(8,128)(2,1)S(1)}, u32[]{:S(2)}, u32[]{:S(2)}) collective-permute-start(bf16[128,1024]{1,0:T(8,128)(2,1)S(1)} %get-tuple-element.96), channel_id=1, source_target_pairs={{0,8},{8,0},{16,24},{24,16},{1,9},{9,1},{17,25},{25,17},{2,10},{10... | collective-permute-start | bytes 786440 | tf_op jit(solution)/shard_map/ppermute | solution.py:26
  143.8 3.5 %collective-permute-start.21 = (bf16[256,512]{1,0:T(8,128)(2,1)S(1)}, bf16[256,512]{1,0:T(8,128)(2,1)S(1)}, u32[]{:S(2)}, u32[]{:S(2)}) collective-permute-start(bf16[256,512]{1,0:T(8,128)(2,1)S(1)} %add_convert_fusion.2), channel_id=1, source_target_pairs={{0,1},{1,0},{2,3},{3,2},{4,5},{5,4},{6,7},{7,6},{8,9},{9,8},{10,11... | collective-permute-start | bytes 786440 | tf_op jit(solution)/shard_map/ppermute | solution.py:26
  147.4 4.1 %collective-permute-done.24.refs_3_ = bf16[128,1024]{1,0:T(8,128)(2,1)S(1)} collective-permute-done((bf16[128,1024]{1,0:T(8,128)(2,1)S(1)}, bf16[128,1024]{1,0:T(8,128)(2,1)S(1)}, u32[]{:S(2)}, u32[]{:S(2)}) %collective-permute-start.24) | collective-permute-done | bytes 262176 | tf_op jit(solution)/shard_map/ppermute | solution.py:26
  151.5 1.3 finish.2.refs_5_
  153.5 1.3 finish.3
  154.7 3.8 %collective-permute-done.21.refs_5_.refs_7_ = bf16[256,512]{1,0:T(8,128)(2,1)S(1)} collective-permute-done((bf16[256,512]{1,0:T(8,128)(2,1)S(1)}, bf16[256,512]{1,0:T(8,128)(2,1)S(1)}, u32[]{:S(2)}, u32[]{:S(2)}) %collective-permute-start.21) | collective-permute-done | bytes 262176 | tf_op jit(solution)/shard_map/ppermute | solution.py:26
  158.5 1.6 average.2.refs_9_
  (61 shorter events, 17.5 us)
Async XLA Ops:
  0.6 5.4 %copy-start.1 = (bf16[2,256,1024]{2,1,0:T(8,128)(2,1)S(1)}, bf16[2,256,1024]{2,1,0:T(8,128)(2,1)}, u32[]{:S(2)}) copy-start(bf16[2,256,1024]{2,1,0:T(8,128)(2,1)} %refs_1_.4) | copy-start | bytes 3145732
  1.4 16.9 %copy-start = (f32[1,1,1024,512]{3,2,1,0:T(8,128)S(1)}, f32[1,1,1024,512]{3,2,1,0:T(8,128)}, u32[]{:S(2)}) copy-start(f32[1,1,1024,512]{3,2,1,0:T(8,128)} %param.8) | copy-start | bytes 6291460
  2.9 10.2 %collective-permute-start.3 = (bf16[128,1024]{1,0:T(8,128)(2,1)S(1)}, bf16[128,1024]{1,0:T(8,128)(2,1)S(1)}, u32[]{:S(2)}, u32[]{:S(2)}) collective-permute-start(bf16[128,1024]{1,0:T(8,128)(2,1)S(1)} %get-tuple-element.59), channel_id=1, source_target_pairs={{0,16},{8,24},{16,0},{24,8},{1,17},{9,25},{17,1},{25,9},{2,18},{10... | collective-permute-start | bytes 786440 | tf_op jit(solution)/shard_map/ppermute | solution.py:26
  6.0 12.3 %collective-permute-start.4 = (bf16[128,1024]{1,0:T(8,128)(2,1)S(1)}, bf16[128,1024]{1,0:T(8,128)(2,1)S(1)}, u32[]{:S(2)}, u32[]{:S(2)}) collective-permute-start(bf16[128,1024]{1,0:T(8,128)(2,1)S(1)} %get-tuple-element.60), channel_id=1, source_target_pairs={{0,24},{8,16},{16,8},{24,0},{1,25},{9,17},{17,9},{25,1},{2,26},{10... | collective-permute-start | bytes 786440 | tf_op jit(solution)/shard_map/ppermute | solution.py:26
  6.3 12.5 %collective-permute-start.5 = (bf16[128,1024]{1,0:T(8,128)(2,1)S(1)}, bf16[128,1024]{1,0:T(8,128)(2,1)S(1)}, u32[]{:S(2)}, u32[]{:S(2)}) collective-permute-start(bf16[128,1024]{1,0:T(8,128)(2,1)S(1)} %get-tuple-element.63), channel_id=1, source_target_pairs={{0,8},{8,0},{16,24},{24,16},{1,9},{9,1},{17,25},{25,17},{2,10},{10... | collective-permute-start | bytes 786440 | tf_op jit(solution)/shard_map/ppermute | solution.py:26
  7.9 10.9 %collective-permute-start.6 = (bf16[128,512]{1,0:T(8,128)(2,1)S(1)}, bf16[128,512]{1,0:T(8,128)(2,1)S(1)}, u32[]{:S(2)}, u32[]{:S(2)}) collective-permute-start(bf16[128,512]{1,0:T(8,128)(2,1)S(1)} %get-tuple-element.65), channel_id=1, source_target_pairs={{0,8},{8,0},{16,24},{24,16},{1,9},{9,1},{17,25},{25,17},{2,10},{10... | collective-permute-start | bytes 393224 | tf_op jit(solution)/shard_map/ppermute | solution.py:26
  8.3 13.3 %collective-permute-start.7 = (bf16[128,512]{1,0:T(8,128)(2,1)S(1)}, bf16[128,512]{1,0:T(8,128)(2,1)S(1)}, u32[]{:S(2)}, u32[]{:S(2)}) collective-permute-start(bf16[128,512]{1,0:T(8,128)(2,1)S(1)} %get-tuple-element.67), channel_id=1, source_target_pairs={{0,16},{8,24},{16,0},{24,8},{1,17},{9,25},{17,1},{25,9},{2,18},{10... | collective-permute-start | bytes 393224 | tf_op jit(solution)/shard_map/ppermute | solution.py:26
  13.1 9.6 %collective-permute-start.8 = (bf16[128,512]{1,0:T(8,128)(2,1)S(1)}, bf16[128,512]{1,0:T(8,128)(2,1)S(1)}, u32[]{:S(2)}, u32[]{:S(2)}) collective-permute-start(bf16[128,512]{1,0:T(8,128)(2,1)S(1)} %get-tuple-element.68), channel_id=1, source_target_pairs={{0,24},{8,16},{16,8},{24,0},{1,25},{9,17},{17,9},{25,1},{2,26},{10... | collective-permute-start | bytes 393224 | tf_op jit(solution)/shard_map/ppermute | solution.py:26
  28.1 42.7 %copy-start.3 = (bf16[2,256,512]{2,1,0:T(8,128)(2,1)S(1)}, bf16[2,256,512]{2,1,0:T(8,128)(2,1)}, u32[]{:S(2)}) copy-start(bf16[2,256,512]{2,1,0:T(8,128)(2,1)} %refs_1_.5) | copy-start | bytes 1572868
  28.1 21.6 %collective-permute-start.10 = (bf16[640,512]{1,0:T(8,128)(2,1)S(1)}, bf16[640,512]{1,0:T(8,128)(2,1)S(1)}, u32[]{:S(2)}, u32[]{:S(2)}) collective-permute-start(bf16[640,512]{1,0:T(8,128)(2,1)S(1)} %get-tuple-element.75), channel_id=1, source_target_pairs={{2,0},{7,1},{4,2},{1,3},{6,4},{3,5},{0,6},{5,7},{10,8},{15,9},{12,... | collective-permute-start | bytes 1966088 | tf_op jit(solution)/shard_map/ppermute | solution.py:31
  31.7 18.0 %collective-permute-start.13 = (bf16[128,512]{1,0:T(8,128)(2,1)S(1)}, bf16[128,512]{1,0:T(8,128)(2,1)S(1)}, u32[]{:S(2)}, u32[]{:S(2)}) collective-permute-start(bf16[128,512]{1,0:T(8,128)(2,1)S(1)} %get-tuple-element.77), channel_id=1, source_target_pairs={{2,0},{7,1},{4,2},{1,3},{6,4},{3,5},{0,6},{5,7},{10,8},{15,9},{12,... | collective-permute-start | bytes 393224 | tf_op jit(solution)/shard_map/ppermute | solution.py:31
  32.2 58.7 %collective-permute-start.11 = (bf16[768,512]{1,0:T(8,128)(2,1)S(1)}, bf16[768,512]{1,0:T(8,128)(2,1)S(1)}, u32[]{:S(2)}, u32[]{:S(2)}) collective-permute-start(bf16[768,512]{1,0:T(8,128)(2,1)S(1)} %get-tuple-element.76), channel_id=1, source_target_pairs={{6,0},{3,1},{0,2},{5,3},{2,4},{7,5},{4,6},{1,7},{14,8},{11,9},{8,1... | collective-permute-start | bytes 2359304 | tf_op jit(solution)/shard_map/ppermute | solution.py:31
  49.9 40.9 %collective-permute-start.14 = (bf16[768,512]{1,0:T(8,128)(2,1)S(1)}, bf16[768,512]{1,0:T(8,128)(2,1)S(1)}, u32[]{:S(2)}, u32[]{:S(2)}) collective-permute-start(bf16[768,512]{1,0:T(8,128)(2,1)S(1)} %add_convert_fusion.1), channel_id=1, source_target_pairs={{0,1},{1,0},{2,3},{3,2},{4,5},{5,4},{6,7},{7,6},{8,9},{9,8},{10,11... | collective-permute-start | bytes 2359304 | tf_op jit(solution)/shard_map/ppermute | solution.py:26
  52.2 22.5 %collective-permute-start.9 = (bf16[256,512]{1,0:T(8,128)(2,1)S(1)}, bf16[256,512]{1,0:T(8,128)(2,1)S(1)}, u32[]{:S(2)}, u32[]{:S(2)}) collective-permute-start(bf16[256,512]{1,0:T(8,128)(2,1)S(1)} %get-tuple-element.73.refs_3_), channel_id=1, source_target_pairs={{2,0},{7,1},{4,2},{1,3},{6,4},{3,5},{0,6},{5,7},{10,8},{15,9},{12,... | collective-permute-start | bytes 786440 | tf_op jit(solution)/shard_map/ppermute | solution.py:31
  71.4 5.0 %collective-permute-start = (bf16[128,1536]{1,0:T(8,128)(2,1)S(1)}, bf16[128,1536]{1,0:T(8,128)(2,1)S(1)}, u32[]{:S(2)}, u32[]{:S(2)}) collective-permute-start(bf16[128,1536]{1,0:T(8,128)(2,1)S(1)} %get-tuple-element.56), channel_id=1, source_target_pairs={{0,8},{8,0},{16,24},{24,16},{1,9},{9,1},{17,25},{25,17},{2,10},{10... | collective-permute-start | bytes 1179656 | tf_op jit(solution)/shard_map/ppermute | solution.py:26
  71.4 12.1 %collective-permute-start.1 = (bf16[128,1536]{1,0:T(8,128)(2,1)S(1)}, bf16[128,1536]{1,0:T(8,128)(2,1)S(1)}, u32[]{:S(2)}, u32[]{:S(2)}) collective-permute-start(bf16[128,1536]{1,0:T(8,128)(2,1)S(1)} %get-tuple-element.57), channel_id=1, source_target_pairs={{0,16},{8,24},{16,0},{24,8},{1,17},{9,25},{17,1},{25,9},{2,18},{10... | collective-permute-start | bytes 1179656 | tf_op jit(solution)/shard_map/ppermute | solution.py:26
  74.7 16.2 %collective-permute-start.2 = (bf16[128,1536]{1,0:T(8,128)(2,1)S(1)}, bf16[128,1536]{1,0:T(8,128)(2,1)S(1)}, u32[]{:S(2)}, u32[]{:S(2)}) collective-permute-start(bf16[128,1536]{1,0:T(8,128)(2,1)S(1)} %get-tuple-element.58), channel_id=1, source_target_pairs={{0,24},{8,16},{16,8},{24,0},{1,25},{9,17},{17,9},{25,1},{2,26},{10... | collective-permute-start | bytes 1179656 | tf_op jit(solution)/shard_map/ppermute | solution.py:26
  76.3 14.5 %collective-permute-start.12 = (bf16[256,512]{1,0:T(8,128)(2,1)S(1)}, bf16[256,512]{1,0:T(8,128)(2,1)S(1)}, u32[]{:S(2)}, u32[]{:S(2)}) collective-permute-start(bf16[256,512]{1,0:T(8,128)(2,1)S(1)} %add_convert_fusion.3), channel_id=1, source_target_pairs={{0,1},{1,0},{2,3},{3,2},{4,5},{5,4},{6,7},{7,6},{8,9},{9,8},{10,11... | collective-permute-start | bytes 786440 | tf_op jit(solution)/shard_map/ppermute | solution.py:26
  83.5 9.0 %collective-permute-start.15 = (bf16[256,512]{1,0:T(8,128)(2,1)S(1)}, bf16[256,512]{1,0:T(8,128)(2,1)S(1)}, u32[]{:S(2)}, u32[]{:S(2)}) collective-permute-start(bf16[256,512]{1,0:T(8,128)(2,1)S(1)} %get-tuple-element.81), channel_id=1, source_target_pairs={{6,0},{3,1},{0,2},{5,3},{2,4},{7,5},{4,6},{1,7},{14,8},{11,9},{8,1... | collective-permute-start | bytes 786440 | tf_op jit(solution)/shard_map/ppermute | solution.py:31
  98.2 36.1 %collective-permute-start.17 = (bf16[640,512]{1,0:T(8,128)(2,1)S(1)}, bf16[640,512]{1,0:T(8,128)(2,1)S(1)}, u32[]{:S(2)}, u32[]{:S(2)}) collective-permute-start(bf16[640,512]{1,0:T(8,128)(2,1)S(1)} %get-tuple-element.89), channel_id=1, source_target_pairs={{2,0},{7,1},{4,2},{1,3},{6,4},{3,5},{0,6},{5,7},{10,8},{15,9},{12,... | collective-permute-start | bytes 1966088 | tf_op jit(solution)/shard_map/ppermute | solution.py:31
  98.3 36.0 %collective-permute-start.18 = (bf16[128,512]{1,0:T(8,128)(2,1)S(1)}, bf16[128,512]{1,0:T(8,128)(2,1)S(1)}, u32[]{:S(2)}, u32[]{:S(2)}) collective-permute-start(bf16[128,512]{1,0:T(8,128)(2,1)S(1)} %get-tuple-element.90), channel_id=1, source_target_pairs={{2,0},{7,1},{4,2},{1,3},{6,4},{3,5},{0,6},{5,7},{10,8},{15,9},{12,... | collective-permute-start | bytes 393224 | tf_op jit(solution)/shard_map/ppermute | solution.py:31
  99.2 35.5 %collective-permute-start.26 = (bf16[128,1024]{1,0:T(8,128)(2,1)S(1)}, bf16[128,1024]{1,0:T(8,128)(2,1)S(1)}, u32[]{:S(2)}, u32[]{:S(2)}) collective-permute-start(bf16[128,1024]{1,0:T(8,128)(2,1)S(1)} %get-tuple-element.102), channel_id=1, source_target_pairs={{0,8},{8,0},{16,24},{24,16},{1,9},{9,1},{17,25},{25,17},{2,10},{10... | collective-permute-start | bytes 786440 | tf_op jit(solution)/shard_map/ppermute | solution.py:26
  100.1 38.1 %collective-permute-start.27 = (bf16[128,1024]{1,0:T(8,128)(2,1)S(1)}, bf16[128,1024]{1,0:T(8,128)(2,1)S(1)}, u32[]{:S(2)}, u32[]{:S(2)}) collective-permute-start(bf16[128,1024]{1,0:T(8,128)(2,1)S(1)} %get-tuple-element.103), channel_id=1, source_target_pairs={{0,16},{8,24},{16,0},{24,8},{1,17},{9,25},{17,1},{25,9},{2,18},{10... | collective-permute-start | bytes 786440 | tf_op jit(solution)/shard_map/ppermute | solution.py:26
  103.9 54.6 %collective-permute-start.19 = (bf16[768,512]{1,0:T(8,128)(2,1)S(1)}, bf16[768,512]{1,0:T(8,128)(2,1)S(1)}, u32[]{:S(2)}, u32[]{:S(2)}) collective-permute-start(bf16[768,512]{1,0:T(8,128)(2,1)S(1)} %get-tuple-element.91), channel_id=1, source_target_pairs={{6,0},{3,1},{0,2},{5,3},{2,4},{7,5},{4,6},{1,7},{14,8},{11,9},{8,1... | collective-permute-start | bytes 2359304 | tf_op jit(solution)/shard_map/ppermute | solution.py:31
  134.5 24.0 %collective-permute-start.22 = (bf16[768,512]{1,0:T(8,128)(2,1)S(1)}, bf16[768,512]{1,0:T(8,128)(2,1)S(1)}, u32[]{:S(2)}, u32[]{:S(2)}) collective-permute-start(bf16[768,512]{1,0:T(8,128)(2,1)S(1)} %add_convert_fusion), channel_id=1, source_target_pairs={{0,1},{1,0},{2,3},{3,2},{4,5},{5,4},{6,7},{7,6},{8,9},{9,8},{10,11... | collective-permute-start | bytes 2359304 | tf_op jit(solution)/shard_map/ppermute | solution.py:26
  134.6 7.7 %collective-permute-start.28 = (bf16[128,1024]{1,0:T(8,128)(2,1)S(1)}, bf16[128,1024]{1,0:T(8,128)(2,1)S(1)}, u32[]{:S(2)}, u32[]{:S(2)}) collective-permute-start(bf16[128,1024]{1,0:T(8,128)(2,1)S(1)} %get-tuple-element.104), channel_id=1, source_target_pairs={{0,24},{8,16},{16,8},{24,0},{1,25},{9,17},{17,9},{25,1},{2,26},{10... | collective-permute-start | bytes 786440 | tf_op jit(solution)/shard_map/ppermute | solution.py:26
  134.7 7.9 %collective-permute-start.16 = (bf16[256,512]{1,0:T(8,128)(2,1)S(1)}, bf16[256,512]{1,0:T(8,128)(2,1)S(1)}, u32[]{:S(2)}, u32[]{:S(2)}) collective-permute-start(bf16[256,512]{1,0:T(8,128)(2,1)S(1)} %get-tuple-element.86.refs_3_), channel_id=1, source_target_pairs={{2,0},{7,1},{4,2},{1,3},{6,4},{3,5},{0,6},{5,7},{10,8},{15,9},{12,... | collective-permute-start | bytes 786440 | tf_op jit(solution)/shard_map/ppermute | solution.py:31
  138.2 5.7 %collective-permute-start.23 = (bf16[128,1024]{1,0:T(8,128)(2,1)S(1)}, bf16[128,1024]{1,0:T(8,128)(2,1)S(1)}, u32[]{:S(2)}, u32[]{:S(2)}) collective-permute-start(bf16[128,1024]{1,0:T(8,128)(2,1)S(1)} %get-tuple-element.96), channel_id=1, source_target_pairs={{0,8},{8,0},{16,24},{24,16},{1,9},{9,1},{17,25},{25,17},{2,10},{10... | collective-permute-start | bytes 786440 | tf_op jit(solution)/shard_map/ppermute | solution.py:26
  142.3 9.2 %collective-permute-start.24 = (bf16[128,1024]{1,0:T(8,128)(2,1)S(1)}, bf16[128,1024]{1,0:T(8,128)(2,1)S(1)}, u32[]{:S(2)}, u32[]{:S(2)}) collective-permute-start(bf16[128,1024]{1,0:T(8,128)(2,1)S(1)} %get-tuple-element.97), channel_id=1, source_target_pairs={{0,16},{8,24},{16,0},{24,8},{1,17},{9,25},{17,1},{25,9},{2,18},{10... | collective-permute-start | bytes 786440 | tf_op jit(solution)/shard_map/ppermute | solution.py:26
  142.6 10.9 %collective-permute-start.25 = (bf16[128,1024]{1,0:T(8,128)(2,1)S(1)}, bf16[128,1024]{1,0:T(8,128)(2,1)S(1)}, u32[]{:S(2)}, u32[]{:S(2)}) collective-permute-start(bf16[128,1024]{1,0:T(8,128)(2,1)S(1)} %get-tuple-element.98), channel_id=1, source_target_pairs={{0,24},{8,16},{16,8},{24,0},{1,25},{9,17},{17,9},{25,1},{2,26},{10... | collective-permute-start | bytes 786440 | tf_op jit(solution)/shard_map/ppermute | solution.py:26
  143.8 14.7 %collective-permute-start.21 = (bf16[256,512]{1,0:T(8,128)(2,1)S(1)}, bf16[256,512]{1,0:T(8,128)(2,1)S(1)}, u32[]{:S(2)}, u32[]{:S(2)}) collective-permute-start(bf16[256,512]{1,0:T(8,128)(2,1)S(1)} %add_convert_fusion.2), channel_id=1, source_target_pairs={{0,1},{1,0},{2,3},{3,2},{4,5},{5,4},{6,7},{7,6},{8,9},{9,8},{10,11... | collective-permute-start | bytes 786440 | tf_op jit(solution)/shard_map/ppermute | solution.py:26
  151.5 8.6 %collective-permute-start.20 = (bf16[256,512]{1,0:T(8,128)(2,1)S(1)}, bf16[256,512]{1,0:T(8,128)(2,1)S(1)}, u32[]{:S(2)}, u32[]{:S(2)}) collective-permute-start(bf16[256,512]{1,0:T(8,128)(2,1)S(1)} %get-tuple-element.92), channel_id=1, source_target_pairs={{6,0},{3,1},{0,2},{5,3},{2,4},{7,5},{4,6},{1,7},{14,8},{11,9},{8,1... | collective-permute-start | bytes 786440 | tf_op jit(solution)/shard_map/ppermute | solution.py:31
  (3 other events, 3.4 us)

commit v8 on v7

--- a/solution.py
+++ b/solution.py
@@ -171,7 +171,7 @@
     return [slice(start, start + tile) for start in range(0, depth, tile)]
 
 
-def part_kernel(sizes, refs):
+def part_kernel(sizes, decay, refs):
     names = iter(refs)
     weight, moment = next(names), next(names)
     rows, grads = grouped(names, sizes)
@@ -181,15 +181,16 @@
     value = dot(take(rows, 0, slopes.shape[0]), weight[...].astype(BF16)) * factor
     slope_rows(grads, 0, value, slopes)
     for span in tiles(depth):
-        partial[span, :] = 0.9 * moment[span, :] + weight_gradient(rows, slopes, span) * factor
-
-
-def part_call(rows, grads, weight, moment):
+        before = moment[span, :] if decay == 1.0 else decay * moment[span, :]
+        partial[span, :] = before + weight_gradient(rows, slopes, span) * factor
+
+
+def part_call(rows, grads, weight, moment, decay):
     depth, width = moment.shape
     total = sum(item.shape[0] for item in rows)
     sizes = sizes_of([rows, grads])
     return pl.pallas_call(
-        lambda *refs: part_kernel(sizes, refs),
+        lambda *refs: part_kernel(sizes, decay, refs),
         out_shape=[
             jax.ShapeDtypeStruct((depth, width), F32),
             jax.ShapeDtypeStruct((total, width), BF16),
@@ -495,11 +496,13 @@
     grads = exchanged(items)
     items = squeeze_call(1, all_picks[1], [tokens, out_grad], every, experts)
     later = exchanged(items)
-    moment, slopes = part_call(rows[:2], grads[:2], weight, moment)
+    moment, slopes = part_call(rows[:2], grads[:2], weight, moment, 0.9)
     all_slopes = [slopes]
-    (pre,) = ahead_call(rows[2:], [[weight]], depth)
+    (pre,) = ahead_call(rows[3:], [[weight]], depth)
+    moment, slopes = part_call(rows[2:3], grads[2:3], weight, moment, 1.0)
+    all_slopes.append(slopes)
     where = [
-        [(m // 2, m) if m < 2 else (1, m - 2) for m in range(experts)],
+        [(0, m) if m < 2 else (min(m - 1, 2), max(m - 3, 0)) for m in range(experts)],
         [(0, m) for m in range(experts)],
     ]
     weights = [weight]
@@ -513,7 +516,7 @@
             all_slopes = [slopes]
         else:
             moment, slopes, low, rest, scale, stepped, share = round_call(
-                rows[2:], grads[2:], 0, 1.0, pre, weights, moment, parts
+                rows[3:], grads[3:], 0, 1.0, pre, weights, moment, parts
             )
             all_slopes.append(slopes)
         stepped_low, ones, twos = second_call(low, rest, scale, share, weights)

time: 161 us -> 162 us (level)
  waiting for transfers between devices: 80.3 us -> 87.6 us
  starting transfers between devices: 52.4 us -> 46.6 us
    ppermute x19, waiting for transfers between devices: 32.8 us -> 37.6 us  [swapped(): lax.ppermute(block, axis, [(i, i ^ bit) for i in range(lax.axis_size(axis...]
    ppermute x10, starting transfers between devices: 29 us -> 26.1 us  [crossed(): lax.ppermute(block, axis, [((i + (-way if i % 2 else way)) % count, i) fo...]
    ppermute x19, starting transfers between devices: 23.4 us -> 20.5 us  [swapped(): lax.ppermute(block, axis, [(i, i ^ bit) for i in range(lax.axis_size(axis...]
    ppermute x10, waiting for transfers between devices: 47.4 us -> 50 us  [crossed(): lax.ppermute(block, axis, [((i + (-way if i % 2 else way)) % count, i) fo...]
  transfers between devices with their start and end apart: 29 -> 29, of which waited for: 15 -> 14; matrix products, arithmetic and copies ran while one was open for 0% -> 0% of each run, Pallas kernels for 7% -> 7%
where the time goes in v8:
time: 162 us
  waiting for transfers between devices  87.6 us (54%)
  starting transfers between devices  46.6 us (29%)
  Pallas kernels  24.4 us (15%)
  local copies, waits for them, and re-layouts  1.82 us (1%)
    ppermute x10, waiting for transfers between devices, crossed(): lax.ppermute(block, axis, [((i + (-way if i % 2 else way)) % count, i) fo...  50 us
    ppermute x19, waiting for transfers between devices, swapped(): lax.ppermute(block, axis, [(i, i ^ bit) for i in range(lax.axis_size(axis...  37.6 us
    ppermute x10, starting transfers between devices, crossed(): lax.ppermute(block, axis, [((i + (-way if i % 2 else way)) % count, i) fo...  26.1 us
    ppermute x19, starting transfers between devices, swapped(): lax.ppermute(block, axis, [(i, i ^ bit) for i in range(lax.axis_size(axis...  20.5 us
    pallas_call x2, Pallas kernels, round_call(): pl.pallas_call(lambda *refs: round_kernel(sizes, place, decay, refs), out...  8.13 us
    pallas_call x4, Pallas kernels, backward_call(): pl.pallas_call(lambda *refs: backward_kernel(sizes, where, refs), out_sha...  3.28 us
  transfers between devices with their start and end apart: 29, of which 14 were waited for; matrix products, arithmetic and copies ran while one was open for 0% of the time, Pallas kernels for 7%

profile of v8, /device:TPU:0, one launch (start us, length us, event | category | flops | bytes accessed | tf_op | source)
XLA Modules:
  0.0 162.2 jit_solution(15552505987790722675)
XLA Ops:
  1.4 1.5 picks.1
  2.9 2.5 %collective-permute-start.3 = (bf16[128,1024]{1,0:T(8,128)(2,1)S(1)}, bf16[128,1024]{1,0:T(8,128)(2,1)S(1)}, u32[]{:S(2)}, u32[]{:S(2)}) collective-permute-start(bf16[128,1024]{1,0:T(8,128)(2,1)S(1)} %get-tuple-element.61), channel_id=1, source_target_pairs={{0,24},{8,16},{16,8},{24,0},{1,25},{9,17},{17,9},{25,1},{2,26},{10... | collective-permute-start | bytes 786440 | tf_op jit(solution)/shard_map/ppermute | solution.py:26
  6.5 1.0 copy-done.2
  8.0 2.0 %collective-permute-start.7 = (bf16[128,512]{1,0:T(8,128)(2,1)S(1)}, bf16[128,512]{1,0:T(8,128)(2,1)S(1)}, u32[]{:S(2)}, u32[]{:S(2)}) collective-permute-start(bf16[128,512]{1,0:T(8,128)(2,1)S(1)} %get-tuple-element.69), channel_id=1, source_target_pairs={{0,16},{8,24},{16,0},{24,8},{1,17},{9,25},{17,1},{25,9},{2,18},{10... | collective-permute-start | bytes 393224 | tf_op jit(solution)/shard_map/ppermute | solution.py:26
  10.0 2.1 %collective-permute-done.3.refs_0_.refs_2_ = bf16[128,1024]{1,0:T(8,128)(2,1)S(1)} collective-permute-done((bf16[128,1024]{1,0:T(8,128)(2,1)S(1)}, bf16[128,1024]{1,0:T(8,128)(2,1)S(1)}, u32[]{:S(2)}, u32[]{:S(2)}) %collective-permute-start.3) | collective-permute-done | bytes 262176 | tf_op jit(solution)/shard_map/ppermute | solution.py:26
  12.1 2.2 %collective-permute-start.8 = (bf16[128,512]{1,0:T(8,128)(2,1)S(1)}, bf16[128,512]{1,0:T(8,128)(2,1)S(1)}, u32[]{:S(2)}, u32[]{:S(2)}) collective-permute-start(bf16[128,512]{1,0:T(8,128)(2,1)S(1)} %get-tuple-element.71), channel_id=1, source_target_pairs={{0,24},{8,16},{16,8},{24,0},{1,25},{9,17},{17,9},{25,1},{2,26},{10... | collective-permute-start | bytes 393224 | tf_op jit(solution)/shard_map/ppermute | solution.py:26
  15.5 6.0 %collective-permute-done.7.refs_3_ = bf16[128,512]{1,0:T(8,128)(2,1)S(1)} collective-permute-done((bf16[128,512]{1,0:T(8,128)(2,1)S(1)}, bf16[128,512]{1,0:T(8,128)(2,1)S(1)}, u32[]{:S(2)}, u32[]{:S(2)}) %collective-permute-start.7) | collective-permute-done | bytes 131104 | tf_op jit(solution)/shard_map/ppermute | solution.py:26
  22.3 1.1 collective-permute-done.8.refs_3_
  23.4 3.8 %muon_round.2 = (f32[1024,512]{1,0:T(8,128)S(1)}, bf16[128,512]{1,0:T(8,128)(2,1)S(1)}, bf16[1024,512]{1,0:T(8,128)(2,1)S(1)}, bf16[512,512]{1,0:T(8,128)(2,1)S(...) custom-call(f32[128,512]{1,0:T(8,128)S(1)} %ahead.2.refs_0_, ...), custom_call_target="tpu_custom_call" | custom-call | tf_op jit(solution)/shard_map/muon_round/pallas_call | solution.py:273
  27.2 1.4 second_half.2
  28.6 4.6 %collective-permute-start.10 = (bf16[640,512]{1,0:T(8,128)(2,1)S(1)}, bf16[640,512]{1,0:T(8,128)(2,1)S(1)}, u32[]{:S(2)}, u32[]{:S(2)}) collective-permute-start(bf16[640,512]{1,0:T(8,128)(2,1)S(1)} %get-tuple-element.78), channel_id=1, source_target_pairs={{2,0},{7,1},{4,2},{1,3},{6,4},{3,5},{0,6},{5,7},{10,8},{15,9},{12,... | collective-permute-start | bytes 1966088 | tf_op jit(solution)/shard_map/ppermute | solution.py:31
  33.6 1.6 collective-permute-start.11
  35.2 15.9 %collective-permute-done.13.refs_15_ = bf16[128,512]{1,0:T(8,128)(2,1)S(1)} collective-permute-done((bf16[128,512]{1,0:T(8,128)(2,1)S(1)}, bf16[128,512]{1,0:T(8,128)(2,1)S(1)}, u32[]{:S(2)}, u32[]{:S(2)}) %collective-permute-start.13) | collective-permute-done | bytes 131104 | tf_op jit(solution)/shard_map/ppermute | solution.py:31
  51.3 2.3 %collective-permute-start.14 = (bf16[768,512]{1,0:T(8,128)(2,1)S(1)}, bf16[768,512]{1,0:T(8,128)(2,1)S(1)}, u32[]{:S(2)}, u32[]{:S(2)}) collective-permute-start(bf16[768,512]{1,0:T(8,128)(2,1)S(1)} %add_convert_fusion.1), channel_id=1, source_target_pairs={{0,1},{1,0},{2,3},{3,2},{4,5},{5,4},{6,7},{7,6},{8,9},{9,8},{10,11... | collective-permute-start | bytes 2359304 | tf_op jit(solution)/shard_map/ppermute | solution.py:26
  53.6 17.3 %collective-permute-start.9 = (bf16[256,512]{1,0:T(8,128)(2,1)S(1)}, bf16[256,512]{1,0:T(8,128)(2,1)S(1)}, u32[]{:S(2)}, u32[]{:S(2)}) collective-permute-start(bf16[256,512]{1,0:T(8,128)(2,1)S(1)} %get-tuple-element.76.refs_3_), channel_id=1, source_target_pairs={{2,0},{7,1},{4,2},{1,3},{6,4},{3,5},{0,6},{5,7},{10,8},{15,9},{12,... | collective-permute-start | bytes 786440 | tf_op jit(solution)/shard_map/ppermute | solution.py:31
  71.6 1.6 collective-permute-start.1
  73.2 1.6 %collective-permute-done.9.refs_6_.refs_13_ = bf16[256,512]{1,0:T(8,128)(2,1)S(1)} collective-permute-done((bf16[256,512]{1,0:T(8,128)(2,1)S(1)}, bf16[256,512]{1,0:T(8,128)(2,1)S(1)}, u32[]{:S(2)}, u32[]{:S(2)}) %collective-permute-start.9) | collective-permute-done | bytes 262176 | tf_op jit(solution)/shard_map/ppermute | solution.py:31
  75.5 8.1 %collective-permute-done.1.refs_2_.refs_4_.refs_8_ = bf16[128,1536]{1,0:T(8,128)(2,1)S(1)} collective-permute-done((bf16[128,1536]{1,0:T(8,128)(2,1)S(1)}, bf16[128,1536]{1,0:T(8,128)(2,1)S(1)}, u32[]{:S(2)}, u32[]{:S(2)}) %collective-permute-start.1) | collective-permute-done | bytes 393248 | tf_op jit(solution)/shard_map/ppermute | solution.py:26
  83.6 7.3 %collective-permute-done.2.refs_3_.refs_5_.refs_9_ = bf16[128,1536]{1,0:T(8,128)(2,1)S(1)} collective-permute-done((bf16[128,1536]{1,0:T(8,128)(2,1)S(1)}, bf16[128,1536]{1,0:T(8,128)(2,1)S(1)}, u32[]{:S(2)}, u32[]{:S(2)}) %collective-permute-start.2) | collective-permute-done | bytes 393248 | tf_op jit(solution)/shard_map/ppermute | solution.py:26
  92.7 4.3 %muon_round.3 = (f32[1024,512]{1,0:T(8,128)}, bf16[512,512]{1,0:T(8,128)(2,1)S(1)}, bf16[1024,512]{1,0:T(8,128)(2,1)S(1)}, bf16[512,512]{1,0:T(8,128)(2,1)S(1)},...) custom-call(f32[512,512]{1,0:T(8,128)S(1)} %get-tuple-element.81.refs_0_, ...), custom_call_target="tpu_custom_call" | custom-call | tf_op jit(solution)/shard_map/muon_round/pallas_call | solution.py:273
  97.0 1.4 second_half.3
  100.2 1.6 collective-permute-start.27
  101.8 2.0 %collective-permute-start.19 = (bf16[768,512]{1,0:T(8,128)(2,1)S(1)}, bf16[768,512]{1,0:T(8,128)(2,1)S(1)}, u32[]{:S(2)}, u32[]{:S(2)}) collective-permute-start(bf16[768,512]{1,0:T(8,128)(2,1)S(1)} %get-tuple-element.94), channel_id=1, source_target_pairs={{6,0},{3,1},{0,2},{5,3},{2,4},{7,5},{4,6},{1,7},{14,8},{11,9},{8,1... | collective-permute-start | bytes 2359304 | tf_op jit(solution)/shard_map/ppermute | solution.py:31
  103.8 30.6 %collective-permute-done.18.refs_4_ = bf16[128,512]{1,0:T(8,128)(2,1)S(1)} collective-permute-done((bf16[128,512]{1,0:T(8,128)(2,1)S(1)}, bf16[128,512]{1,0:T(8,128)(2,1)S(1)}, u32[]{:S(2)}, u32[]{:S(2)}) %collective-permute-start.18) | collective-permute-done | bytes 131104 | tf_op jit(solution)/shard_map/ppermute | solution.py:31
  135.7 1.6 collective-permute-start.23
  138.2 5.2 %collective-permute-done.28.refs_4_ = bf16[128,1024]{1,0:T(8,128)(2,1)S(1)} collective-permute-done((bf16[128,1024]{1,0:T(8,128)(2,1)S(1)}, bf16[128,1024]{1,0:T(8,128)(2,1)S(1)}, u32[]{:S(2)}, u32[]{:S(2)}) %collective-permute-start.28) | collective-permute-done | bytes 262176 | tf_op jit(solution)/shard_map/ppermute | solution.py:26
  145.0 3.5 %collective-permute-start.21 = (bf16[256,512]{1,0:T(8,128)(2,1)S(1)}, bf16[256,512]{1,0:T(8,128)(2,1)S(1)}, u32[]{:S(2)}, u32[]{:S(2)}) collective-permute-start(bf16[256,512]{1,0:T(8,128)(2,1)S(1)} %add_convert_fusion.2), channel_id=1, source_target_pairs={{0,1},{1,0},{2,3},{3,2},{4,5},{5,4},{6,7},{7,6},{8,9},{9,8},{10,11... | collective-permute-start | bytes 786440 | tf_op jit(solution)/shard_map/ppermute | solution.py:26
  148.4 4.1 %collective-permute-done.24.refs_3_ = bf16[128,1024]{1,0:T(8,128)(2,1)S(1)} collective-permute-done((bf16[128,1024]{1,0:T(8,128)(2,1)S(1)}, bf16[128,1024]{1,0:T(8,128)(2,1)S(1)}, u32[]{:S(2)}, u32[]{:S(2)}) %collective-permute-start.24) | collective-permute-done | bytes 262176 | tf_op jit(solution)/shard_map/ppermute | solution.py:26
  152.5 1.3 finish.2.refs_5_
  153.8 2.8 %collective-permute-done.25.refs_4_ = bf16[128,1024]{1,0:T(8,128)(2,1)S(1)} collective-permute-done((bf16[128,1024]{1,0:T(8,128)(2,1)S(1)}, bf16[128,1024]{1,0:T(8,128)(2,1)S(1)}, u32[]{:S(2)}, u32[]{:S(2)}) %collective-permute-start.25) | collective-permute-done | bytes 262176 | tf_op jit(solution)/shard_map/ppermute | solution.py:26
  156.6 1.3 finish.3
  158.7 1.6 average.2.refs_9_
  (62 shorter events, 16.0 us)
Async XLA Ops:
  1.4 12.9 %copy-start = (f32[1,1,1024,512]{3,2,1,0:T(8,128)S(1)}, f32[1,1,1024,512]{3,2,1,0:T(8,128)}, u32[]{:S(2)}) copy-start(f32[1,1,1024,512]{3,2,1,0:T(8,128)} %param.8) | copy-start | bytes 6291460
  2.9 9.2 %collective-permute-start.3 = (bf16[128,1024]{1,0:T(8,128)(2,1)S(1)}, bf16[128,1024]{1,0:T(8,128)(2,1)S(1)}, u32[]{:S(2)}, u32[]{:S(2)}) collective-permute-start(bf16[128,1024]{1,0:T(8,128)(2,1)S(1)} %get-tuple-element.61), channel_id=1, source_target_pairs={{0,24},{8,16},{16,8},{24,0},{1,25},{9,17},{17,9},{25,1},{2,26},{10... | collective-permute-start | bytes 786440 | tf_op jit(solution)/shard_map/ppermute | solution.py:26
  5.7 8.9 %collective-permute-start.4 = (bf16[128,1024]{1,0:T(8,128)(2,1)S(1)}, bf16[128,1024]{1,0:T(8,128)(2,1)S(1)}, u32[]{:S(2)}, u32[]{:S(2)}) collective-permute-start(bf16[128,1024]{1,0:T(8,128)(2,1)S(1)} %get-tuple-element.64), channel_id=1, source_target_pairs={{0,8},{8,0},{16,24},{24,16},{1,9},{9,1},{17,25},{25,17},{2,10},{10... | collective-permute-start | bytes 786440 | tf_op jit(solution)/shard_map/ppermute | solution.py:26
  6.5 15.1 %collective-permute-start.6 = (bf16[128,1024]{1,0:T(8,128)(2,1)S(1)}, bf16[128,1024]{1,0:T(8,128)(2,1)S(1)}, u32[]{:S(2)}, u32[]{:S(2)}) collective-permute-start(bf16[128,1024]{1,0:T(8,128)(2,1)S(1)} %get-tuple-element.68), channel_id=1, source_target_pairs={{0,16},{8,24},{16,0},{24,8},{1,17},{9,25},{17,1},{25,9},{2,18},{10... | collective-permute-start | bytes 786440 | tf_op jit(solution)/shard_map/ppermute | solution.py:26
  7.5 7.1 %copy-start.4 = (f32[1,1,1024,512]{3,2,1,0:T(8,128)S(1)}, f32[1,1,1024,512]{3,2,1,0:T(8,128)}, u32[]{:S(2)}) copy-start(f32[1,1,1024,512]{3,2,1,0:T(8,128)} %param.9) | copy-start | bytes 6291460
  7.8 6.8 %collective-permute-start.5 = (bf16[128,512]{1,0:T(8,128)(2,1)S(1)}, bf16[128,512]{1,0:T(8,128)(2,1)S(1)}, u32[]{:S(2)}, u32[]{:S(2)}) collective-permute-start(bf16[128,512]{1,0:T(8,128)(2,1)S(1)} %get-tuple-element.66), channel_id=1, source_target_pairs={{0,8},{8,0},{16,24},{24,16},{1,9},{9,1},{17,25},{25,17},{2,10},{10... | collective-permute-start | bytes 393224 | tf_op jit(solution)/shard_map/ppermute | solution.py:26
  8.0 13.6 %collective-permute-start.7 = (bf16[128,512]{1,0:T(8,128)(2,1)S(1)}, bf16[128,512]{1,0:T(8,128)(2,1)S(1)}, u32[]{:S(2)}, u32[]{:S(2)}) collective-permute-start(bf16[128,512]{1,0:T(8,128)(2,1)S(1)} %get-tuple-element.69), channel_id=1, source_target_pairs={{0,16},{8,24},{16,0},{24,8},{1,17},{9,25},{17,1},{25,9},{2,18},{10... | collective-permute-start | bytes 393224 | tf_op jit(solution)/shard_map/ppermute | solution.py:26
  12.1 11.2 %collective-permute-start.8 = (bf16[128,512]{1,0:T(8,128)(2,1)S(1)}, bf16[128,512]{1,0:T(8,128)(2,1)S(1)}, u32[]{:S(2)}, u32[]{:S(2)}) collective-permute-start(bf16[128,512]{1,0:T(8,128)(2,1)S(1)} %get-tuple-element.71), channel_id=1, source_target_pairs={{0,24},{8,16},{16,8},{24,0},{1,25},{9,17},{17,9},{25,1},{2,26},{10... | collective-permute-start | bytes 393224 | tf_op jit(solution)/shard_map/ppermute | solution.py:26
  28.5 42.4 %copy-start.3 = (bf16[2,256,512]{2,1,0:T(8,128)(2,1)S(1)}, bf16[2,256,512]{2,1,0:T(8,128)(2,1)}, u32[]{:S(2)}) copy-start(bf16[2,256,512]{2,1,0:T(8,128)(2,1)} %refs_1_.5) | copy-start | bytes 1572868
  28.6 22.6 %collective-permute-start.10 = (bf16[640,512]{1,0:T(8,128)(2,1)S(1)}, bf16[640,512]{1,0:T(8,128)(2,1)S(1)}, u32[]{:S(2)}, u32[]{:S(2)}) collective-permute-start(bf16[640,512]{1,0:T(8,128)(2,1)S(1)} %get-tuple-element.78), channel_id=1, source_target_pairs={{2,0},{7,1},{4,2},{1,3},{6,4},{3,5},{0,6},{5,7},{10,8},{15,9},{12,... | collective-permute-start | bytes 1966088 | tf_op jit(solution)/shard_map/ppermute | solution.py:31
  33.1 18.0 %collective-permute-start.13 = (bf16[128,512]{1,0:T(8,128)(2,1)S(1)}, bf16[128,512]{1,0:T(8,128)(2,1)S(1)}, u32[]{:S(2)}, u32[]{:S(2)}) collective-permute-start(bf16[128,512]{1,0:T(8,128)(2,1)S(1)} %get-tuple-element.80), channel_id=1, source_target_pairs={{2,0},{7,1},{4,2},{1,3},{6,4},{3,5},{0,6},{5,7},{10,8},{15,9},{12,... | collective-permute-start | bytes 393224 | tf_op jit(solution)/shard_map/ppermute | solution.py:31
  33.6 57.4 %collective-permute-start.11 = (bf16[768,512]{1,0:T(8,128)(2,1)S(1)}, bf16[768,512]{1,0:T(8,128)(2,1)S(1)}, u32[]{:S(2)}, u32[]{:S(2)}) collective-permute-start(bf16[768,512]{1,0:T(8,128)(2,1)S(1)} %get-tuple-element.79), channel_id=1, source_target_pairs={{6,0},{3,1},{0,2},{5,3},{2,4},{7,5},{4,6},{1,7},{14,8},{11,9},{8,1... | collective-permute-start | bytes 2359304 | tf_op jit(solution)/shard_map/ppermute | solution.py:31
  51.3 39.6 %collective-permute-start.14 = (bf16[768,512]{1,0:T(8,128)(2,1)S(1)}, bf16[768,512]{1,0:T(8,128)(2,1)S(1)}, u32[]{:S(2)}, u32[]{:S(2)}) collective-permute-start(bf16[768,512]{1,0:T(8,128)(2,1)S(1)} %add_convert_fusion.1), channel_id=1, source_target_pairs={{0,1},{1,0},{2,3},{3,2},{4,5},{5,4},{6,7},{7,6},{8,9},{9,8},{10,11... | collective-permute-start | bytes 2359304 | tf_op jit(solution)/shard_map/ppermute | solution.py:26
  53.6 21.2 %collective-permute-start.9 = (bf16[256,512]{1,0:T(8,128)(2,1)S(1)}, bf16[256,512]{1,0:T(8,128)(2,1)S(1)}, u32[]{:S(2)}, u32[]{:S(2)}) collective-permute-start(bf16[256,512]{1,0:T(8,128)(2,1)S(1)} %get-tuple-element.76.refs_3_), channel_id=1, source_target_pairs={{2,0},{7,1},{4,2},{1,3},{6,4},{3,5},{0,6},{5,7},{10,8},{15,9},{12,... | collective-permute-start | bytes 786440 | tf_op jit(solution)/shard_map/ppermute | solution.py:31
  71.5 3.4 %collective-permute-start = (bf16[128,1536]{1,0:T(8,128)(2,1)S(1)}, bf16[128,1536]{1,0:T(8,128)(2,1)S(1)}, u32[]{:S(2)}, u32[]{:S(2)}) collective-permute-start(bf16[128,1536]{1,0:T(8,128)(2,1)S(1)} %get-tuple-element.58), channel_id=1, source_target_pairs={{0,8},{8,0},{16,24},{24,16},{1,9},{9,1},{17,25},{25,17},{2,10},{10... | collective-permute-start | bytes 1179656 | tf_op jit(solution)/shard_map/ppermute | solution.py:26
  71.6 12.1 %collective-permute-start.1 = (bf16[128,1536]{1,0:T(8,128)(2,1)S(1)}, bf16[128,1536]{1,0:T(8,128)(2,1)S(1)}, u32[]{:S(2)}, u32[]{:S(2)}) collective-permute-start(bf16[128,1536]{1,0:T(8,128)(2,1)S(1)} %get-tuple-element.59), channel_id=1, source_target_pairs={{0,16},{8,24},{16,0},{24,8},{1,17},{9,25},{17,1},{25,9},{2,18},{10... | collective-permute-start | bytes 1179656 | tf_op jit(solution)/shard_map/ppermute | solution.py:26
  74.8 16.2 %collective-permute-start.2 = (bf16[128,1536]{1,0:T(8,128)(2,1)S(1)}, bf16[128,1536]{1,0:T(8,128)(2,1)S(1)}, u32[]{:S(2)}, u32[]{:S(2)}) collective-permute-start(bf16[128,1536]{1,0:T(8,128)(2,1)S(1)} %get-tuple-element.60), channel_id=1, source_target_pairs={{0,24},{8,16},{16,8},{24,0},{1,25},{9,17},{17,9},{25,1},{2,26},{10... | collective-permute-start | bytes 1179656 | tf_op jit(solution)/shard_map/ppermute | solution.py:26
  74.9 16.1 %collective-permute-start.12 = (bf16[256,512]{1,0:T(8,128)(2,1)S(1)}, bf16[256,512]{1,0:T(8,128)(2,1)S(1)}, u32[]{:S(2)}, u32[]{:S(2)}) collective-permute-start(bf16[256,512]{1,0:T(8,128)(2,1)S(1)} %add_convert_fusion.3), channel_id=1, source_target_pairs={{0,1},{1,0},{2,3},{3,2},{4,5},{5,4},{6,7},{7,6},{8,9},{9,8},{10,11... | collective-permute-start | bytes 786440 | tf_op jit(solution)/shard_map/ppermute | solution.py:26
  83.6 9.0 %collective-permute-start.15 = (bf16[256,512]{1,0:T(8,128)(2,1)S(1)}, bf16[256,512]{1,0:T(8,128)(2,1)S(1)}, u32[]{:S(2)}, u32[]{:S(2)}) collective-permute-start(bf16[256,512]{1,0:T(8,128)(2,1)S(1)} %get-tuple-element.84), channel_id=1, source_target_pairs={{6,0},{3,1},{0,2},{5,3},{2,4},{7,5},{4,6},{1,7},{14,8},{11,9},{8,1... | collective-permute-start | bytes 786440 | tf_op jit(solution)/shard_map/ppermute | solution.py:31
  98.3 36.1 %collective-permute-start.17 = (bf16[640,512]{1,0:T(8,128)(2,1)S(1)}, bf16[640,512]{1,0:T(8,128)(2,1)S(1)}, u32[]{:S(2)}, u32[]{:S(2)}) collective-permute-start(bf16[640,512]{1,0:T(8,128)(2,1)S(1)} %get-tuple-element.92), channel_id=1, source_target_pairs={{2,0},{7,1},{4,2},{1,3},{6,4},{3,5},{0,6},{5,7},{10,8},{15,9},{12,... | collective-permute-start | bytes 1966088 | tf_op jit(solution)/shard_map/ppermute | solution.py:31
  98.4 36.0 %collective-permute-start.18 = (bf16[128,512]{1,0:T(8,128)(2,1)S(1)}, bf16[128,512]{1,0:T(8,128)(2,1)S(1)}, u32[]{:S(2)}, u32[]{:S(2)}) collective-permute-start(bf16[128,512]{1,0:T(8,128)(2,1)S(1)} %get-tuple-element.93), channel_id=1, source_target_pairs={{2,0},{7,1},{4,2},{1,3},{6,4},{3,5},{0,6},{5,7},{10,8},{15,9},{12,... | collective-permute-start | bytes 393224 | tf_op jit(solution)/shard_map/ppermute | solution.py:31
  99.3 35.5 %collective-permute-start.26 = (bf16[128,1024]{1,0:T(8,128)(2,1)S(1)}, bf16[128,1024]{1,0:T(8,128)(2,1)S(1)}, u32[]{:S(2)}, u32[]{:S(2)}) collective-permute-start(bf16[128,1024]{1,0:T(8,128)(2,1)S(1)} %get-tuple-element.106), channel_id=1, source_target_pairs={{0,8},{8,0},{16,24},{24,16},{1,9},{9,1},{17,25},{25,17},{2,10},{10... | collective-permute-start | bytes 786440 | tf_op jit(solution)/shard_map/ppermute | solution.py:26
  100.2 35.5 %collective-permute-start.27 = (bf16[128,1024]{1,0:T(8,128)(2,1)S(1)}, bf16[128,1024]{1,0:T(8,128)(2,1)S(1)}, u32[]{:S(2)}, u32[]{:S(2)}) collective-permute-start(bf16[128,1024]{1,0:T(8,128)(2,1)S(1)} %get-tuple-element.107), channel_id=1, source_target_pairs={{0,16},{8,24},{16,0},{24,8},{1,17},{9,25},{17,1},{25,9},{2,18},{10... | collective-permute-start | bytes 786440 | tf_op jit(solution)/shard_map/ppermute | solution.py:26
  101.8 56.9 %collective-permute-start.19 = (bf16[768,512]{1,0:T(8,128)(2,1)S(1)}, bf16[768,512]{1,0:T(8,128)(2,1)S(1)}, u32[]{:S(2)}, u32[]{:S(2)}) collective-permute-start(bf16[768,512]{1,0:T(8,128)(2,1)S(1)} %get-tuple-element.94), channel_id=1, source_target_pairs={{6,0},{3,1},{0,2},{5,3},{2,4},{7,5},{4,6},{1,7},{14,8},{11,9},{8,1... | collective-permute-start | bytes 2359304 | tf_op jit(solution)/shard_map/ppermute | solution.py:31
  134.7 24.0 %collective-permute-start.22 = (bf16[768,512]{1,0:T(8,128)(2,1)S(1)}, bf16[768,512]{1,0:T(8,128)(2,1)S(1)}, u32[]{:S(2)}, u32[]{:S(2)}) collective-permute-start(bf16[768,512]{1,0:T(8,128)(2,1)S(1)} %add_convert_fusion), channel_id=1, source_target_pairs={{0,1},{1,0},{2,3},{3,2},{4,5},{5,4},{6,7},{7,6},{8,9},{9,8},{10,11... | collective-permute-start | bytes 2359304 | tf_op jit(solution)/shard_map/ppermute | solution.py:26
  134.7 8.6 %collective-permute-start.28 = (bf16[128,1024]{1,0:T(8,128)(2,1)S(1)}, bf16[128,1024]{1,0:T(8,128)(2,1)S(1)}, u32[]{:S(2)}, u32[]{:S(2)}) collective-permute-start(bf16[128,1024]{1,0:T(8,128)(2,1)S(1)} %get-tuple-element.108), channel_id=1, source_target_pairs={{0,24},{8,16},{16,8},{24,0},{1,25},{9,17},{17,9},{25,1},{2,26},{10... | collective-permute-start | bytes 786440 | tf_op jit(solution)/shard_map/ppermute | solution.py:26
  134.8 9.2 %collective-permute-start.16 = (bf16[256,512]{1,0:T(8,128)(2,1)S(1)}, bf16[256,512]{1,0:T(8,128)(2,1)S(1)}, u32[]{:S(2)}, u32[]{:S(2)}) collective-permute-start(bf16[256,512]{1,0:T(8,128)(2,1)S(1)} %get-tuple-element.89.refs_3_), channel_id=1, source_target_pairs={{2,0},{7,1},{4,2},{1,3},{6,4},{3,5},{0,6},{5,7},{10,8},{15,9},{12,... | collective-permute-start | bytes 786440 | tf_op jit(solution)/shard_map/ppermute | solution.py:31
  135.7 9.2 %collective-permute-start.23 = (bf16[128,1024]{1,0:T(8,128)(2,1)S(1)}, bf16[128,1024]{1,0:T(8,128)(2,1)S(1)}, u32[]{:S(2)}, u32[]{:S(2)}) collective-permute-start(bf16[128,1024]{1,0:T(8,128)(2,1)S(1)} %get-tuple-element.99), channel_id=1, source_target_pairs={{0,8},{8,0},{16,24},{24,16},{1,9},{9,1},{17,25},{25,17},{2,10},{10... | collective-permute-start | bytes 786440 | tf_op jit(solution)/shard_map/ppermute | solution.py:26
  143.3 9.2 %collective-permute-start.24 = (bf16[128,1024]{1,0:T(8,128)(2,1)S(1)}, bf16[128,1024]{1,0:T(8,128)(2,1)S(1)}, u32[]{:S(2)}, u32[]{:S(2)}) collective-permute-start(bf16[128,1024]{1,0:T(8,128)(2,1)S(1)} %get-tuple-element.100), channel_id=1, source_target_pairs={{0,16},{8,24},{16,0},{24,8},{1,17},{9,25},{17,1},{25,9},{2,18},{10... | collective-permute-start | bytes 786440 | tf_op jit(solution)/shard_map/ppermute | solution.py:26
  144.0 12.6 %collective-permute-start.25 = (bf16[128,1024]{1,0:T(8,128)(2,1)S(1)}, bf16[128,1024]{1,0:T(8,128)(2,1)S(1)}, u32[]{:S(2)}, u32[]{:S(2)}) collective-permute-start(bf16[128,1024]{1,0:T(8,128)(2,1)S(1)} %get-tuple-element.101), channel_id=1, source_target_pairs={{0,24},{8,16},{16,8},{24,0},{1,25},{9,17},{17,9},{25,1},{2,26},{10... | collective-permute-start | bytes 786440 | tf_op jit(solution)/shard_map/ppermute | solution.py:26
  145.0 13.7 %collective-permute-start.21 = (bf16[256,512]{1,0:T(8,128)(2,1)S(1)}, bf16[256,512]{1,0:T(8,128)(2,1)S(1)}, u32[]{:S(2)}, u32[]{:S(2)}) collective-permute-start(bf16[256,512]{1,0:T(8,128)(2,1)S(1)} %add_convert_fusion.2), channel_id=1, source_target_pairs={{0,1},{1,0},{2,3},{3,2},{4,5},{5,4},{6,7},{7,6},{8,9},{9,8},{10,11... | collective-permute-start | bytes 786440 | tf_op jit(solution)/shard_map/ppermute | solution.py:26
  152.5 8.6 %collective-permute-start.20 = (bf16[256,512]{1,0:T(8,128)(2,1)S(1)}, bf16[256,512]{1,0:T(8,128)(2,1)S(1)}, u32[]{:S(2)}, u32[]{:S(2)}) collective-permute-start(bf16[256,512]{1,0:T(8,128)(2,1)S(1)} %get-tuple-element.95), channel_id=1, source_target_pairs={{6,0},{3,1},{0,2},{5,3},{2,4},{7,5},{4,6},{1,7},{14,8},{11,9},{8,1... | collective-permute-start | bytes 786440 | tf_op jit(solution)/shard_map/ppermute | solution.py:31
  (3 other events, 6.6 us)
